TPU v7x, 512 devices: a whole 4x4x16 slice. The times are simulated.
512 devices in a mesh: fsdp: 16 (over x, y_lo, core), tm: 32 (over y_hi, z).
Axes of the slice: x: 4, y: 4 (y_hi: 2, y_lo: 2; y = y_hi * 2 + y_lo), z: 16, core: 2. Of those that a mesh axis runs over, the one named last changes fastest.
Arguments:
- tokens: bfloat16 [32, 32, 256, 1024], P('fsdp', 'tm'), may hold values from -6 to 6
- spatial_gain: float32 [1024], replicated, may hold values from 0.25 to 1.75
- spatial_qkv: bfloat16 [1024, 1536], P('fsdp'), may hold values from -16 to 16
- spatial_out: bfloat16 [512, 1024], P('fsdp'), may hold values from -0.25 to 0.25
- temporal_gain: float32 [1024], replicated, may hold values from 0.25 to 1.75
- temporal_qkv: bfloat16 [1024, 1536], P('fsdp'), may hold values from -16 to 16
- temporal_out: bfloat16 [512, 1024], P('fsdp'), may hold values from -0.25 to 0.25
Outputs:
- encoded: bfloat16 [32, 32, 256, 1024], P('fsdp', 'tm')
All inputs are finite; a program needn't handle non-finite values.
Results may differ from a plain program's by a relative error of at most 0.0061.
Values may be sent and summed in bfloat16 or wider, within the bound.
No kernel may reach another device: no remote copies, remote signals or barrier semaphores. Data moves between devices by JAX's collectives and lax.ppermute only.
A program may use at most 64 MiB of HBM per device.

v0:
```python
import jax
import jax.numpy as jnp
from jax import lax
from jax.sharding import PartitionSpec as P

HEAD = 64
HEADS = 8
INNER = 512


EPSILON = 1e-06


def laid_out(pieces, dim):
    pieces = jnp.moveaxis(pieces, 0, dim)
    shape = pieces.shape
    return pieces.reshape(*shape[:dim], shape[dim] * shape[dim + 1], *shape[dim + 2 :])


def sent_to_all(shard, axis):
    copies = jnp.broadcast_to(shard, (lax.axis_size(axis), *shard.shape))
    return lax.all_to_all(copies, axis, split_axis=0, concat_axis=0, tiled=True)


def gathered_copies(shard, axis, dim):
    return laid_out(sent_to_all(shard, axis), dim)


def norm_rows(source, norm_gain):
    values = source.astype(jnp.float32)
    centre = values - jnp.mean(values, axis=-1, keepdims=True)
    spread = jnp.mean(centre * centre, axis=-1, keepdims=True)
    return (centre * lax.rsqrt(spread + EPSILON) * norm_gain).astype(jnp.bfloat16)


def attention_core(projected):
    inner_width = projected.shape[-1] // 3
    lead_shape = projected.shape[:-1]
    queries = projected[..., :inner_width].reshape(lead_shape + (HEADS, HEAD))
    key_rows = projected[..., inner_width : 2 * inner_width].reshape(lead_shape + (HEADS, HEAD))
    value_rows = (
        projected[..., 2 * inner_width :].astype(jnp.bfloat16).reshape(lead_shape + (HEADS, HEAD))
    )
    scores = jnp.einsum("blmhe,bkmhe->bmhlk", queries, key_rows) * HEAD ** (-0.5)
    row_max = jnp.max(scores, axis=-1, keepdims=True)
    exponent = jnp.exp(scores - row_max)
    weights = (exponent / jnp.sum(exponent, axis=-1, keepdims=True)).astype(jnp.bfloat16)
    context = jnp.einsum(
        "bmhlk,bkmhe->blmhe", weights, value_rows, preferred_element_type=jnp.float32
    )
    return context.astype(jnp.bfloat16).reshape(lead_shape + (inner_width,))


def project_inputs(normed, weight):

    def add_rows(running, segment, offset):
        return jnp.dot(normed, segment, preferred_element_type=jnp.float32)

    initial = jnp.zeros((normed.shape[0], weight.shape[1]), jnp.float32)
    return add_rows(initial, lax.all_gather(weight, "fsdp", axis=0, tiled=True), jnp.int32(0))


def project_outputs(context, weight):

    def add_rows(running, segment, offset):
        return jnp.dot(context, segment, preferred_element_type=jnp.float32)

    initial = jnp.zeros((context.shape[0], weight.shape[1]), jnp.float32)
    return add_rows(initial, gathered_copies(weight, "fsdp", 0), jnp.int32(0))


def shards(
    tokens, spatial_gain, spatial_qkv, spatial_out, temporal_gain, temporal_qkv, temporal_out
):
    clip_count, frames, places, feature_width = tokens.shape
    row_count = clip_count * frames * places
    normed = norm_rows(tokens, spatial_gain).reshape(row_count, feature_width)
    projected = project_inputs(normed, spatial_qkv).reshape(
        clip_count * frames, places, 1, 3 * INNER
    )
    context = attention_core(projected).reshape(row_count, INNER)
    middle = (
        tokens.reshape(row_count, feature_width).astype(jnp.float32)
        + project_outputs(context, spatial_out)
    ).astype(jnp.bfloat16)
    middle = middle.reshape(clip_count, frames, places, feature_width)
    arrived = lax.all_to_all(middle, "tm", split_axis=2, concat_axis=1, tiled=True)
    full_frames = arrived.shape[1]
    few_places = arrived.shape[2]
    normed_t = norm_rows(arrived, temporal_gain).reshape(row_count, feature_width)
    projected_t = project_inputs(normed_t, temporal_qkv).reshape(
        clip_count, full_frames, few_places, 3 * INNER
    )
    context_t = attention_core(projected_t)
    returned_ctx = lax.all_to_all(context_t, "tm", split_axis=1, concat_axis=2, tiled=True)
    finished = middle.reshape(row_count, feature_width).astype(jnp.float32) + project_outputs(
        returned_ctx.reshape(row_count, INNER), temporal_out
    )
    return finished.astype(jnp.bfloat16).reshape(clip_count, frames, places, feature_width)


def solution(mesh):
    placed = (
        P("fsdp", "tm", None, None),
        P(),
        P("fsdp", None),
        P("fsdp", None),
        P(),
        P("fsdp", None),
        P("fsdp", None),
    )
    return jax.shard_map(
        shards, mesh=mesh, in_specs=placed, out_specs=P("fsdp", "tm", None, None), check_vma=False
    )
```

profile of v0, /device:TPU:32, one launch (start us, length us, event | category | flops | bytes accessed | tf_op | source)
XLA Modules:
  0.0 228.6 jit_solution(6030307744431917893)
XLA Ops:
  6.5 0.7 all-gather.3.cloned.1.call-update
  7.3 1.9 broadcast_in_dim.4
  9.2 5.6 %all-to-all-start = ((bf16[16,32,1024]{2,1,0:T(8,128)(2,1)}), bf16[16,32,1024]{2,1,0:T(8,128)(2,1)}, u32[]{:S(2)}, u32[]{:S(2)}) async-start(bf16[16,32,1024]{2,1,0:T(8,128)(2,1)} %broadcast_in_dim.4), calls=%async_computation | async-start | bytes 2097152 | tf_op jit(solution)/shard_map/all_to_all | solution.py:22
  14.9 0.7 all-gather.5.cloned.1.call-update
  16.2 40.8 %all-gather.3.cloned.1.call-done = bf16[1024,1536]{1,0:T(8,128)(2,1)} async-done(((bf16[64,1536]{1,0:T(8,128)(2,1)}), bf16[1024,1536]{1,0:T(8,128)(2,1)}) %all-gather.3.cloned.1.call-update) | async-done | bytes 3145744 | tf_op jit(solution)/shard_map/all_gather | solution.py:60
  57.0 3.8 %convolution_bitcast_fusion = bf16[2,256,1,1536]{3,1,0,2:T(8,128)(2,1)S(1)} fusion(bf16[1024,1536]{1,0:T(8,128)(2,1)} %all-gather.3.cloned.1.call-done, bf16[2,1,256,1024]{3,2,1,0:T(8,128)(2,1)S(1)} %copy-done, f32[1024]{0:T(1024)S(1)} %copy-done.4, f32[2,256]{1,0:T(2,128)S(1)} %add_rsqrt_fusion.1, f32[2,256]{1,0:T(2,128)S(1)} %broadcast_multiply_fusion.1), kind=kOutput, calls=%fused_computation.6 | convolution fusion | flops 1613234176 | bytes 5775360 | tf_op jit(solution)/shard_map/dot_general | solution.py:57
  61.6 3.5 %fusion.39 = (f32[2,8,256]{2,1,0:T(8,128)S(1)}, f32[2,8,256,256]{2,3,1,0:T(8,128)}) fusion(bf16[2,256,8,64]{1,3,2,0:T(8,128)(2,1)S(1)} %bitcast.67, bf16[2,256,8,64]{1,3,2,0:T(8,128)(2,1)S(1)} %bitcast.69), kind=kOutput, calls=%fused_computation.56 | convolution fusion | flops 137363712 | bytes 5259264 | tf_op jit(solution)/shard_map/sub | solution.py:46
  65.0 2.7 %fusion.20 = bf16[2,256,1,8,64]{1,4,3,0,2:T(8,128)(2,1)S(1)} fusion(bf16[2,256,8,64]{1,3,2,0:T(8,128)(2,1)S(1)} %bitcast.70, f32[2,8,256,256]{2,3,1,0:T(8,128)} %get-tuple-element.12, f32[2,8,256]{2,1,0:T(8,128)S(1)} %get-tuple-element.11), kind=kOutput, calls=%fused_computation.33 | convolution fusion | flops 136577024 | bytes 5259264 | tf_op jit(solution)/shard_map/bmhlk,bkmhe->blmhe/dot_general | solution.py:48
  68.4 2.0 fusion.8
  70.3 1.1 copy.83
  71.4 71.4 %all_to_all.28 = bf16[2,1,256,1024]{3,0,1,2:T(2,128)(2,1)S(1)} all-to-all(bf16[2,1,256,1024]{3,0,1,2:T(2,128)(2,1)S(1)} %copy.83), channel_id=1, replica_groups=mesh['fsdp'=16,'tm'=32] {'tm'}, dimensions={2} | all-to-all | bytes 2097152 | tf_op jit(solution)/shard_map/all_to_all | solution.py:87
  142.9 0.9 convert_reduce_fusion.1
  143.8 1.8 multiply_reduce_fusion.1
  146.2 0.9 convert.12
  147.1 4.0 %fusion.5 = bf16[2,32,8,1536]{3,2,1,0:T(8,128)(2,1)S(1)} fusion(bf16[1024,1536]{1,0:T(8,128)(2,1)} %all-gather.5.cloned.1.call-done, f32[2,32,8,1024]{3,0,2,1:T(2,128)S(1)} %convert.12, f32[1024]{0:T(1024)S(1)} %copy-done.5, f32[2,32,8]{2,1,0:T(8,128)S(1)} %copy.118, f32[2,32,8]{2,1,0:T(8,128)S(1)} %copy.119), kind=kOutput, calls=%fused_computation.7 | convolution fusion | flops 1612709888 | bytes 6823936 | tf_op jit(solution)/shard_map/dot_general | solution.py:57
  152.3 1.5 reshape.162
  153.9 3.2 %fusion.40 = (f32[2,8,8,32]{3,2,1,0:T(8,128)S(1)}, f32[2,8,8,32,32]{3,4,2,1,0:T(8,128)}) fusion(bf16[2,32,8,8,64]{4,3,2,1,0:T(8,128)(2,1)S(1)} %reshape.164, bf16[2,32,8,8,64]{4,3,2,1,0:T(8,128)(2,1)S(1)} %reshape.163), kind=kOutput, calls=%fused_computation.57 | convolution fusion | flops 17170464 | bytes 1589248 | tf_op jit(solution)/shard_map/sub | solution.py:46
  157.1 2.9 %fusion.18 = bf16[2,32,8,8,64]{4,1,3,2,0:T(8,128)(2,1)S(1)} fusion(f32[2,8,8,32,32]{3,4,2,1,0:T(8,128)} %get-tuple-element.14, bf16[2,32,8,8,64]{4,3,2,1,0:T(8,128)(2,1)} %reshape.162, f32[2,8,8,32]{3,2,1,0:T(8,128)S(1)} %get-tuple-element.13), kind=kOutput, calls=%fused_computation.31 | convolution fusion | flops 17301504 | bytes 1589248 | tf_op jit(solution)/shard_map/bmhlk,bkmhe->blmhe/dot_general | solution.py:48
  160.3 0.6 reshape.173
  161.0 37.9 %all_to_all.29 = bf16[2,32,8,512]{3,2,0,1:T(8,128)(2,1)S(1)} all-to-all(bf16[2,32,8,512]{3,2,0,1:T(8,128)(2,1)S(1)} %reshape.173), channel_id=1, replica_groups=mesh['fsdp'=16,'tm'=32] {'tm'}, dimensions={1} | all-to-all | bytes 1048576 | tf_op jit(solution)/shard_map/all_to_all | solution.py:95
  198.8 1.1 broadcast_in_dim.5
  199.9 3.7 %all-to-all-start.3 = ((bf16[16,32,1024]{2,1,0:T(8,128)(2,1)}), bf16[16,32,1024]{2,1,0:T(8,128)(2,1)S(1)}, u32[]{:S(2)}, u32[]{:S(2)}) async-start(bf16[16,32,1024]{2,1,0:T(8,128)(2,1)} %broadcast_in_dim.5), calls=%async_computation.3 | async-start | bytes 2097152 | tf_op jit(solution)/shard_map/all_to_all | solution.py:22
  203.7 16.4 %all-to-all-done.3 = bf16[16,32,1024]{2,1,0:T(8,128)(2,1)S(1)} async-done(((bf16[16,32,1024]{2,1,0:T(8,128)(2,1)}), bf16[16,32,1024]{2,1,0:T(8,128)(2,1)S(1)}, u32[]{:S(2)}, u32[]{:S(2)}) %all-to-all-start.3) | async-done | bytes 1048608 | tf_op jit(solution)/shard_map/all_to_all | solution.py:22
  220.1 1.7 add_convert_fusion
  (36 shorter events, 4.3 us)
Async XLA Ops:
  6.5 9.0 %copy-start = (bf16[2,1,256,1024]{3,2,1,0:T(8,128)(2,1)S(1)}, bf16[2,1,256,1024]{3,2,1,0:T(8,128)(2,1)}, u32[]{:S(2)}) copy-start(bf16[2,1,256,1024]{3,2,1,0:T(8,128)(2,1)} %param.7) | copy-start | bytes 3145732
  6.5 50.5 %all-gather.3.cloned.1.call-start = ((), (), s32[]{:S(2)}) async-start(), calls=%async_computation.4 | async-start | bytes 3342336 | tf_op jit(solution)/shard_map/all_gather | solution.py:60
  9.2 47.8 %copy-start.4 = (f32[1024]{0:T(1024)S(1)}, f32[1024]{0:T(1024)}, u32[]{:S(2)}) copy-start(f32[1024]{0:T(1024)} %param.8) | copy-start | bytes 12292
  9.2 59.2 %all-to-all-start = ((bf16[16,32,1024]{2,1,0:T(8,128)(2,1)}), bf16[16,32,1024]{2,1,0:T(8,128)(2,1)}, u32[]{:S(2)}, u32[]{:S(2)}) async-start(bf16[16,32,1024]{2,1,0:T(8,128)(2,1)} %broadcast_in_dim.4), calls=%async_computation | async-start | bytes 2097152 | tf_op jit(solution)/shard_map/all_to_all | solution.py:22
  14.8 132.3 %all-gather.5.cloned.1.call-start = ((), (), s32[]{:S(2)}) async-start(), calls=%async_computation.5 | async-start | bytes 3342336 | tf_op jit(solution)/shard_map/all_gather | solution.py:60
  70.3 72.5 %copy-start.1 = (bf16[512,1024]{1,0:T(8,128)(2,1)}, bf16[512,1024]{1,0:T(8,128)(2,1)S(1)}, u32[]{:S(2)}) copy-start(bf16[512,1024]{1,0:T(8,128)(2,1)S(1)} %fusion.8) | copy-start | bytes 3145732
  145.6 1.5 copy-start.5
  159.9 38.9 %copy-start.3 = (bf16[32,1024]{1,0:T(8,128)(2,1)S(1)}, bf16[32,1024]{1,0:T(8,128)(2,1)}, u32[]{:S(2)}) copy-start(bf16[32,1024]{1,0:T(8,128)(2,1)} %param.13) | copy-start | bytes 196612
  198.8 21.2 %copy-start.2 = (bf16[512,1024]{1,0:T(8,128)(2,1)S(1)}, bf16[512,1024]{1,0:T(8,128)(2,1)}, u32[]{:S(2)}) copy-start(bf16[512,1024]{1,0:T(8,128)(2,1)} %copy-done.1) | copy-start | bytes 3145732
  199.9 20.1 %all-to-all-start.3 = ((bf16[16,32,1024]{2,1,0:T(8,128)(2,1)}), bf16[16,32,1024]{2,1,0:T(8,128)(2,1)S(1)}, u32[]{:S(2)}, u32[]{:S(2)}) async-start(bf16[16,32,1024]{2,1,0:T(8,128)(2,1)} %broadcast_in_dim.5), calls=%async_computation.3 | async-start | bytes 2097152 | tf_op jit(solution)/shard_map/all_to_all | solution.py:22
Sparse Core Ops, SparseCore 0:
  9.5 47.4 all-gather.2
  59.1 44.3 all-gather.4
where the time goes:
time: 229 us
  blocking collectives  109 us (48%)
  waiting for transfers between devices  58.6 us (26%)
  matrix products  23.6 us (10%)
  between operations  13.6 us (6%)
  local copies, waits for them, and re-layouts  9.84 us (4%)
  starting transfers between devices  9.3 us (4%)
  other arithmetic  4.31 us (2%)
    all_to_all x1, blocking collectives, shards(): lax.all_to_all(middle, 'tm', split_axis=2, concat_axis=1, tiled=True)  71.4 us
    all_gather x2, waiting for transfers between devices, project_inputs(): lax.all_gather(weight, 'fsdp', axis=0, tiled=True)  40.8 us
    all_to_all x1, blocking collectives, shards(): lax.all_to_all(context_t, 'tm', split_axis=1, concat_axis=2, tiled=True)  37.9 us
    all_to_all x2, waiting for transfers between devices, sent_to_all(): return lax.all_to_all(copies, axis, split_axis=0, concat_axis=0, tiled=True)  16.4 us
    all_to_all x2, starting transfers between devices, sent_to_all(): return lax.all_to_all(copies, axis, split_axis=0, concat_axis=0, tiled=True)  9.25 us
    dot_general x2, matrix products, add_rows(): return jnp.dot(normed, segment, preferred_element_type=jnp.float32)  7.8 us
    sub x2, matrix products, attention_core(): exponent = jnp.exp(scores - row_max)  6.63 us
    dot_general x2, matrix products, attention_core(): jnp.einsum('bmhlk,bkmhe->blmhe', weights, value_rows, preferred_element_t...  5.53 us
  transfers between devices with their start and end apart: 4, of which 2 were waited for; matrix products, arithmetic and copies ran while one was open for 9% of the time, Pallas kernels for 0%

commit v1 on v0

v1 whole, which is shorter than its diff:
```python
import functools

import jax
import jax.numpy as jnp
from jax import lax
from jax.experimental import pallas as pl
from jax.experimental.pallas import tpu as pltpu
from jax.sharding import PartitionSpec as P

HEAD = 64
HEADS = 8
INNER = 512
EPSILON = 1e-06
BF16, F32 = jnp.bfloat16, jnp.float32
GROUP = 8
PAIR = 2 * HEAD
ROWS = 256
MIB = 1 << 20


def norm_rows(values, gain):
    centre = values - jnp.mean(values, axis=-1, keepdims=True)
    spread = jnp.mean(centre * centre, axis=-1, keepdims=True)
    return centre * lax.rsqrt(spread + EPSILON) * gain


def attend(qkv, rows, same):
    low = lax.broadcasted_iota(jnp.int32, (ROWS, PAIR), 1) < HEAD
    outs = []
    for pair in range(HEADS // 2):
        queries = qkv[rows, pl.ds(pair * PAIR, PAIR)]
        keys = qkv[rows, pl.ds(INNER + pair * PAIR, PAIR)]
        values = qkv[rows, pl.ds(2 * INNER + pair * PAIR, PAIR)]
        halves = []
        for mine in (low, ~low):
            own = jnp.where(mine, queries, jnp.zeros_like(queries))
            scores = lax.dot_general(own, keys, (((1,), (1,)), ((), ())), preferred_element_type=F32)
            if same is not None:
                scores = jnp.where(same, scores, -1e30)
            exponent = jnp.exp(scores - jnp.max(scores, axis=-1, keepdims=True))
            weights = exponent * (1.0 / jnp.sum(exponent, axis=-1, keepdims=True))
            halves.append(jnp.dot(weights.astype(BF16), values, preferred_element_type=F32))
        outs.append(jnp.where(low, halves[0], halves[1]))
    return jnp.concatenate(outs, axis=1)


def out_weight(packed):
    parts, twice, width = packed.shape
    half = twice // 2
    left = packed[:, :half].reshape(parts * half, width)
    right = packed[:, half:].reshape(parts * half, width)
    return left, right


def start_weights(weights, qkv_weight, out_ref, sems):
    qkv_copy = pltpu.make_async_copy(weights.at[:, :, pl.ds(0, 3 * INNER)], qkv_weight, sems.at[0])
    out_copy = pltpu.make_async_copy(weights.at[:, :, pl.ds(3 * INNER, INNER)], out_ref, sems.at[1])
    return qkv_copy, out_copy


def project(normed, qkv_weight, store):
    depth = normed.shape[1]
    for piece in range(3 * INNER // 256):
        columns = pl.ds(piece * 256, 256)
        weight = qkv_weight[:, :, columns].reshape(depth, 256)
        product = jnp.dot(normed, weight, preferred_element_type=F32)
        if piece < INNER // 256:
            product = product * HEAD**-0.5
        store(columns, product)


def spatial_kernel(tokens, gain, weights, context, middle, qkv_weight, out_ref, qkv, sems):
    qkv_copy, out_copy = start_weights(weights, qkv_weight, out_ref, sems)
    qkv_copy.start()
    out_copy.start()
    normed = norm_rows(tokens[...].astype(F32), gain[...]).astype(BF16)
    qkv_copy.wait()

    def store(columns, product):
        qkv[:, columns] = product.astype(BF16)

    project(normed, qkv_weight, store)
    for clip in range(tokens.shape[0] // ROWS):
        rows = pl.ds(clip * ROWS, ROWS)
        context[rows, :] = attend(qkv, rows, None).astype(BF16)
    out_copy.wait()
    for half, weight in enumerate(out_weight(out_ref[...])):
        columns = pl.ds(half * INNER, INNER)
        added = jnp.dot(context[...], weight, preferred_element_type=F32)
        middle[:, columns] = (tokens[:, columns].astype(F32) + added).astype(BF16)


def temporal_kernel(frames, tokens, arrived, gain, first, second, context, qkv_weight, out_ref, qkv, sems):
    out_copy = pltpu.make_async_copy(first.at[:, :, pl.ds(3 * INNER, INNER)], out_ref, sems.at[0])
    qkv_copy = pltpu.make_async_copy(second.at[:, :, pl.ds(0, 3 * INNER)], qkv_weight, sems.at[1])
    out_copy.start()
    qkv_copy.start()
    depth = tokens.shape[1]
    out_copy.wait()
    added = jnp.concatenate(
        [jnp.dot(arrived[...], weight, preferred_element_type=F32) for weight in out_weight(out_ref[...])], axis=1
    )
    middle = (tokens[...].astype(F32) + added).astype(BF16).astype(F32)
    normed = norm_rows(middle, gain[...]).astype(BF16)
    qkv_copy.wait()
    places = tokens.shape[0] // frames

    def store(columns, product):
        split = product.reshape(frames, places, product.shape[1])
        for group in range(places // GROUP):
            own = split[:, group * GROUP : (group + 1) * GROUP].reshape(ROWS, product.shape[1])
            qkv[pl.ds(group * ROWS, ROWS), columns] = own.astype(BF16)

    project(normed, qkv_weight, store)
    place = lax.broadcasted_iota(jnp.int32, (ROWS, ROWS), 0) % GROUP
    same = place == lax.broadcasted_iota(jnp.int32, (ROWS, ROWS), 1) % GROUP
    outs = []
    for group in range(places // GROUP):
        out = attend(qkv, pl.ds(group * ROWS, ROWS), same)
        outs.append(out.reshape(frames, GROUP, INNER))
    context[...] = jnp.concatenate(outs, axis=1).reshape(tokens.shape[0], INNER).astype(BF16)


def kernel_call(body, ins, outs, members, operands, flops):
    depth = 2 * INNER
    rows = depth // members
    whole = pl.BlockSpec(memory_space=pltpu.VMEM)
    return pl.pallas_call(
        body,
        out_shape=outs,
        in_specs=[pl.BlockSpec(memory_space=pltpu.HBM) if far else whole for far in ins],
        out_specs=[whole] * len(outs),
        scratch_shapes=[
            pltpu.VMEM((members, rows, 3 * INNER), BF16),
            pltpu.VMEM((members, rows, INNER), BF16),
            pltpu.VMEM((2 * ROWS, 3 * INNER), BF16),
            pltpu.SemaphoreType.DMA((2,)),
        ],
        compiler_params=pltpu.CompilerParams(vmem_limit_bytes=40 * MIB),
        cost_estimate=pl.CostEstimate(flops=flops, bytes_accessed=8 * MIB, transcendentals=2 * MIB),
    )(*operands)


def side_by_side(qkv, out):
    return jnp.concatenate([qkv, jnp.concatenate([out[:, :INNER], out[:, INNER:]], axis=0)], axis=1)


def shards(tokens, spatial_gain, spatial_qkv, spatial_out, temporal_gain, temporal_qkv, temporal_out):
    clips, _, places, depth = tokens.shape
    frames = lax.axis_size("tm")
    members = lax.axis_size("fsdp")
    rows = clips * places
    block = rows // frames
    flat = tokens.reshape(rows, depth)

    def gathered(qkv, out):
        return lax.all_gather(side_by_side(qkv, out), "fsdp", axis=0, tiled=False)

    def exchanged(array):
        sent = array.reshape(frames, block, array.shape[1])
        return lax.all_to_all(sent, "tm", split_axis=0, concat_axis=0, tiled=True).reshape(array.shape)

    first = gathered(spatial_qkv, spatial_out)
    second = gathered(temporal_qkv, temporal_out)
    early = exchanged(flat)
    context, middle = kernel_call(
        spatial_kernel,
        [False, False, True],
        [jax.ShapeDtypeStruct((rows, INNER), BF16), jax.ShapeDtypeStruct((rows, depth), BF16)],
        members,
        (flat, spatial_gain.reshape(1, depth), first),
        4 * rows * depth * depth,
    )
    arrived = exchanged(context)
    (context_t,) = kernel_call(
        functools.partial(temporal_kernel, frames),
        [False, False, False, True, True],
        [jax.ShapeDtypeStruct((rows, INNER), BF16)],
        members,
        (early, arrived, temporal_gain.reshape(1, depth), first, second),
        4 * rows * depth * depth,
    )
    weight = jnp.concatenate(out_weight(second[:, :, 3 * INNER :]), axis=1)
    returned = exchanged(context_t)
    encoded = middle.astype(F32) + jnp.dot(returned, weight, preferred_element_type=F32)
    return encoded.astype(BF16).reshape(tokens.shape)


def solution(mesh):
    placed = (
        P("fsdp", "tm", None, None),
        P(),
        P("fsdp", None),
        P("fsdp", None),
        P(),
        P("fsdp", None),
        P("fsdp", None),
    )
    return jax.shard_map(
        shards, mesh=mesh, in_specs=placed, out_specs=P("fsdp", "tm", None, None), check_vma=False
    )
```

time: 229 us -> 182 us (0.79)
  blocking collectives: 109 us -> 0 us
  waiting for transfers between devices: 58.6 us -> 114 us
  matrix products: 23.6 us -> 1.68 us
  starting transfers between devices: 9.3 us -> 26.6 us
  Pallas kernels: 0 us -> 13 us
    all_to_all x2 -> x0, blocking collectives: 109 us -> none  [the longest x1 71.4 us: shards(): lax.all_to_all(middle, 'tm', split_axis=2, concat_axis=1, tiled=True)]
    all_to_all x2 -> x3, waiting for transfers between devices: 16.4 us -> 61.8 us  [exchanged(): lax.all_to_all(sent, 'tm', split_axis=0, concat_axis=0, tiled=True)]
    all_to_all x2 -> x3, starting transfers between devices: 9.25 us -> 26.6 us  [exchanged(): lax.all_to_all(sent, 'tm', split_axis=0, concat_axis=0, tiled=True)]
    dot_general x6 -> x1, matrix products: 17 us -> 1.68 us  [shards(): jnp.dot(returned, weight, preferred_element_type=F32)]
    pallas_call x0 -> x2, Pallas kernels: none -> 13 us  [kernel_call(): pl.pallas_call(body, out_shape=outs, in_specs=[pl.BlockSpec(memory_space=...]
    all_gather x2, waiting for transfers between devices: 40.8 us -> 52.1 us  [gathered(): return lax.all_gather(side_by_side(qkv, out), 'fsdp', axis=0, tiled=False)]
    sub x2 -> x0, matrix products: 6.63 us -> none  [attention_core(): exponent = jnp.exp(scores - row_max)]
    unnamed x13 -> x12, local copies, waits for them, and re-layouts: 0.11 us -> 6.58 us
  transfers between devices with their start and end apart: 4 -> 5, of which waited for: 2 -> 5; matrix products, arithmetic and copies ran while one was open for 9% -> 2% of each run, Pallas kernels for 0% -> 3%
where the time goes in v1:
time: 182 us; the launch traced here: 181 us
  waiting for transfers between devices  114 us (63%)
  starting transfers between devices  26.6 us (15%)
  between operations  13.5 us (7%)
  Pallas kernels  13 us (7%)
  local copies, waits for them, and re-layouts  9.51 us (5%)
  other arithmetic  3.29 us (2%)
    all_to_all x3, waiting for transfers between devices, exchanged(): lax.all_to_all(sent, 'tm', split_axis=0, concat_axis=0, tiled=True)  61.8 us
    all_gather x2, waiting for transfers between devices, gathered(): return lax.all_gather(side_by_side(qkv, out), 'fsdp', axis=0, tiled=False)  52.1 us
    all_to_all x3, starting transfers between devices, exchanged(): lax.all_to_all(sent, 'tm', split_axis=0, concat_axis=0, tiled=True)  26.6 us
    pallas_call x2, Pallas kernels, kernel_call(): pl.pallas_call(body, out_shape=outs, in_specs=[pl.BlockSpec(memory_space=...  13 us
    unnamed x12, local copies, waits for them, and re-layouts  6.58 us
  transfers between devices with their start and end apart: 5, of which 5 were waited for; matrix products, arithmetic and copies ran while one was open for 2% of the time, Pallas kernels for 3%

profile of v1, /device:TPU:32, one launch (start us, length us, event | category | flops | bytes accessed | tf_op | source)
XLA Modules:
  0.0 181.5 jit_solution(7380985885595716188)
XLA Ops:
  6.5 0.0 all-gather.5.cloned.1.call-start
  6.5 0.9 fusion.6
  7.4 1.6 maximum_maximum_fusion
  9.1 0.0 all-gather.5.cloned.1.call-update
  9.1 0.0 all-gather.7.cloned.1.call-start
  9.1 0.8 fusion.5
  9.9 1.6 maximum_maximum_fusion.1
  11.6 0.0 all-gather.7.cloned.1.call-update
  11.6 18.0 %all-to-all-start = ((bf16[32,16,1024]{2,1,0:T(8,128)(2,1)}), bf16[32,16,1024]{2,1,0:T(8,128)(2,1)S(1)}, u32[]{:S(2)}, u32[]{:S(2)}) async-start(bf16[32,16,1024]{2,1,0:T(8,128)(2,1)} %bitcast.23), calls=%async_computation | async-start | bytes 2097152 | tf_op jit(solution)/shard_map/all_to_all | solution.py:161
  29.6 31.0 %all-gather.5.cloned.1.call-done = bf16[1024,2048]{1,0:T(8,128)(2,1)} async-done(((bf16[64,2048]{1,0:T(8,128)(2,1)}), bf16[1024,2048]{1,0:T(8,128)(2,1)}) %all-gather.5.cloned.1.call-update) | async-done | bytes 4194320 | tf_op jit(solution)/shard_map/all_gather | solution.py:157
  60.6 0.0 copy-done.3
  60.6 2.2 %copy-done.1 = bf16[1024,2048]{1,0:T(8,128)(2,1)S(1)} copy-done((bf16[1024,2048]{1,0:T(8,128)(2,1)S(1)}, bf16[1024,2048]{1,0:T(8,128)(2,1)}, u32[]{:S(2)}) %copy-start.1) | copy-done | bytes 4194328
  62.8 6.2 %shard_map.73 = (bf16[512,512]{1,0:T(8,128)(2,1)}, bf16[512,1024]{1,0:T(8,128)(2,1)S(1)}) custom-call(bf16[512,1024]{1,0:T(8,128)(2,1)S(1)} %bitcast.24, f32[1,1024]{1,0:T(1,128)S(1)} %bitcast.26, bf16[16,64,2048]{2,1,0:T(8,128)(2,1)S(1)} %bitcast.19), custom_call_target="tpu_custom_call" | custom-call | flops 2147483648 | bytes 8388608 | tf_op jit(solution)/shard_map/pallas_call | solution.py:128
  69.0 16.6 %all-to-all-done = bf16[32,16,1024]{2,1,0:T(8,128)(2,1)S(1)} async-done(((bf16[32,16,1024]{2,1,0:T(8,128)(2,1)}), bf16[32,16,1024]{2,1,0:T(8,128)(2,1)S(1)}, u32[]{:S(2)}, u32[]{:S(2)}) %all-to-all-start) | async-done | bytes 1048608 | tf_op jit(solution)/shard_map/all_to_all | solution.py:161
  85.6 4.4 %all-to-all-start.1 = ((bf16[32,16,512]{2,1,0:T(8,128)(2,1)}), bf16[32,16,512]{2,1,0:T(8,128)(2,1)S(1)}, u32[]{:S(2)}, u32[]{:S(2)}) async-start(bf16[32,16,512]{2,1,0:T(8,128)(2,1)} %bitcast.5), calls=%async_computation.1 | async-start | bytes 1048576 | tf_op jit(solution)/shard_map/all_to_all | solution.py:161
  90.0 21.1 %all-gather.7.cloned.1.call-done = bf16[1024,2048]{1,0:T(8,128)(2,1)} async-done(((bf16[64,2048]{1,0:T(8,128)(2,1)}), bf16[1024,2048]{1,0:T(8,128)(2,1)}) %all-gather.7.cloned.1.call-update) | async-done | bytes 4194320 | tf_op jit(solution)/shard_map/all_gather | solution.py:157
  111.1 12.6 %all-to-all-done.1 = bf16[32,16,512]{2,1,0:T(8,128)(2,1)S(1)} async-done(((bf16[32,16,512]{2,1,0:T(8,128)(2,1)}), bf16[32,16,512]{2,1,0:T(8,128)(2,1)S(1)}, u32[]{:S(2)}, u32[]{:S(2)}) %all-to-all-start.1) | async-done | bytes 524320 | tf_op jit(solution)/shard_map/all_to_all | solution.py:161
  123.7 2.2 %copy-done = bf16[1024,2048]{1,0:T(8,128)(2,1)S(1)} copy-done((bf16[1024,2048]{1,0:T(8,128)(2,1)S(1)}, bf16[1024,2048]{1,0:T(8,128)(2,1)}, u32[]{:S(2)}) %copy-start) | copy-done | bytes 4194328
  125.9 2.2 %copy-done.2 = bf16[1024,2048]{1,0:T(8,128)(2,1)S(1)} copy-done((bf16[1024,2048]{1,0:T(8,128)(2,1)S(1)}, bf16[1024,2048]{1,0:T(8,128)(2,1)}, u32[]{:S(2)}) %copy-start.2) | copy-done | bytes 4194328
  128.1 6.8 %shard_map.74 = bf16[512,512]{1,0:T(8,128)(2,1)} custom-call(bf16[512,1024]{1,0:T(8,128)(2,1)S(1)} %bitcast.21, bf16[512,512]{1,0:T(8,128)(2,1)S(1)} %bitcast.22, f32[1,1024]{1,0:T(1,128)S(1)} %bitcast.25, bf16[16,64,2048]{2,1,0:T(8,128)(2,1)S(1)} %bitcast.20, bf16[16,64,2048]{2,1,0:T(8,128)(2,1)S(1)} %bitcast.18), custom_call_target="tpu_custom_call" | custom-call | flops 2147483648 | bytes 8388608 | tf_op jit(solution)/shard_map/pallas_call | solution.py:128
  134.9 4.2 %all-to-all-start.2 = ((bf16[32,16,512]{2,1,0:T(8,128)(2,1)}), bf16[32,16,512]{2,1,0:T(8,128)(2,1)S(1)}, u32[]{:S(2)}, u32[]{:S(2)}) async-start(bf16[32,16,512]{2,1,0:T(8,128)(2,1)} %bitcast.9), calls=%async_computation.2 | async-start | bytes 1048576 | tf_op jit(solution)/shard_map/all_to_all | solution.py:161
  139.1 1.3 fusion.4
  140.4 32.6 %all-to-all-done.2 = bf16[32,16,512]{2,1,0:T(8,128)(2,1)S(1)} async-done(((bf16[32,16,512]{2,1,0:T(8,128)(2,1)}), bf16[32,16,512]{2,1,0:T(8,128)(2,1)S(1)}, u32[]{:S(2)}, u32[]{:S(2)}) %all-to-all-start.2) | async-done | bytes 524320 | tf_op jit(solution)/shard_map/all_to_all | solution.py:161
  172.9 1.7 add_convert_fusion
  (8 shorter events, 0.0 us)
Async XLA Ops:
  6.5 54.1 %copy-start.3 = (bf16[2,1,256,1024]{3,2,1,0:T(8,128)(2,1)S(1)}, bf16[2,1,256,1024]{3,2,1,0:T(8,128)(2,1)}, u32[]{:S(2)}) copy-start(bf16[2,1,256,1024]{3,2,1,0:T(8,128)(2,1)} %param.7) | copy-start | bytes 3145732
  6.5 54.1 %copy-start.5 = (f32[1024]{0:T(1024)S(1)}, f32[1024]{0:T(1024)}, u32[]{:S(2)}) copy-start(f32[1024]{0:T(1024)} %param.8) | copy-start | bytes 12292
  6.5 54.0 %all-gather.5.cloned.1.call-start = ((), (), s32[]{:S(2)}) async-start(), calls=%async_computation.3 | async-start | bytes 4456448 | tf_op jit(solution)/shard_map/all_gather | solution.py:157
  9.1 102.0 %all-gather.7.cloned.1.call-start = ((), (), s32[]{:S(2)}) async-start(), calls=%async_computation.4 | async-start | bytes 4456448 | tf_op jit(solution)/shard_map/all_gather | solution.py:157
  11.6 74.0 %all-to-all-start = ((bf16[32,16,1024]{2,1,0:T(8,128)(2,1)}), bf16[32,16,1024]{2,1,0:T(8,128)(2,1)S(1)}, u32[]{:S(2)}, u32[]{:S(2)}) async-start(bf16[32,16,1024]{2,1,0:T(8,128)(2,1)} %bitcast.23), calls=%async_computation | async-start | bytes 2097152 | tf_op jit(solution)/shard_map/all_to_all | solution.py:161
  60.6 2.2 %copy-start.1 = (bf16[1024,2048]{1,0:T(8,128)(2,1)S(1)}, bf16[1024,2048]{1,0:T(8,128)(2,1)}, u32[]{:S(2)}) copy-start(bf16[1024,2048]{1,0:T(8,128)(2,1)} %all-gather.5.cloned.1.call-done) | copy-start | bytes 12582916
  62.8 61.0 %copy-start.4 = (f32[1024]{0:T(1024)S(1)}, f32[1024]{0:T(1024)}, u32[]{:S(2)}) copy-start(f32[1024]{0:T(1024)} %param.11) | copy-start | bytes 12292
  85.6 38.2 %all-to-all-start.1 = ((bf16[32,16,512]{2,1,0:T(8,128)(2,1)}), bf16[32,16,512]{2,1,0:T(8,128)(2,1)S(1)}, u32[]{:S(2)}, u32[]{:S(2)}) async-start(bf16[32,16,512]{2,1,0:T(8,128)(2,1)} %bitcast.5), calls=%async_computation.1 | async-start | bytes 1048576 | tf_op jit(solution)/shard_map/all_to_all | solution.py:161
  123.7 2.2 %copy-start = (bf16[1024,2048]{1,0:T(8,128)(2,1)S(1)}, bf16[1024,2048]{1,0:T(8,128)(2,1)}, u32[]{:S(2)}) copy-start(bf16[1024,2048]{1,0:T(8,128)(2,1)} %all-gather.7.cloned.1.call-done) | copy-start | bytes 12582916
  125.9 2.2 %copy-start.2 = (bf16[1024,2048]{1,0:T(8,128)(2,1)S(1)}, bf16[1024,2048]{1,0:T(8,128)(2,1)}, u32[]{:S(2)}) copy-start(bf16[1024,2048]{1,0:T(8,128)(2,1)} %all-gather.5.cloned.1.call-done) | copy-start | bytes 12582916
  134.9 38.0 %all-to-all-start.2 = ((bf16[32,16,512]{2,1,0:T(8,128)(2,1)}), bf16[32,16,512]{2,1,0:T(8,128)(2,1)S(1)}, u32[]{:S(2)}, u32[]{:S(2)}) async-start(bf16[32,16,512]{2,1,0:T(8,128)(2,1)} %bitcast.9), calls=%async_computation.2 | async-start | bytes 1048576 | tf_op jit(solution)/shard_map/all_to_all | solution.py:161
Sparse Core Ops, SparseCore 0:
  9.5 51.0 all-gather.4
  62.7 48.3 all-gather.6

commit v2 on v1

v2 whole, which is shorter than its diff:
```python
import functools

import jax
import jax.numpy as jnp
from jax import lax
from jax.experimental import pallas as pl
from jax.experimental.pallas import tpu as pltpu
from jax.sharding import PartitionSpec as P

HEAD = 64
HEADS = 8
INNER = 512
EPSILON = 1e-06
BF16, F32 = jnp.bfloat16, jnp.float32
GROUP = 8
PAIR = 2 * HEAD
ROWS = 256
MIB = 1 << 20


def norm_rows(values, gain):
    centre = values - jnp.mean(values, axis=-1, keepdims=True)
    spread = jnp.mean(centre * centre, axis=-1, keepdims=True)
    return centre * lax.rsqrt(spread + EPSILON) * gain


def attend(qkv, rows, same):
    low = lax.broadcasted_iota(jnp.int32, (ROWS, PAIR), 1) < HEAD
    outs = []
    for pair in range(HEADS // 2):
        queries = qkv[rows, pl.ds(pair * PAIR, PAIR)]
        keys = qkv[rows, pl.ds(INNER + pair * PAIR, PAIR)]
        values = qkv[rows, pl.ds(2 * INNER + pair * PAIR, PAIR)]
        halves = []
        for mine in (low, ~low):
            own = jnp.where(mine, queries, jnp.zeros_like(queries))
            scores = lax.dot_general(own, keys, (((1,), (1,)), ((), ())), preferred_element_type=F32)
            if same is not None:
                scores = jnp.where(same, scores, -1e30)
            exponent = jnp.exp(scores - jnp.max(scores, axis=-1, keepdims=True))
            weights = exponent * (1.0 / jnp.sum(exponent, axis=-1, keepdims=True))
            halves.append(jnp.dot(weights.astype(BF16), values, preferred_element_type=F32))
        outs.append(jnp.where(low, halves[0], halves[1]))
    return jnp.concatenate(outs, axis=1)


def out_weight(packed):
    parts, twice, width = packed.shape
    half = twice // 2
    left = packed[:, :half].reshape(parts * half, width)
    right = packed[:, half:].reshape(parts * half, width)
    return left, right


def project(normed, weights, store):
    depth = normed.shape[1]
    for piece in range(3 * INNER // 256):
        columns = pl.ds(piece * 256, 256)
        product = jnp.dot(normed, weights[:, :, columns].reshape(depth, 256), preferred_element_type=F32)
        if piece < INNER // 256:
            product = product * HEAD**-0.5
        store(columns, product)


def pack_kernel(qkv, out, packed, sems):
    depth, width = qkv.shape
    half = out.shape[1] // 2
    copies = []
    for index in range(packed.shape[0]):
        target = packed.at[index]
        copies += [
            pltpu.make_async_copy(qkv, target.at[:, pl.ds(0, width)], sems.at[index, 0]),
            pltpu.make_async_copy(
                out.at[:, pl.ds(0, half)], target.at[pl.ds(0, depth // 2), pl.ds(width, half)], sems.at[index, 1]
            ),
            pltpu.make_async_copy(
                out.at[:, pl.ds(half, half)], target.at[pl.ds(depth // 2, depth // 2), pl.ds(width, half)], sems.at[index, 2]
            ),
        ]
    for copy in copies:
        copy.start()
    for copy in copies:
        copy.wait()


def packed_weights(qkv, out, copies):
    depth = qkv.shape[0]
    far = pl.BlockSpec(memory_space=pl.ANY)
    return pl.pallas_call(
        pack_kernel,
        out_shape=jax.ShapeDtypeStruct((copies, depth, qkv.shape[1] + INNER), BF16),
        in_specs=[far, far],
        out_specs=far,
        scratch_shapes=[pltpu.SemaphoreType.DMA((copies, 3))],
        cost_estimate=pl.CostEstimate(flops=0, bytes_accessed=copies * MIB // 2, transcendentals=0),
    )(qkv, out)


def place_kernel(here, mine, other, placed, sems):
    across, beside, core = here[0], here[1], here[2]
    copies = []
    for side, source in enumerate((mine, other)):
        for index in range(source.shape[0]):
            step = (0, -1, 1, 2)[index // 2]
            target = placed.at[(across + step + 4) % 4, (beside + index) % 2, (core + side) % 2]
            copies.append(pltpu.make_async_copy(source.at[index], target, sems.at[side, index]))
    for copy in copies:
        copy.start()
    for copy in copies:
        copy.wait()


def in_order(here, mine, other):
    parts, depth, width = mine.shape
    far = pl.BlockSpec(memory_space=pl.ANY)
    placed = pl.pallas_call(
        place_kernel,
        out_shape=jax.ShapeDtypeStruct((4, 2, 2, depth, width), BF16),
        in_specs=[pl.BlockSpec(memory_space=pltpu.SMEM), far, far],
        out_specs=far,
        scratch_shapes=[pltpu.SemaphoreType.DMA((2, parts))],
        cost_estimate=pl.CostEstimate(flops=0, bytes_accessed=8 * MIB, transcendentals=0),
    )(here, mine, other)
    return placed.reshape(2 * parts, depth, width)


def spatial_kernel(here, tokens, gain, mine, other, middle, weights, qkv, context, sems):
    core = here[2]
    copies = [
        pltpu.make_async_copy(mine, weights.at[:, core], sems.at[0]),
        pltpu.make_async_copy(other, weights.at[:, 1 - core], sems.at[1]),
    ]
    for copy in copies:
        copy.start()
    normed = norm_rows(tokens[...].astype(F32), gain[...]).astype(BF16)
    for copy in copies:
        copy.wait()
    parts, cores, depth, width = weights.shape
    whole = weights.reshape(parts * cores, depth, width)

    def store(columns, product):
        qkv[:, columns] = product.astype(BF16)

    project(normed, whole, store)
    for clip in range(tokens.shape[0] // ROWS):
        rows = pl.ds(clip * ROWS, ROWS)
        context[rows, :] = attend(qkv, rows, None).astype(BF16)
    for half, weight in enumerate(out_weight(whole[:, :, pl.ds(3 * INNER, INNER)])):
        columns = pl.ds(half * INNER, INNER)
        added = jnp.dot(context[...], weight, preferred_element_type=F32)
        middle[:, columns] = (tokens[:, columns].astype(F32) + added).astype(BF16)


def temporal_kernel(frames, middle, gain, placed, context, weights, qkv, sems):
    copy = pltpu.make_async_copy(placed.at[:, :, pl.ds(0, 3 * INNER)], weights, sems.at[0])
    copy.start()
    normed = norm_rows(middle[...].astype(F32), gain[...]).astype(BF16)
    copy.wait()
    places = middle.shape[0] // frames

    def store(columns, product):
        split = product.reshape(frames, places, product.shape[1])
        for group in range(places // GROUP):
            own = split[:, group * GROUP : (group + 1) * GROUP].reshape(ROWS, product.shape[1])
            qkv[pl.ds(group * ROWS, ROWS), columns] = own.astype(BF16)

    project(normed, weights, store)
    place = lax.broadcasted_iota(jnp.int32, (ROWS, ROWS), 0) % GROUP
    same = place == lax.broadcasted_iota(jnp.int32, (ROWS, ROWS), 1) % GROUP
    outs = []
    for group in range(places // GROUP):
        out = attend(qkv, pl.ds(group * ROWS, ROWS), same)
        outs.append(out.reshape(frames, GROUP, INNER))
    context[...] = jnp.concatenate(outs, axis=1).reshape(middle.shape[0], INNER).astype(BF16)


def kernel_call(body, kinds, out, scratch, operands):
    near = pl.BlockSpec(memory_space=pltpu.VMEM)
    specs = {"s": pl.BlockSpec(memory_space=pltpu.SMEM), "v": near, "h": pl.BlockSpec(memory_space=pl.ANY)}
    rows, depth = 2 * ROWS, 2 * INNER
    return pl.pallas_call(
        body,
        out_shape=out,
        in_specs=[specs[kind] for kind in kinds],
        out_specs=near,
        scratch_shapes=scratch,
        compiler_params=pltpu.CompilerParams(vmem_limit_bytes=57 * MIB),
        cost_estimate=pl.CostEstimate(flops=4 * rows * depth * depth, bytes_accessed=8 * MIB, transcendentals=2 * MIB),
    )(*operands)


def moved(array, change):
    pairs = []
    for index in range(lax.axis_size("fsdp")):
        x, yl, core = change(index // 4, index // 2 % 2, index % 2)
        pairs.append((index, (x % 4 * 2 + yl) * 2 + core))
    return lax.ppermute(array, "fsdp", pairs)


def other_core(array):
    return moved(array, lambda x, yl, core: (x, yl, 1 - core))


def gathered_by_hops(own):
    depth = own.shape[0]
    ahead = lambda x, yl, core: (x + 1, yl, core)
    back = lambda x, yl, core: (x + 3, yl, core)
    both = jnp.concatenate([own, moved(own, lambda x, yl, core: (x, 1 - yl, core))], axis=0)
    left, right = moved(both, ahead), moved(both, back)
    far = moved(left[:depth], ahead), moved(right[depth:], back)
    mine = jnp.concatenate([both, left, right, *far], axis=0).reshape(8, depth, own.shape[1])
    return mine, other_core(mine)


def shards(tokens, spatial_gain, spatial_qkv, spatial_out, temporal_gain, temporal_qkv, temporal_out):
    clips, _, places, depth = tokens.shape
    frames = lax.axis_size("tm")
    members = lax.axis_size("fsdp")
    parts = members // 2
    rows = clips * places
    block = rows // frames
    flat = tokens.reshape(rows, depth)
    index = lax.axis_index("fsdp")
    here = jnp.stack([index // 4, index // 2 % 2, index % 2]).astype(jnp.int32)
    cores = [list(range(core, members, 2)) for core in range(2)]
    width = 4 * INNER

    def exchanged(array):
        sent = array.reshape(frames, block, array.shape[1])
        return lax.all_to_all(sent, "tm", split_axis=0, concat_axis=0, tiled=True).reshape(array.shape)

    mine = lax.all_to_all(
        packed_weights(spatial_qkv, spatial_out, parts), "fsdp", 0, 0, axis_index_groups=cores, tiled=True
    )
    middle = kernel_call(
        spatial_kernel,
        "svvhh",
        jax.ShapeDtypeStruct((rows, depth), BF16),
        [
            pltpu.VMEM((parts, 2, depth // members, width), BF16),
            pltpu.VMEM((rows, 3 * INNER), BF16),
            pltpu.VMEM((rows, INNER), BF16),
            pltpu.SemaphoreType.DMA((2,)),
        ],
        (here, flat, spatial_gain.reshape(1, depth), mine, other_core(mine)),
    )
    arrived = exchanged(middle)
    own, _ = lax.optimization_barrier((packed_weights(temporal_qkv, temporal_out, 1)[0], middle[:8, :128]))
    placed = in_order(here, *gathered_by_hops(own))
    context = kernel_call(
        functools.partial(temporal_kernel, frames),
        "vvh",
        jax.ShapeDtypeStruct((rows, INNER), BF16),
        [
            pltpu.VMEM((members, depth // members, 3 * INNER), BF16),
            pltpu.VMEM((rows, 3 * INNER), BF16),
            pltpu.SemaphoreType.DMA((1,)),
        ],
        (arrived, temporal_gain.reshape(1, depth), placed),
    )
    weight = jnp.concatenate(out_weight(placed[:, :, 3 * INNER :]), axis=1)
    returned = exchanged(context)
    encoded = middle.astype(F32) + jnp.dot(returned, weight, preferred_element_type=F32)
    return encoded.astype(BF16).reshape(tokens.shape)


def solution(mesh):
    placed = (
        P("fsdp", "tm", None, None),
        P(),
        P("fsdp", None),
        P("fsdp", None),
        P(),
        P("fsdp", None),
        P("fsdp", None),
    )
    return jax.shard_map(
        shards, mesh=mesh, in_specs=placed, out_specs=P("fsdp", "tm", None, None), check_vma=False
    )
```

time: 182 us -> 377 us (2.07)
  Pallas kernels: 13 us -> 220 us
  waiting for transfers between devices: 114 us -> 64.9 us
  blocking collectives: 0 us -> 32 us
  starting transfers between devices: 26.6 us -> 52 us
  between operations: 13.5 us -> 0.27 us
  local copies, waits for them, and re-layouts: 9.51 us -> 3.41 us
    pallas_call x2 -> x5, Pallas kernels: 13 us -> 220 us  [the longest x1 129 us: in_order(): pl.pallas_call(place_kernel, out_shape=jax.ShapeDtypeStruct((4, 2, 2, dep...]
    all_gather x2 -> x0, waiting for transfers between devices: 52.1 us -> none  [gathered(): return lax.all_gather(side_by_side(qkv, out), 'fsdp', axis=0, tiled=False)]
    ppermute x0 -> x7, waiting for transfers between devices: none -> 32 us  [moved(): return lax.ppermute(array, 'fsdp', pairs)]
    all_to_all x0 -> x1, blocking collectives: none -> 32 us  [shards(): lax.all_to_all(packed_weights(spatial_qkv, spatial_out, parts), 'fsdp', 0...]
    all_to_all x3 -> x2, waiting for transfers between devices: 61.8 us -> 32.9 us  [exchanged(): lax.all_to_all(sent, 'tm', split_axis=0, concat_axis=0, tiled=True)]
    ppermute x0 -> x7, starting transfers between devices: none -> 18.7 us  [moved(): return lax.ppermute(array, 'fsdp', pairs)]
    all_to_all x3 -> x2, starting transfers between devices: 26.6 us -> 33.3 us  [exchanged(): lax.all_to_all(sent, 'tm', split_axis=0, concat_axis=0, tiled=True)]
    unnamed x12 -> x13, local copies, waits for them, and re-layouts: 6.58 us -> 2.06 us
  transfers between devices with their start and end apart: 5 -> 9, of which waited for: 5 -> 6; matrix products, arithmetic and copies ran while one was open for 2% -> 1% of each run, Pallas kernels for 3% -> 37%
where the time goes in v2:
time: 377 us; the launch traced here: 376 us
  Pallas kernels  220 us (58%)
  waiting for transfers between devices  64.9 us (17%)
  starting transfers between devices  52 us (14%)
  blocking collectives  32 us (8%)
    pallas_call x1, Pallas kernels, in_order(): pl.pallas_call(place_kernel, out_shape=jax.ShapeDtypeStruct((4, 2, 2, dep...  129 us
    pallas_call x2, Pallas kernels, packed_weights(): pl.pallas_call(pack_kernel, out_shape=jax.ShapeDtypeStruct((copies, depth...  73.9 us
    all_to_all x2, starting transfers between devices, exchanged(): lax.all_to_all(sent, 'tm', split_axis=0, concat_axis=0, tiled=True)  33.3 us
    all_to_all x2, waiting for transfers between devices, exchanged(): lax.all_to_all(sent, 'tm', split_axis=0, concat_axis=0, tiled=True)  32.9 us
    ppermute x7, waiting for transfers between devices, moved(): return lax.ppermute(array, 'fsdp', pairs)  32 us
    all_to_all x1, blocking collectives, shards(): lax.all_to_all(packed_weights(spatial_qkv, spatial_out, parts), 'fsdp', 0...  32 us
    ppermute x7, starting transfers between devices, moved(): return lax.ppermute(array, 'fsdp', pairs)  18.7 us
    pallas_call x2, Pallas kernels, kernel_call(): pl.pallas_call(body, out_shape=out, in_specs=[specs[kind] for kind in kin...  17 us
  transfers between devices with their start and end apart: 9, of which 6 were waited for; matrix products, arithmetic and copies ran while one was open for 1% of the time, Pallas kernels for 37%

profile of v2, /device:TPU:32, one launch (start us, length us, event | category | flops | bytes accessed | tf_op | source)
XLA Modules:
  0.0 375.8 jit_solution(2578743021084836187)
XLA Ops:
  0.0 64.8 %shard_map.73 = bf16[8,64,2048]{2,1,0:T(8,128)(2,1)} custom-call(bf16[64,1536]{1,0:T(8,128)(2,1)} %qkv.2, bf16[32,1024]{1,0:T(8,128)(2,1)} %out.2), custom_call_target="tpu_custom_call" | custom-call | bytes 4194304 | tf_op jit(solution)/shard_map/pallas_call | solution.py:89
  64.8 32.0 %all_to_all.15.mine = bf16[8,64,2048]{2,1,0:T(8,128)(2,1)S(1)} all-to-all(bf16[8,64,2048]{2,1,0:T(8,128)(2,1)} %shard_map.73), channel_id=1, replica_groups={{0,64,128,192,256,320,384,448},{32,96,160,224,288,352,416,480},{1,65,12..., dimensions={0} | all-to-all | bytes 4194304 | tf_op jit(solution)/shard_map/all_to_all | solution.py:232
  96.8 1.9 collective-permute-start
  99.4 3.6 collective-permute-done.other
  103.0 9.0 %shard_map.74 = bf16[512,1024]{1,0:T(8,128)(2,1)} custom-call(s32[3]{0:T(128)} %pad_add_fusion.here, bf16[512,1024]{1,0:T(8,128)(2,1)} %bitcast.32, f32[1,1024]{1,0:T(1,128)} %bitcast.33, bf16[8,64,2048]{2,1,0:T(8,128)(2,1)} %copy-done.1, bf16[8,64,2048]{2,1,0:T(8,128)(2,1)} %collective-permute-done.other), custom_call_target="tpu_custom_call" | custom-call | flops 2147483648 | bytes 8388608 | tf_op jit(solution)/shard_map/pallas_call | solution.py:181
  112.0 17.7 %all-to-all-start.1 = ((bf16[32,16,1024]{2,1,0:T(8,128)(2,1)}), bf16[32,16,1024]{2,1,0:T(8,128)(2,1)S(1)}, u32[]{:S(2)}, u32[]{:S(2)}) async-start(bf16[32,16,1024]{2,1,0:T(8,128)(2,1)} %bitcast.26), calls=%async_computation.1 | async-start | bytes 2097152 | tf_op jit(solution)/shard_map/all_to_all | solution.py:230
  129.7 9.1 %shard_map.75 = bf16[1,64,2048]{2,1,0:T(8,128)(2,1)} custom-call(bf16[64,1536]{1,0:T(8,128)(2,1)} %qkv.3, bf16[32,1024]{1,0:T(8,128)(2,1)} %out.3), custom_call_target="tpu_custom_call" | custom-call | bytes 524288 | tf_op jit(solution)/shard_map/pallas_call | solution.py:89
  138.8 2.8 collective-permute-start.1
  141.6 8.5 %collective-permute-done.1 = bf16[64,2048]{1,0:T(8,128)(2,1)S(1)} collective-permute-done((bf16[64,2048]{1,0:T(8,128)(2,1)}, bf16[64,2048]{1,0:T(8,128)(2,1)S(1)}, u32[]{:S(2)}, u32[]{:S(2)}) %collective-permute-start.1) | collective-permute-done | bytes 262176 | tf_op jit(solution)/shard_map/ppermute | solution.py:197
  150.1 1.0 pad_maximum_fusion
  151.1 3.1 collective-permute-start.3
  154.2 2.7 collective-permute-start.2
  158.0 8.2 %collective-permute-done.3 = bf16[128,2048]{1,0:T(8,128)(2,1)S(1)} collective-permute-done((bf16[128,2048]{1,0:T(8,128)(2,1)S(1)}, bf16[128,2048]{1,0:T(8,128)(2,1)S(1)}, u32[]{:S(2)}, u32[]{:S(2)}) %collective-permute-start.3) | collective-permute-done | bytes 524320 | tf_op jit(solution)/shard_map/ppermute | solution.py:197
  166.2 4.3 %collective-permute-start.5 = (bf16[64,2048]{1,0:T(8,128)(2,1)S(1)}, bf16[64,2048]{1,0:T(8,128)(2,1)S(1)}, u32[]{:S(2)}, u32[]{:S(2)}) collective-permute-start(bf16[64,2048]{1,0:T(8,128)(2,1)S(1)} %slice.21), channel_id=1, source_target_pairs={{0,384},{32,416},{64,448},{96,480},{128,0},{160,32},{192,64},{224,... | collective-permute-start | bytes 786440 | tf_op jit(solution)/shard_map/ppermute | solution.py:197
  170.6 1.9 collective-permute-start.4
  172.6 7.5 %collective-permute-done.4 = bf16[64,2048]{1,0:T(8,128)(2,1)S(1)} collective-permute-done((bf16[64,2048]{1,0:T(8,128)(2,1)S(1)}, bf16[64,2048]{1,0:T(8,128)(2,1)S(1)}, u32[]{:S(2)}, u32[]{:S(2)}) %collective-permute-start.4) | collective-permute-done | bytes 262176 | tf_op jit(solution)/shard_map/ppermute | solution.py:197
  180.1 1.9 collective-permute-start.6
  182.0 4.3 %collective-permute-done.6.other = bf16[8,64,2048]{2,1,0:T(8,128)(2,1)} collective-permute-done((bf16[8,64,2048]{2,1,0:T(8,128)(2,1)S(1)}, bf16[8,64,2048]{2,1,0:T(8,128)(2,1)}, u32[]{:S(2)}, u32[]{:S(2)}) %collective-permute-start.6) | collective-permute-done | bytes 2097184 | tf_op jit(solution)/shard_map/ppermute | solution.py:197
  186.3 129.0 %shard_map.76 = bf16[4,2,2,64,2048]{4,3,2,1,0:T(8,128)(2,1)} custom-call(s32[3]{0:T(128)} %pad_add_fusion.here, bf16[8,64,2048]{2,1,0:T(8,128)(2,1)} %bitcast.22, bf16[8,64,2048]{2,1,0:T(8,128)(2,1)} %collective-permute-done.6.other), custom_call_target="tpu_custom_call" | custom-call | bytes 8388608 | tf_op jit(solution)/shard_map/pallas_call | solution.py:116
  316.3 8.0 %shard_map.77 = bf16[512,512]{1,0:T(8,128)(2,1)} custom-call(bf16[512,1024]{1,0:T(8,128)(2,1)} %bitcast.27, f32[1,1024]{1,0:T(1,128)} %bitcast.34, bf16[16,64,2048]{2,1,0:T(8,128)(2,1)} %bitcast.19), custom_call_target="tpu_custom_call" | custom-call | flops 2147483648 | bytes 8388608 | tf_op jit(solution)/shard_map/pallas_call | solution.py:181
  324.3 15.6 %all-to-all-start.2 = ((bf16[32,16,512]{2,1,0:T(8,128)(2,1)}), bf16[32,16,512]{2,1,0:T(8,128)(2,1)S(1)}, u32[]{:S(2)}, u32[]{:S(2)}) async-start(bf16[32,16,512]{2,1,0:T(8,128)(2,1)} %bitcast.29), calls=%async_computation.2 | async-start | bytes 1048576 | tf_op jit(solution)/shard_map/all_to_all | solution.py:230
  339.9 1.3 fusion.7
  341.2 32.9 %all-to-all-done.2 = bf16[32,16,512]{2,1,0:T(8,128)(2,1)S(1)} async-done(((bf16[32,16,512]{2,1,0:T(8,128)(2,1)}), bf16[32,16,512]{2,1,0:T(8,128)(2,1)S(1)}, u32[]{:S(2)}, u32[]{:S(2)}) %all-to-all-start.2) | async-done | bytes 524320 | tf_op jit(solution)/shard_map/all_to_all | solution.py:230
  374.1 1.7 add_convert_fusion
  (20 shorter events, 2.7 us)
Async XLA Ops:
  96.8 6.2 %copy-start.1 = (bf16[8,64,2048]{2,1,0:T(8,128)(2,1)}, bf16[8,64,2048]{2,1,0:T(8,128)(2,1)S(1)}, u32[]{:S(2)}) copy-start(bf16[8,64,2048]{2,1,0:T(8,128)(2,1)S(1)} %all_to_all.15.mine) | copy-start | bytes 6291460
  96.8 6.2 %collective-permute-start = (bf16[8,64,2048]{2,1,0:T(8,128)(2,1)S(1)}, bf16[8,64,2048]{2,1,0:T(8,128)(2,1)}, u32[]{:S(2)}, u32[]{:S(2)}) collective-permute-start(bf16[8,64,2048]{2,1,0:T(8,128)(2,1)S(1)} %all_to_all.15.mine), channel_id=1, source_target_pairs={{0,32},{32,0},{64,96},{96,64},{128,160},{160,128},{192,224},{224,1... | collective-permute-start | bytes 6291464 | tf_op jit(solution)/shard_map/ppermute | solution.py:197
  112.0 203.2 %all-to-all-start.1 = ((bf16[32,16,1024]{2,1,0:T(8,128)(2,1)}), bf16[32,16,1024]{2,1,0:T(8,128)(2,1)S(1)}, u32[]{:S(2)}, u32[]{:S(2)}) async-start(bf16[32,16,1024]{2,1,0:T(8,128)(2,1)} %bitcast.26), calls=%async_computation.1 | async-start | bytes 2097152 | tf_op jit(solution)/shard_map/all_to_all | solution.py:230
  138.8 11.3 %collective-permute-start.1 = (bf16[64,2048]{1,0:T(8,128)(2,1)}, bf16[64,2048]{1,0:T(8,128)(2,1)S(1)}, u32[]{:S(2)}, u32[]{:S(2)}) collective-permute-start(bf16[64,2048]{1,0:T(8,128)(2,1)} %bitcast.23), channel_id=1, source_target_pairs={{0,64},{32,96},{64,0},{96,32},{128,192},{160,224},{192,128},{224,1... | collective-permute-start | bytes 786440 | tf_op jit(solution)/shard_map/ppermute | solution.py:197
  151.1 15.0 %collective-permute-start.3 = (bf16[128,2048]{1,0:T(8,128)(2,1)S(1)}, bf16[128,2048]{1,0:T(8,128)(2,1)S(1)}, u32[]{:S(2)}, u32[]{:S(2)}) collective-permute-start(bf16[128,2048]{1,0:T(8,128)(2,1)S(1)} %pad_maximum_fusion), channel_id=1, source_target_pairs={{0,384},{32,416},{64,448},{96,480},{128,0},{160,32},{192,64},{224,... | collective-permute-start | bytes 1572872 | tf_op jit(solution)/shard_map/ppermute | solution.py:197
  154.2 16.3 %collective-permute-start.2 = (bf16[128,2048]{1,0:T(8,128)(2,1)S(1)}, bf16[128,2048]{1,0:T(8,128)(2,1)S(1)}, u32[]{:S(2)}, u32[]{:S(2)}) collective-permute-start(bf16[128,2048]{1,0:T(8,128)(2,1)S(1)} %pad_maximum_fusion), channel_id=1, source_target_pairs={{0,128},{32,160},{64,192},{96,224},{128,256},{160,288},{192,320},{... | collective-permute-start | bytes 1572872 | tf_op jit(solution)/shard_map/ppermute | solution.py:197
  166.2 13.9 %collective-permute-start.5 = (bf16[64,2048]{1,0:T(8,128)(2,1)S(1)}, bf16[64,2048]{1,0:T(8,128)(2,1)S(1)}, u32[]{:S(2)}, u32[]{:S(2)}) collective-permute-start(bf16[64,2048]{1,0:T(8,128)(2,1)S(1)} %slice.21), channel_id=1, source_target_pairs={{0,384},{32,416},{64,448},{96,480},{128,0},{160,32},{192,64},{224,... | collective-permute-start | bytes 786440 | tf_op jit(solution)/shard_map/ppermute | solution.py:197
  170.6 9.5 %collective-permute-start.4 = (bf16[64,2048]{1,0:T(8,128)(2,1)S(1)}, bf16[64,2048]{1,0:T(8,128)(2,1)S(1)}, u32[]{:S(2)}, u32[]{:S(2)}) collective-permute-start(bf16[64,2048]{1,0:T(8,128)(2,1)S(1)} %slice.20), channel_id=1, source_target_pairs={{0,128},{32,160},{64,192},{96,224},{128,256},{160,288},{192,320},{... | collective-permute-start | bytes 786440 | tf_op jit(solution)/shard_map/ppermute | solution.py:197
  180.1 6.2 %copy-start = (bf16[512,2048]{1,0:T(8,128)(2,1)}, bf16[512,2048]{1,0:T(8,128)(2,1)S(1)}, u32[]{:S(2)}) copy-start(bf16[512,2048]{1,0:T(8,128)(2,1)S(1)} %constant_dynamic-update-slice_fusion) | copy-start | bytes 6291460
  180.1 6.2 %collective-permute-start.6 = (bf16[8,64,2048]{2,1,0:T(8,128)(2,1)S(1)}, bf16[8,64,2048]{2,1,0:T(8,128)(2,1)}, u32[]{:S(2)}, u32[]{:S(2)}) collective-permute-start(bf16[8,64,2048]{2,1,0:T(8,128)(2,1)S(1)} %bitcast.21), channel_id=1, source_target_pairs={{0,32},{32,0},{64,96},{96,64},{128,160},{160,128},{192,224},{224,1... | collective-permute-start | bytes 6291464 | tf_op jit(solution)/shard_map/ppermute | solution.py:197
  315.3 1.0 copy-start.3
  324.3 49.8 %copy-start.2 = (bf16[512,1024]{1,0:T(8,128)(2,1)S(1)}, bf16[512,1024]{1,0:T(8,128)(2,1)}, u32[]{:S(2)}) copy-start(bf16[512,1024]{1,0:T(8,128)(2,1)} %shard_map.74) | copy-start | bytes 3145732
  324.3 49.8 %all-to-all-start.2 = ((bf16[32,16,512]{2,1,0:T(8,128)(2,1)}), bf16[32,16,512]{2,1,0:T(8,128)(2,1)S(1)}, u32[]{:S(2)}, u32[]{:S(2)}) async-start(bf16[32,16,512]{2,1,0:T(8,128)(2,1)} %bitcast.29), calls=%async_computation.2 | async-start | bytes 1048576 | tf_op jit(solution)/shard_map/all_to_all | solution.py:230

commit v3 on v2

--- a/solution.py
+++ b/solution.py
@@ -62,66 +62,65 @@
         store(columns, product)
 
 
-def pack_kernel(qkv, out, packed, sems):
+def pack_kernel(qkv, out, next_qkv, next_out, packed, next_packed):
     depth, width = qkv.shape
     half = out.shape[1] // 2
-    copies = []
+
+    def pack(qkv, out, target):
+        target[:, pl.ds(0, width)] = qkv[...]
+        target[pl.ds(0, depth // 2), pl.ds(width, half)] = out[:, pl.ds(0, half)]
+        target[pl.ds(depth // 2, depth // 2), pl.ds(width, half)] = out[:, pl.ds(half, half)]
+
     for index in range(packed.shape[0]):
-        target = packed.at[index]
-        copies += [
-            pltpu.make_async_copy(qkv, target.at[:, pl.ds(0, width)], sems.at[index, 0]),
-            pltpu.make_async_copy(
-                out.at[:, pl.ds(0, half)], target.at[pl.ds(0, depth // 2), pl.ds(width, half)], sems.at[index, 1]
-            ),
-            pltpu.make_async_copy(
-                out.at[:, pl.ds(half, half)], target.at[pl.ds(depth // 2, depth // 2), pl.ds(width, half)], sems.at[index, 2]
-            ),
-        ]
-    for copy in copies:
-        copy.start()
-    for copy in copies:
-        copy.wait()
-
-
-def packed_weights(qkv, out, copies):
-    depth = qkv.shape[0]
-    far = pl.BlockSpec(memory_space=pl.ANY)
+        pack(qkv, out, packed.at[index])
+    pack(next_qkv, next_out, next_packed)
+
+
+def packed_weights(qkv, out, next_qkv, next_out, copies):
+    depth, width = qkv.shape[0], qkv.shape[1] + INNER
+    near = pl.BlockSpec(memory_space=pltpu.VMEM)
     return pl.pallas_call(
         pack_kernel,
-        out_shape=jax.ShapeDtypeStruct((copies, depth, qkv.shape[1] + INNER), BF16),
-        in_specs=[far, far],
-        out_specs=far,
-        scratch_shapes=[pltpu.SemaphoreType.DMA((copies, 3))],
-        cost_estimate=pl.CostEstimate(flops=0, bytes_accessed=copies * MIB // 2, transcendentals=0),
-    )(qkv, out)
-
-
-def place_kernel(here, mine, other, placed, sems):
+        out_shape=[
+            jax.ShapeDtypeStruct((copies, depth, width), BF16),
+            jax.ShapeDtypeStruct((depth, width), BF16),
+        ],
+        in_specs=[near] * 4,
+        out_specs=[near] * 2,
+        cost_estimate=pl.CostEstimate(flops=0, bytes_accessed=3 * MIB, transcendentals=0),
+    )(qkv, out, next_qkv, next_out)
+
+
+def fetches(here, mine, other, columns, placed, sems):
     across, beside, core = here[0], here[1], here[2]
     copies = []
     for side, source in enumerate((mine, other)):
         for index in range(source.shape[0]):
-            step = (0, -1, 1, 2)[index // 2]
-            target = placed.at[(across + step + 4) % 4, (beside + index) % 2, (core + side) % 2]
-            copies.append(pltpu.make_async_copy(source.at[index], target, sems.at[side, index]))
+            step = (0, 3, 1, 2)[index // 2]
+            row = ((across + step) % 4 * 2 + (beside + index) % 2) * 2 + (core + side) % 2
+            copies.append(pltpu.make_async_copy(source.at[index, :, columns], placed.at[row], sems.at[side, index]))
+    return copies
+
+
+def place_kernel(here, mine, other, placed, sems):
+    copies = fetches(here, mine, other, pl.ds(3 * INNER, INNER), placed, sems)
     for copy in copies:
         copy.start()
     for copy in copies:
         copy.wait()
 
 
-def in_order(here, mine, other):
-    parts, depth, width = mine.shape
+def out_in_order(here, mine, other):
+    parts, depth, _ = mine.shape
     far = pl.BlockSpec(memory_space=pl.ANY)
-    placed = pl.pallas_call(
+    return pl.pallas_call(
         place_kernel,
-        out_shape=jax.ShapeDtypeStruct((4, 2, 2, depth, width), BF16),
+        out_shape=jax.ShapeDtypeStruct((2 * parts, depth, INNER), BF16),
         in_specs=[pl.BlockSpec(memory_space=pltpu.SMEM), far, far],
-        out_specs=far,
+        out_specs=pl.BlockSpec(memory_space=pltpu.VMEM),
         scratch_shapes=[pltpu.SemaphoreType.DMA((2, parts))],
-        cost_estimate=pl.CostEstimate(flops=0, bytes_accessed=8 * MIB, transcendentals=0),
+        cost_estimate=pl.CostEstimate(flops=0, bytes_accessed=2 * MIB, transcendentals=0),
     )(here, mine, other)
-    return placed.reshape(2 * parts, depth, width)
 
 
 def spatial_kernel(here, tokens, gain, mine, other, middle, weights, qkv, context, sems):
@@ -151,11 +150,13 @@
         middle[:, columns] = (tokens[:, columns].astype(F32) + added).astype(BF16)
 
 
-def temporal_kernel(frames, middle, gain, placed, context, weights, qkv, sems):
-    copy = pltpu.make_async_copy(placed.at[:, :, pl.ds(0, 3 * INNER)], weights, sems.at[0])
-    copy.start()
+def temporal_kernel(frames, here, middle, gain, mine, other, context, weights, qkv, sems):
+    copies = fetches(here, mine, other, pl.ds(0, 3 * INNER), weights, sems)
+    for copy in copies:
+        copy.start()
     normed = norm_rows(middle[...].astype(F32), gain[...]).astype(BF16)
-    copy.wait()
+    for copy in copies:
+        copy.wait()
     places = middle.shape[0] // frames
 
     def store(columns, product):
@@ -184,7 +185,7 @@
         in_specs=[specs[kind] for kind in kinds],
         out_specs=near,
         scratch_shapes=scratch,
-        compiler_params=pltpu.CompilerParams(vmem_limit_bytes=57 * MIB),
+        compiler_params=pltpu.CompilerParams(vmem_limit_bytes=40 * MIB),
         cost_estimate=pl.CostEstimate(flops=4 * rows * depth * depth, bytes_accessed=8 * MIB, transcendentals=2 * MIB),
     )(*operands)
 
@@ -201,14 +202,13 @@
     return moved(array, lambda x, yl, core: (x, yl, 1 - core))
 
 
-def gathered_by_hops(own):
-    depth = own.shape[0]
+def gathered_by_hops(both):
+    depth = both.shape[0] // 2
     ahead = lambda x, yl, core: (x + 1, yl, core)
     back = lambda x, yl, core: (x + 3, yl, core)
-    both = jnp.concatenate([own, moved(own, lambda x, yl, core: (x, 1 - yl, core))], axis=0)
     left, right = moved(both, ahead), moved(both, back)
     far = moved(left[:depth], ahead), moved(right[depth:], back)
-    mine = jnp.concatenate([both, left, right, *far], axis=0).reshape(8, depth, own.shape[1])
+    mine = jnp.concatenate([both, left, right, *far], axis=0).reshape(8, depth, both.shape[1])
     return mine, other_core(mine)
 
 
@@ -229,9 +229,10 @@
         sent = array.reshape(frames, block, array.shape[1])
         return lax.all_to_all(sent, "tm", split_axis=0, concat_axis=0, tiled=True).reshape(array.shape)
 
-    mine = lax.all_to_all(
-        packed_weights(spatial_qkv, spatial_out, parts), "fsdp", 0, 0, axis_index_groups=cores, tiled=True
-    )
+    packed, own = packed_weights(spatial_qkv, spatial_out, temporal_qkv, temporal_out, parts)
+    mine = lax.all_to_all(packed, "fsdp", 0, 0, axis_index_groups=cores, tiled=True)
+    own, mine = lax.optimization_barrier((own, mine))
+    beside = moved(own, lambda x, yl, core: (x, 1 - yl, core))
     middle = kernel_call(
         spatial_kernel,
         "svvhh",
@@ -244,21 +245,21 @@
         ],
         (here, flat, spatial_gain.reshape(1, depth), mine, other_core(mine)),
     )
+    own, beside, middle = lax.optimization_barrier((own, beside, middle))
     arrived = exchanged(middle)
-    own, _ = lax.optimization_barrier((packed_weights(temporal_qkv, temporal_out, 1)[0], middle[:8, :128]))
-    placed = in_order(here, *gathered_by_hops(own))
+    mine, other = gathered_by_hops(jnp.concatenate([own, beside], axis=0))
     context = kernel_call(
         functools.partial(temporal_kernel, frames),
-        "vvh",
+        "svvhh",
         jax.ShapeDtypeStruct((rows, INNER), BF16),
         [
             pltpu.VMEM((members, depth // members, 3 * INNER), BF16),
             pltpu.VMEM((rows, 3 * INNER), BF16),
-            pltpu.SemaphoreType.DMA((1,)),
+            pltpu.SemaphoreType.DMA((2, parts)),
         ],
-        (arrived, temporal_gain.reshape(1, depth), placed),
-    )
-    weight = jnp.concatenate(out_weight(placed[:, :, 3 * INNER :]), axis=1)
+        (here, arrived, temporal_gain.reshape(1, depth), mine, other),
+    )
+    weight = jnp.concatenate(out_weight(out_in_order(here, mine, other)), axis=1)
     returned = exchanged(context)
     encoded = middle.astype(F32) + jnp.dot(returned, weight, preferred_element_type=F32)
     return encoded.astype(BF16).reshape(tokens.shape)

time: 377 us -> 174 us (0.46)
  Pallas kernels: 220 us -> 19.7 us
  starting transfers between devices: 52 us -> 41.5 us
  waiting for transfers between devices: 64.9 us -> 69.5 us
    pallas_call x3 -> x2, Pallas kernels: 203 us -> 5.68 us  [the longest x1 3.08 us: out_in_order(): pl.pallas_call(place_kernel, out_shape=jax.ShapeDtypeStruct((2 * parts, d...]
    all_to_all x2, waiting for transfers between devices: 32.9 us -> 47.5 us  [exchanged(): lax.all_to_all(sent, 'tm', split_axis=0, concat_axis=0, tiled=True)]
    all_to_all x2, starting transfers between devices: 33.3 us -> 22.1 us  [exchanged(): lax.all_to_all(sent, 'tm', split_axis=0, concat_axis=0, tiled=True)]
    ppermute x7, waiting for transfers between devices: 32 us -> 22 us  [moved(): return lax.ppermute(array, 'fsdp', pairs)]
  transfers between devices with their start and end apart: 9 -> 9, of which waited for: 6 -> 6; matrix products, arithmetic and copies ran while one was open for 1% -> 1% of each run, Pallas kernels for 37% -> 6%
where the time goes in v3:
time: 174 us; the launch traced here: 173 us
  waiting for transfers between devices  69.5 us (40%)
  starting transfers between devices  41.5 us (24%)
  blocking collectives  32.1 us (18%)
  Pallas kernels  19.7 us (11%)
  local copies, waits for them, and re-layouts  6.91 us (4%)
  matrix products  2.91 us (2%)
    all_to_all x2, waiting for transfers between devices, exchanged(): lax.all_to_all(sent, 'tm', split_axis=0, concat_axis=0, tiled=True)  47.5 us
    all_to_all x1, blocking collectives, shards(): lax.all_to_all(packed, 'fsdp', 0, 0, axis_index_groups=cores, tiled=True)  32.1 us
    all_to_all x2, starting transfers between devices, exchanged(): lax.all_to_all(sent, 'tm', split_axis=0, concat_axis=0, tiled=True)  22.1 us
    ppermute x7, waiting for transfers between devices, moved(): return lax.ppermute(array, 'fsdp', pairs)  22 us
    ppermute x7, starting transfers between devices, moved(): return lax.ppermute(array, 'fsdp', pairs)  19.4 us
    pallas_call x2, Pallas kernels, kernel_call(): pl.pallas_call(body, out_shape=out, in_specs=[specs[kind] for kind in kin...  14 us
    unnamed x24, local copies, waits for them, and re-layouts  4.59 us
  transfers between devices with their start and end apart: 9, of which 6 were waited for; matrix products, arithmetic and copies ran while one was open for 1% of the time, Pallas kernels for 6%

profile of v3, /device:TPU:32, one launch (start us, length us, event | category | flops | bytes accessed | tf_op | source)
XLA Modules:
  0.0 172.9 jit_solution(4842767072438997292)
XLA Ops:
  0.0 2.6 %shard_map.73 = (bf16[8,64,2048]{2,1,0:T(8,128)(2,1)}, bf16[64,2048]{1,0:T(8,128)(2,1)}) custom-call(bf16[64,1536]{1,0:T(8,128)(2,1)} %qkv.1, bf16[32,1024]{1,0:T(8,128)(2,1)} %out.1, bf16[64,1536]{1,0:T(8,128)(2,1)} %next_qkv.1, bf16[32,1024]{1,0:T(8,128)(2,1)} %next_out.1), custom_call_target="tpu_custom_call" | custom-call | bytes 3145728 | tf_op jit(solution)/shard_map/pallas_call | solution.py:82
  2.6 32.1 %all_to_all.15.mine = bf16[8,64,2048]{2,1,0:T(8,128)(2,1)S(1)} all-to-all(bf16[8,64,2048]{2,1,0:T(8,128)(2,1)} %get-tuple-element.13), channel_id=1, replica_groups={{0,64,128,192,256,320,384,448},{32,96,160,224,288,352,416,480},{1,65,12..., dimensions={0} | all-to-all | bytes 4194304 | tf_op jit(solution)/shard_map/all_to_all | solution.py:233
  34.7 1.9 %collective-permute-start.1 = (bf16[8,64,2048]{2,1,0:T(8,128)(2,1)S(1)}, bf16[8,64,2048]{2,1,0:T(8,128)(2,1)}, u32[]{:S(2)}, u32[]{:S(2)}) collective-permute-start(bf16[8,64,2048]{2,1,0:T(8,128)(2,1)S(1)} %all_to_all.15.mine), channel_id=1, source_target_pairs={{0,32},{32,0},{64,96},{96,64},{128,160},{160,128},{192,224},{224,1... | collective-permute-start | bytes 6291464 | tf_op jit(solution)/shard_map/ppermute | solution.py:198
  36.7 3.4 %collective-permute-start = (bf16[64,2048]{1,0:T(8,128)(2,1)S(1)}, bf16[64,2048]{1,0:T(8,128)(2,1)S(1)}, u32[]{:S(2)}, u32[]{:S(2)}) collective-permute-start(bf16[64,2048]{1,0:T(8,128)(2,1)S(1)} %copy-done.8), channel_id=1, source_target_pairs={{0,64},{32,96},{64,0},{96,32},{128,192},{160,224},{192,128},{224,1... | collective-permute-start | bytes 786440 | tf_op jit(solution)/shard_map/ppermute | solution.py:198
  40.9 7.9 %shard_map.74 = bf16[512,1024]{1,0:T(8,128)(2,1)} custom-call(s32[3]{0:T(128)S(1)} %pad_add_fusion.here, bf16[512,1024]{1,0:T(8,128)(2,1)S(1)} %bitcast.22, f32[1,1024]{1,0:T(1,128)S(1)} %bitcast.23, bf16[8,64,2048]{2,1,0:T(8,128)(2,1)S(1)} %all_to_all.15.mine, bf16[8,64,2048]{2,1,0:T(8,128)(2,1)} %collective-permute-done.1.other), custom_call_target="tpu_custom_call" | custom-call | flops 2147483648 | bytes 8388608 | tf_op jit(solution)/shard_map/pallas_call | solution.py:182
  49.5 17.7 %all-to-all-start.1 = ((bf16[32,16,1024]{2,1,0:T(8,128)(2,1)}), bf16[32,16,1024]{2,1,0:T(8,128)(2,1)S(1)}, u32[]{:S(2)}, u32[]{:S(2)}) async-start(bf16[32,16,1024]{2,1,0:T(8,128)(2,1)} %bitcast.5), calls=%async_computation.1 | async-start | bytes 2097152 | tf_op jit(solution)/shard_map/all_to_all | solution.py:230
  67.2 1.0 constant_dynamic-update-slice_fusion
  68.2 3.2 %collective-permute-start.3 = (bf16[128,2048]{1,0:T(8,128)(2,1)S(1)}, bf16[128,2048]{1,0:T(8,128)(2,1)S(1)}, u32[]{:S(2)}, u32[]{:S(2)}) collective-permute-start(bf16[128,2048]{1,0:T(8,128)(2,1)S(1)} %get-tuple-element.21), channel_id=1, source_target_pairs={{0,384},{32,416},{64,448},{96,480},{128,0},{160,32},{192,64},{224,... | collective-permute-start | bytes 1572872 | tf_op jit(solution)/shard_map/ppermute | solution.py:198
  71.5 2.6 %collective-permute-start.2 = (bf16[128,2048]{1,0:T(8,128)(2,1)S(1)}, bf16[128,2048]{1,0:T(8,128)(2,1)S(1)}, u32[]{:S(2)}, u32[]{:S(2)}) collective-permute-start(bf16[128,2048]{1,0:T(8,128)(2,1)S(1)} %get-tuple-element.21), channel_id=1, source_target_pairs={{0,128},{32,160},{64,192},{96,224},{128,256},{160,288},{192,320},{... | collective-permute-start | bytes 1572872 | tf_op jit(solution)/shard_map/ppermute | solution.py:198
  74.1 9.4 %collective-permute-done.3 = bf16[128,2048]{1,0:T(8,128)(2,1)S(1)} collective-permute-done((bf16[128,2048]{1,0:T(8,128)(2,1)S(1)}, bf16[128,2048]{1,0:T(8,128)(2,1)S(1)}, u32[]{:S(2)}, u32[]{:S(2)}) %collective-permute-start.3) | collective-permute-done | bytes 524320 | tf_op jit(solution)/shard_map/ppermute | solution.py:198
  83.6 4.4 %collective-permute-start.5 = (bf16[64,2048]{1,0:T(8,128)(2,1)S(1)}, bf16[64,2048]{1,0:T(8,128)(2,1)S(1)}, u32[]{:S(2)}, u32[]{:S(2)}) collective-permute-start(bf16[64,2048]{1,0:T(8,128)(2,1)S(1)} %slice.17), channel_id=1, source_target_pairs={{0,384},{32,416},{64,448},{96,480},{128,0},{160,32},{192,64},{224,... | collective-permute-start | bytes 786440 | tf_op jit(solution)/shard_map/ppermute | solution.py:198
  88.1 1.9 %collective-permute-start.4 = (bf16[64,2048]{1,0:T(8,128)(2,1)S(1)}, bf16[64,2048]{1,0:T(8,128)(2,1)S(1)}, u32[]{:S(2)}, u32[]{:S(2)}) collective-permute-start(bf16[64,2048]{1,0:T(8,128)(2,1)S(1)} %slice.16), channel_id=1, source_target_pairs={{0,128},{32,160},{64,192},{96,224},{128,256},{160,288},{192,320},{... | collective-permute-start | bytes 786440 | tf_op jit(solution)/shard_map/ppermute | solution.py:198
  90.1 7.7 %collective-permute-done.4 = bf16[64,2048]{1,0:T(8,128)(2,1)S(1)} collective-permute-done((bf16[64,2048]{1,0:T(8,128)(2,1)S(1)}, bf16[64,2048]{1,0:T(8,128)(2,1)S(1)}, u32[]{:S(2)}, u32[]{:S(2)}) %collective-permute-start.4) | collective-permute-done | bytes 262176 | tf_op jit(solution)/shard_map/ppermute | solution.py:198
  97.8 1.9 %collective-permute-start.6 = (bf16[8,64,2048]{2,1,0:T(8,128)(2,1)S(1)}, bf16[8,64,2048]{2,1,0:T(8,128)(2,1)S(1)}, u32[]{:S(2)}, u32[]{:S(2)}) collective-permute-start(bf16[8,64,2048]{2,1,0:T(8,128)(2,1)S(1)} %bitcast.17), channel_id=1, source_target_pairs={{0,32},{32,0},{64,96},{96,64},{128,160},{160,128},{192,224},{224,1... | collective-permute-start | bytes 6291464 | tf_op jit(solution)/shard_map/ppermute | solution.py:198
  99.8 4.1 %collective-permute-done.6.other = bf16[8,64,2048]{2,1,0:T(8,128)(2,1)S(1)} collective-permute-done((bf16[8,64,2048]{2,1,0:T(8,128)(2,1)S(1)}, bf16[8,64,2048]{2,1,0:T(8,128)(2,1)S(1)}, u32[]{:S(2)}, u32[]{:S(2)}) %collective-permute-start.6) | collective-permute-done | bytes 2097184 | tf_op jit(solution)/shard_map/ppermute | solution.py:198
  103.9 1.3 copy-done.1
  105.2 18.2 %all-to-all-done.1 = bf16[32,16,1024]{2,1,0:T(8,128)(2,1)S(1)} async-done(((bf16[32,16,1024]{2,1,0:T(8,128)(2,1)}), bf16[32,16,1024]{2,1,0:T(8,128)(2,1)S(1)}, u32[]{:S(2)}, u32[]{:S(2)}) %all-to-all-start.1) | async-done | bytes 1048608 | tf_op jit(solution)/shard_map/all_to_all | solution.py:230
  123.4 1.6 copy-done.2
  125.0 6.1 %shard_map.75 = bf16[512,512]{1,0:T(8,128)(2,1)S(1)} custom-call(s32[3]{0:T(128)S(1)} %pad_add_fusion.here, bf16[512,1024]{1,0:T(8,128)(2,1)S(1)} %bitcast.20, f32[1,1024]{1,0:T(1,128)S(1)} %bitcast.24, bf16[8,64,2048]{2,1,0:T(8,128)(2,1)S(1)} %bitcast.18, bf16[8,64,2048]{2,1,0:T(8,128)(2,1)S(1)} %copy-done.2), custom_call_target="tpu_custom_call" | custom-call | flops 2147483648 | bytes 8388608 | tf_op jit(solution)/shard_map/pallas_call | solution.py:182
  131.9 4.4 %all-to-all-start.2 = ((bf16[32,16,512]{2,1,0:T(8,128)(2,1)}), bf16[32,16,512]{2,1,0:T(8,128)(2,1)S(1)}, u32[]{:S(2)}, u32[]{:S(2)}) async-start(bf16[32,16,512]{2,1,0:T(8,128)(2,1)} %bitcast.21), calls=%async_computation.2 | async-start | bytes 1048576 | tf_op jit(solution)/shard_map/all_to_all | solution.py:230
  136.4 3.1 %shard_map.76 = bf16[16,64,512]{2,1,0:T(8,128)(2,1)} custom-call(s32[3]{0:T(128)} %copy-done.4, bf16[8,64,2048]{2,1,0:T(8,128)(2,1)} %bitcast.19, bf16[8,64,2048]{2,1,0:T(8,128)(2,1)} %copy-done.1), custom_call_target="tpu_custom_call" | custom-call | bytes 2097152 | tf_op jit(solution)/shard_map/pallas_call | solution.py:116
  139.5 1.3 fusion.7
  140.8 29.3 %all-to-all-done.2 = bf16[32,16,512]{2,1,0:T(8,128)(2,1)S(1)} async-done(((bf16[32,16,512]{2,1,0:T(8,128)(2,1)}), bf16[32,16,512]{2,1,0:T(8,128)(2,1)S(1)}, u32[]{:S(2)}, u32[]{:S(2)}) %all-to-all-start.2) | async-done | bytes 524320 | tf_op jit(solution)/shard_map/all_to_all | solution.py:230
  170.0 2.9 %add_convert_fusion = bf16[512,1024]{1,0:T(8,128)(2,1)} fusion(bf16[512,1024]{1,0:T(8,128)(2,1)} %shard_map.74, bf16[512,512]{1,0:T(8,128)(2,1)S(1)} %bitcast.25, bf16[512,512]{1,0:T(8,128)(2,1)S(1)} %bitcast.27, bf16[512,512]{1,0:T(8,128)(2,1)S(1)} %bitcast.26), kind=kOutput, calls=%fused_computation | convolution fusion | flops 540540928 | bytes 3670016 | tf_op jit(solution)/shard_map/dot_general | solution.py:264
  (30 shorter events, 2.5 us)
Async XLA Ops:
  2.6 34.1 %copy-start.8 = (bf16[64,2048]{1,0:T(8,128)(2,1)S(1)}, bf16[64,2048]{1,0:T(8,128)(2,1)}, u32[]{:S(2)}) copy-start(bf16[64,2048]{1,0:T(8,128)(2,1)} %get-tuple-element.17) | copy-start | bytes 786436
  2.6 38.3 %copy-start.5 = (bf16[2,1,256,1024]{3,2,1,0:T(8,128)(2,1)S(1)}, bf16[2,1,256,1024]{3,2,1,0:T(8,128)(2,1)}, u32[]{:S(2)}) copy-start(bf16[2,1,256,1024]{3,2,1,0:T(8,128)(2,1)} %param.7) | copy-start | bytes 3145732
  2.6 38.3 %copy-start.6 = (f32[1024]{0:T(1024)S(1)}, f32[1024]{0:T(1024)}, u32[]{:S(2)}) copy-start(f32[1024]{0:T(1024)} %param.8) | copy-start | bytes 12292
  34.7 6.2 %collective-permute-start.1 = (bf16[8,64,2048]{2,1,0:T(8,128)(2,1)S(1)}, bf16[8,64,2048]{2,1,0:T(8,128)(2,1)}, u32[]{:S(2)}, u32[]{:S(2)}) collective-permute-start(bf16[8,64,2048]{2,1,0:T(8,128)(2,1)S(1)} %all_to_all.15.mine), channel_id=1, source_target_pairs={{0,32},{32,0},{64,96},{96,64},{128,160},{160,128},{192,224},{224,1... | collective-permute-start | bytes 6291464 | tf_op jit(solution)/shard_map/ppermute | solution.py:198
  36.7 12.1 %collective-permute-start = (bf16[64,2048]{1,0:T(8,128)(2,1)S(1)}, bf16[64,2048]{1,0:T(8,128)(2,1)S(1)}, u32[]{:S(2)}, u32[]{:S(2)}) collective-permute-start(bf16[64,2048]{1,0:T(8,128)(2,1)S(1)} %copy-done.8), channel_id=1, source_target_pairs={{0,64},{32,96},{64,0},{96,32},{128,192},{160,224},{192,128},{224,1... | collective-permute-start | bytes 786440 | tf_op jit(solution)/shard_map/ppermute | solution.py:198
  40.1 83.3 %copy-start.4 = (s32[3]{0:T(128)}, s32[3]{0:T(128)S(1)}, u32[]{:S(2)}) copy-start(s32[3]{0:T(128)S(1)} %pad_add_fusion.here) | copy-start | bytes 40
  48.8 0.7 copy-start.9
  49.5 73.9 %all-to-all-start.1 = ((bf16[32,16,1024]{2,1,0:T(8,128)(2,1)}), bf16[32,16,1024]{2,1,0:T(8,128)(2,1)S(1)}, u32[]{:S(2)}, u32[]{:S(2)}) async-start(bf16[32,16,1024]{2,1,0:T(8,128)(2,1)} %bitcast.5), calls=%async_computation.1 | async-start | bytes 2097152 | tf_op jit(solution)/shard_map/all_to_all | solution.py:230
  68.2 55.2 %copy-start.7 = (f32[1024]{0:T(1024)S(1)}, f32[1024]{0:T(1024)}, u32[]{:S(2)}) copy-start(f32[1024]{0:T(1024)} %param.11) | copy-start | bytes 12292
  68.2 15.3 %collective-permute-start.3 = (bf16[128,2048]{1,0:T(8,128)(2,1)S(1)}, bf16[128,2048]{1,0:T(8,128)(2,1)S(1)}, u32[]{:S(2)}, u32[]{:S(2)}) collective-permute-start(bf16[128,2048]{1,0:T(8,128)(2,1)S(1)} %get-tuple-element.21), channel_id=1, source_target_pairs={{0,384},{32,416},{64,448},{96,480},{128,0},{160,32},{192,64},{224,... | collective-permute-start | bytes 1572872 | tf_op jit(solution)/shard_map/ppermute | solution.py:198
  71.5 16.5 %collective-permute-start.2 = (bf16[128,2048]{1,0:T(8,128)(2,1)S(1)}, bf16[128,2048]{1,0:T(8,128)(2,1)S(1)}, u32[]{:S(2)}, u32[]{:S(2)}) collective-permute-start(bf16[128,2048]{1,0:T(8,128)(2,1)S(1)} %get-tuple-element.21), channel_id=1, source_target_pairs={{0,128},{32,160},{64,192},{96,224},{128,256},{160,288},{192,320},{... | collective-permute-start | bytes 1572872 | tf_op jit(solution)/shard_map/ppermute | solution.py:198
  83.6 14.2 %collective-permute-start.5 = (bf16[64,2048]{1,0:T(8,128)(2,1)S(1)}, bf16[64,2048]{1,0:T(8,128)(2,1)S(1)}, u32[]{:S(2)}, u32[]{:S(2)}) collective-permute-start(bf16[64,2048]{1,0:T(8,128)(2,1)S(1)} %slice.17), channel_id=1, source_target_pairs={{0,384},{32,416},{64,448},{96,480},{128,0},{160,32},{192,64},{224,... | collective-permute-start | bytes 786440 | tf_op jit(solution)/shard_map/ppermute | solution.py:198
  88.1 9.7 %collective-permute-start.4 = (bf16[64,2048]{1,0:T(8,128)(2,1)S(1)}, bf16[64,2048]{1,0:T(8,128)(2,1)S(1)}, u32[]{:S(2)}, u32[]{:S(2)}) collective-permute-start(bf16[64,2048]{1,0:T(8,128)(2,1)S(1)} %slice.16), channel_id=1, source_target_pairs={{0,128},{32,160},{64,192},{96,224},{128,256},{160,288},{192,320},{... | collective-permute-start | bytes 786440 | tf_op jit(solution)/shard_map/ppermute | solution.py:198
  97.8 33.3 %copy-start = (bf16[512,2048]{1,0:T(8,128)(2,1)}, bf16[512,2048]{1,0:T(8,128)(2,1)S(1)}, u32[]{:S(2)}) copy-start(bf16[512,2048]{1,0:T(8,128)(2,1)S(1)} %constant_dynamic-update-slice_fusion.2) | copy-start | bytes 6291460
  97.8 6.1 %collective-permute-start.6 = (bf16[8,64,2048]{2,1,0:T(8,128)(2,1)S(1)}, bf16[8,64,2048]{2,1,0:T(8,128)(2,1)S(1)}, u32[]{:S(2)}, u32[]{:S(2)}) collective-permute-start(bf16[8,64,2048]{2,1,0:T(8,128)(2,1)S(1)} %bitcast.17), channel_id=1, source_target_pairs={{0,32},{32,0},{64,96},{96,64},{128,160},{160,128},{192,224},{224,1... | collective-permute-start | bytes 6291464 | tf_op jit(solution)/shard_map/ppermute | solution.py:198
  103.9 1.3 copy-start.1
  123.4 1.6 copy-start.2
  131.1 0.8 copy-start.3
  131.9 38.1 %all-to-all-start.2 = ((bf16[32,16,512]{2,1,0:T(8,128)(2,1)}), bf16[32,16,512]{2,1,0:T(8,128)(2,1)S(1)}, u32[]{:S(2)}, u32[]{:S(2)}) async-start(bf16[32,16,512]{2,1,0:T(8,128)(2,1)} %bitcast.21), calls=%async_computation.2 | async-start | bytes 1048576 | tf_op jit(solution)/shard_map/all_to_all | solution.py:230

commit v4 on v1

v4 whole, which is shorter than its diff:
```python
import functools

import jax
import jax.numpy as jnp
from jax import lax
from jax.experimental import pallas as pl
from jax.experimental.pallas import tpu as pltpu
from jax.sharding import PartitionSpec as P

HEAD = 64
HEADS = 8
INNER = 512
EPSILON = 1e-06
BF16, F32 = jnp.bfloat16, jnp.float32
GROUP = 8
PAIR = 2 * HEAD
ROWS = 256
MIB = 1 << 20


def norm_rows(values, gain):
    centre = values - jnp.mean(values, axis=-1, keepdims=True)
    spread = jnp.mean(centre * centre, axis=-1, keepdims=True)
    return centre * lax.rsqrt(spread + EPSILON) * gain


def attend(qkv, rows, same):
    low = lax.broadcasted_iota(jnp.int32, (ROWS, PAIR), 1) < HEAD
    outs = []
    for pair in range(HEADS // 2):
        queries = qkv[rows, pl.ds(pair * PAIR, PAIR)]
        keys = qkv[rows, pl.ds(INNER + pair * PAIR, PAIR)]
        values = qkv[rows, pl.ds(2 * INNER + pair * PAIR, PAIR)]
        halves = []
        for mine in (low, ~low):
            own = jnp.where(mine, queries, jnp.zeros_like(queries))
            scores = lax.dot_general(own, keys, (((1,), (1,)), ((), ())), preferred_element_type=F32)
            if same is not None:
                scores = jnp.where(same, scores, -1e30)
            exponent = jnp.exp(scores - jnp.max(scores, axis=-1, keepdims=True))
            weights = exponent * (1.0 / jnp.sum(exponent, axis=-1, keepdims=True))
            halves.append(jnp.dot(weights.astype(BF16), values, preferred_element_type=F32))
        outs.append(jnp.where(low, halves[0], halves[1]))
    return jnp.concatenate(outs, axis=1)


def project(product, store):
    for piece in range(3 * INNER // 256):
        columns = pl.ds(piece * 256, 256)
        value = product(columns)
        if piece < INNER // 256:
            value = value * HEAD**-0.5
        store(columns, value)


def pack_kernel(qkv, out, packed):
    depth, width = qkv.shape
    half = out.shape[1] // 2
    for index in range(packed.shape[0]):
        packed[index, :, pl.ds(0, width)] = qkv[...]
        packed[index, pl.ds(0, depth // 2), pl.ds(width, half)] = out[:, pl.ds(0, half)]
        packed[index, pl.ds(depth // 2, depth // 2), pl.ds(width, half)] = out[:, pl.ds(half, half)]


def run(copies):
    for copy in copies:
        copy.start()
    return copies


def wait(copies):
    for copy in copies:
        copy.wait()


def norm_kernel(here, tokens, gain, mine, other):
    normed = norm_rows(tokens[...].astype(F32), gain[...]).astype(BF16)
    depth, width = normed.shape[1], mine.shape[1]
    source = lax.broadcasted_iota(jnp.int32, (depth, width), 0)
    target = lax.broadcasted_iota(jnp.int32, (depth, width), 1)
    block = depth // 16
    first = target // block * (2 * block) + target % block
    for out, core in ((mine, here[2]), (other, 1 - here[2])):
        chosen = (source == first + core * block).astype(F32).astype(BF16)
        out[...] = jnp.dot(normed, chosen, preferred_element_type=F32).astype(BF16)


def half_kernel(normed, weights, partial):
    depth = normed.shape[1]
    for piece in range(partial.shape[1] // 256):
        columns = pl.ds(piece * 256, 256)
        partial[:, columns] = jnp.dot(
            normed[...], weights[:, :, columns].reshape(depth, 256), preferred_element_type=F32
        )


def spatial_kernel(here, tokens, partial, normed, mine, other, middle, out_ref, qkv, context, sems):
    core = here[2]
    outs = pl.ds(3 * INNER, INNER)
    copies = run(
        [
            pltpu.make_async_copy(mine.at[:, :, outs], out_ref.at[:, core], sems.at[0]),
            pltpu.make_async_copy(other.at[:, :, outs], out_ref.at[:, 1 - core], sems.at[1]),
        ]
    )
    depth = normed.shape[1]

    def product(columns):
        weight = other[:, :, columns].reshape(depth, 256)
        return partial[:, columns] + jnp.dot(normed[...], weight, preferred_element_type=F32)

    def store(columns, value):
        qkv[:, columns] = value.astype(BF16)

    project(product, store)
    for clip in range(tokens.shape[0] // ROWS):
        rows = pl.ds(clip * ROWS, ROWS)
        context[rows, :] = attend(qkv, rows, None).astype(BF16)
    wait(copies)
    parts, cores, twice, width = out_ref.shape
    half = twice // 2
    for side in range(2):
        columns = pl.ds(side * width, width)
        weight = out_ref[:, :, pl.ds(side * half, half)].reshape(parts * cores * half, width)
        added = jnp.dot(context[...], weight, preferred_element_type=F32)
        middle[:, columns] = (tokens[:, columns].astype(F32) + added).astype(BF16)


def fetches(here, mine, other, placed, sems):
    copies = []
    for side, source in enumerate((mine, other)):
        for beside in range(2):
            target = placed.at[:, (here[1] + beside) % 2, (here[2] + side) % 2]
            copies.append(pltpu.make_async_copy(source.at[beside], target, sems.at[side, beside]))
    return run(copies)


def place_kernel(here, mine, other, placed, sems):
    wait(fetches(here, mine, other, placed, sems))


def temporal_kernel(frames, middle, gain, placed, context, qkv):
    normed = norm_rows(middle[...].astype(F32), gain[...]).astype(BF16)
    rows, depth = middle.shape
    places = rows // frames

    def product(columns):
        weight = placed[:, :, :, :, columns].reshape(depth, 256)
        return jnp.dot(normed, weight, preferred_element_type=F32)

    def store(columns, value):
        split = value.reshape(frames, places, value.shape[1])
        for group in range(places // GROUP):
            own = split[:, group * GROUP : (group + 1) * GROUP].reshape(ROWS, value.shape[1])
            qkv[pl.ds(group * ROWS, ROWS), columns] = own.astype(BF16)

    project(product, store)
    place = lax.broadcasted_iota(jnp.int32, (ROWS, ROWS), 0) % GROUP
    same = place == lax.broadcasted_iota(jnp.int32, (ROWS, ROWS), 1) % GROUP
    outs = []
    for group in range(places // GROUP):
        out = attend(qkv, pl.ds(group * ROWS, ROWS), same)
        outs.append(out.reshape(frames, GROUP, INNER))
    context[...] = jnp.concatenate(outs, axis=1).reshape(rows, INNER).astype(BF16)


def kernel_call(body, kinds, out, operands, scratch=(), gflops=0, mib=4):
    near = pl.BlockSpec(memory_space=pltpu.VMEM)
    specs = {"s": pl.BlockSpec(memory_space=pltpu.SMEM), "v": near, "h": pl.BlockSpec(memory_space=pl.ANY)}
    return pl.pallas_call(
        body,
        out_shape=out,
        in_specs=[specs[kind] for kind in kinds],
        out_specs=jax.tree.map(lambda _: near, out),
        scratch_shapes=scratch,
        compiler_params=pltpu.CompilerParams(vmem_limit_bytes=24 * MIB),
        cost_estimate=pl.CostEstimate(flops=int(gflops * 1e9), bytes_accessed=mib * MIB, transcendentals=0),
    )(*operands)


def moved(array, change):
    pairs = []
    for index in range(lax.axis_size("fsdp")):
        x, yl, core = change(index // 4, index // 2 % 2, index % 2)
        pairs.append((index, (x * 2 + yl) * 2 + core))
    return lax.ppermute(array, "fsdp", pairs)


def other_core(array):
    return moved(array, lambda x, yl, core: (x, yl, 1 - core))


def along_x(shard):
    lines = [list(range(start, 16, 4)) for start in range(4)]
    own = lax.all_gather(shard, "fsdp", axis_index_groups=lines)
    mine = jnp.stack([own, moved(own, lambda x, yl, core: (x, 1 - yl, core))])
    return mine, other_core(mine)


def shards(tokens, spatial_gain, spatial_qkv, spatial_out, temporal_gain, temporal_qkv, temporal_out):
    clips, _, places, depth = tokens.shape
    frames = lax.axis_size("tm")
    members = lax.axis_size("fsdp")
    parts, part = members // 2, depth // members
    rows = clips * places
    block = rows // frames
    flat = tokens.reshape(rows, depth)
    index = lax.axis_index("fsdp")
    here = jnp.stack([index // 4, index // 2 % 2, index % 2]).astype(jnp.int32)
    cores = [list(range(core, members, 2)) for core in range(2)]
    shape = jax.ShapeDtypeStruct

    def exchanged(array):
        sent = array.reshape(frames, block, array.shape[1])
        return lax.all_to_all(sent, "tm", split_axis=0, concat_axis=0, tiled=True).reshape(array.shape)

    def in_order(shard):
        return kernel_call(
            place_kernel,
            "shh",
            shape((4, 2, 2, *shard.shape), BF16),
            (here, *along_x(shard)),
            [pltpu.SemaphoreType.DMA((2, 2))],
        )

    packed = kernel_call(pack_kernel, "vv", shape((parts, part, 4 * INNER), BF16), (spatial_qkv, spatial_out))
    mine = lax.all_to_all(packed, "fsdp", 0, 0, axis_index_groups=cores, tiled=True)
    normed, normed_other = kernel_call(
        norm_kernel,
        "svv",
        [shape((rows, depth // 2), BF16)] * 2,
        (here, flat, spatial_gain.reshape(1, depth)),
        gflops=2,
    )
    mine, normed, normed_other = lax.optimization_barrier((mine, normed, normed_other))
    partial = kernel_call(half_kernel, "vv", shape((rows, 3 * INNER), F32), (normed, mine), gflops=1)
    middle = kernel_call(
        spatial_kernel,
        "svvvvv",
        shape((rows, depth), BF16),
        (here, flat, partial, normed_other, mine, other_core(mine)),
        [
            pltpu.VMEM((parts, 2, part, INNER), BF16),
            pltpu.VMEM((rows, 3 * INNER), BF16),
            pltpu.VMEM((rows, INNER), BF16),
            pltpu.SemaphoreType.DMA((2,)),
        ],
        gflops=3,
    )
    shard, middle = lax.optimization_barrier((temporal_qkv, middle))
    arrived = exchanged(middle)
    context = kernel_call(
        functools.partial(temporal_kernel, frames),
        "vvv",
        shape((rows, INNER), BF16),
        (arrived, temporal_gain.reshape(1, depth), in_order(shard)),
        [pltpu.VMEM((rows, 3 * INNER), BF16)],
        gflops=4,
    )
    shard, context = lax.optimization_barrier((temporal_out, context))
    returned = exchanged(context)
    weight = in_order(shard).reshape(INNER, depth)
    encoded = middle.astype(F32) + jnp.dot(returned, weight, preferred_element_type=F32)
    return encoded.astype(BF16).reshape(tokens.shape)


def solution(mesh):
    placed = (
        P("fsdp", "tm", None, None),
        P(),
        P("fsdp", None),
        P("fsdp", None),
        P(),
        P("fsdp", None),
        P("fsdp", None),
    )
    return jax.shard_map(
        shards, mesh=mesh, in_specs=placed, out_specs=P("fsdp", "tm", None, None), check_vma=False
    )
```

time: 182 us -> 174 us (0.956)
  waiting for transfers between devices: 114 us -> 83.4 us
  blocking collectives: 0 us -> 26.8 us
  between operations: 13.5 us -> 0.17 us
  starting transfers between devices: 26.6 us -> 37.7 us
  local copies, waits for them, and re-layouts: 9.51 us -> 4.61 us
  Pallas kernels: 13 us -> 17.7 us
  other arithmetic: 3.29 us -> 0.27 us
    all_gather x2 -> x0, waiting for transfers between devices: 52.1 us -> none  [gathered(): return lax.all_gather(side_by_side(qkv, out), 'fsdp', axis=0, tiled=False)]
    all_to_all x3 -> x2, waiting for transfers between devices: 61.8 us -> 20.2 us  [exchanged(): lax.all_to_all(sent, 'tm', split_axis=0, concat_axis=0, tiled=True)]
    ppermute x0 -> x5, waiting for transfers between devices: none -> 36.5 us  [moved(): return lax.ppermute(array, 'fsdp', pairs)]
    all_gather x0 -> x2, blocking collectives: none -> 26.8 us  [along_x(): own = lax.all_gather(shard, 'fsdp', axis_index_groups=lines)]
    all_to_all x0 -> x1, waiting for transfers between devices: none -> 26.7 us  [shards(): lax.all_to_all(packed, 'fsdp', 0, 0, axis_index_groups=cores, tiled=True)]
    ppermute x0 -> x5, starting transfers between devices: none -> 9.88 us  [moved(): return lax.ppermute(array, 'fsdp', pairs)]
    all_to_all x0 -> x1, starting transfers between devices: none -> 5.44 us  [shards(): lax.all_to_all(packed, 'fsdp', 0, 0, axis_index_groups=cores, tiled=True)]
    pallas_call x2 -> x7, Pallas kernels: 13 us -> 17.7 us  [kernel_call(): pl.pallas_call(body, out_shape=out, in_specs=[specs[kind] for kind in kin...]
  transfers between devices with their start and end apart: 5 -> 8, of which waited for: 5 -> 8; matrix products, arithmetic and copies ran while one was open for 2% -> 0% of each run, Pallas kernels for 3% -> 3%
where the time goes in v4:
time: 174 us; the launch traced here: 173 us
  waiting for transfers between devices  83.4 us (48%)
  starting transfers between devices  37.7 us (22%)
  blocking collectives  26.8 us (15%)
  Pallas kernels  17.7 us (10%)
  local copies, waits for them, and re-layouts  4.61 us (3%)
  matrix products  2.91 us (2%)
    ppermute x5, waiting for transfers between devices, moved(): return lax.ppermute(array, 'fsdp', pairs)  36.5 us
    all_gather x2, blocking collectives, along_x(): own = lax.all_gather(shard, 'fsdp', axis_index_groups=lines)  26.8 us
    all_to_all x1, waiting for transfers between devices, shards(): lax.all_to_all(packed, 'fsdp', 0, 0, axis_index_groups=cores, tiled=True)  26.7 us
    all_to_all x2, starting transfers between devices, exchanged(): lax.all_to_all(sent, 'tm', split_axis=0, concat_axis=0, tiled=True)  22.3 us
    all_to_all x2, waiting for transfers between devices, exchanged(): lax.all_to_all(sent, 'tm', split_axis=0, concat_axis=0, tiled=True)  20.2 us
    pallas_call x7, Pallas kernels, kernel_call(): pl.pallas_call(body, out_shape=out, in_specs=[specs[kind] for kind in kin...  17.7 us
    ppermute x5, starting transfers between devices, moved(): return lax.ppermute(array, 'fsdp', pairs)  9.88 us
    all_to_all x1, starting transfers between devices, shards(): lax.all_to_all(packed, 'fsdp', 0, 0, axis_index_groups=cores, tiled=True)  5.44 us
  transfers between devices with their start and end apart: 8, of which 8 were waited for; matrix products, arithmetic and copies ran while one was open for 0% of the time, Pallas kernels for 3%

profile of v4, /device:TPU:32, one launch (start us, length us, event | category | flops | bytes accessed | tf_op | source)
XLA Modules:
  0.0 173.5 jit_solution(12125992125616589682)
XLA Ops:
  1.8 1.5 shard_map.73
  3.2 5.4 %all-to-all-start = ((bf16[8,64,2048]{2,1,0:T(8,128)(2,1)}), bf16[8,64,2048]{2,1,0:T(8,128)(2,1)S(1)}, u32[]{:S(2)}, u32[]{:S(2)}) async-start(bf16[8,64,2048]{2,1,0:T(8,128)(2,1)} %shard_map.73), calls=%async_computation | async-start | bytes 4194304 | tf_op jit(solution)/shard_map/all_to_all | solution.py:227
  8.8 1.2 copy-done.3
  10.0 2.4 %shard_map.74 = (bf16[512,512]{1,0:T(8,128)(2,1)S(1)}, bf16[512,512]{1,0:T(8,128)(2,1)S(1)}) custom-call(s32[3]{0:T(128)S(1)} %pad_add_fusion.here, bf16[512,1024]{1,0:T(8,128)(2,1)S(1)} %bitcast.24, f32[1,1024]{1,0:T(1,128)S(1)} %bitcast.26), custom_call_target="tpu_custom_call" | custom-call | flops 2000000000 | bytes 4194304 | tf_op jit(solution)/shard_map/pallas_call | solution.py:170
  13.1 26.7 %all-to-all-done.weights.mine = bf16[8,64,2048]{2,1,0:T(8,128)(2,1)S(1)} async-done(((bf16[8,64,2048]{2,1,0:T(8,128)(2,1)}), bf16[8,64,2048]{2,1,0:T(8,128)(2,1)S(1)}, u32[]{:S(2)}, u32[]{:S(2)}) %all-to-all-start) | async-done | bytes 2097184 | tf_op jit(solution)/shard_map/all_to_all | solution.py:227
  39.9 2.0 %collective-permute-start = (bf16[8,64,2048]{2,1,0:T(8,128)(2,1)S(1)}, bf16[8,64,2048]{2,1,0:T(8,128)(2,1)S(1)}, u32[]{:S(2)}, u32[]{:S(2)}) collective-permute-start(bf16[8,64,2048]{2,1,0:T(8,128)(2,1)S(1)} %all-to-all-done.weights.mine), channel_id=1, source_target_pairs={{0,32},{32,0},{64,96},{96,64},{128,160},{160,128},{192,224},{224,1... | collective-permute-start | bytes 6291464 | tf_op jit(solution)/shard_map/ppermute | solution.py:186
  42.9 3.1 %collective-permute-done.other = bf16[8,64,2048]{2,1,0:T(8,128)(2,1)S(1)} collective-permute-done((bf16[8,64,2048]{2,1,0:T(8,128)(2,1)S(1)}, bf16[8,64,2048]{2,1,0:T(8,128)(2,1)S(1)}, u32[]{:S(2)}, u32[]{:S(2)}) %collective-permute-start) | collective-permute-done | bytes 2097184 | tf_op jit(solution)/shard_map/ppermute | solution.py:186
  46.0 5.7 %shard_map.76 = bf16[512,1024]{1,0:T(8,128)(2,1)} custom-call(s32[3]{0:T(128)S(1)} %pad_add_fusion.here, bf16[512,1024]{1,0:T(8,128)(2,1)S(1)} %bitcast.25, f32[512,1536]{1,0:T(8,128)S(1)} %shard_map.75.partial, bf16[512,512]{1,0:T(8,128)(2,1)S(1)} %copy-done.8, bf16[8,64,2048]{2,1,0:T(8,128)(2,1)S(1)} %all-to-all-done.weights.mine, ...), custom_call_target="tpu_custom_call" | custom-call | flops 3000000000 | bytes 4194304 | tf_op jit(solution)/shard_map/pallas_call | solution.py:170
  51.8 17.9 %all-to-all-start.1 = ((bf16[32,16,1024]{2,1,0:T(8,128)(2,1)}), bf16[32,16,1024]{2,1,0:T(8,128)(2,1)}, u32[]{:S(2)}, u32[]{:S(2)}) async-start(bf16[32,16,1024]{2,1,0:T(8,128)(2,1)} %bitcast.5), calls=%async_computation.1 | async-start | bytes 2097152 | tf_op jit(solution)/shard_map/all_to_all | solution.py:215
  69.7 14.4 %all-gather = bf16[256,1536]{1,0:T(8,128)(2,1)S(1)} all-gather(bf16[64,1536]{1,0:T(8,128)(2,1)S(1)} %copy-done.9), channel_id=2, replica_groups={{0,128,256,384},{32,160,288,416},{64,192,320,448},{96,224,352,480},{1,1..., dimensions={0}, use_global_device_ids=true | all-gather | bytes 983040 | tf_op jit(solution)/shard_map/all_gather | solution.py:195
  84.1 1.9 %collective-permute-start.1 = (bf16[4,64,1536]{2,1,0:T(8,128)(2,1)S(1)}, bf16[4,64,1536]{2,1,0:T(8,128)(2,1)S(1)}, u32[]{:S(2)}, u32[]{:S(2)}) collective-permute-start(bf16[4,64,1536]{2,1,0:T(8,128)(2,1)S(1)} %bitcast.28), channel_id=1, source_target_pairs={{0,64},{32,96},{64,0},{96,32},{128,192},{160,224},{192,128},{224,1... | collective-permute-start | bytes 2359304 | tf_op jit(solution)/shard_map/ppermute | solution.py:186
  86.0 21.2 %collective-permute-done.1 = bf16[4,64,1536]{2,1,0:T(8,128)(2,1)S(1)} collective-permute-done((bf16[4,64,1536]{2,1,0:T(8,128)(2,1)S(1)}, bf16[4,64,1536]{2,1,0:T(8,128)(2,1)S(1)}, u32[]{:S(2)}, u32[]{:S(2)}) %collective-permute-start.1) | collective-permute-done | bytes 786464 | tf_op jit(solution)/shard_map/ppermute | solution.py:186
  107.3 2.1 %collective-permute-start.2 = (bf16[2,4,64,1536]{3,2,1,0:T(8,128)(2,1)S(1)}, bf16[2,4,64,1536]{3,2,1,0:T(8,128)(2,1)S(1)}, u32[]{:S(2)}, u32[]{:S(2)}) collective-permute-start(bf16[2,4,64,1536]{3,2,1,0:T(8,128)(2,1)S(1)} %pad_maximum_fusion.mine), channel_id=1, source_target_pairs={{0,32},{32,0},{64,96},{96,64},{128,160},{160,128},{192,224},{224,1... | collective-permute-start | bytes 4718600 | tf_op jit(solution)/shard_map/ppermute | solution.py:186
  109.4 3.2 %collective-permute-done.2.other = bf16[2,4,64,1536]{3,2,1,0:T(8,128)(2,1)S(1)} collective-permute-done((bf16[2,4,64,1536]{3,2,1,0:T(8,128)(2,1)S(1)}, bf16[2,4,64,1536]{3,2,1,0:T(8,128)(2,1)S(1)}, u32[]{:S(2)}, u32[]{:S(2)}) %collective-permute-start.2) | collective-permute-done | bytes 1572896 | tf_op jit(solution)/shard_map/ppermute | solution.py:186
  113.4 12.5 %all-to-all-done.1 = bf16[32,16,1024]{2,1,0:T(8,128)(2,1)} async-done(((bf16[32,16,1024]{2,1,0:T(8,128)(2,1)}), bf16[32,16,1024]{2,1,0:T(8,128)(2,1)}, u32[]{:S(2)}, u32[]{:S(2)}) %all-to-all-start.1) | async-done | bytes 1048608 | tf_op jit(solution)/shard_map/all_to_all | solution.py:215
  126.0 5.7 %shard_map.78 = bf16[512,512]{1,0:T(8,128)(2,1)S(1)} custom-call(bf16[512,1024]{1,0:T(8,128)(2,1)} %bitcast.6.middle, f32[1,1024]{1,0:T(1,128)S(1)} %bitcast.27, bf16[4,2,2,64,1536]{4,3,2,1,0:T(8,128)(2,1)S(1)} %shard_map.77.placed), custom_call_target="tpu_custom_call" | custom-call | flops 4000000000 | bytes 4194304 | tf_op jit(solution)/shard_map/pallas_call | solution.py:170
  132.5 4.4 %all-to-all-start.2 = ((bf16[32,16,512]{2,1,0:T(8,128)(2,1)}), bf16[32,16,512]{2,1,0:T(8,128)(2,1)S(1)}, u32[]{:S(2)}, u32[]{:S(2)}) async-start(bf16[32,16,512]{2,1,0:T(8,128)(2,1)} %bitcast.23), calls=%async_computation.2 | async-start | bytes 1048576 | tf_op jit(solution)/shard_map/all_to_all | solution.py:215
  136.9 12.4 %all-gather.1 = bf16[128,1024]{1,0:T(8,128)(2,1)S(1)} all-gather(bf16[32,1024]{1,0:T(8,128)(2,1)S(1)} %copy-done.10), channel_id=3, replica_groups={{0,128,256,384},{32,160,288,416},{64,192,320,448},{96,224,352,480},{1,1..., dimensions={0}, use_global_device_ids=true | all-gather | bytes 327680 | tf_op jit(solution)/shard_map/all_gather | solution.py:195
  149.3 1.9 %collective-permute-start.3 = (bf16[4,32,1024]{2,1,0:T(8,128)(2,1)S(1)}, bf16[4,32,1024]{2,1,0:T(8,128)(2,1)S(1)}, u32[]{:S(2)}, u32[]{:S(2)}) collective-permute-start(bf16[4,32,1024]{2,1,0:T(8,128)(2,1)S(1)} %bitcast.30), channel_id=1, source_target_pairs={{0,64},{32,96},{64,0},{96,32},{128,192},{160,224},{192,128},{224,1... | collective-permute-start | bytes 786440 | tf_op jit(solution)/shard_map/ppermute | solution.py:186
  151.2 7.1 %collective-permute-done.3 = bf16[4,32,1024]{2,1,0:T(8,128)(2,1)S(1)} collective-permute-done((bf16[4,32,1024]{2,1,0:T(8,128)(2,1)S(1)}, bf16[4,32,1024]{2,1,0:T(8,128)(2,1)S(1)}, u32[]{:S(2)}, u32[]{:S(2)}) %collective-permute-start.3) | collective-permute-done | bytes 262176 | tf_op jit(solution)/shard_map/ppermute | solution.py:186
  158.3 1.9 %collective-permute-start.4 = (bf16[2,4,32,1024]{3,2,1,0:T(8,128)(2,1)S(1)}, bf16[2,4,32,1024]{3,2,1,0:T(8,128)(2,1)S(1)}, u32[]{:S(2)}, u32[]{:S(2)}) collective-permute-start(bf16[2,4,32,1024]{3,2,1,0:T(8,128)(2,1)S(1)} %pad_maximum_fusion.1.mine), channel_id=1, source_target_pairs={{0,32},{32,0},{64,96},{96,64},{128,160},{160,128},{192,224},{224,1... | collective-permute-start | bytes 1572872 | tf_op jit(solution)/shard_map/ppermute | solution.py:186
  160.3 1.9 %collective-permute-done.4.other = bf16[2,4,32,1024]{3,2,1,0:T(8,128)(2,1)S(1)} collective-permute-done((bf16[2,4,32,1024]{3,2,1,0:T(8,128)(2,1)S(1)}, bf16[2,4,32,1024]{3,2,1,0:T(8,128)(2,1)S(1)}, u32[]{:S(2)}, u32[]{:S(2)}) %collective-permute-start.4) | collective-permute-done | bytes 524320 | tf_op jit(solution)/shard_map/ppermute | solution.py:186
  162.8 7.7 %all-to-all-done.2 = bf16[32,16,512]{2,1,0:T(8,128)(2,1)S(1)} async-done(((bf16[32,16,512]{2,1,0:T(8,128)(2,1)}), bf16[32,16,512]{2,1,0:T(8,128)(2,1)S(1)}, u32[]{:S(2)}, u32[]{:S(2)}) %all-to-all-start.2) | async-done | bytes 524320 | tf_op jit(solution)/shard_map/all_to_all | solution.py:215
  170.6 2.9 %add_convert_fusion = bf16[512,1024]{1,0:T(8,128)(2,1)} fusion(bf16[512,1024]{1,0:T(8,128)(2,1)} %shard_map.76, bf16[512,512]{1,0:T(8,128)(2,1)S(1)} %bitcast.33, bf16[512,1024]{1,0:T(8,128)(2,1)S(1)} %bitcast.22), kind=kOutput, calls=%fused_computation | convolution fusion | flops 538443776 | bytes 3670016 | tf_op jit(solution)/shard_map/dot_general | solution.py:263
  (27 shorter events, 6.1 us)
Async XLA Ops:
  0.0 0.9 copy-start.1
  0.9 0.8 copy-start.2
  3.2 5.5 %copy-start.5 = (f32[1024]{0:T(1024)S(1)}, f32[1024]{0:T(1024)}, u32[]{:S(2)}) copy-start(f32[1024]{0:T(1024)} %param.8) | copy-start | bytes 12292
  3.2 36.6 %all-to-all-start = ((bf16[8,64,2048]{2,1,0:T(8,128)(2,1)}), bf16[8,64,2048]{2,1,0:T(8,128)(2,1)S(1)}, u32[]{:S(2)}, u32[]{:S(2)}) async-start(bf16[8,64,2048]{2,1,0:T(8,128)(2,1)} %shard_map.73), calls=%async_computation | async-start | bytes 4194304 | tf_op jit(solution)/shard_map/all_to_all | solution.py:227
  8.8 1.2 copy-start.3
  12.4 0.8 copy-start.7
  39.9 6.2 %copy-start.4 = (bf16[2,1,256,1024]{3,2,1,0:T(8,128)(2,1)S(1)}, bf16[2,1,256,1024]{3,2,1,0:T(8,128)(2,1)}, u32[]{:S(2)}) copy-start(bf16[2,1,256,1024]{3,2,1,0:T(8,128)(2,1)} %param.7) | copy-start | bytes 3145732
  39.9 6.2 %copy-start.8 = (bf16[512,512]{1,0:T(8,128)(2,1)S(1)}, bf16[512,512]{1,0:T(8,128)(2,1)}, u32[]{:S(2)}) copy-start(bf16[512,512]{1,0:T(8,128)(2,1)} %copy-done.7) | copy-start | bytes 1572868
  39.9 6.2 %collective-permute-start = (bf16[8,64,2048]{2,1,0:T(8,128)(2,1)S(1)}, bf16[8,64,2048]{2,1,0:T(8,128)(2,1)S(1)}, u32[]{:S(2)}, u32[]{:S(2)}) collective-permute-start(bf16[8,64,2048]{2,1,0:T(8,128)(2,1)S(1)} %all-to-all-done.weights.mine), channel_id=1, source_target_pairs={{0,32},{32,0},{64,96},{96,64},{128,160},{160,128},{192,224},{224,1... | collective-permute-start | bytes 6291464 | tf_op jit(solution)/shard_map/ppermute | solution.py:186
  51.8 17.9 %copy-start.9 = (bf16[64,1536]{1,0:T(8,128)(2,1)S(1)}, bf16[64,1536]{1,0:T(8,128)(2,1)}, u32[]{:S(2)}) copy-start(bf16[64,1536]{1,0:T(8,128)(2,1)} %param.12) | copy-start | bytes 589828
  51.8 74.2 %all-to-all-start.1 = ((bf16[32,16,1024]{2,1,0:T(8,128)(2,1)}), bf16[32,16,1024]{2,1,0:T(8,128)(2,1)}, u32[]{:S(2)}, u32[]{:S(2)}) async-start(bf16[32,16,1024]{2,1,0:T(8,128)(2,1)} %bitcast.5), calls=%async_computation.1 | async-start | bytes 2097152 | tf_op jit(solution)/shard_map/all_to_all | solution.py:215
  84.1 23.1 %collective-permute-start.1 = (bf16[4,64,1536]{2,1,0:T(8,128)(2,1)S(1)}, bf16[4,64,1536]{2,1,0:T(8,128)(2,1)S(1)}, u32[]{:S(2)}, u32[]{:S(2)}) collective-permute-start(bf16[4,64,1536]{2,1,0:T(8,128)(2,1)S(1)} %bitcast.28), channel_id=1, source_target_pairs={{0,64},{32,96},{64,0},{96,32},{128,192},{160,224},{192,128},{224,1... | collective-permute-start | bytes 2359304 | tf_op jit(solution)/shard_map/ppermute | solution.py:186
  107.3 18.7 %copy-start.6 = (f32[1024]{0:T(1024)S(1)}, f32[1024]{0:T(1024)}, u32[]{:S(2)}) copy-start(f32[1024]{0:T(1024)} %param.11) | copy-start | bytes 12292
  107.3 5.3 %collective-permute-start.2 = (bf16[2,4,64,1536]{3,2,1,0:T(8,128)(2,1)S(1)}, bf16[2,4,64,1536]{3,2,1,0:T(8,128)(2,1)S(1)}, u32[]{:S(2)}, u32[]{:S(2)}) collective-permute-start(bf16[2,4,64,1536]{3,2,1,0:T(8,128)(2,1)S(1)} %pad_maximum_fusion.mine), channel_id=1, source_target_pairs={{0,32},{32,0},{64,96},{96,64},{128,160},{160,128},{192,224},{224,1... | collective-permute-start | bytes 4718600 | tf_op jit(solution)/shard_map/ppermute | solution.py:186
  126.0 11.0 %copy-start.10 = (bf16[32,1024]{1,0:T(8,128)(2,1)S(1)}, bf16[32,1024]{1,0:T(8,128)(2,1)}, u32[]{:S(2)}) copy-start(bf16[32,1024]{1,0:T(8,128)(2,1)} %param.13) | copy-start | bytes 196612
  131.7 0.8 copy-start
  132.5 38.1 %all-to-all-start.2 = ((bf16[32,16,512]{2,1,0:T(8,128)(2,1)}), bf16[32,16,512]{2,1,0:T(8,128)(2,1)S(1)}, u32[]{:S(2)}, u32[]{:S(2)}) async-start(bf16[32,16,512]{2,1,0:T(8,128)(2,1)} %bitcast.23), calls=%async_computation.2 | async-start | bytes 1048576 | tf_op jit(solution)/shard_map/all_to_all | solution.py:215
  149.3 9.0 %collective-permute-start.3 = (bf16[4,32,1024]{2,1,0:T(8,128)(2,1)S(1)}, bf16[4,32,1024]{2,1,0:T(8,128)(2,1)S(1)}, u32[]{:S(2)}, u32[]{:S(2)}) collective-permute-start(bf16[4,32,1024]{2,1,0:T(8,128)(2,1)S(1)} %bitcast.30), channel_id=1, source_target_pairs={{0,64},{32,96},{64,0},{96,32},{128,192},{160,224},{192,128},{224,1... | collective-permute-start | bytes 786440 | tf_op jit(solution)/shard_map/ppermute | solution.py:186
  158.3 3.8 %collective-permute-start.4 = (bf16[2,4,32,1024]{3,2,1,0:T(8,128)(2,1)S(1)}, bf16[2,4,32,1024]{3,2,1,0:T(8,128)(2,1)S(1)}, u32[]{:S(2)}, u32[]{:S(2)}) collective-permute-start(bf16[2,4,32,1024]{3,2,1,0:T(8,128)(2,1)S(1)} %pad_maximum_fusion.1.mine), channel_id=1, source_target_pairs={{0,32},{32,0},{64,96},{96,64},{128,160},{160,128},{192,224},{224,1... | collective-permute-start | bytes 1572872 | tf_op jit(solution)/shard_map/ppermute | solution.py:186

commit v5 on v4

v5 whole, which is shorter than its diff:
```python
import functools

import jax
import jax.numpy as jnp
from jax import lax
from jax.experimental import pallas as pl
from jax.experimental.pallas import tpu as pltpu
from jax.sharding import PartitionSpec as P

HEAD = 64
HEADS = 8
INNER = 512
EPSILON = 1e-06
BF16, F32 = jnp.bfloat16, jnp.float32
GROUP = 8
PAIR = 2 * HEAD
ROWS = 256
MIB = 1 << 20


def norm_rows(values, gain):
    centre = values - jnp.mean(values, axis=-1, keepdims=True)
    spread = jnp.mean(centre * centre, axis=-1, keepdims=True)
    return centre * lax.rsqrt(spread + EPSILON) * gain


def attend(qkv, rows, same):
    low = lax.broadcasted_iota(jnp.int32, (ROWS, PAIR), 1) < HEAD
    outs = []
    for pair in range(HEADS // 2):
        queries = qkv[rows, pl.ds(pair * PAIR, PAIR)]
        keys = qkv[rows, pl.ds(INNER + pair * PAIR, PAIR)]
        values = qkv[rows, pl.ds(2 * INNER + pair * PAIR, PAIR)]
        halves = []
        for mine in (low, ~low):
            own = jnp.where(mine, queries, jnp.zeros_like(queries))
            scores = lax.dot_general(own, keys, (((1,), (1,)), ((), ())), preferred_element_type=F32)
            if same is not None:
                scores = jnp.where(same, scores, -1e30)
            exponent = jnp.exp(scores - jnp.max(scores, axis=-1, keepdims=True))
            weights = exponent * (1.0 / jnp.sum(exponent, axis=-1, keepdims=True))
            halves.append(jnp.dot(weights.astype(BF16), values, preferred_element_type=F32))
        outs.append(jnp.where(low, halves[0], halves[1]))
    return jnp.concatenate(outs, axis=1)


def project(product, store):
    for piece in range(3 * INNER // 256):
        columns = pl.ds(piece * 256, 256)
        value = product(columns)
        if piece < INNER // 256:
            value = value * HEAD**-0.5
        store(columns, value)


def run(copies):
    for copy in copies:
        copy.start()
    return copies


def wait(copies):
    for copy in copies:
        copy.wait()


def norm_kernel(here, tokens, gain, normed):
    values = norm_rows(tokens[...].astype(F32), gain[...]).astype(BF16)
    sides, _, width = normed.shape
    depth = values.shape[1]
    part = width // 4
    source = lax.broadcasted_iota(jnp.int32, (depth, width), 0)
    target = lax.broadcasted_iota(jnp.int32, (depth, width), 1)
    first = target // part * (4 * part) + target % part
    for side in range(sides):
        yl, core = (here[1] + side // 2) % 2, (here[2] + side % 2) % 2
        chosen = (source == first + (yl * 2 + core) * part).astype(F32).astype(BF16)
        normed[side] = jnp.dot(values, chosen, preferred_element_type=F32).astype(BF16)


def half_product(normed, side, weights, columns):
    width = normed.shape[2]
    return sum(
        jnp.dot(
            normed[side + index], weight[:, :, columns].reshape(width, 256), preferred_element_type=F32
        )
        for index, weight in enumerate(weights)
    )


def half_kernel(normed, mine, other, partial):
    for piece in range(partial.shape[1] // 256):
        columns = pl.ds(piece * 256, 256)
        partial[:, columns] = half_product(normed, 0, (mine, other), columns)


def spatial_kernel(partial, normed, mine, other, context, qkv):
    def product(columns):
        return partial[:, columns] + half_product(normed, 2, (mine, other), columns)

    def store(columns, value):
        qkv[:, columns] = value.astype(BF16)

    project(product, store)
    for clip in range(context.shape[0] // ROWS):
        rows = pl.ds(clip * ROWS, ROWS)
        context[rows, :] = attend(qkv, rows, None).astype(BF16)


def place_kernel(here, *refs):
    pieces, placed, sems = refs[:-2], refs[-2], refs[-1]
    copies = []
    for side, piece in enumerate(pieces):
        target = placed.at[:, (here[1] + side // 2) % 2, (here[2] + side % 2) % 2]
        copies.append(pltpu.make_async_copy(piece, target, sems.at[side]))
    wait(run(copies))


def middle_kernel(tokens, context, weight, middle):
    added = jnp.dot(context[...], weight[...], preferred_element_type=F32)
    middle[...] = (tokens[...].astype(F32) + added).astype(BF16)


def temporal_kernel(frames, tokens, arrived, out_weight, gain, placed, context, qkv):
    added = jnp.dot(arrived[...], out_weight[...], preferred_element_type=F32)
    middle = (tokens[...].astype(F32) + added).astype(BF16)
    normed = norm_rows(middle.astype(F32), gain[...]).astype(BF16)
    rows, depth = middle.shape
    places = rows // frames

    def product(columns):
        weight = placed[:, :, :, :, columns].reshape(depth, 256)
        return jnp.dot(normed, weight, preferred_element_type=F32)

    def store(columns, value):
        split = value.reshape(frames, places, value.shape[1])
        for group in range(places // GROUP):
            own = split[:, group * GROUP : (group + 1) * GROUP].reshape(ROWS, value.shape[1])
            qkv[pl.ds(group * ROWS, ROWS), columns] = own.astype(BF16)

    project(product, store)
    place = lax.broadcasted_iota(jnp.int32, (ROWS, ROWS), 0) % GROUP
    same = place == lax.broadcasted_iota(jnp.int32, (ROWS, ROWS), 1) % GROUP
    outs = []
    for group in range(places // GROUP):
        out = attend(qkv, pl.ds(group * ROWS, ROWS), same)
        outs.append(out.reshape(frames, GROUP, INNER))
    context[...] = jnp.concatenate(outs, axis=1).reshape(rows, INNER).astype(BF16)


def kernel_call(body, kinds, out, operands, scratch=(), gflops=0, mib=4):
    near = pl.BlockSpec(memory_space=pltpu.VMEM)
    specs = {"s": pl.BlockSpec(memory_space=pltpu.SMEM), "v": near, "h": pl.BlockSpec(memory_space=pl.ANY)}
    return pl.pallas_call(
        body,
        out_shape=out,
        in_specs=[specs[kind] for kind in kinds],
        out_specs=jax.tree.map(lambda _: near, out),
        scratch_shapes=scratch,
        compiler_params=pltpu.CompilerParams(vmem_limit_bytes=24 * MIB),
        cost_estimate=pl.CostEstimate(flops=int(gflops * 1e9), bytes_accessed=mib * MIB, transcendentals=0),
    )(*operands)


def moved(array, change):
    pairs = []
    for index in range(lax.axis_size("fsdp")):
        x, yl, core = change(index // 4, index // 2 % 2, index % 2)
        pairs.append((index, (x * 2 + yl) * 2 + core))
    return lax.ppermute(array, "fsdp", pairs)


def other_core(array):
    return moved(array, lambda x, yl, core: (x, yl, 1 - core))


def other_yl(array):
    return moved(array, lambda x, yl, core: (x, 1 - yl, core))


def along_x(shard):
    lines = [list(range(start, 16, 4)) for start in range(4)]
    return lax.all_gather(shard, "fsdp", axis_index_groups=lines)


def after(array, *others):
    return lax.optimization_barrier((array, *others))[0]


def shards(tokens, spatial_gain, spatial_qkv, spatial_out, temporal_gain, temporal_qkv, temporal_out):
    clips, _, places, depth = tokens.shape
    frames = lax.axis_size("tm")
    members = lax.axis_size("fsdp")
    rows = clips * places
    block = rows // frames
    flat = tokens.reshape(rows, depth)
    index = lax.axis_index("fsdp")
    here = jnp.stack([index // 4, index // 2 % 2, index % 2]).astype(jnp.int32)
    shape = jax.ShapeDtypeStruct

    def exchanged(array):
        sent = array.reshape(frames, block, array.shape[1])
        return lax.all_to_all(sent, "tm", split_axis=0, concat_axis=0, tiled=True).reshape(array.shape)

    def in_order(*pieces):
        part, width = pieces[0].shape[1:]
        return kernel_call(
            place_kernel,
            "s" + "h" * 4,
            shape((4, 2, 2, part, width), BF16),
            (here, *pieces),
            [pltpu.SemaphoreType.DMA((4,))],
        )

    early = exchanged(flat)
    normed = kernel_call(
        norm_kernel, "svv", shape((4, rows, depth // 4), BF16), (here, flat, spatial_gain.reshape(1, depth)), gflops=2
    )
    own = along_x(spatial_qkv)
    beside = other_yl(own)
    own_t = along_x(after(temporal_qkv, own))
    partial = kernel_call(
        half_kernel, "vvv", shape((rows, 3 * INNER), F32), (normed, own, other_core(own)), gflops=1
    )
    beside, own_t, partial = lax.optimization_barrier((beside, own_t, partial))
    beside_t = other_yl(own_t)
    context = kernel_call(
        spatial_kernel,
        "vvvv",
        shape((rows, INNER), BF16),
        (partial, normed, beside, other_core(beside)),
        [pltpu.VMEM((rows, 3 * INNER), BF16)],
        gflops=3,
    )
    shard, context, early, beside_t = lax.optimization_barrier((spatial_out, context, early, beside_t))
    arrived = exchanged(context)
    placed = in_order(own_t, other_core(own_t), beside_t, other_core(beside_t))
    own_o = along_x(shard)
    beside_o = other_yl(own_o)
    swapped = other_core(jnp.stack([own_o, beside_o]))
    out_weight = in_order(own_o, swapped[0], beside_o, swapped[1]).reshape(INNER, depth)
    context_t = kernel_call(
        functools.partial(temporal_kernel, frames),
        "vvvvv",
        shape((rows, INNER), BF16),
        (early, arrived, out_weight, temporal_gain.reshape(1, depth), placed),
        [pltpu.VMEM((rows, 3 * INNER), BF16)],
        gflops=4,
    )
    shard, context, context_t = lax.optimization_barrier((temporal_out, context, context_t))
    returned = exchanged(context_t)
    own_o = along_x(shard)
    beside_o = other_yl(own_o)
    swapped = other_core(jnp.stack([own_o, beside_o]))
    weight = in_order(own_o, swapped[0], beside_o, swapped[1]).reshape(INNER, depth)
    middle = kernel_call(middle_kernel, "vvv", shape((rows, depth), BF16), (flat, context, out_weight), gflops=1)
    encoded = middle.astype(F32) + jnp.dot(returned, weight, preferred_element_type=F32)
    return encoded.astype(BF16).reshape(tokens.shape)


def solution(mesh):
    placed = (
        P("fsdp", "tm", None, None),
        P(),
        P("fsdp", None),
        P("fsdp", None),
        P(),
        P("fsdp", None),
        P("fsdp", None),
    )
    return jax.shard_map(
        shards, mesh=mesh, in_specs=placed, out_specs=P("fsdp", "tm", None, None), check_vma=False
    )
```

time: 174 us -> 190 us (1.092)
  the two profiles are of different devices: /device:TPU:32 before, /device:TPU:35 now
where the time goes in v5:
time: 190 us; the launch traced here: 189 us
  starting transfers between devices  79.2 us (42%)
  blocking collectives  43.9 us (23%)
  waiting for transfers between devices  38.7 us (20%)
  Pallas kernels  18.9 us (10%)
  local copies, waits for them, and re-layouts  5.37 us (3%)
  matrix products  2.73 us (1%)
    all_gather x4, blocking collectives, along_x(): return lax.all_gather(shard, 'fsdp', axis_index_groups=lines)  43.9 us
    all_to_all x3, starting transfers between devices, exchanged(): lax.all_to_all(sent, 'tm', split_axis=0, concat_axis=0, tiled=True)  42.7 us
    ppermute x10, starting transfers between devices, moved(): return lax.ppermute(array, 'fsdp', pairs)  36.5 us
    ppermute x10, waiting for transfers between devices, moved(): return lax.ppermute(array, 'fsdp', pairs)  29.5 us
    pallas_call x8, Pallas kernels, kernel_call(): pl.pallas_call(body, out_shape=out, in_specs=[specs[kind] for kind in kin...  18.9 us
    all_to_all x3, waiting for transfers between devices, exchanged(): lax.all_to_all(sent, 'tm', split_axis=0, concat_axis=0, tiled=True)  9.15 us
    unnamed x32, local copies, waits for them, and re-layouts  5.29 us
  transfers between devices with their start and end apart: 13, of which 5 were waited for; matrix products, arithmetic and copies ran while one was open for 0% of the time, Pallas kernels for 7%

profile of v5, /device:TPU:35, one launch (start us, length us, event | category | flops | bytes accessed | tf_op | source)
XLA Modules:
  0.0 189.3 jit_solution(14816227640343910189)
XLA Ops:
  0.0 17.6 %all-to-all-start = ((bf16[32,16,1024]{2,1,0:T(8,128)(2,1)}), bf16[32,16,1024]{2,1,0:T(8,128)(2,1)}, u32[]{:S(2)}, u32[]{:S(2)}) async-start(bf16[32,16,1024]{2,1,0:T(8,128)(2,1)} %bitcast.50), calls=%async_computation | async-start | bytes 2097152 | tf_op jit(solution)/shard_map/all_to_all | solution.py:203
  17.6 11.7 %all-gather = bf16[256,1536]{1,0:T(8,128)(2,1)S(1)} all-gather(bf16[64,1536]{1,0:T(8,128)(2,1)S(1)} %copy-done.12), channel_id=2, replica_groups={{0,128,256,384},{32,160,288,416},{64,192,320,448},{96,224,352,480},{1,1..., dimensions={0}, use_global_device_ids=true | all-gather | bytes 983040 | tf_op jit(solution)/shard_map/all_gather | solution.py:183
  29.3 5.8 %collective-permute-start.1 = (bf16[4,64,1536]{2,1,0:T(8,128)(2,1)S(1)}, bf16[4,64,1536]{2,1,0:T(8,128)(2,1)S(1)}, u32[]{:S(2)}, u32[]{:S(2)}) collective-permute-start(bf16[4,64,1536]{2,1,0:T(8,128)(2,1)S(1)} %bitcast.38), channel_id=1, source_target_pairs={{0,32},{32,0},{64,96},{96,64},{128,160},{160,128},{192,224},{224,1... | collective-permute-start | bytes 2359304 | tf_op jit(solution)/shard_map/ppermute | solution.py:170
  35.1 2.3 %collective-permute-start = (bf16[4,64,1536]{2,1,0:T(8,128)(2,1)S(1)}, bf16[4,64,1536]{2,1,0:T(8,128)(2,1)}, u32[]{:S(2)}, u32[]{:S(2)}) collective-permute-start(bf16[4,64,1536]{2,1,0:T(8,128)(2,1)S(1)} %bitcast.39), channel_id=1, source_target_pairs={{0,64},{32,96},{64,0},{96,32},{128,192},{160,224},{192,128},{224,1... | collective-permute-start | bytes 2359304 | tf_op jit(solution)/shard_map/ppermute | solution.py:170
  37.6 2.4 %shard_map.73.normed = bf16[4,512,256]{2,1,0:T(8,128)(2,1)S(1)} custom-call(s32[3]{0:T(128)S(1)} %pad_add_fusion.here, bf16[512,1024]{1,0:T(8,128)(2,1)S(1)} %bitcast.51, f32[1,1024]{1,0:T(1,128)S(1)} %bitcast.56), custom_call_target="tpu_custom_call" | custom-call | flops 2000000000 | bytes 4194304 | tf_op jit(solution)/shard_map/pallas_call | solution.py:154
  40.0 12.0 %all-gather.1 = bf16[256,1536]{1,0:T(8,128)(2,1)S(1)} all-gather(bf16[64,1536]{1,0:T(8,128)(2,1)S(1)} %copy-done.13), channel_id=3, replica_groups={{0,128,256,384},{32,160,288,416},{64,192,320,448},{96,224,352,480},{1,1..., dimensions={0}, use_global_device_ids=true | all-gather | bytes 983040 | tf_op jit(solution)/shard_map/all_gather | solution.py:183
  52.9 9.6 %collective-permute-done.mine = bf16[4,64,1536]{2,1,0:T(8,128)(2,1)} collective-permute-done((bf16[4,64,1536]{2,1,0:T(8,128)(2,1)S(1)}, bf16[4,64,1536]{2,1,0:T(8,128)(2,1)}, u32[]{:S(2)}, u32[]{:S(2)}) %collective-permute-start) | collective-permute-done | bytes 786464 | tf_op jit(solution)/shard_map/ppermute | solution.py:170
  62.6 2.6 %collective-permute-start.2 = (bf16[4,64,1536]{2,1,0:T(8,128)(2,1)}, bf16[4,64,1536]{2,1,0:T(8,128)(2,1)S(1)}, u32[]{:S(2)}, u32[]{:S(2)}) collective-permute-start(bf16[4,64,1536]{2,1,0:T(8,128)(2,1)} %collective-permute-done.mine), channel_id=1, source_target_pairs={{0,32},{32,0},{64,96},{96,64},{128,160},{160,128},{192,224},{224,1... | collective-permute-start | bytes 2359304 | tf_op jit(solution)/shard_map/ppermute | solution.py:170
  65.1 2.5 %collective-permute-start.3 = (bf16[4,64,1536]{2,1,0:T(8,128)(2,1)S(1)}, bf16[4,64,1536]{2,1,0:T(8,128)(2,1)S(1)}, u32[]{:S(2)}, u32[]{:S(2)}) collective-permute-start(bf16[4,64,1536]{2,1,0:T(8,128)(2,1)S(1)} %bitcast.35), channel_id=1, source_target_pairs={{0,64},{32,96},{64,0},{96,32},{128,192},{160,224},{192,128},{224,1... | collective-permute-start | bytes 2359304 | tf_op jit(solution)/shard_map/ppermute | solution.py:170
  67.6 5.2 %shard_map.75.context = bf16[512,512]{1,0:T(8,128)(2,1)} custom-call(f32[512,1536]{1,0:T(8,128)S(1)} %shard_map.74.partial, bf16[4,512,256]{2,1,0:T(8,128)(2,1)S(1)} %shard_map.73.normed, bf16[4,64,1536]{2,1,0:T(8,128)(2,1)} %collective-permute-done.mine, bf16[4,64,1536]{2,1,0:T(8,128)(2,1)S(1)} %collective-permute-done.2.other), custom_call_target="tpu_custom_call" | custom-call | flops 3000000000 | bytes 4194304 | tf_op jit(solution)/shard_map/pallas_call | solution.py:154
  72.8 13.8 %collective-permute-done.3.refs_2_ = bf16[4,64,1536]{2,1,0:T(8,128)(2,1)S(1)} collective-permute-done((bf16[4,64,1536]{2,1,0:T(8,128)(2,1)S(1)}, bf16[4,64,1536]{2,1,0:T(8,128)(2,1)S(1)}, u32[]{:S(2)}, u32[]{:S(2)}) %collective-permute-start.3) | collective-permute-done | bytes 786464 | tf_op jit(solution)/shard_map/ppermute | solution.py:170
  86.6 12.9 %all-to-all-start.1 = ((bf16[32,16,512]{2,1,0:T(8,128)(2,1)}), bf16[32,16,512]{2,1,0:T(8,128)(2,1)}, u32[]{:S(2)}, u32[]{:S(2)}) async-start(bf16[32,16,512]{2,1,0:T(8,128)(2,1)} %bitcast.9), calls=%async_computation.1 | async-start | bytes 1048576 | tf_op jit(solution)/shard_map/all_to_all | solution.py:203
  99.5 9.7 %all-gather.2 = bf16[128,1024]{1,0:T(8,128)(2,1)S(1)} all-gather(bf16[32,1024]{1,0:T(8,128)(2,1)S(1)} %copy-done.14), channel_id=4, replica_groups={{0,128,256,384},{32,160,288,416},{64,192,320,448},{96,224,352,480},{1,1..., dimensions={0}, use_global_device_ids=true | all-gather | bytes 327680 | tf_op jit(solution)/shard_map/all_gather | solution.py:183
  109.2 2.2 %collective-permute-start.4 = (bf16[4,32,1024]{2,1,0:T(8,128)(2,1)S(1)}, bf16[4,32,1024]{2,1,0:T(8,128)(2,1)S(1)}, u32[]{:S(2)}, u32[]{:S(2)}) collective-permute-start(bf16[4,32,1024]{2,1,0:T(8,128)(2,1)S(1)} %bitcast.41), channel_id=1, source_target_pairs={{0,64},{32,96},{64,0},{96,32},{128,192},{160,224},{192,128},{224,1... | collective-permute-start | bytes 786440 | tf_op jit(solution)/shard_map/ppermute | solution.py:170
  111.5 6.2 %collective-permute-start.6 = (bf16[4,64,1536]{2,1,0:T(8,128)(2,1)S(1)}, bf16[4,64,1536]{2,1,0:T(8,128)(2,1)S(1)}, u32[]{:S(2)}, u32[]{:S(2)}) collective-permute-start(bf16[4,64,1536]{2,1,0:T(8,128)(2,1)S(1)} %bitcast.36), channel_id=1, source_target_pairs={{0,32},{32,0},{64,96},{96,64},{128,160},{160,128},{192,224},{224,1... | collective-permute-start | bytes 2359304 | tf_op jit(solution)/shard_map/ppermute | solution.py:170
  119.7 5.0 %collective-permute-start.5 = (bf16[2,4,32,1024]{3,2,1,0:T(8,128)(2,1)S(1)}, bf16[2,4,32,1024]{3,2,1,0:T(8,128)(2,1)S(1)}, u32[]{:S(2)}, u32[]{:S(2)}) collective-permute-start(bf16[2,4,32,1024]{3,2,1,0:T(8,128)(2,1)S(1)} %pad_maximum_fusion), channel_id=1, source_target_pairs={{0,32},{32,0},{64,96},{96,64},{128,160},{160,128},{192,224},{224,1... | collective-permute-start | bytes 1572872 | tf_op jit(solution)/shard_map/ppermute | solution.py:170
  129.5 2.2 %all-to-all-done.1 = bf16[32,16,512]{2,1,0:T(8,128)(2,1)} async-done(((bf16[32,16,512]{2,1,0:T(8,128)(2,1)}), bf16[32,16,512]{2,1,0:T(8,128)(2,1)}, u32[]{:S(2)}, u32[]{:S(2)}) %all-to-all-start.1) | async-done | bytes 524320 | tf_op jit(solution)/shard_map/all_to_all | solution.py:203
  133.0 6.4 %shard_map.78 = bf16[512,512]{1,0:T(8,128)(2,1)S(1)} custom-call(bf16[512,1024]{1,0:T(8,128)(2,1)} %bitcast.8.tokens, bf16[512,512]{1,0:T(8,128)(2,1)} %bitcast.10.arrived, bf16[512,1024]{1,0:T(8,128)(2,1)S(1)} %bitcast.47, f32[1,1024]{1,0:T(1,128)S(1)} %bitcast.57, bf16[4,2,2,64,1536]{4,3,2,1,0:T(8,128)(2,1)S(1)} %shard_map.77.placed), custom_call_target="tpu_custom_call" | custom-call | flops 4000000000 | bytes 4194304 | tf_op jit(solution)/shard_map/pallas_call | solution.py:154
  140.2 12.1 %all-to-all-start.2 = ((bf16[32,16,512]{2,1,0:T(8,128)(2,1)}), bf16[32,16,512]{2,1,0:T(8,128)(2,1)}, u32[]{:S(2)}, u32[]{:S(2)}) async-start(bf16[32,16,512]{2,1,0:T(8,128)(2,1)} %bitcast.55), calls=%async_computation.2 | async-start | bytes 1048576 | tf_op jit(solution)/shard_map/all_to_all | solution.py:203
  152.4 10.6 %all-gather.3 = bf16[128,1024]{1,0:T(8,128)(2,1)S(1)} all-gather(bf16[32,1024]{1,0:T(8,128)(2,1)S(1)} %copy-done.15), channel_id=5, replica_groups={{0,128,256,384},{32,160,288,416},{64,192,320,448},{96,224,352,480},{1,1..., dimensions={0}, use_global_device_ids=true | all-gather | bytes 327680 | tf_op jit(solution)/shard_map/all_gather | solution.py:183
  165.0 6.1 %collective-permute-done.8.refs_2_ = bf16[4,32,1024]{2,1,0:T(8,128)(2,1)S(1)} collective-permute-done((bf16[4,32,1024]{2,1,0:T(8,128)(2,1)S(1)}, bf16[4,32,1024]{2,1,0:T(8,128)(2,1)S(1)}, u32[]{:S(2)}, u32[]{:S(2)}) %collective-permute-start.8) | collective-permute-done | bytes 262176 | tf_op jit(solution)/shard_map/ppermute | solution.py:170
  171.1 6.0 %collective-permute-start.9 = (bf16[2,4,32,1024]{3,2,1,0:T(8,128)(2,1)S(1)}, bf16[2,4,32,1024]{3,2,1,0:T(8,128)(2,1)S(1)}, u32[]{:S(2)}, u32[]{:S(2)}) collective-permute-start(bf16[2,4,32,1024]{3,2,1,0:T(8,128)(2,1)S(1)} %pad_maximum_fusion.1), channel_id=1, source_target_pairs={{0,32},{32,0},{64,96},{96,64},{128,160},{160,128},{192,224},{224,1... | collective-permute-start | bytes 1572872 | tf_op jit(solution)/shard_map/ppermute | solution.py:170
  179.7 6.9 %all-to-all-done.2 = bf16[32,16,512]{2,1,0:T(8,128)(2,1)} async-done(((bf16[32,16,512]{2,1,0:T(8,128)(2,1)}), bf16[32,16,512]{2,1,0:T(8,128)(2,1)}, u32[]{:S(2)}, u32[]{:S(2)}) %all-to-all-start.2) | async-done | bytes 524320 | tf_op jit(solution)/shard_map/all_to_all | solution.py:203
  186.6 2.7 %add_convert_fusion = bf16[512,1024]{1,0:T(8,128)(2,1)} fusion(bf16[512,1024]{1,0:T(8,128)(2,1)S(1)} %shard_map.79, bf16[512,512]{1,0:T(8,128)(2,1)} %bitcast.19, bf16[512,1024]{1,0:T(8,128)(2,1)S(1)} %bitcast.49), kind=kOutput, calls=%fused_computation | convolution fusion | flops 538443776 | bytes 3670016 | tf_op jit(solution)/shard_map/dot_general | solution.py:257
  (52 shorter events, 14.4 us)
Async XLA Ops:
  0.0 37.6 %copy-start.5 = (bf16[2,1,256,1024]{3,2,1,0:T(8,128)(2,1)S(1)}, bf16[2,1,256,1024]{3,2,1,0:T(8,128)(2,1)}, u32[]{:S(2)}) copy-start(bf16[2,1,256,1024]{3,2,1,0:T(8,128)(2,1)} %param.7) | copy-start | bytes 3145732
  0.0 17.6 %copy-start.12 = (bf16[64,1536]{1,0:T(8,128)(2,1)S(1)}, bf16[64,1536]{1,0:T(8,128)(2,1)}, u32[]{:S(2)}) copy-start(bf16[64,1536]{1,0:T(8,128)(2,1)} %param.9) | copy-start | bytes 589828
  0.0 37.6 %copy-start.10 = (f32[1024]{0:T(1024)S(1)}, f32[1024]{0:T(1024)}, u32[]{:S(2)}) copy-start(f32[1024]{0:T(1024)} %param.8) | copy-start | bytes 12292
  0.0 86.5 %all-to-all-start = ((bf16[32,16,1024]{2,1,0:T(8,128)(2,1)}), bf16[32,16,1024]{2,1,0:T(8,128)(2,1)}, u32[]{:S(2)}, u32[]{:S(2)}) async-start(bf16[32,16,1024]{2,1,0:T(8,128)(2,1)} %bitcast.50), calls=%async_computation | async-start | bytes 2097152 | tf_op jit(solution)/shard_map/all_to_all | solution.py:203
  29.3 22.6 %collective-permute-start.1 = (bf16[4,64,1536]{2,1,0:T(8,128)(2,1)S(1)}, bf16[4,64,1536]{2,1,0:T(8,128)(2,1)S(1)}, u32[]{:S(2)}, u32[]{:S(2)}) collective-permute-start(bf16[4,64,1536]{2,1,0:T(8,128)(2,1)S(1)} %bitcast.38), channel_id=1, source_target_pairs={{0,32},{32,0},{64,96},{96,64},{128,160},{160,128},{192,224},{224,1... | collective-permute-start | bytes 2359304 | tf_op jit(solution)/shard_map/ppermute | solution.py:170
  35.1 27.4 %collective-permute-start = (bf16[4,64,1536]{2,1,0:T(8,128)(2,1)S(1)}, bf16[4,64,1536]{2,1,0:T(8,128)(2,1)}, u32[]{:S(2)}, u32[]{:S(2)}) collective-permute-start(bf16[4,64,1536]{2,1,0:T(8,128)(2,1)S(1)} %bitcast.39), channel_id=1, source_target_pairs={{0,64},{32,96},{64,0},{96,32},{128,192},{160,224},{192,128},{224,1... | collective-permute-start | bytes 2359304 | tf_op jit(solution)/shard_map/ppermute | solution.py:170
  37.6 2.4 %copy-start.13 = (bf16[64,1536]{1,0:T(8,128)(2,1)S(1)}, bf16[64,1536]{1,0:T(8,128)(2,1)}, u32[]{:S(2)}) copy-start(bf16[64,1536]{1,0:T(8,128)(2,1)} %param.12) | copy-start | bytes 589828
  51.9 59.5 %copy-start = (bf16[256,1536]{1,0:T(8,128)(2,1)}, bf16[256,1536]{1,0:T(8,128)(2,1)S(1)}, u32[]{:S(2)}) copy-start(bf16[256,1536]{1,0:T(8,128)(2,1)S(1)} %all-gather.1) | copy-start | bytes 2359300
  62.6 36.9 %copy-start.14 = (bf16[32,1024]{1,0:T(8,128)(2,1)S(1)}, bf16[32,1024]{1,0:T(8,128)(2,1)}, u32[]{:S(2)}) copy-start(bf16[32,1024]{1,0:T(8,128)(2,1)} %param.10) | copy-start | bytes 196612
  62.6 5.0 %collective-permute-start.2 = (bf16[4,64,1536]{2,1,0:T(8,128)(2,1)}, bf16[4,64,1536]{2,1,0:T(8,128)(2,1)S(1)}, u32[]{:S(2)}, u32[]{:S(2)}) collective-permute-start(bf16[4,64,1536]{2,1,0:T(8,128)(2,1)} %collective-permute-done.mine), channel_id=1, source_target_pairs={{0,32},{32,0},{64,96},{96,64},{128,160},{160,128},{192,224},{224,1... | collective-permute-start | bytes 2359304 | tf_op jit(solution)/shard_map/ppermute | solution.py:170
  65.1 21.4 %collective-permute-start.3 = (bf16[4,64,1536]{2,1,0:T(8,128)(2,1)S(1)}, bf16[4,64,1536]{2,1,0:T(8,128)(2,1)S(1)}, u32[]{:S(2)}, u32[]{:S(2)}) collective-permute-start(bf16[4,64,1536]{2,1,0:T(8,128)(2,1)S(1)} %bitcast.35), channel_id=1, source_target_pairs={{0,64},{32,96},{64,0},{96,32},{128,192},{160,224},{192,128},{224,1... | collective-permute-start | bytes 2359304 | tf_op jit(solution)/shard_map/ppermute | solution.py:170
  86.5 38.1 %copy-start.7 = (bf16[4,64,1536]{2,1,0:T(8,128)(2,1)}, bf16[4,64,1536]{2,1,0:T(8,128)(2,1)S(1)}, u32[]{:S(2)}) copy-start(bf16[4,64,1536]{2,1,0:T(8,128)(2,1)S(1)} %collective-permute-done.3.refs_2_) | copy-start | bytes 2359300
  86.6 45.2 %all-to-all-start.1 = ((bf16[32,16,512]{2,1,0:T(8,128)(2,1)}), bf16[32,16,512]{2,1,0:T(8,128)(2,1)}, u32[]{:S(2)}, u32[]{:S(2)}) async-start(bf16[32,16,512]{2,1,0:T(8,128)(2,1)} %bitcast.9), calls=%async_computation.1 | async-start | bytes 1048576 | tf_op jit(solution)/shard_map/all_to_all | solution.py:203
  109.2 10.3 %collective-permute-start.4 = (bf16[4,32,1024]{2,1,0:T(8,128)(2,1)S(1)}, bf16[4,32,1024]{2,1,0:T(8,128)(2,1)S(1)}, u32[]{:S(2)}, u32[]{:S(2)}) collective-permute-start(bf16[4,32,1024]{2,1,0:T(8,128)(2,1)S(1)} %bitcast.41), channel_id=1, source_target_pairs={{0,64},{32,96},{64,0},{96,32},{128,192},{160,224},{192,128},{224,1... | collective-permute-start | bytes 786440 | tf_op jit(solution)/shard_map/ppermute | solution.py:170
  111.5 13.2 %collective-permute-start.6 = (bf16[4,64,1536]{2,1,0:T(8,128)(2,1)S(1)}, bf16[4,64,1536]{2,1,0:T(8,128)(2,1)S(1)}, u32[]{:S(2)}, u32[]{:S(2)}) collective-permute-start(bf16[4,64,1536]{2,1,0:T(8,128)(2,1)S(1)} %bitcast.36), channel_id=1, source_target_pairs={{0,32},{32,0},{64,96},{96,64},{128,160},{160,128},{192,224},{224,1... | collective-permute-start | bytes 2359304 | tf_op jit(solution)/shard_map/ppermute | solution.py:170
  117.7 7.0 %collective-permute-start.7 = (bf16[4,64,1536]{2,1,0:T(8,128)(2,1)S(1)}, bf16[4,64,1536]{2,1,0:T(8,128)(2,1)S(1)}, u32[]{:S(2)}, u32[]{:S(2)}) collective-permute-start(bf16[4,64,1536]{2,1,0:T(8,128)(2,1)S(1)} %collective-permute-done.3.refs_2_), channel_id=1, source_target_pairs={{0,32},{32,0},{64,96},{96,64},{128,160},{160,128},{192,224},{224,1... | collective-permute-start | bytes 2359304 | tf_op jit(solution)/shard_map/ppermute | solution.py:170
  119.7 8.1 %collective-permute-start.5 = (bf16[2,4,32,1024]{3,2,1,0:T(8,128)(2,1)S(1)}, bf16[2,4,32,1024]{3,2,1,0:T(8,128)(2,1)S(1)}, u32[]{:S(2)}, u32[]{:S(2)}) collective-permute-start(bf16[2,4,32,1024]{3,2,1,0:T(8,128)(2,1)S(1)} %pad_maximum_fusion), channel_id=1, source_target_pairs={{0,32},{32,0},{64,96},{96,64},{128,160},{160,128},{192,224},{224,1... | collective-permute-start | bytes 1572872 | tf_op jit(solution)/shard_map/ppermute | solution.py:170
  127.8 4.0 %copy-start.11 = (f32[1024]{0:T(1024)S(1)}, f32[1024]{0:T(1024)}, u32[]{:S(2)}) copy-start(f32[1024]{0:T(1024)} %param.11) | copy-start | bytes 12292
  133.0 19.4 %copy-start.15 = (bf16[32,1024]{1,0:T(8,128)(2,1)S(1)}, bf16[32,1024]{1,0:T(8,128)(2,1)}, u32[]{:S(2)}) copy-start(bf16[32,1024]{1,0:T(8,128)(2,1)} %param.13) | copy-start | bytes 196612
  140.2 36.9 %copy-start.4 = (bf16[4,2,2,32,1024]{4,3,2,1,0:T(8,128)(2,1)S(1)}, bf16[4,2,2,32,1024]{4,3,2,1,0:T(8,128)(2,1)}, u32[]{:S(2)}) copy-start(bf16[4,2,2,32,1024]{4,3,2,1,0:T(8,128)(2,1)} %copy-done.2) | copy-start | bytes 3145732
  140.2 36.9 %copy-start.6 = (bf16[2,1,256,1024]{3,2,1,0:T(8,128)(2,1)S(1)}, bf16[2,1,256,1024]{3,2,1,0:T(8,128)(2,1)}, u32[]{:S(2)}) copy-start(bf16[2,1,256,1024]{3,2,1,0:T(8,128)(2,1)} %param.7) | copy-start | bytes 3145732
  140.2 46.3 %all-to-all-start.2 = ((bf16[32,16,512]{2,1,0:T(8,128)(2,1)}), bf16[32,16,512]{2,1,0:T(8,128)(2,1)}, u32[]{:S(2)}, u32[]{:S(2)}) async-start(bf16[32,16,512]{2,1,0:T(8,128)(2,1)} %bitcast.55), calls=%async_computation.2 | async-start | bytes 1048576 | tf_op jit(solution)/shard_map/all_to_all | solution.py:203
  162.9 8.1 %collective-permute-start.8 = (bf16[4,32,1024]{2,1,0:T(8,128)(2,1)S(1)}, bf16[4,32,1024]{2,1,0:T(8,128)(2,1)S(1)}, u32[]{:S(2)}, u32[]{:S(2)}) collective-permute-start(bf16[4,32,1024]{2,1,0:T(8,128)(2,1)S(1)} %bitcast.44), channel_id=1, source_target_pairs={{0,64},{32,96},{64,0},{96,32},{128,192},{160,224},{192,128},{224,1... | collective-permute-start | bytes 786440 | tf_op jit(solution)/shard_map/ppermute | solution.py:170
  171.1 7.8 %collective-permute-start.9 = (bf16[2,4,32,1024]{3,2,1,0:T(8,128)(2,1)S(1)}, bf16[2,4,32,1024]{3,2,1,0:T(8,128)(2,1)S(1)}, u32[]{:S(2)}, u32[]{:S(2)}) collective-permute-start(bf16[2,4,32,1024]{3,2,1,0:T(8,128)(2,1)S(1)} %pad_maximum_fusion.1), channel_id=1, source_target_pairs={{0,32},{32,0},{64,96},{96,64},{128,160},{160,128},{192,224},{224,1... | collective-permute-start | bytes 1572872 | tf_op jit(solution)/shard_map/ppermute | solution.py:170
  (5 other events, 5.3 us)

commit v6 on v5

--- a/solution.py
+++ b/solution.py
@@ -175,7 +175,16 @@
 
 
 def other_yl(array):
-    return moved(array, lambda x, yl, core: (x, 1 - yl, core))
+    members, frames = lax.axis_size("fsdp"), lax.axis_size("tm")
+    half = array.shape[0] // 2
+    pieces = []
+    for turn, piece in enumerate((array[:half], array[half:])):
+        pairs = []
+        for source in range(members * frames):
+            member, frame = source // frames, source % frames
+            pairs.append((source, (member ^ 2) * frames + (frame + turn * frames // 2) % frames))
+        pieces.append(lax.ppermute(piece, ("fsdp", "tm"), pairs))
+    return jnp.concatenate(pieces, axis=0)
 
 
 def along_x(shard):
@@ -232,7 +241,7 @@
         [pltpu.VMEM((rows, 3 * INNER), BF16)],
         gflops=3,
     )
-    shard, context, early, beside_t = lax.optimization_barrier((spatial_out, context, early, beside_t))
+    shard, context, early = lax.optimization_barrier((spatial_out, context, early))
     arrived = exchanged(context)
     placed = in_order(own_t, other_core(own_t), beside_t, other_core(beside_t))
     own_o = along_x(shard)

time: 190 us -> 178 us (0.937)
  waiting for transfers between devices: 38.7 us -> 11.6 us
  starting transfers between devices: 79.2 us -> 92 us
    ppermute x10 -> x6, waiting for transfers between devices: 29.5 us -> 0.02 us  [moved(): return lax.ppermute(array, 'fsdp', pairs)]
    ppermute x0 -> x8, starting transfers between devices: none -> 24.3 us  [other_yl(): pieces.append(lax.ppermute(piece, ('fsdp', 'tm'), pairs))]
    ppermute x10 -> x6, starting transfers between devices: 36.5 us -> 29 us  [moved(): return lax.ppermute(array, 'fsdp', pairs)]
    ppermute x0 -> x8, waiting for transfers between devices: none -> 4.02 us  [other_yl(): pieces.append(lax.ppermute(piece, ('fsdp', 'tm'), pairs))]
    all_to_all x3, starting transfers between devices: 42.7 us -> 38.8 us  [exchanged(): lax.all_to_all(sent, 'tm', split_axis=0, concat_axis=0, tiled=True)]
    unnamed x32 -> x31, local copies, waits for them, and re-layouts: 5.29 us -> 5.27 us
  transfers between devices with their start and end apart: 13 -> 17, of which waited for: 5 -> 4; matrix products, arithmetic and copies ran while one was open for 0% -> 1% of each run, Pallas kernels for 7% -> 6%
where the time goes in v6:
time: 178 us; the launch traced here: 177 us
  starting transfers between devices  92 us (52%)
  blocking collectives  45.3 us (25%)
  Pallas kernels  17.7 us (10%)
  waiting for transfers between devices  11.6 us (7%)
  local copies, waits for them, and re-layouts  6.28 us (4%)
  matrix products  2.73 us (2%)
    all_gather x4, blocking collectives, along_x(): return lax.all_gather(shard, 'fsdp', axis_index_groups=lines)  45.3 us
    all_to_all x3, starting transfers between devices, exchanged(): lax.all_to_all(sent, 'tm', split_axis=0, concat_axis=0, tiled=True)  38.8 us
    ppermute x6, starting transfers between devices, moved(): return lax.ppermute(array, 'fsdp', pairs)  29 us
    ppermute x8, starting transfers between devices, other_yl(): pieces.append(lax.ppermute(piece, ('fsdp', 'tm'), pairs))  24.3 us
    pallas_call x8, Pallas kernels, kernel_call(): pl.pallas_call(body, out_shape=out, in_specs=[specs[kind] for kind in kin...  17.7 us
    all_to_all x3, waiting for transfers between devices, exchanged(): lax.all_to_all(sent, 'tm', split_axis=0, concat_axis=0, tiled=True)  7.61 us
    unnamed x31, local copies, waits for them, and re-layouts  5.27 us
    ppermute x8, waiting for transfers between devices, other_yl(): pieces.append(lax.ppermute(piece, ('fsdp', 'tm'), pairs))  4.02 us
  transfers between devices with their start and end apart: 17, of which 4 were waited for; matrix products, arithmetic and copies ran while one was open for 1% of the time, Pallas kernels for 6%

profile of v6, /device:TPU:35, one launch (start us, length us, event | category | flops | bytes accessed | tf_op | source)
XLA Modules:
  0.0 177.4 jit_solution(2464846047838306113)
XLA Ops:
  0.0 17.6 %all-to-all-start = ((bf16[32,16,1024]{2,1,0:T(8,128)(2,1)}), bf16[32,16,1024]{2,1,0:T(8,128)(2,1)}, u32[]{:S(2)}, u32[]{:S(2)}) async-start(bf16[32,16,1024]{2,1,0:T(8,128)(2,1)} %bitcast.55), calls=%async_computation | async-start | bytes 2097152 | tf_op jit(solution)/shard_map/all_to_all | solution.py:212
  17.6 11.7 %all-gather = bf16[256,1536]{1,0:T(8,128)(2,1)S(1)} all-gather(bf16[64,1536]{1,0:T(8,128)(2,1)S(1)} %copy-done.10), channel_id=2, replica_groups={{0,128,256,384},{32,160,288,416},{64,192,320,448},{96,224,352,480},{1,1..., dimensions={0}, use_global_device_ids=true | all-gather | bytes 983040 | tf_op jit(solution)/shard_map/all_gather | solution.py:192
  30.1 3.6 %collective-permute-start.1 = (bf16[2,64,1536]{2,1,0:T(8,128)(2,1)}, bf16[2,64,1536]{2,1,0:T(8,128)(2,1)S(1)}, u32[]{:S(2)}, u32[]{:S(2)}) collective-permute-start(bf16[2,64,1536]{2,1,0:T(8,128)(2,1)} %bitcast.2), channel_id=1, source_target_pairs={{0,80},{1,81},{2,82},{3,83},{4,84},{5,85},{6,86},{7,87},{8,88},{9,... | collective-permute-start | bytes 1179656 | tf_op jit(solution)/shard_map/ppermute | solution.py:186
  35.7 7.0 %collective-permute-start.2 = (bf16[4,64,1536]{2,1,0:T(8,128)(2,1)S(1)}, bf16[4,64,1536]{2,1,0:T(8,128)(2,1)S(1)}, u32[]{:S(2)}, u32[]{:S(2)}) collective-permute-start(bf16[4,64,1536]{2,1,0:T(8,128)(2,1)S(1)} %bitcast.44), channel_id=1, source_target_pairs={{0,32},{32,0},{64,96},{96,64},{128,160},{160,128},{192,224},{224,1... | collective-permute-start | bytes 2359304 | tf_op jit(solution)/shard_map/ppermute | solution.py:170
  42.8 2.4 %shard_map.73.normed = bf16[4,512,256]{2,1,0:T(8,128)(2,1)S(1)} custom-call(s32[3]{0:T(128)S(1)} %pad_add_fusion.here, bf16[512,1024]{1,0:T(8,128)(2,1)S(1)} %bitcast.56, f32[1,1024]{1,0:T(1,128)S(1)} %bitcast.59), custom_call_target="tpu_custom_call" | custom-call | flops 2000000000 | bytes 4194304 | tf_op jit(solution)/shard_map/pallas_call | solution.py:154
  45.2 12.5 %all-gather.1 = bf16[256,1536]{1,0:T(8,128)(2,1)S(1)} all-gather(bf16[64,1536]{1,0:T(8,128)(2,1)S(1)} %copy-done.11), channel_id=3, replica_groups={{0,128,256,384},{32,160,288,416},{64,192,320,448},{96,224,352,480},{1,1..., dimensions={0}, use_global_device_ids=true | all-gather | bytes 983040 | tf_op jit(solution)/shard_map/all_gather | solution.py:192
  59.8 3.9 %collective-permute-start.3 = (bf16[4,64,1536]{2,1,0:T(8,128)(2,1)S(1)}, bf16[4,64,1536]{2,1,0:T(8,128)(2,1)S(1)}, u32[]{:S(2)}, u32[]{:S(2)}) collective-permute-start(bf16[4,64,1536]{2,1,0:T(8,128)(2,1)S(1)} %pad_maximum_fusion.mine), channel_id=1, source_target_pairs={{0,32},{32,0},{64,96},{96,64},{128,160},{160,128},{192,224},{224,1... | collective-permute-start | bytes 2359304 | tf_op jit(solution)/shard_map/ppermute | solution.py:170
  63.7 3.6 %collective-permute-start.8 = (bf16[2,64,1536]{2,1,0:T(8,128)(2,1)S(1)}, bf16[2,64,1536]{2,1,0:T(8,128)(2,1)S(1)}, u32[]{:S(2)}, u32[]{:S(2)}) collective-permute-start(bf16[2,64,1536]{2,1,0:T(8,128)(2,1)S(1)} %get-tuple-element.26), channel_id=1, source_target_pairs={{0,64},{1,65},{2,66},{3,67},{4,68},{5,69},{6,70},{7,71},{8,72},{9,... | collective-permute-start | bytes 1179656 | tf_op jit(solution)/shard_map/ppermute | solution.py:186
  67.4 4.0 %shard_map.75.context = bf16[512,512]{1,0:T(8,128)(2,1)} custom-call(f32[512,1536]{1,0:T(8,128)S(1)} %shard_map.74.partial, bf16[4,512,256]{2,1,0:T(8,128)(2,1)S(1)} %shard_map.73.normed, bf16[4,64,1536]{2,1,0:T(8,128)(2,1)S(1)} %pad_maximum_fusion.mine, bf16[4,64,1536]{2,1,0:T(8,128)(2,1)S(1)} %collective-permute-done.3.other), custom_call_target="tpu_custom_call" | custom-call | flops 3000000000 | bytes 4194304 | tf_op jit(solution)/shard_map/pallas_call | solution.py:154
  71.4 2.5 %all-to-all-done = bf16[32,16,1024]{2,1,0:T(8,128)(2,1)} async-done(((bf16[32,16,1024]{2,1,0:T(8,128)(2,1)}), bf16[32,16,1024]{2,1,0:T(8,128)(2,1)}, u32[]{:S(2)}, u32[]{:S(2)}) %all-to-all-start) | async-done | bytes 1048608 | tf_op jit(solution)/shard_map/all_to_all | solution.py:212
  73.8 9.1 %all-to-all-start.1 = ((bf16[32,16,512]{2,1,0:T(8,128)(2,1)}), bf16[32,16,512]{2,1,0:T(8,128)(2,1)}, u32[]{:S(2)}, u32[]{:S(2)}) async-start(bf16[32,16,512]{2,1,0:T(8,128)(2,1)} %bitcast.11), calls=%async_computation.1 | async-start | bytes 1048576 | tf_op jit(solution)/shard_map/all_to_all | solution.py:212
  83.0 2.8 %collective-permute-start.7 = (bf16[4,64,1536]{2,1,0:T(8,128)(2,1)S(1)}, bf16[4,64,1536]{2,1,0:T(8,128)(2,1)S(1)}, u32[]{:S(2)}, u32[]{:S(2)}) collective-permute-start(bf16[4,64,1536]{2,1,0:T(8,128)(2,1)S(1)} %bitcast.42), channel_id=1, source_target_pairs={{0,32},{32,0},{64,96},{96,64},{128,160},{160,128},{192,224},{224,1... | collective-permute-start | bytes 2359304 | tf_op jit(solution)/shard_map/ppermute | solution.py:170
  85.8 4.4 %collective-permute-start.9 = (bf16[2,64,1536]{2,1,0:T(8,128)(2,1)S(1)}, bf16[2,64,1536]{2,1,0:T(8,128)(2,1)S(1)}, u32[]{:S(2)}, u32[]{:S(2)}) collective-permute-start(bf16[2,64,1536]{2,1,0:T(8,128)(2,1)S(1)} %get-tuple-element.25), channel_id=1, source_target_pairs={{0,80},{1,81},{2,82},{3,83},{4,84},{5,85},{6,86},{7,87},{8,88},{9,... | collective-permute-start | bytes 1179656 | tf_op jit(solution)/shard_map/ppermute | solution.py:186
  90.3 10.6 %all-gather.2 = bf16[128,1024]{1,0:T(8,128)(2,1)S(1)} all-gather(bf16[32,1024]{1,0:T(8,128)(2,1)S(1)} %copy-done.12), channel_id=4, replica_groups={{0,128,256,384},{32,160,288,416},{64,192,320,448},{96,224,352,480},{1,1..., dimensions={0}, use_global_device_ids=true | all-gather | bytes 327680 | tf_op jit(solution)/shard_map/all_gather | solution.py:192
  105.2 4.2 %collective-permute-start.10 = (bf16[4,64,1536]{2,1,0:T(8,128)(2,1)S(1)}, bf16[4,64,1536]{2,1,0:T(8,128)(2,1)S(1)}, u32[]{:S(2)}, u32[]{:S(2)}) collective-permute-start(bf16[4,64,1536]{2,1,0:T(8,128)(2,1)S(1)} %constant_dynamic-update-slice_fusion.2.refs_2_), channel_id=1, source_target_pairs={{0,32},{32,0},{64,96},{96,64},{128,160},{160,128},{192,224},{224,1... | collective-permute-start | bytes 2359304 | tf_op jit(solution)/shard_map/ppermute | solution.py:170
  110.4 4.8 %collective-permute-start.6 = (bf16[2,4,32,1024]{3,2,1,0:T(8,128)(2,1)S(1)}, bf16[2,4,32,1024]{3,2,1,0:T(8,128)(2,1)S(1)}, u32[]{:S(2)}, u32[]{:S(2)}) collective-permute-start(bf16[2,4,32,1024]{3,2,1,0:T(8,128)(2,1)S(1)} %pad_maximum_fusion.1), channel_id=1, source_target_pairs={{0,32},{32,0},{64,96},{96,64},{128,160},{160,128},{192,224},{224,1... | collective-permute-start | bytes 1572872 | tf_op jit(solution)/shard_map/ppermute | solution.py:170
  121.2 6.4 %shard_map.78 = bf16[512,512]{1,0:T(8,128)(2,1)S(1)} custom-call(bf16[512,1024]{1,0:T(8,128)(2,1)} %bitcast.10.tokens, bf16[512,512]{1,0:T(8,128)(2,1)} %bitcast.12.arrived, bf16[512,1024]{1,0:T(8,128)(2,1)S(1)} %bitcast.52, f32[1,1024]{1,0:T(1,128)S(1)} %bitcast.60, bf16[4,2,2,64,1536]{4,3,2,1,0:T(8,128)(2,1)S(1)} %copy-done.1), custom_call_target="tpu_custom_call" | custom-call | flops 4000000000 | bytes 4194304 | tf_op jit(solution)/shard_map/pallas_call | solution.py:154
  128.5 12.0 %all-to-all-start.2 = ((bf16[32,16,512]{2,1,0:T(8,128)(2,1)}), bf16[32,16,512]{2,1,0:T(8,128)(2,1)}, u32[]{:S(2)}, u32[]{:S(2)}) async-start(bf16[32,16,512]{2,1,0:T(8,128)(2,1)} %bitcast.58), calls=%async_computation.2 | async-start | bytes 1048576 | tf_op jit(solution)/shard_map/all_to_all | solution.py:212
  140.5 10.6 %all-gather.3 = bf16[128,1024]{1,0:T(8,128)(2,1)S(1)} all-gather(bf16[32,1024]{1,0:T(8,128)(2,1)S(1)} %copy-done.13), channel_id=5, replica_groups={{0,128,256,384},{32,160,288,416},{64,192,320,448},{96,224,352,480},{1,1..., dimensions={0}, use_global_device_ids=true | all-gather | bytes 327680 | tf_op jit(solution)/shard_map/all_gather | solution.py:192
  153.0 4.5 %collective-permute-start.12 = (bf16[2,32,1024]{2,1,0:T(8,128)(2,1)S(1)}, bf16[2,32,1024]{2,1,0:T(8,128)(2,1)S(1)}, u32[]{:S(2)}, u32[]{:S(2)}) collective-permute-start(bf16[2,32,1024]{2,1,0:T(8,128)(2,1)S(1)} %bitcast.64), channel_id=1, source_target_pairs={{0,80},{1,81},{2,82},{3,83},{4,84},{5,85},{6,86},{7,87},{8,88},{9,... | collective-permute-start | bytes 393224 | tf_op jit(solution)/shard_map/ppermute | solution.py:186
  157.5 3.1 %collective-permute-done.12 = bf16[2,32,1024]{2,1,0:T(8,128)(2,1)S(1)} collective-permute-done((bf16[2,32,1024]{2,1,0:T(8,128)(2,1)S(1)}, bf16[2,32,1024]{2,1,0:T(8,128)(2,1)S(1)}, u32[]{:S(2)}, u32[]{:S(2)}) %collective-permute-start.12) | collective-permute-done | bytes 131104 | tf_op jit(solution)/shard_map/ppermute | solution.py:186
  160.7 6.3 %collective-permute-start.13 = (bf16[2,4,32,1024]{3,2,1,0:T(8,128)(2,1)S(1)}, bf16[2,4,32,1024]{3,2,1,0:T(8,128)(2,1)S(1)}, u32[]{:S(2)}, u32[]{:S(2)}) collective-permute-start(bf16[2,4,32,1024]{3,2,1,0:T(8,128)(2,1)S(1)} %pad_maximum_fusion.2), channel_id=1, source_target_pairs={{0,32},{32,0},{64,96},{96,64},{128,160},{160,128},{192,224},{224,1... | collective-permute-start | bytes 1572872 | tf_op jit(solution)/shard_map/ppermute | solution.py:170
  169.5 5.2 %all-to-all-done.2 = bf16[32,16,512]{2,1,0:T(8,128)(2,1)} async-done(((bf16[32,16,512]{2,1,0:T(8,128)(2,1)}), bf16[32,16,512]{2,1,0:T(8,128)(2,1)}, u32[]{:S(2)}, u32[]{:S(2)}) %all-to-all-start.2) | async-done | bytes 524320 | tf_op jit(solution)/shard_map/all_to_all | solution.py:212
  174.7 2.7 %add_convert_fusion = bf16[512,1024]{1,0:T(8,128)(2,1)} fusion(bf16[512,1024]{1,0:T(8,128)(2,1)S(1)} %shard_map.79, bf16[512,512]{1,0:T(8,128)(2,1)} %bitcast.23, bf16[512,1024]{1,0:T(8,128)(2,1)S(1)} %bitcast.54), kind=kOutput, calls=%fused_computation | convolution fusion | flops 538443776 | bytes 3670016 | tf_op jit(solution)/shard_map/dot_general | solution.py:266
  (67 shorter events, 21.5 us)
Async XLA Ops:
  0.0 17.6 %copy-start.10 = (bf16[64,1536]{1,0:T(8,128)(2,1)S(1)}, bf16[64,1536]{1,0:T(8,128)(2,1)}, u32[]{:S(2)}) copy-start(bf16[64,1536]{1,0:T(8,128)(2,1)} %param.9) | copy-start | bytes 589828
  0.0 42.8 %copy-start.5 = (bf16[2,1,256,1024]{3,2,1,0:T(8,128)(2,1)S(1)}, bf16[2,1,256,1024]{3,2,1,0:T(8,128)(2,1)}, u32[]{:S(2)}) copy-start(bf16[2,1,256,1024]{3,2,1,0:T(8,128)(2,1)} %param.7) | copy-start | bytes 3145732
  0.0 42.8 %copy-start.8 = (f32[1024]{0:T(1024)S(1)}, f32[1024]{0:T(1024)}, u32[]{:S(2)}) copy-start(f32[1024]{0:T(1024)} %param.8) | copy-start | bytes 12292
  0.0 73.8 %all-to-all-start = ((bf16[32,16,1024]{2,1,0:T(8,128)(2,1)}), bf16[32,16,1024]{2,1,0:T(8,128)(2,1)}, u32[]{:S(2)}, u32[]{:S(2)}) async-start(bf16[32,16,1024]{2,1,0:T(8,128)(2,1)} %bitcast.55), calls=%async_computation | async-start | bytes 2097152 | tf_op jit(solution)/shard_map/all_to_all | solution.py:212
  30.1 27.6 %collective-permute-start.1 = (bf16[2,64,1536]{2,1,0:T(8,128)(2,1)}, bf16[2,64,1536]{2,1,0:T(8,128)(2,1)S(1)}, u32[]{:S(2)}, u32[]{:S(2)}) collective-permute-start(bf16[2,64,1536]{2,1,0:T(8,128)(2,1)} %bitcast.2), channel_id=1, source_target_pairs={{0,80},{1,81},{2,82},{3,83},{4,84},{5,85},{6,86},{7,87},{8,88},{9,... | collective-permute-start | bytes 1179656 | tf_op jit(solution)/shard_map/ppermute | solution.py:186
  33.7 23.9 %collective-permute-start = (bf16[2,64,1536]{2,1,0:T(8,128)(2,1)S(1)}, bf16[2,64,1536]{2,1,0:T(8,128)(2,1)}, u32[]{:S(2)}, u32[]{:S(2)}) collective-permute-start(bf16[2,64,1536]{2,1,0:T(8,128)(2,1)S(1)} %bitcast.61), channel_id=1, source_target_pairs={{0,64},{1,65},{2,66},{3,67},{4,68},{5,69},{6,70},{7,71},{8,72},{9,... | collective-permute-start | bytes 1179656 | tf_op jit(solution)/shard_map/ppermute | solution.py:186
  35.7 23.1 %collective-permute-start.2 = (bf16[4,64,1536]{2,1,0:T(8,128)(2,1)S(1)}, bf16[4,64,1536]{2,1,0:T(8,128)(2,1)S(1)}, u32[]{:S(2)}, u32[]{:S(2)}) collective-permute-start(bf16[4,64,1536]{2,1,0:T(8,128)(2,1)S(1)} %bitcast.44), channel_id=1, source_target_pairs={{0,32},{32,0},{64,96},{96,64},{128,160},{160,128},{192,224},{224,1... | collective-permute-start | bytes 2359304 | tf_op jit(solution)/shard_map/ppermute | solution.py:170
  59.8 7.6 %collective-permute-start.3 = (bf16[4,64,1536]{2,1,0:T(8,128)(2,1)S(1)}, bf16[4,64,1536]{2,1,0:T(8,128)(2,1)S(1)}, u32[]{:S(2)}, u32[]{:S(2)}) collective-permute-start(bf16[4,64,1536]{2,1,0:T(8,128)(2,1)S(1)} %pad_maximum_fusion.mine), channel_id=1, source_target_pairs={{0,32},{32,0},{64,96},{96,64},{128,160},{160,128},{192,224},{224,1... | collective-permute-start | bytes 2359304 | tf_op jit(solution)/shard_map/ppermute | solution.py:170
  63.7 26.6 %copy-start.12 = (bf16[32,1024]{1,0:T(8,128)(2,1)S(1)}, bf16[32,1024]{1,0:T(8,128)(2,1)}, u32[]{:S(2)}) copy-start(bf16[32,1024]{1,0:T(8,128)(2,1)} %param.10) | copy-start | bytes 196612
  63.7 26.5 %collective-permute-start.8 = (bf16[2,64,1536]{2,1,0:T(8,128)(2,1)S(1)}, bf16[2,64,1536]{2,1,0:T(8,128)(2,1)S(1)}, u32[]{:S(2)}, u32[]{:S(2)}) collective-permute-start(bf16[2,64,1536]{2,1,0:T(8,128)(2,1)S(1)} %get-tuple-element.26), channel_id=1, source_target_pairs={{0,64},{1,65},{2,66},{3,67},{4,68},{5,69},{6,70},{7,71},{8,72},{9,... | collective-permute-start | bytes 1179656 | tf_op jit(solution)/shard_map/ppermute | solution.py:186
  73.8 45.6 %all-to-all-start.1 = ((bf16[32,16,512]{2,1,0:T(8,128)(2,1)}), bf16[32,16,512]{2,1,0:T(8,128)(2,1)}, u32[]{:S(2)}, u32[]{:S(2)}) async-start(bf16[32,16,512]{2,1,0:T(8,128)(2,1)} %bitcast.11), calls=%async_computation.1 | async-start | bytes 1048576 | tf_op jit(solution)/shard_map/all_to_all | solution.py:212
  83.0 32.2 %collective-permute-start.7 = (bf16[4,64,1536]{2,1,0:T(8,128)(2,1)S(1)}, bf16[4,64,1536]{2,1,0:T(8,128)(2,1)S(1)}, u32[]{:S(2)}, u32[]{:S(2)}) collective-permute-start(bf16[4,64,1536]{2,1,0:T(8,128)(2,1)S(1)} %bitcast.42), channel_id=1, source_target_pairs={{0,32},{32,0},{64,96},{96,64},{128,160},{160,128},{192,224},{224,1... | collective-permute-start | bytes 2359304 | tf_op jit(solution)/shard_map/ppermute | solution.py:170
  85.8 19.4 %collective-permute-start.9 = (bf16[2,64,1536]{2,1,0:T(8,128)(2,1)S(1)}, bf16[2,64,1536]{2,1,0:T(8,128)(2,1)S(1)}, u32[]{:S(2)}, u32[]{:S(2)}) collective-permute-start(bf16[2,64,1536]{2,1,0:T(8,128)(2,1)S(1)} %get-tuple-element.25), channel_id=1, source_target_pairs={{0,80},{1,81},{2,82},{3,83},{4,84},{5,85},{6,86},{7,87},{8,88},{9,... | collective-permute-start | bytes 1179656 | tf_op jit(solution)/shard_map/ppermute | solution.py:186
  100.9 8.5 %collective-permute-start.4 = (bf16[2,32,1024]{2,1,0:T(8,128)(2,1)S(1)}, bf16[2,32,1024]{2,1,0:T(8,128)(2,1)S(1)}, u32[]{:S(2)}, u32[]{:S(2)}) collective-permute-start(bf16[2,32,1024]{2,1,0:T(8,128)(2,1)S(1)} %bitcast.63), channel_id=1, source_target_pairs={{0,64},{1,65},{2,66},{3,67},{4,68},{5,69},{6,70},{7,71},{8,72},{9,... | collective-permute-start | bytes 393224 | tf_op jit(solution)/shard_map/ppermute | solution.py:186
  102.8 7.6 %collective-permute-start.5 = (bf16[2,32,1024]{2,1,0:T(8,128)(2,1)S(1)}, bf16[2,32,1024]{2,1,0:T(8,128)(2,1)S(1)}, u32[]{:S(2)}, u32[]{:S(2)}) collective-permute-start(bf16[2,32,1024]{2,1,0:T(8,128)(2,1)S(1)} %bitcast.62), channel_id=1, source_target_pairs={{0,80},{1,81},{2,82},{3,83},{4,84},{5,85},{6,86},{7,87},{8,88},{9,... | collective-permute-start | bytes 393224 | tf_op jit(solution)/shard_map/ppermute | solution.py:186
  105.2 10.1 %collective-permute-start.10 = (bf16[4,64,1536]{2,1,0:T(8,128)(2,1)S(1)}, bf16[4,64,1536]{2,1,0:T(8,128)(2,1)S(1)}, u32[]{:S(2)}, u32[]{:S(2)}) collective-permute-start(bf16[4,64,1536]{2,1,0:T(8,128)(2,1)S(1)} %constant_dynamic-update-slice_fusion.2.refs_2_), channel_id=1, source_target_pairs={{0,32},{32,0},{64,96},{96,64},{128,160},{160,128},{192,224},{224,1... | collective-permute-start | bytes 2359304 | tf_op jit(solution)/shard_map/ppermute | solution.py:170
  110.4 7.3 %collective-permute-start.6 = (bf16[2,4,32,1024]{3,2,1,0:T(8,128)(2,1)S(1)}, bf16[2,4,32,1024]{3,2,1,0:T(8,128)(2,1)S(1)}, u32[]{:S(2)}, u32[]{:S(2)}) collective-permute-start(bf16[2,4,32,1024]{3,2,1,0:T(8,128)(2,1)S(1)} %pad_maximum_fusion.1), channel_id=1, source_target_pairs={{0,32},{32,0},{64,96},{96,64},{128,160},{160,128},{192,224},{224,1... | collective-permute-start | bytes 1572872 | tf_op jit(solution)/shard_map/ppermute | solution.py:170
  121.2 19.3 %copy-start.13 = (bf16[32,1024]{1,0:T(8,128)(2,1)S(1)}, bf16[32,1024]{1,0:T(8,128)(2,1)}, u32[]{:S(2)}) copy-start(bf16[32,1024]{1,0:T(8,128)(2,1)} %param.13) | copy-start | bytes 196612
  128.4 38.6 %copy-start.4 = (bf16[4,2,2,32,1024]{4,3,2,1,0:T(8,128)(2,1)S(1)}, bf16[4,2,2,32,1024]{4,3,2,1,0:T(8,128)(2,1)}, u32[]{:S(2)}) copy-start(bf16[4,2,2,32,1024]{4,3,2,1,0:T(8,128)(2,1)} %copy-done.2) | copy-start | bytes 3145732
  128.5 38.6 %copy-start.6 = (bf16[2,1,256,1024]{3,2,1,0:T(8,128)(2,1)S(1)}, bf16[2,1,256,1024]{3,2,1,0:T(8,128)(2,1)}, u32[]{:S(2)}) copy-start(bf16[2,1,256,1024]{3,2,1,0:T(8,128)(2,1)} %param.7) | copy-start | bytes 3145732
  128.5 46.2 %all-to-all-start.2 = ((bf16[32,16,512]{2,1,0:T(8,128)(2,1)}), bf16[32,16,512]{2,1,0:T(8,128)(2,1)}, u32[]{:S(2)}, u32[]{:S(2)}) async-start(bf16[32,16,512]{2,1,0:T(8,128)(2,1)} %bitcast.58), calls=%async_computation.2 | async-start | bytes 1048576 | tf_op jit(solution)/shard_map/all_to_all | solution.py:212
  151.1 6.4 %collective-permute-start.11 = (bf16[2,32,1024]{2,1,0:T(8,128)(2,1)S(1)}, bf16[2,32,1024]{2,1,0:T(8,128)(2,1)S(1)}, u32[]{:S(2)}, u32[]{:S(2)}) collective-permute-start(bf16[2,32,1024]{2,1,0:T(8,128)(2,1)S(1)} %bitcast.65), channel_id=1, source_target_pairs={{0,64},{1,65},{2,66},{3,67},{4,68},{5,69},{6,70},{7,71},{8,72},{9,... | collective-permute-start | bytes 393224 | tf_op jit(solution)/shard_map/ppermute | solution.py:186
  153.0 7.6 %collective-permute-start.12 = (bf16[2,32,1024]{2,1,0:T(8,128)(2,1)S(1)}, bf16[2,32,1024]{2,1,0:T(8,128)(2,1)S(1)}, u32[]{:S(2)}, u32[]{:S(2)}) collective-permute-start(bf16[2,32,1024]{2,1,0:T(8,128)(2,1)S(1)} %bitcast.64), channel_id=1, source_target_pairs={{0,80},{1,81},{2,82},{3,83},{4,84},{5,85},{6,86},{7,87},{8,88},{9,... | collective-permute-start | bytes 393224 | tf_op jit(solution)/shard_map/ppermute | solution.py:186
  160.7 8.1 %collective-permute-start.13 = (bf16[2,4,32,1024]{3,2,1,0:T(8,128)(2,1)S(1)}, bf16[2,4,32,1024]{3,2,1,0:T(8,128)(2,1)S(1)}, u32[]{:S(2)}, u32[]{:S(2)}) collective-permute-start(bf16[2,4,32,1024]{3,2,1,0:T(8,128)(2,1)S(1)} %pad_maximum_fusion.2), channel_id=1, source_target_pairs={{0,32},{32,0},{64,96},{96,64},{128,160},{160,128},{192,224},{224,1... | collective-permute-start | bytes 1572872 | tf_op jit(solution)/shard_map/ppermute | solution.py:170
  (7 other events, 11.0 us)

commit v7 on v4

--- a/solution.py
+++ b/solution.py
@@ -53,13 +53,21 @@
         store(columns, value)
 
 
-def pack_kernel(qkv, out, packed):
+def pack_kernel(qkv, out, next_qkv, next_out, packed, next_packed, sems):
     depth, width = qkv.shape
     half = out.shape[1] // 2
-    for index in range(packed.shape[0]):
-        packed[index, :, pl.ds(0, width)] = qkv[...]
-        packed[index, pl.ds(0, depth // 2), pl.ds(width, half)] = out[:, pl.ds(0, half)]
-        packed[index, pl.ds(depth // 2, depth // 2), pl.ds(width, half)] = out[:, pl.ds(half, half)]
+    copies = []
+    for index in range(packed.shape[0] + 1):
+        if index < packed.shape[0]:
+            pair, target = (qkv, out), packed.at[index]
+        else:
+            pair, target = (next_qkv, next_out), next_packed
+        copies.append(pltpu.make_async_copy(pair[0], target.at[:, pl.ds(0, width)], sems.at[index, 0]))
+        for side in range(2):
+            rows, columns = pl.ds(side * depth // 2, depth // 2), pl.ds(side * half, half)
+            place = target.at[rows, pl.ds(width, half)]
+            copies.append(pltpu.make_async_copy(pair[1].at[:, columns], place, sems.at[index, 1 + side]))
+    wait(run(copies))
 
 
 def run(copies):
@@ -126,26 +134,42 @@
         middle[:, columns] = (tokens[:, columns].astype(F32) + added).astype(BF16)
 
 
-def fetches(here, mine, other, placed, sems):
+def place_kernel(here, mine, other, qkv, out, sems):
+    _, depth, width = qkv.shape
+    half = out.shape[2] // 2
     copies = []
     for side, source in enumerate((mine, other)):
-        for beside in range(2):
-            target = placed.at[:, (here[1] + beside) % 2, (here[2] + side) % 2]
-            copies.append(pltpu.make_async_copy(source.at[beside], target, sems.at[side, beside]))
-    return run(copies)
-
-
-def place_kernel(here, mine, other, placed, sems):
-    wait(fetches(here, mine, other, placed, sems))
-
-
-def temporal_kernel(frames, middle, gain, placed, context, qkv):
+        for index in range(source.shape[0]):
+            step = (0, 3, 1, 2)[index // 2]
+            row = ((here[0] + step) % 4 * 2 + (here[1] + index) % 2) * 2 + (here[2] + side) % 2
+            block = source.at[index]
+            copies.append(pltpu.make_async_copy(block.at[:, pl.ds(0, width)], qkv.at[row], sems.at[side, index, 0]))
+            for part in range(2):
+                rows, columns = pl.ds(part * depth // 2, depth // 2), pl.ds(part * half, half)
+                piece = block.at[rows, pl.ds(width, half)]
+                copies.append(pltpu.make_async_copy(piece, out.at[row, :, columns], sems.at[side, index, 1 + part]))
+    wait(run(copies))
+
+
+def copy_kernel(source, target):
+    target[...] = source[...]
+
+
+def temporal_kernel(frames, middle, gain, placed, context, weights, qkv, sems):
+    pieces = [pl.ds(piece * 256, 256) for piece in range(3 * INNER // 256)]
+    copies = run(
+        [
+            pltpu.make_async_copy(placed.at[:, :, columns], weights.at[:, :, columns], sems.at[piece])
+            for piece, columns in enumerate(pieces)
+        ]
+    )
     normed = norm_rows(middle[...].astype(F32), gain[...]).astype(BF16)
     rows, depth = middle.shape
     places = rows // frames
 
     def product(columns):
-        weight = placed[:, :, :, :, columns].reshape(depth, 256)
+        copies[columns.start // 256].wait()
+        weight = weights[:, :, columns].reshape(depth, 256)
         return jnp.dot(normed, weight, preferred_element_type=F32)
 
     def store(columns, value):
@@ -164,7 +188,7 @@
     context[...] = jnp.concatenate(outs, axis=1).reshape(rows, INNER).astype(BF16)
 
 
-def kernel_call(body, kinds, out, operands, scratch=(), gflops=0, mib=4):
+def kernel_call(body, kinds, out, operands, scratch=(), gflops=0, mib=4, room=24):
     near = pl.BlockSpec(memory_space=pltpu.VMEM)
     specs = {"s": pl.BlockSpec(memory_space=pltpu.SMEM), "v": near, "h": pl.BlockSpec(memory_space=pl.ANY)}
     return pl.pallas_call(
@@ -173,7 +197,7 @@
         in_specs=[specs[kind] for kind in kinds],
         out_specs=jax.tree.map(lambda _: near, out),
         scratch_shapes=scratch,
-        compiler_params=pltpu.CompilerParams(vmem_limit_bytes=24 * MIB),
+        compiler_params=pltpu.CompilerParams(vmem_limit_bytes=room * MIB),
         cost_estimate=pl.CostEstimate(flops=int(gflops * 1e9), bytes_accessed=mib * MIB, transcendentals=0),
     )(*operands)
 
@@ -190,10 +214,13 @@
     return moved(array, lambda x, yl, core: (x, yl, 1 - core))
 
 
-def along_x(shard):
-    lines = [list(range(start, 16, 4)) for start in range(4)]
-    own = lax.all_gather(shard, "fsdp", axis_index_groups=lines)
-    mine = jnp.stack([own, moved(own, lambda x, yl, core: (x, 1 - yl, core))])
+def gathered_by_hops(both):
+    depth = both.shape[0] // 2
+    ahead = lambda x, yl, core: ((x + 1) % 4, yl, core)
+    back = lambda x, yl, core: ((x + 3) % 4, yl, core)
+    left, right = moved(both, ahead), moved(both, back)
+    far = moved(left[:depth], ahead), moved(right[depth:], back)
+    mine = jnp.concatenate([both, left, right, *far], axis=0).reshape(8, depth, both.shape[1])
     return mine, other_core(mine)
 
 
@@ -214,25 +241,24 @@
         sent = array.reshape(frames, block, array.shape[1])
         return lax.all_to_all(sent, "tm", split_axis=0, concat_axis=0, tiled=True).reshape(array.shape)
 
-    def in_order(shard):
-        return kernel_call(
-            place_kernel,
-            "shh",
-            shape((4, 2, 2, *shard.shape), BF16),
-            (here, *along_x(shard)),
-            [pltpu.SemaphoreType.DMA((2, 2))],
-        )
-
-    packed = kernel_call(pack_kernel, "vv", shape((parts, part, 4 * INNER), BF16), (spatial_qkv, spatial_out))
+    packed, own = kernel_call(
+        pack_kernel,
+        "hhhh",
+        [shape((parts, part, 4 * INNER), BF16), shape((part, 4 * INNER), BF16)],
+        (spatial_qkv, spatial_out, temporal_qkv, temporal_out),
+        [pltpu.SemaphoreType.DMA((parts + 1, 3))],
+        room=60,
+    )
     mine = lax.all_to_all(packed, "fsdp", 0, 0, axis_index_groups=cores, tiled=True)
+    own, gain, mine = lax.optimization_barrier((own, spatial_gain, mine))
+    beside = moved(own, lambda x, yl, core: (x, 1 - yl, core))
     normed, normed_other = kernel_call(
         norm_kernel,
         "svv",
         [shape((rows, depth // 2), BF16)] * 2,
-        (here, flat, spatial_gain.reshape(1, depth)),
+        (here, flat, gain.reshape(1, depth)),
         gflops=2,
     )
-    mine, normed, normed_other = lax.optimization_barrier((mine, normed, normed_other))
     partial = kernel_call(half_kernel, "vv", shape((rows, 3 * INNER), F32), (normed, mine), gflops=1)
     middle = kernel_call(
         spatial_kernel,
@@ -247,20 +273,33 @@
         ],
         gflops=3,
     )
-    shard, middle = lax.optimization_barrier((temporal_qkv, middle))
+    own, beside, middle = lax.optimization_barrier((own, beside, middle))
     arrived = exchanged(middle)
+    placed, weight = kernel_call(
+        place_kernel,
+        "shh",
+        [shape((members, part, 3 * INNER), BF16), shape((members, INNER // members, depth), BF16)],
+        (here, *gathered_by_hops(jnp.concatenate([own, beside], axis=0))),
+        [pltpu.SemaphoreType.DMA((2, parts, 3))],
+        room=60,
+    )
     context = kernel_call(
         functools.partial(temporal_kernel, frames),
-        "vvv",
+        "vvh",
         shape((rows, INNER), BF16),
-        (arrived, temporal_gain.reshape(1, depth), in_order(shard)),
-        [pltpu.VMEM((rows, 3 * INNER), BF16)],
+        (arrived, temporal_gain.reshape(1, depth), placed),
+        [
+            pltpu.VMEM((members, part, 3 * INNER), BF16),
+            pltpu.VMEM((rows, 3 * INNER), BF16),
+            pltpu.SemaphoreType.DMA((6,)),
+        ],
         gflops=4,
-    )
-    shard, context = lax.optimization_barrier((temporal_out, context))
+        room=50,
+    )
+    middle, context = lax.optimization_barrier((middle, context))
     returned = exchanged(context)
-    weight = in_order(shard).reshape(INNER, depth)
-    encoded = middle.astype(F32) + jnp.dot(returned, weight, preferred_element_type=F32)
+    kept = kernel_call(copy_kernel, "v", shape((rows, depth), BF16), (middle,))
+    encoded = kept.astype(F32) + jnp.dot(returned, weight.reshape(INNER, depth), preferred_element_type=F32)
     return encoded.astype(BF16).reshape(tokens.shape)
 
 

time: 174 us -> 175 us (level)
  waiting for transfers between devices: 83.4 us -> 65.6 us
  Pallas kernels: 17.7 us -> 28.5 us
  starting transfers between devices: 37.7 us -> 43.9 us
  blocking collectives: 26.8 us -> 32.1 us
  local copies, waits for them, and re-layouts: 4.61 us -> 1.9 us
    all_to_all x0 -> x1, blocking collectives: none -> 32.1 us  [shards(): lax.all_to_all(packed, 'fsdp', 0, 0, axis_index_groups=cores, tiled=True)]
    all_to_all x2, waiting for transfers between devices: 20.2 us -> 47.9 us  [exchanged(): lax.all_to_all(sent, 'tm', split_axis=0, concat_axis=0, tiled=True)]
    all_gather x2 -> x0, blocking collectives: 26.8 us -> none  [along_x(): own = lax.all_gather(shard, 'fsdp', axis_index_groups=lines)]
    all_to_all x1 -> x0, waiting for transfers between devices: 26.7 us -> none  [shards(): lax.all_to_all(packed, 'fsdp', 0, 0, axis_index_groups=cores, tiled=True)]
    ppermute x5 -> x7, waiting for transfers between devices: 36.5 us -> 17.7 us  [moved(): return lax.ppermute(array, 'fsdp', pairs)]
    ppermute x5 -> x7, starting transfers between devices: 9.88 us -> 21.6 us  [moved(): return lax.ppermute(array, 'fsdp', pairs)]
    pallas_call x7, Pallas kernels: 17.7 us -> 28.5 us  [kernel_call(): pl.pallas_call(body, out_shape=out, in_specs=[specs[kind] for kind in kin...]
    all_to_all x1 -> x0, starting transfers between devices: 5.44 us -> none  [shards(): lax.all_to_all(packed, 'fsdp', 0, 0, axis_index_groups=cores, tiled=True)]
  transfers between devices with their start and end apart: 8 -> 9, of which waited for: 8 -> 6; matrix products, arithmetic and copies ran while one was open for 0% -> 1% of each run, Pallas kernels for 3% -> 10%
where the time goes in v7:
time: 175 us; the launch traced here: 174 us
  waiting for transfers between devices  65.6 us (37%)
  starting transfers between devices  43.9 us (25%)
  blocking collectives  32.1 us (18%)
  Pallas kernels  28.5 us (16%)
  local copies, waits for them, and re-layouts  1.9 us (1%)
    all_to_all x2, waiting for transfers between devices, exchanged(): lax.all_to_all(sent, 'tm', split_axis=0, concat_axis=0, tiled=True)  47.9 us
    all_to_all x1, blocking collectives, shards(): lax.all_to_all(packed, 'fsdp', 0, 0, axis_index_groups=cores, tiled=True)  32.1 us
    pallas_call x7, Pallas kernels, kernel_call(): pl.pallas_call(body, out_shape=out, in_specs=[specs[kind] for kind in kin...  28.5 us
    all_to_all x2, starting transfers between devices, exchanged(): lax.all_to_all(sent, 'tm', split_axis=0, concat_axis=0, tiled=True)  22.2 us
    ppermute x7, starting transfers between devices, moved(): return lax.ppermute(array, 'fsdp', pairs)  21.6 us
    ppermute x7, waiting for transfers between devices, moved(): return lax.ppermute(array, 'fsdp', pairs)  17.7 us
  transfers between devices with their start and end apart: 9, of which 6 were waited for; matrix products, arithmetic and copies ran while one was open for 1% of the time, Pallas kernels for 10%

profile of v7, /device:TPU:32, one launch (start us, length us, event | category | flops | bytes accessed | tf_op | source)
XLA Modules:
  0.0 174.1 jit_solution(14710590619971666922)
XLA Ops:
  0.0 3.8 %shard_map.73 = (bf16[8,64,2048]{2,1,0:T(8,128)(2,1)}, bf16[64,2048]{1,0:T(8,128)(2,1)}) custom-call(bf16[64,1536]{1,0:T(8,128)(2,1)} %qkv.1, bf16[32,1024]{1,0:T(8,128)(2,1)} %out.1, bf16[64,1536]{1,0:T(8,128)(2,1)} %next_qkv.1, bf16[32,1024]{1,0:T(8,128)(2,1)} %next_out.1), custom_call_target="tpu_custom_call" | custom-call | bytes 4194304 | tf_op jit(solution)/shard_map/pallas_call | solution.py:194
  3.8 32.1 %all_to_all.15.weights.mine = bf16[8,64,2048]{2,1,0:T(8,128)(2,1)S(1)} all-to-all(bf16[8,64,2048]{2,1,0:T(8,128)(2,1)} %get-tuple-element.20), channel_id=1, replica_groups={{0,64,128,192,256,320,384,448},{32,96,160,224,288,352,416,480},{1,65,12..., dimensions={0} | all-to-all | bytes 4194304 | tf_op jit(solution)/shard_map/all_to_all | solution.py:252
  35.9 1.9 %collective-permute-start.1 = (bf16[8,64,2048]{2,1,0:T(8,128)(2,1)S(1)}, bf16[8,64,2048]{2,1,0:T(8,128)(2,1)}, u32[]{:S(2)}, u32[]{:S(2)}) collective-permute-start(bf16[8,64,2048]{2,1,0:T(8,128)(2,1)S(1)} %all_to_all.15.weights.mine), channel_id=1, source_target_pairs={{0,32},{32,0},{64,96},{96,64},{128,160},{160,128},{192,224},{224,1... | collective-permute-start | bytes 6291464 | tf_op jit(solution)/shard_map/ppermute | solution.py:210
  38.0 3.4 %collective-permute-start = (bf16[64,2048]{1,0:T(8,128)(2,1)S(1)}, bf16[64,2048]{1,0:T(8,128)(2,1)S(1)}, u32[]{:S(2)}, u32[]{:S(2)}) collective-permute-start(bf16[64,2048]{1,0:T(8,128)(2,1)S(1)} %copy-done.5), channel_id=1, source_target_pairs={{0,64},{32,96},{64,0},{96,32},{128,192},{160,224},{192,128},{224,1... | collective-permute-start | bytes 786440 | tf_op jit(solution)/shard_map/ppermute | solution.py:210
  41.4 2.3 %shard_map.74 = (bf16[512,512]{1,0:T(8,128)(2,1)S(1)}, bf16[512,512]{1,0:T(8,128)(2,1)S(1)}) custom-call(s32[3]{0:T(128)S(1)} %pad_add_fusion.here, bf16[512,1024]{1,0:T(8,128)(2,1)S(1)} %bitcast.18, f32[1,1024]{1,0:T(1,128)S(1)} %bitcast.20), custom_call_target="tpu_custom_call" | custom-call | flops 2000000000 | bytes 4194304 | tf_op jit(solution)/shard_map/pallas_call | solution.py:194
  43.7 1.0 shard_map.75.partial
  44.7 6.8 %shard_map.76.source = bf16[512,1024]{1,0:T(8,128)(2,1)} custom-call(s32[3]{0:T(128)S(1)} %pad_add_fusion.here, bf16[512,1024]{1,0:T(8,128)(2,1)S(1)} %bitcast.19, f32[512,1536]{1,0:T(8,128)S(1)} %shard_map.75.partial, bf16[512,512]{1,0:T(8,128)(2,1)S(1)} %get-tuple-element.25.normed, bf16[8,64,2048]{2,1,0:T(8,128)(2,1)S(1)} %all_to_all.15.weights.mine, ...), custom_call_target="tpu_custom_call" | custom-call | flops 3000000000 | bytes 4194304 | tf_op jit(solution)/shard_map/pallas_call | solution.py:194
  52.2 17.7 %all-to-all-start.1 = ((bf16[32,16,1024]{2,1,0:T(8,128)(2,1)}), bf16[32,16,1024]{2,1,0:T(8,128)(2,1)S(1)}, u32[]{:S(2)}, u32[]{:S(2)}) async-start(bf16[32,16,1024]{2,1,0:T(8,128)(2,1)} %bitcast.5), calls=%async_computation.1 | async-start | bytes 2097152 | tf_op jit(solution)/shard_map/all_to_all | solution.py:242
  70.9 2.5 %collective-permute-start.2 = (bf16[128,2048]{1,0:T(8,128)(2,1)S(1)}, bf16[128,2048]{1,0:T(8,128)(2,1)S(1)}, u32[]{:S(2)}, u32[]{:S(2)}) collective-permute-start(bf16[128,2048]{1,0:T(8,128)(2,1)S(1)} %get-tuple-element.33), channel_id=1, source_target_pairs={{0,128},{32,160},{64,192},{96,224},{128,256},{160,288},{192,320},{... | collective-permute-start | bytes 1572872 | tf_op jit(solution)/shard_map/ppermute | solution.py:210
  73.4 4.6 %collective-permute-start.3 = (bf16[128,2048]{1,0:T(8,128)(2,1)S(1)}, bf16[128,2048]{1,0:T(8,128)(2,1)S(1)}, u32[]{:S(2)}, u32[]{:S(2)}) collective-permute-start(bf16[128,2048]{1,0:T(8,128)(2,1)S(1)} %get-tuple-element.33), channel_id=1, source_target_pairs={{0,384},{32,416},{64,448},{96,480},{128,0},{160,32},{192,64},{224,... | collective-permute-start | bytes 1572872 | tf_op jit(solution)/shard_map/ppermute | solution.py:210
  78.0 9.5 %collective-permute-done.2 = bf16[128,2048]{1,0:T(8,128)(2,1)S(1)} collective-permute-done((bf16[128,2048]{1,0:T(8,128)(2,1)S(1)}, bf16[128,2048]{1,0:T(8,128)(2,1)S(1)}, u32[]{:S(2)}, u32[]{:S(2)}) %collective-permute-start.2) | collective-permute-done | bytes 524320 | tf_op jit(solution)/shard_map/ppermute | solution.py:210
  87.6 1.9 %collective-permute-start.4 = (bf16[64,2048]{1,0:T(8,128)(2,1)S(1)}, bf16[64,2048]{1,0:T(8,128)(2,1)S(1)}, u32[]{:S(2)}, u32[]{:S(2)}) collective-permute-start(bf16[64,2048]{1,0:T(8,128)(2,1)S(1)} %slice.8), channel_id=1, source_target_pairs={{0,128},{32,160},{64,192},{96,224},{128,256},{160,288},{192,320},{... | collective-permute-start | bytes 786440 | tf_op jit(solution)/shard_map/ppermute | solution.py:210
  89.5 5.1 %collective-permute-start.5 = (bf16[64,2048]{1,0:T(8,128)(2,1)S(1)}, bf16[64,2048]{1,0:T(8,128)(2,1)S(1)}, u32[]{:S(2)}, u32[]{:S(2)}) collective-permute-start(bf16[64,2048]{1,0:T(8,128)(2,1)S(1)} %slice.9), channel_id=1, source_target_pairs={{0,384},{32,416},{64,448},{96,480},{128,0},{160,32},{192,64},{224,... | collective-permute-start | bytes 786440 | tf_op jit(solution)/shard_map/ppermute | solution.py:210
  94.8 2.9 %collective-permute-done.4 = bf16[64,2048]{1,0:T(8,128)(2,1)S(1)} collective-permute-done((bf16[64,2048]{1,0:T(8,128)(2,1)S(1)}, bf16[64,2048]{1,0:T(8,128)(2,1)S(1)}, u32[]{:S(2)}, u32[]{:S(2)}) %collective-permute-start.4) | collective-permute-done | bytes 262176 | tf_op jit(solution)/shard_map/ppermute | solution.py:210
  97.7 1.2 collective-permute-done.5
  98.9 2.2 %collective-permute-start.6 = (bf16[8,64,2048]{2,1,0:T(8,128)(2,1)S(1)}, bf16[8,64,2048]{2,1,0:T(8,128)(2,1)}, u32[]{:S(2)}, u32[]{:S(2)}) collective-permute-start(bf16[8,64,2048]{2,1,0:T(8,128)(2,1)S(1)} %bitcast.22), channel_id=1, source_target_pairs={{0,32},{32,0},{64,96},{96,64},{128,160},{160,128},{192,224},{224,1... | collective-permute-start | bytes 6291464 | tf_op jit(solution)/shard_map/ppermute | solution.py:210
  101.1 4.1 %collective-permute-done.6.other = bf16[8,64,2048]{2,1,0:T(8,128)(2,1)} collective-permute-done((bf16[8,64,2048]{2,1,0:T(8,128)(2,1)S(1)}, bf16[8,64,2048]{2,1,0:T(8,128)(2,1)}, u32[]{:S(2)}, u32[]{:S(2)}) %collective-permute-start.6) | collective-permute-done | bytes 2097184 | tf_op jit(solution)/shard_map/ppermute | solution.py:210
  105.2 5.5 %shard_map.77 = (bf16[16,64,1536]{2,1,0:T(8,128)(2,1)}, bf16[16,32,1024]{2,1,0:T(8,128)(2,1)}) custom-call(s32[3]{0:T(128)} %copy-done, bf16[8,64,2048]{2,1,0:T(8,128)(2,1)} %bitcast.23, bf16[8,64,2048]{2,1,0:T(8,128)(2,1)} %collective-permute-done.6.other), custom_call_target="tpu_custom_call" | custom-call | bytes 4194304 | tf_op jit(solution)/shard_map/pallas_call | solution.py:194
  110.7 15.6 %all-to-all-done.1 = bf16[32,16,1024]{2,1,0:T(8,128)(2,1)S(1)} async-done(((bf16[32,16,1024]{2,1,0:T(8,128)(2,1)}), bf16[32,16,1024]{2,1,0:T(8,128)(2,1)S(1)}, u32[]{:S(2)}, u32[]{:S(2)}) %all-to-all-start.1) | async-done | bytes 1048608 | tf_op jit(solution)/shard_map/all_to_all | solution.py:242
  126.3 7.9 %shard_map.78 = bf16[512,512]{1,0:T(8,128)(2,1)} custom-call(bf16[512,1024]{1,0:T(8,128)(2,1)S(1)} %bitcast.17, f32[1,1024]{1,0:T(1,128)S(1)} %bitcast.21, bf16[16,64,1536]{2,1,0:T(8,128)(2,1)} %get-tuple-element.29.placed), custom_call_target="tpu_custom_call" | custom-call | flops 4000000000 | bytes 4194304 | tf_op jit(solution)/shard_map/pallas_call | solution.py:194
  134.2 4.6 %all-to-all-start.2 = ((bf16[32,16,512]{2,1,0:T(8,128)(2,1)}), bf16[32,16,512]{2,1,0:T(8,128)(2,1)S(1)}, u32[]{:S(2)}, u32[]{:S(2)}) async-start(bf16[32,16,512]{2,1,0:T(8,128)(2,1)} %bitcast.9), calls=%async_computation.2 | async-start | bytes 1048576 | tf_op jit(solution)/shard_map/all_to_all | solution.py:242
  138.7 1.3 shard_map.79
  140.0 32.4 %all-to-all-done.2 = bf16[32,16,512]{2,1,0:T(8,128)(2,1)S(1)} async-done(((bf16[32,16,512]{2,1,0:T(8,128)(2,1)}), bf16[32,16,512]{2,1,0:T(8,128)(2,1)S(1)}, u32[]{:S(2)}, u32[]{:S(2)}) %all-to-all-start.2) | async-done | bytes 524320 | tf_op jit(solution)/shard_map/all_to_all | solution.py:242
  172.4 1.7 add_convert_fusion
  (28 shorter events, 2.0 us)
Async XLA Ops:
  3.8 34.2 %copy-start.5 = (bf16[64,2048]{1,0:T(8,128)(2,1)S(1)}, bf16[64,2048]{1,0:T(8,128)(2,1)}, u32[]{:S(2)}) copy-start(bf16[64,2048]{1,0:T(8,128)(2,1)} %get-tuple-element.27) | copy-start | bytes 786436
  3.8 37.5 %copy-start.1 = (bf16[2,1,256,1024]{3,2,1,0:T(8,128)(2,1)S(1)}, bf16[2,1,256,1024]{3,2,1,0:T(8,128)(2,1)}, u32[]{:S(2)}) copy-start(bf16[2,1,256,1024]{3,2,1,0:T(8,128)(2,1)} %param.7) | copy-start | bytes 3145732
  3.8 37.5 %copy-start.2 = (f32[1024]{0:T(1024)S(1)}, f32[1024]{0:T(1024)}, u32[]{:S(2)}) copy-start(f32[1024]{0:T(1024)} %param.8) | copy-start | bytes 12292
  35.9 8.8 %collective-permute-start.1 = (bf16[8,64,2048]{2,1,0:T(8,128)(2,1)S(1)}, bf16[8,64,2048]{2,1,0:T(8,128)(2,1)}, u32[]{:S(2)}, u32[]{:S(2)}) collective-permute-start(bf16[8,64,2048]{2,1,0:T(8,128)(2,1)S(1)} %all_to_all.15.weights.mine), channel_id=1, source_target_pairs={{0,32},{32,0},{64,96},{96,64},{128,160},{160,128},{192,224},{224,1... | collective-permute-start | bytes 6291464 | tf_op jit(solution)/shard_map/ppermute | solution.py:210
  38.0 6.8 %copy-start = (s32[3]{0:T(128)}, s32[3]{0:T(128)S(1)}, u32[]{:S(2)}) copy-start(s32[3]{0:T(128)S(1)} %pad_add_fusion.here) | copy-start | bytes 40
  38.0 13.5 %collective-permute-start = (bf16[64,2048]{1,0:T(8,128)(2,1)S(1)}, bf16[64,2048]{1,0:T(8,128)(2,1)S(1)}, u32[]{:S(2)}, u32[]{:S(2)}) collective-permute-start(bf16[64,2048]{1,0:T(8,128)(2,1)S(1)} %copy-done.5), channel_id=1, source_target_pairs={{0,64},{32,96},{64,0},{96,32},{128,192},{160,224},{192,128},{224,1... | collective-permute-start | bytes 786440 | tf_op jit(solution)/shard_map/ppermute | solution.py:210
  51.5 0.7 copy-start.6
  52.2 74.0 %all-to-all-start.1 = ((bf16[32,16,1024]{2,1,0:T(8,128)(2,1)}), bf16[32,16,1024]{2,1,0:T(8,128)(2,1)S(1)}, u32[]{:S(2)}, u32[]{:S(2)}) async-start(bf16[32,16,1024]{2,1,0:T(8,128)(2,1)} %bitcast.5), calls=%async_computation.1 | async-start | bytes 2097152 | tf_op jit(solution)/shard_map/all_to_all | solution.py:242
  70.9 16.6 %collective-permute-start.2 = (bf16[128,2048]{1,0:T(8,128)(2,1)S(1)}, bf16[128,2048]{1,0:T(8,128)(2,1)S(1)}, u32[]{:S(2)}, u32[]{:S(2)}) collective-permute-start(bf16[128,2048]{1,0:T(8,128)(2,1)S(1)} %get-tuple-element.33), channel_id=1, source_target_pairs={{0,128},{32,160},{64,192},{96,224},{128,256},{160,288},{192,320},{... | collective-permute-start | bytes 1572872 | tf_op jit(solution)/shard_map/ppermute | solution.py:210
  73.4 16.1 %collective-permute-start.3 = (bf16[128,2048]{1,0:T(8,128)(2,1)S(1)}, bf16[128,2048]{1,0:T(8,128)(2,1)S(1)}, u32[]{:S(2)}, u32[]{:S(2)}) collective-permute-start(bf16[128,2048]{1,0:T(8,128)(2,1)S(1)} %get-tuple-element.33), channel_id=1, source_target_pairs={{0,384},{32,416},{64,448},{96,480},{128,0},{160,32},{192,64},{224,... | collective-permute-start | bytes 1572872 | tf_op jit(solution)/shard_map/ppermute | solution.py:210
  87.6 10.1 %collective-permute-start.4 = (bf16[64,2048]{1,0:T(8,128)(2,1)S(1)}, bf16[64,2048]{1,0:T(8,128)(2,1)S(1)}, u32[]{:S(2)}, u32[]{:S(2)}) collective-permute-start(bf16[64,2048]{1,0:T(8,128)(2,1)S(1)} %slice.8), channel_id=1, source_target_pairs={{0,128},{32,160},{64,192},{96,224},{128,256},{160,288},{192,320},{... | collective-permute-start | bytes 786440 | tf_op jit(solution)/shard_map/ppermute | solution.py:210
  89.5 9.3 %collective-permute-start.5 = (bf16[64,2048]{1,0:T(8,128)(2,1)S(1)}, bf16[64,2048]{1,0:T(8,128)(2,1)S(1)}, u32[]{:S(2)}, u32[]{:S(2)}) collective-permute-start(bf16[64,2048]{1,0:T(8,128)(2,1)S(1)} %slice.9), channel_id=1, source_target_pairs={{0,384},{32,416},{64,448},{96,480},{128,0},{160,32},{192,64},{224,... | collective-permute-start | bytes 786440 | tf_op jit(solution)/shard_map/ppermute | solution.py:210
  98.9 6.3 %copy-start.4 = (bf16[512,2048]{1,0:T(8,128)(2,1)}, bf16[512,2048]{1,0:T(8,128)(2,1)S(1)}, u32[]{:S(2)}) copy-start(bf16[512,2048]{1,0:T(8,128)(2,1)S(1)} %constant_dynamic-update-slice_fusion.2) | copy-start | bytes 6291460
  98.9 27.4 %copy-start.3 = (f32[1024]{0:T(1024)S(1)}, f32[1024]{0:T(1024)}, u32[]{:S(2)}) copy-start(f32[1024]{0:T(1024)} %param.11) | copy-start | bytes 12292
  98.9 6.3 %collective-permute-start.6 = (bf16[8,64,2048]{2,1,0:T(8,128)(2,1)S(1)}, bf16[8,64,2048]{2,1,0:T(8,128)(2,1)}, u32[]{:S(2)}, u32[]{:S(2)}) collective-permute-start(bf16[8,64,2048]{2,1,0:T(8,128)(2,1)S(1)} %bitcast.22), channel_id=1, source_target_pairs={{0,32},{32,0},{64,96},{96,64},{128,160},{160,128},{192,224},{224,1... | collective-permute-start | bytes 6291464 | tf_op jit(solution)/shard_map/ppermute | solution.py:210
  134.2 38.2 %copy-start.7 = (bf16[16,32,1024]{2,1,0:T(8,128)(2,1)S(1)}, bf16[16,32,1024]{2,1,0:T(8,128)(2,1)}, u32[]{:S(2)}) copy-start(bf16[16,32,1024]{2,1,0:T(8,128)(2,1)} %get-tuple-element.32) | copy-start | bytes 3145732
  134.2 38.2 %all-to-all-start.2 = ((bf16[32,16,512]{2,1,0:T(8,128)(2,1)}), bf16[32,16,512]{2,1,0:T(8,128)(2,1)S(1)}, u32[]{:S(2)}, u32[]{:S(2)}) async-start(bf16[32,16,512]{2,1,0:T(8,128)(2,1)} %bitcast.9), calls=%async_computation.2 | async-start | bytes 1048576 | tf_op jit(solution)/shard_map/all_to_all | solution.py:242

commit v8 on v5

v8 whole, which is shorter than its diff:
```python
import functools

import jax
import jax.numpy as jnp
from jax import lax
from jax.experimental import pallas as pl
from jax.experimental.pallas import tpu as pltpu
from jax.sharding import PartitionSpec as P

HEAD = 64
HEADS = 8
INNER = 512
EPSILON = 1e-06
BF16, F32 = jnp.bfloat16, jnp.float32
GROUP = 8
PAIR = 2 * HEAD
ROWS = 256
MIB = 1 << 20


def norm_rows(values, gain):
    centre = values - jnp.mean(values, axis=-1, keepdims=True)
    spread = jnp.mean(centre * centre, axis=-1, keepdims=True)
    return centre * lax.rsqrt(spread + EPSILON) * gain


def attend(qkv, rows, same):
    low = lax.broadcasted_iota(jnp.int32, (ROWS, PAIR), 1) < HEAD
    outs = []
    for pair in range(HEADS // 2):
        queries = qkv[rows, pl.ds(pair * PAIR, PAIR)]
        keys = qkv[rows, pl.ds(INNER + pair * PAIR, PAIR)]
        values = qkv[rows, pl.ds(2 * INNER + pair * PAIR, PAIR)]
        halves = []
        for mine in (low, ~low):
            own = jnp.where(mine, queries, jnp.zeros_like(queries))
            scores = lax.dot_general(own, keys, (((1,), (1,)), ((), ())), preferred_element_type=F32)
            if same is not None:
                scores = jnp.where(same, scores, -1e30)
            exponent = jnp.exp(scores - jnp.max(scores, axis=-1, keepdims=True))
            weights = exponent * (1.0 / jnp.sum(exponent, axis=-1, keepdims=True))
            halves.append(jnp.dot(weights.astype(BF16), values, preferred_element_type=F32))
        outs.append(jnp.where(low, halves[0], halves[1]))
    return jnp.concatenate(outs, axis=1)


def project(product, store):
    for piece in range(3 * INNER // 256):
        columns = pl.ds(piece * 256, 256)
        value = product(columns)
        if piece < INNER // 256:
            value = value * HEAD**-0.5
        store(columns, value)


def run(copies):
    for copy in copies:
        copy.start()
    return copies


def wait(copies):
    for copy in copies:
        copy.wait()


def pack_kernel(qkv, out, packed, sems):
    depth, width = qkv.shape
    half = out.shape[1] // 2
    copies = [pltpu.make_async_copy(qkv, packed.at[:, pl.ds(0, width)], sems.at[0])]
    for side in range(2):
        piece = out.at[:, pl.ds(side * half, half)]
        target = packed.at[pl.ds(side * depth // 2, depth // 2), pl.ds(width, half)]
        copies.append(pltpu.make_async_copy(piece, target, sems.at[1 + side]))
    wait(run(copies))


def place_kernel(here, *refs):
    pieces, placed, sems = refs[:-2], refs[-2], refs[-1]
    copies = []
    for side, piece in enumerate(pieces):
        target = placed.at[:, (here[1] + side // 2) % 2, (here[2] + side % 2) % 2]
        copies.append(pltpu.make_async_copy(piece, target, sems.at[side]))
    wait(run(copies))


def norm_kernel(tokens, gain, normed):
    normed[...] = norm_rows(tokens[...].astype(F32), gain[...]).astype(BF16)


def fetches(gathered, weights, sems):
    copies = []
    for piece in range(3 * INNER // 256):
        columns = pl.ds(piece * 256, 256)
        copies.append(pltpu.make_async_copy(gathered.at[:, :, columns], weights.at[:, :, columns], sems.at[piece]))
    return run(copies)


def multiplied(normed, weights, copies):
    def product(columns):
        copies[columns.start // 256].wait()
        weight = weights[:, :, columns].reshape(normed.shape[1], 256)
        return jnp.dot(normed, weight, preferred_element_type=F32)

    return product


def out_halves(packed):
    parts, twice, width = packed.shape
    half = twice // 2
    return [packed[:, side * half : (side + 1) * half].reshape(parts * half, width) for side in range(2)]


def spatial_kernel(normed, first, context, weights, qkv, sems):
    copies = fetches(first, weights, sems)

    def store(columns, value):
        qkv[:, columns] = value.astype(BF16)

    project(multiplied(normed[...], weights, copies), store)
    for clip in range(context.shape[0] // ROWS):
        rows = pl.ds(clip * ROWS, ROWS)
        context[rows, :] = attend(qkv, rows, None).astype(BF16)


def middle_kernel(tokens, context, second, middle, out_ref, sems):
    wait(run([pltpu.make_async_copy(second.at[:, :, pl.ds(3 * INNER, INNER)], out_ref, sems.at[0])]))
    for side, weight in enumerate(out_halves(out_ref[...])):
        columns = pl.ds(side * INNER, INNER)
        added = jnp.dot(context[...], weight, preferred_element_type=F32)
        middle[:, columns] = (tokens[:, columns].astype(F32) + added).astype(BF16)


def temporal_kernel(frames, tokens, arrived, gain, second, context, out_ref, weights, qkv, sems, out_sem):
    out_copy = run([pltpu.make_async_copy(second.at[:, :, pl.ds(3 * INNER, INNER)], out_ref, out_sem.at[0])])
    copies = fetches(second, weights, sems)
    wait(out_copy)
    added = [jnp.dot(arrived[...], weight, preferred_element_type=F32) for weight in out_halves(out_ref[...])]
    middle = (tokens[...].astype(F32) + jnp.concatenate(added, axis=1)).astype(BF16)
    normed = norm_rows(middle.astype(F32), gain[...]).astype(BF16)
    rows = middle.shape[0]
    places = rows // frames

    def store(columns, value):
        split = value.reshape(frames, places, value.shape[1])
        for group in range(places // GROUP):
            own = split[:, group * GROUP : (group + 1) * GROUP].reshape(ROWS, value.shape[1])
            qkv[pl.ds(group * ROWS, ROWS), columns] = own.astype(BF16)

    project(multiplied(normed, weights, copies), store)
    place = lax.broadcasted_iota(jnp.int32, (ROWS, ROWS), 0) % GROUP
    same = place == lax.broadcasted_iota(jnp.int32, (ROWS, ROWS), 1) % GROUP
    outs = []
    for group in range(places // GROUP):
        out = attend(qkv, pl.ds(group * ROWS, ROWS), same)
        outs.append(out.reshape(frames, GROUP, INNER))
    context[...] = jnp.concatenate(outs, axis=1).reshape(rows, INNER).astype(BF16)


def kernel_call(body, kinds, out, operands, scratch=(), gflops=0, mib=4, room=24):
    near = pl.BlockSpec(memory_space=pltpu.VMEM)
    specs = {"s": pl.BlockSpec(memory_space=pltpu.SMEM), "v": near, "h": pl.BlockSpec(memory_space=pl.ANY)}
    return pl.pallas_call(
        body,
        out_shape=out,
        in_specs=[specs[kind] for kind in kinds],
        out_specs=jax.tree.map(lambda _: near, out),
        scratch_shapes=scratch,
        compiler_params=pltpu.CompilerParams(vmem_limit_bytes=room * MIB),
        cost_estimate=pl.CostEstimate(flops=int(gflops * 1e9), bytes_accessed=mib * MIB, transcendentals=0),
    )(*operands)


def moved(array, change):
    pairs = []
    for index in range(lax.axis_size("fsdp")):
        x, yl, core = change(index // 4, index // 2 % 2, index % 2)
        pairs.append((index, (x * 2 + yl) * 2 + core))
    return lax.ppermute(array, "fsdp", pairs)


def along_x(shard):
    lines = [list(range(start, 16, 4)) for start in range(4)]
    return lax.all_gather(shard, "fsdp", axis_index_groups=lines)


def shards(tokens, spatial_gain, spatial_qkv, spatial_out, temporal_gain, temporal_qkv, temporal_out):
    clips, _, places, depth = tokens.shape
    frames = lax.axis_size("tm")
    members = lax.axis_size("fsdp")
    part = depth // members
    index = lax.axis_index("fsdp")
    here = jnp.stack([index // 4, index // 2 % 2, index % 2]).astype(jnp.int32)
    rows = clips * places
    block = rows // frames
    flat = tokens.reshape(rows, depth)
    shape = jax.ShapeDtypeStruct
    tied = lax.optimization_barrier
    qkv_room = [
        pltpu.VMEM((members, part, 3 * INNER), BF16),
        pltpu.VMEM((rows, 3 * INNER), BF16),
        pltpu.SemaphoreType.DMA((3 * INNER // 256,)),
    ]
    out_room = pltpu.VMEM((members, part, INNER), BF16)
    one = pltpu.SemaphoreType.DMA((1,))

    def exchanged(array):
        sent = array.reshape(frames, block, array.shape[1])
        return lax.all_to_all(sent, "tm", split_axis=0, concat_axis=0, tiled=True).reshape(array.shape)

    def gathered(shard):
        return lax.all_gather(shard, "fsdp", axis=0, tiled=False)

    first = gathered(spatial_qkv)
    early = exchanged(flat)
    normed = kernel_call(norm_kernel, "vv", shape((rows, depth), BF16), (flat, spatial_gain.reshape(1, depth)))
    packed = kernel_call(
        pack_kernel,
        "hh",
        shape((part, 4 * INNER), BF16),
        (temporal_qkv, spatial_out),
        [pltpu.SemaphoreType.DMA((3,))],
        room=60,
    )
    second = gathered(packed)
    own = along_x(temporal_out)
    beside = moved(own, lambda x, yl, core: (x, 1 - yl, core))
    swapped = moved(jnp.stack([own, beside]), lambda x, yl, core: (x, yl, 1 - core))
    third = kernel_call(
        place_kernel,
        "shhhh",
        shape((4, 2, 2, INNER // members, depth), BF16),
        (here, own, swapped[0], beside, swapped[1]),
        [pltpu.SemaphoreType.DMA((4,))],
    )
    context = kernel_call(
        spatial_kernel, "vh", shape((rows, INNER), BF16), (normed, first), qkv_room, gflops=3, room=50
    )
    context, early, third = tied((context, early, third))
    arrived = exchanged(context)
    context_t = kernel_call(
        functools.partial(temporal_kernel, frames),
        "vvvh",
        shape((rows, INNER), BF16),
        (early, arrived, temporal_gain.reshape(1, depth), second),
        [out_room, *qkv_room, one],
        gflops=4,
        room=50,
    )
    context, context_t = tied((context, context_t))
    returned = exchanged(context_t)
    middle = kernel_call(
        middle_kernel, "vvh", shape((rows, depth), BF16), (flat, context, second), [out_room, one], gflops=1
    )
    encoded = middle.astype(F32) + jnp.dot(returned, third.reshape(INNER, depth), preferred_element_type=F32)
    return encoded.astype(BF16).reshape(tokens.shape)


def solution(mesh):
    placed = (
        P("fsdp", "tm", None, None),
        P(),
        P("fsdp", None),
        P("fsdp", None),
        P(),
        P("fsdp", None),
        P("fsdp", None),
    )
    return jax.shard_map(
        shards, mesh=mesh, in_specs=placed, out_specs=P("fsdp", "tm", None, None), check_vma=False
    )
```

time: 190 us -> 184 us (0.968)
  the two profiles are of different devices: /device:TPU:35 before, /device:TPU:32 now
where the time goes in v8:
time: 184 us; the launch traced here: 183 us
  waiting for transfers between devices  92.3 us (50%)
  starting transfers between devices  33.2 us (18%)
  Pallas kernels  23.4 us (13%)
  between operations  13.7 us (7%)
  blocking collectives  12.8 us (7%)
  local copies, waits for them, and re-layouts  4.28 us (2%)
  matrix products  2.73 us (1%)
    all_to_all x3, waiting for transfers between devices, exchanged(): lax.all_to_all(sent, 'tm', split_axis=0, concat_axis=0, tiled=True)  48.7 us
    all_to_all x3, starting transfers between devices, exchanged(): lax.all_to_all(sent, 'tm', split_axis=0, concat_axis=0, tiled=True)  28.8 us
    all_gather x2, waiting for transfers between devices, gathered(): return lax.all_gather(shard, 'fsdp', axis=0, tiled=False)  24.7 us
    pallas_call x6, Pallas kernels, kernel_call(): pl.pallas_call(body, out_shape=out, in_specs=[specs[kind] for kind in kin...  23.4 us
    ppermute x2, waiting for transfers between devices, moved(): return lax.ppermute(array, 'fsdp', pairs)  18.2 us
    all_gather x1, blocking collectives, along_x(): return lax.all_gather(shard, 'fsdp', axis_index_groups=lines)  12.8 us
    ppermute x2, starting transfers between devices, moved(): return lax.ppermute(array, 'fsdp', pairs)  4.31 us
    unnamed x20, local copies, waits for them, and re-layouts  4.24 us
  transfers between devices with their start and end apart: 7, of which 6 were waited for; matrix products, arithmetic and copies ran while one was open for 1% of the time, Pallas kernels for 7%

profile of v8, /device:TPU:32, one launch (start us, length us, event | category | flops | bytes accessed | tf_op | source)
XLA Modules:
  0.0 183.3 jit_solution(15994055658665252147)
XLA Ops:
  6.5 0.7 all-gather.6.cloned.1.call-update
  7.3 1.8 shard_map.76
  9.2 18.0 %all-to-all-start = ((bf16[32,16,1024]{2,1,0:T(8,128)(2,1)}), bf16[32,16,1024]{2,1,0:T(8,128)(2,1)S(1)}, u32[]{:S(2)}, u32[]{:S(2)}) async-start(bf16[32,16,1024]{2,1,0:T(8,128)(2,1)} %bitcast.27), calls=%async_computation | async-start | bytes 2097152 | tf_op jit(solution)/shard_map/all_to_all | solution.py:209
  27.2 12.8 %all-gather.1 = bf16[128,1024]{1,0:T(8,128)(2,1)S(1)} all-gather(bf16[32,1024]{1,0:T(8,128)(2,1)S(1)} %copy-done.9), channel_id=3, replica_groups={{0,128,256,384},{32,160,288,416},{64,192,320,448},{96,224,352,480},{1,1..., dimensions={0}, use_global_device_ids=true | all-gather | bytes 327680 | tf_op jit(solution)/shard_map/all_gather | solution.py:184
  40.0 2.4 %collective-permute-start = (bf16[4,32,1024]{2,1,0:T(8,128)(2,1)S(1)}, bf16[4,32,1024]{2,1,0:T(8,128)(2,1)S(1)}, u32[]{:S(2)}, u32[]{:S(2)}) collective-permute-start(bf16[4,32,1024]{2,1,0:T(8,128)(2,1)S(1)} %bitcast.32), channel_id=1, source_target_pairs={{0,64},{32,96},{64,0},{96,32},{128,192},{160,224},{192,128},{224,1... | collective-permute-start | bytes 786440 | tf_op jit(solution)/shard_map/ppermute | solution.py:179
  42.4 17.0 %collective-permute-done.refs_2_ = bf16[4,32,1024]{2,1,0:T(8,128)(2,1)S(1)} collective-permute-done((bf16[4,32,1024]{2,1,0:T(8,128)(2,1)S(1)}, bf16[4,32,1024]{2,1,0:T(8,128)(2,1)S(1)}, u32[]{:S(2)}, u32[]{:S(2)}) %collective-permute-start) | collective-permute-done | bytes 262176 | tf_op jit(solution)/shard_map/ppermute | solution.py:179
  59.4 0.9 pad_maximum_fusion
  60.3 1.9 %collective-permute-start.1 = (bf16[2,4,32,1024]{3,2,1,0:T(8,128)(2,1)}, bf16[2,4,32,1024]{3,2,1,0:T(8,128)(2,1)S(1)}, u32[]{:S(2)}, u32[]{:S(2)}) collective-permute-start(bf16[2,4,32,1024]{3,2,1,0:T(8,128)(2,1)} %pad_maximum_fusion), channel_id=1, source_target_pairs={{0,32},{32,0},{64,96},{96,64},{128,160},{160,128},{192,224},{224,1... | collective-permute-start | bytes 1572872 | tf_op jit(solution)/shard_map/ppermute | solution.py:179
  62.3 0.7 shard_map.73.normed
  63.1 1.2 collective-permute-done.1
  64.4 0.7 shard_map.75
  65.1 1.2 copy-done.3
  66.3 7.9 %shard_map.74.context = bf16[512,512]{1,0:T(8,128)(2,1)} custom-call(bf16[512,1024]{1,0:T(8,128)(2,1)S(1)} %copy-done.3, bf16[16,64,1536]{2,1,0:T(8,128)(2,1)} %bitcast.41), custom_call_target="tpu_custom_call" | custom-call | flops 3000000000 | bytes 4194304 | tf_op jit(solution)/shard_map/pallas_call | solution.py:163
  74.2 8.9 %all-to-all-done = bf16[32,16,1024]{2,1,0:T(8,128)(2,1)S(1)} async-done(((bf16[32,16,1024]{2,1,0:T(8,128)(2,1)}), bf16[32,16,1024]{2,1,0:T(8,128)(2,1)S(1)}, u32[]{:S(2)}, u32[]{:S(2)}) %all-to-all-start) | async-done | bytes 1048608 | tf_op jit(solution)/shard_map/all_to_all | solution.py:209
  83.1 4.7 %all-to-all-start.1 = ((bf16[32,16,512]{2,1,0:T(8,128)(2,1)}), bf16[32,16,512]{2,1,0:T(8,128)(2,1)}, u32[]{:S(2)}, u32[]{:S(2)}) async-start(bf16[32,16,512]{2,1,0:T(8,128)(2,1)} %bitcast.13), calls=%async_computation.1 | async-start | bytes 1048576 | tf_op jit(solution)/shard_map/all_to_all | solution.py:209
  87.8 24.7 %all-gather.8.cloned.1.call-done = bf16[1024,2048]{1,0:T(8,128)(2,1)} async-done(((bf16[64,2048]{1,0:T(8,128)(2,1)}), bf16[1024,2048]{1,0:T(8,128)(2,1)}) %all-gather.8.cloned.1.call-update) | async-done | bytes 4194320 | tf_op jit(solution)/shard_map/all_gather | solution.py:212
  112.5 9.5 %all-to-all-done.1 = bf16[32,16,512]{2,1,0:T(8,128)(2,1)} async-done(((bf16[32,16,512]{2,1,0:T(8,128)(2,1)}), bf16[32,16,512]{2,1,0:T(8,128)(2,1)}, u32[]{:S(2)}, u32[]{:S(2)}) %all-to-all-start.1) | async-done | bytes 524320 | tf_op jit(solution)/shard_map/all_to_all | solution.py:209
  122.0 10.4 %shard_map.77 = bf16[512,512]{1,0:T(8,128)(2,1)S(1)} custom-call(bf16[512,1024]{1,0:T(8,128)(2,1)S(1)} %bitcast.36, bf16[512,512]{1,0:T(8,128)(2,1)} %bitcast.14.arrived, f32[1,1024]{1,0:T(1,128)S(1)} %bitcast.40, bf16[16,64,2048]{2,1,0:T(8,128)(2,1)} %bitcast.30), custom_call_target="tpu_custom_call" | custom-call | flops 4000000000 | bytes 4194304 | tf_op jit(solution)/shard_map/pallas_call | solution.py:163
  132.5 0.8 copy-done.6
  133.3 6.1 %all-to-all-start.2 = ((bf16[32,16,512]{2,1,0:T(8,128)(2,1)}), bf16[32,16,512]{2,1,0:T(8,128)(2,1)}, u32[]{:S(2)}, u32[]{:S(2)}) async-start(bf16[32,16,512]{2,1,0:T(8,128)(2,1)} %bitcast.38), calls=%async_computation.2 | async-start | bytes 1048576 | tf_op jit(solution)/shard_map/all_to_all | solution.py:209
  139.4 2.2 %copy-done.1 = bf16[1024,2048]{1,0:T(8,128)(2,1)S(1)} copy-done((bf16[1024,2048]{1,0:T(8,128)(2,1)S(1)}, bf16[1024,2048]{1,0:T(8,128)(2,1)}, u32[]{:S(2)}) %copy-start.1) | copy-done | bytes 4194328
  141.6 1.9 %shard_map.78 = bf16[512,1024]{1,0:T(8,128)(2,1)S(1)} custom-call(bf16[512,1024]{1,0:T(8,128)(2,1)S(1)} %bitcast.29, bf16[512,512]{1,0:T(8,128)(2,1)} %shard_map.74.context, bf16[16,64,2048]{2,1,0:T(8,128)(2,1)S(1)} %bitcast.31), custom_call_target="tpu_custom_call" | custom-call | flops 1000000000 | bytes 4194304 | tf_op jit(solution)/shard_map/pallas_call | solution.py:163
  143.5 30.2 %all-to-all-done.2 = bf16[32,16,512]{2,1,0:T(8,128)(2,1)} async-done(((bf16[32,16,512]{2,1,0:T(8,128)(2,1)}), bf16[32,16,512]{2,1,0:T(8,128)(2,1)}, u32[]{:S(2)}, u32[]{:S(2)}) %all-to-all-start.2) | async-done | bytes 524320 | tf_op jit(solution)/shard_map/all_to_all | solution.py:209
  173.7 2.7 %add_convert_fusion = bf16[512,1024]{1,0:T(8,128)(2,1)} fusion(bf16[512,1024]{1,0:T(8,128)(2,1)S(1)} %shard_map.78, bf16[512,512]{1,0:T(8,128)(2,1)} %bitcast.18, bf16[512,1024]{1,0:T(8,128)(2,1)S(1)} %bitcast.35), kind=kOutput, calls=%fused_computation | convolution fusion | flops 538443776 | bytes 3670016 | tf_op jit(solution)/shard_map/dot_general | solution.py:255
  (23 shorter events, 0.2 us)
Async XLA Ops:
  6.5 20.6 %copy-start.9 = (bf16[32,1024]{1,0:T(8,128)(2,1)S(1)}, bf16[32,1024]{1,0:T(8,128)(2,1)}, u32[]{:S(2)}) copy-start(bf16[32,1024]{1,0:T(8,128)(2,1)} %param.13) | copy-start | bytes 196612
  6.5 58.5 %all-gather.6.cloned.1.call-start = ((), (), s32[]{:S(2)}) async-start(), calls=%async_computation.3 | async-start | bytes 3342336 | tf_op jit(solution)/shard_map/all_gather | solution.py:212
  7.3 55.0 %copy-start = (bf16[2,1,256,1024]{3,2,1,0:T(8,128)(2,1)S(1)}, bf16[2,1,256,1024]{3,2,1,0:T(8,128)(2,1)}, u32[]{:S(2)}) copy-start(bf16[2,1,256,1024]{3,2,1,0:T(8,128)(2,1)} %param.7) | copy-start | bytes 3145732
  7.3 55.0 %copy-start.7 = (f32[1024]{0:T(1024)S(1)}, f32[1024]{0:T(1024)}, u32[]{:S(2)}) copy-start(f32[1024]{0:T(1024)} %param.8) | copy-start | bytes 12292
  7.3 105.2 %all-gather.8.cloned.1.call-start = ((), (), s32[]{:S(2)}) async-start(), calls=%async_computation.4 | async-start | bytes 4456448 | tf_op jit(solution)/shard_map/all_gather | solution.py:212
  9.2 74.0 %all-to-all-start = ((bf16[32,16,1024]{2,1,0:T(8,128)(2,1)}), bf16[32,16,1024]{2,1,0:T(8,128)(2,1)S(1)}, u32[]{:S(2)}, u32[]{:S(2)}) async-start(bf16[32,16,1024]{2,1,0:T(8,128)(2,1)} %bitcast.27), calls=%async_computation | async-start | bytes 2097152 | tf_op jit(solution)/shard_map/all_to_all | solution.py:209
  40.0 19.4 %collective-permute-start = (bf16[4,32,1024]{2,1,0:T(8,128)(2,1)S(1)}, bf16[4,32,1024]{2,1,0:T(8,128)(2,1)S(1)}, u32[]{:S(2)}, u32[]{:S(2)}) collective-permute-start(bf16[4,32,1024]{2,1,0:T(8,128)(2,1)S(1)} %bitcast.32), channel_id=1, source_target_pairs={{0,64},{32,96},{64,0},{96,32},{128,192},{160,224},{192,128},{224,1... | collective-permute-start | bytes 786440 | tf_op jit(solution)/shard_map/ppermute | solution.py:179
  59.4 2.9 %copy-start.4 = (bf16[4,32,1024]{2,1,0:T(8,128)(2,1)}, bf16[4,32,1024]{2,1,0:T(8,128)(2,1)S(1)}, u32[]{:S(2)}) copy-start(bf16[4,32,1024]{2,1,0:T(8,128)(2,1)S(1)} %collective-permute-done.refs_2_) | copy-start | bytes 786436
  60.3 4.0 %collective-permute-start.1 = (bf16[2,4,32,1024]{3,2,1,0:T(8,128)(2,1)}, bf16[2,4,32,1024]{3,2,1,0:T(8,128)(2,1)S(1)}, u32[]{:S(2)}, u32[]{:S(2)}) collective-permute-start(bf16[2,4,32,1024]{3,2,1,0:T(8,128)(2,1)} %pad_maximum_fusion), channel_id=1, source_target_pairs={{0,32},{32,0},{64,96},{96,64},{128,160},{160,128},{192,224},{224,1... | collective-permute-start | bytes 1572872 | tf_op jit(solution)/shard_map/ppermute | solution.py:179
  62.3 2.1 %copy-start.5 = (bf16[4,32,1024]{2,1,0:T(8,128)(2,1)S(1)}, bf16[4,32,1024]{2,1,0:T(8,128)(2,1)}, u32[]{:S(2)}) copy-start(bf16[4,32,1024]{2,1,0:T(8,128)(2,1)} %copy-done.4) | copy-start | bytes 786436
  63.0 1.4 copy-start.2
  65.1 1.2 copy-start.3
  66.3 55.7 %copy-start.8 = (f32[1024]{0:T(1024)S(1)}, f32[1024]{0:T(1024)}, u32[]{:S(2)}) copy-start(f32[1024]{0:T(1024)} %param.11) | copy-start | bytes 12292
  83.1 38.9 %all-to-all-start.1 = ((bf16[32,16,512]{2,1,0:T(8,128)(2,1)}), bf16[32,16,512]{2,1,0:T(8,128)(2,1)}, u32[]{:S(2)}, u32[]{:S(2)}) async-start(bf16[32,16,512]{2,1,0:T(8,128)(2,1)} %bitcast.13), calls=%async_computation.1 | async-start | bytes 1048576 | tf_op jit(solution)/shard_map/all_to_all | solution.py:209
  132.5 0.8 copy-start.6
  133.3 40.5 %all-to-all-start.2 = ((bf16[32,16,512]{2,1,0:T(8,128)(2,1)}), bf16[32,16,512]{2,1,0:T(8,128)(2,1)}, u32[]{:S(2)}, u32[]{:S(2)}) async-start(bf16[32,16,512]{2,1,0:T(8,128)(2,1)} %bitcast.38), calls=%async_computation.2 | async-start | bytes 1048576 | tf_op jit(solution)/shard_map/all_to_all | solution.py:209
  139.4 2.2 %copy-start.1 = (bf16[1024,2048]{1,0:T(8,128)(2,1)S(1)}, bf16[1024,2048]{1,0:T(8,128)(2,1)}, u32[]{:S(2)}) copy-start(bf16[1024,2048]{1,0:T(8,128)(2,1)} %all-gather.8.cloned.1.call-done) | copy-start | bytes 12582916
Sparse Core Ops, SparseCore 0:
  9.5 54.5 all-gather.5
  66.3 46.2 all-gather.7

commit v9 on v4

--- a/solution.py
+++ b/solution.py
@@ -126,17 +126,17 @@
         middle[:, columns] = (tokens[:, columns].astype(F32) + added).astype(BF16)
 
 
-def fetches(here, mine, other, placed, sems):
+def place_kernel(here, *refs):
+    pieces, placed, sems = refs[:-2], refs[-2], refs[-1]
     copies = []
-    for side, source in enumerate((mine, other)):
-        for beside in range(2):
-            target = placed.at[:, (here[1] + beside) % 2, (here[2] + side) % 2]
-            copies.append(pltpu.make_async_copy(source.at[beside], target, sems.at[side, beside]))
-    return run(copies)
-
-
-def place_kernel(here, mine, other, placed, sems):
-    wait(fetches(here, mine, other, placed, sems))
+    for side, piece in enumerate(pieces):
+        target = placed.at[:, (here[1] + side // 2) % 2, (here[2] + side % 2) % 2]
+        copies.append(pltpu.make_async_copy(piece, target, sems.at[side]))
+    wait(run(copies))
+
+
+def copy_kernel(source, target):
+    target[...] = source[...]
 
 
 def temporal_kernel(frames, middle, gain, placed, context, qkv):
@@ -164,7 +164,7 @@
     context[...] = jnp.concatenate(outs, axis=1).reshape(rows, INNER).astype(BF16)
 
 
-def kernel_call(body, kinds, out, operands, scratch=(), gflops=0, mib=4):
+def kernel_call(body, kinds, out, operands, scratch=(), gflops=0, mib=4, room=24):
     near = pl.BlockSpec(memory_space=pltpu.VMEM)
     specs = {"s": pl.BlockSpec(memory_space=pltpu.SMEM), "v": near, "h": pl.BlockSpec(memory_space=pl.ANY)}
     return pl.pallas_call(
@@ -173,7 +173,7 @@
         in_specs=[specs[kind] for kind in kinds],
         out_specs=jax.tree.map(lambda _: near, out),
         scratch_shapes=scratch,
-        compiler_params=pltpu.CompilerParams(vmem_limit_bytes=24 * MIB),
+        compiler_params=pltpu.CompilerParams(vmem_limit_bytes=room * MIB),
         cost_estimate=pl.CostEstimate(flops=int(gflops * 1e9), bytes_accessed=mib * MIB, transcendentals=0),
     )(*operands)
 
@@ -190,11 +190,22 @@
     return moved(array, lambda x, yl, core: (x, yl, 1 - core))
 
 
+def other_yl(array):
+    members, frames = lax.axis_size("fsdp"), lax.axis_size("tm")
+    half = array.shape[0] // 2
+    pieces = []
+    for turn, piece in enumerate((array[:half], array[half:])):
+        pairs = []
+        for source in range(members * frames):
+            member, frame = source // frames, source % frames
+            pairs.append((source, (member ^ 2) * frames + (frame + turn * frames // 2) % frames))
+        pieces.append(lax.ppermute(piece, ("fsdp", "tm"), pairs))
+    return jnp.concatenate(pieces, axis=0)
+
+
 def along_x(shard):
     lines = [list(range(start, 16, 4)) for start in range(4)]
-    own = lax.all_gather(shard, "fsdp", axis_index_groups=lines)
-    mine = jnp.stack([own, moved(own, lambda x, yl, core: (x, 1 - yl, core))])
-    return mine, other_core(mine)
+    return lax.all_gather(shard, "fsdp", axis_index_groups=lines)
 
 
 def shards(tokens, spatial_gain, spatial_qkv, spatial_out, temporal_gain, temporal_qkv, temporal_out):
@@ -214,16 +225,18 @@
         sent = array.reshape(frames, block, array.shape[1])
         return lax.all_to_all(sent, "tm", split_axis=0, concat_axis=0, tiled=True).reshape(array.shape)
 
-    def in_order(shard):
+    def in_order(*pieces):
         return kernel_call(
             place_kernel,
-            "shh",
-            shape((4, 2, 2, *shard.shape), BF16),
-            (here, *along_x(shard)),
-            [pltpu.SemaphoreType.DMA((2, 2))],
+            "s" + "h" * 4,
+            shape((4, 2, 2, *pieces[0].shape[1:]), BF16),
+            (here, *pieces),
+            [pltpu.SemaphoreType.DMA((4,))],
         )
 
-    packed = kernel_call(pack_kernel, "vv", shape((parts, part, 4 * INNER), BF16), (spatial_qkv, spatial_out))
+    packed = kernel_call(
+        pack_kernel, "vv", shape((parts, part, 4 * INNER), BF16), (spatial_qkv, spatial_out), room=60
+    )
     mine = lax.all_to_all(packed, "fsdp", 0, 0, axis_index_groups=cores, tiled=True)
     normed, normed_other = kernel_call(
         norm_kernel,
@@ -232,7 +245,6 @@
         (here, flat, spatial_gain.reshape(1, depth)),
         gflops=2,
     )
-    mine, normed, normed_other = lax.optimization_barrier((mine, normed, normed_other))
     partial = kernel_call(half_kernel, "vv", shape((rows, 3 * INNER), F32), (normed, mine), gflops=1)
     middle = kernel_call(
         spatial_kernel,
@@ -249,18 +261,25 @@
     )
     shard, middle = lax.optimization_barrier((temporal_qkv, middle))
     arrived = exchanged(middle)
+    own = along_x(shard)
+    beside = other_yl(own)
+    placed = in_order(own, other_core(own), beside, other_core(beside))
     context = kernel_call(
         functools.partial(temporal_kernel, frames),
         "vvv",
         shape((rows, INNER), BF16),
-        (arrived, temporal_gain.reshape(1, depth), in_order(shard)),
+        (arrived, temporal_gain.reshape(1, depth), placed),
         [pltpu.VMEM((rows, 3 * INNER), BF16)],
         gflops=4,
     )
-    shard, context = lax.optimization_barrier((temporal_out, context))
+    shard, middle, context = lax.optimization_barrier((temporal_out, middle, context))
     returned = exchanged(context)
-    weight = in_order(shard).reshape(INNER, depth)
-    encoded = middle.astype(F32) + jnp.dot(returned, weight, preferred_element_type=F32)
+    own = along_x(shard)
+    beside = moved(own, lambda x, yl, core: (x, 1 - yl, core))
+    swapped = other_core(jnp.stack([own, beside]))
+    weight = in_order(own, swapped[0], beside, swapped[1]).reshape(INNER, depth)
+    kept = kernel_call(copy_kernel, "v", shape((rows, depth), BF16), (middle,))
+    encoded = kept.astype(F32) + jnp.dot(returned, weight, preferred_element_type=F32)
     return encoded.astype(BF16).reshape(tokens.shape)
 
 

time: 174 us -> 169 us (0.971)
  waiting for transfers between devices: 83.4 us -> 45.2 us
  blocking collectives: 26.8 us -> 58.5 us
  local copies, waits for them, and re-layouts: 4.61 us -> 0.96 us
  Pallas kernels: 17.7 us -> 20.9 us
  starting transfers between devices: 37.7 us -> 40.3 us
    all_to_all x0 -> x1, blocking collectives: none -> 32.1 us  [shards(): lax.all_to_all(packed, 'fsdp', 0, 0, axis_index_groups=cores, tiled=True)]
    all_to_all x1 -> x0, waiting for transfers between devices: 26.7 us -> none  [shards(): lax.all_to_all(packed, 'fsdp', 0, 0, axis_index_groups=cores, tiled=True)]
    ppermute x5, waiting for transfers between devices: 36.5 us -> 10.2 us  [moved(): return lax.ppermute(array, 'fsdp', pairs)]
    all_to_all x2, waiting for transfers between devices: 20.2 us -> 28.2 us  [exchanged(): lax.all_to_all(sent, 'tm', split_axis=0, concat_axis=0, tiled=True)]
    ppermute x0 -> x2, starting transfers between devices: none -> 7.36 us  [other_yl(): pieces.append(lax.ppermute(piece, ('fsdp', 'tm'), pairs))]
    ppermute x0 -> x2, waiting for transfers between devices: none -> 6.72 us  [other_yl(): pieces.append(lax.ppermute(piece, ('fsdp', 'tm'), pairs))]
    all_to_all x1 -> x0, starting transfers between devices: 5.44 us -> none  [shards(): lax.all_to_all(packed, 'fsdp', 0, 0, axis_index_groups=cores, tiled=True)]
    unnamed x22 -> x13, local copies, waits for them, and re-layouts: 4.61 us -> 0.84 us
  transfers between devices with their start and end apart: 8 -> 9, of which waited for: 8 -> 8; matrix products, arithmetic and copies ran while one was open for 0% -> 0% of each run, Pallas kernels for 3% -> 4%
where the time goes in v9:
time: 169 us; the launch traced here: 168 us
  blocking collectives  58.5 us (35%)
  waiting for transfers between devices  45.2 us (27%)
  starting transfers between devices  40.3 us (24%)
  Pallas kernels  20.9 us (12%)
  matrix products  1.69 us (1%)
    all_to_all x1, blocking collectives, shards(): lax.all_to_all(packed, 'fsdp', 0, 0, axis_index_groups=cores, tiled=True)  32.1 us
    all_to_all x2, waiting for transfers between devices, exchanged(): lax.all_to_all(sent, 'tm', split_axis=0, concat_axis=0, tiled=True)  28.2 us
    all_gather x2, blocking collectives, along_x(): return lax.all_gather(shard, 'fsdp', axis_index_groups=lines)  26.4 us
    all_to_all x2, starting transfers between devices, exchanged(): lax.all_to_all(sent, 'tm', split_axis=0, concat_axis=0, tiled=True)  22.3 us
    pallas_call x8, Pallas kernels, kernel_call(): pl.pallas_call(body, out_shape=out, in_specs=[specs[kind] for kind in kin...  20.9 us
    ppermute x5, starting transfers between devices, moved(): return lax.ppermute(array, 'fsdp', pairs)  10.6 us
    ppermute x5, waiting for transfers between devices, moved(): return lax.ppermute(array, 'fsdp', pairs)  10.2 us
    ppermute x2, starting transfers between devices, other_yl(): pieces.append(lax.ppermute(piece, ('fsdp', 'tm'), pairs))  7.36 us
  transfers between devices with their start and end apart: 9, of which 8 were waited for; matrix products, arithmetic and copies ran while one was open for 0% of the time, Pallas kernels for 4%

profile of v9, /device:TPU:32, one launch (start us, length us, event | category | flops | bytes accessed | tf_op | source)
XLA Modules:
  0.0 167.9 jit_solution(13999013527330449453)
XLA Ops:
  0.0 2.4 %shard_map.74 = bf16[8,64,2048]{2,1,0:T(8,128)(2,1)} custom-call(bf16[64,1536]{1,0:T(8,128)(2,1)} %qkv.1, bf16[32,1024]{1,0:T(8,128)(2,1)} %out.1), custom_call_target="tpu_custom_call" | custom-call | bytes 4194304 | tf_op jit(solution)/shard_map/pallas_call | solution.py:170
  2.4 32.1 %all_to_all.15.weights.mine = bf16[8,64,2048]{2,1,0:T(8,128)(2,1)S(1)} all-to-all(bf16[8,64,2048]{2,1,0:T(8,128)(2,1)} %shard_map.74), channel_id=1, replica_groups={{0,64,128,192,256,320,384,448},{32,96,160,224,288,352,416,480},{1,65,12..., dimensions={0} | all-to-all | bytes 4194304 | tf_op jit(solution)/shard_map/all_to_all | solution.py:240
  34.5 1.9 %collective-permute-start = (bf16[8,64,2048]{2,1,0:T(8,128)(2,1)S(1)}, bf16[8,64,2048]{2,1,0:T(8,128)(2,1)}, u32[]{:S(2)}, u32[]{:S(2)}) collective-permute-start(bf16[8,64,2048]{2,1,0:T(8,128)(2,1)S(1)} %all_to_all.15.weights.mine), channel_id=1, source_target_pairs={{0,32},{32,0},{64,96},{96,64},{128,160},{160,128},{192,224},{224,1... | collective-permute-start | bytes 6291464 | tf_op jit(solution)/shard_map/ppermute | solution.py:186
  36.5 2.4 %shard_map.73 = (bf16[512,512]{1,0:T(8,128)(2,1)S(1)}, bf16[512,512]{1,0:T(8,128)(2,1)S(1)}) custom-call(s32[3]{0:T(128)S(1)} %pad_add_fusion.here, bf16[512,1024]{1,0:T(8,128)(2,1)S(1)} %bitcast.34, f32[1,1024]{1,0:T(1,128)S(1)} %bitcast.36), custom_call_target="tpu_custom_call" | custom-call | flops 2000000000 | bytes 4194304 | tf_op jit(solution)/shard_map/pallas_call | solution.py:170
  40.7 6.7 %shard_map.76.source = bf16[512,1024]{1,0:T(8,128)(2,1)} custom-call(s32[3]{0:T(128)S(1)} %pad_add_fusion.here, bf16[512,1024]{1,0:T(8,128)(2,1)S(1)} %bitcast.35, f32[512,1536]{1,0:T(8,128)S(1)} %shard_map.75.partial, bf16[512,512]{1,0:T(8,128)(2,1)S(1)} %get-tuple-element.13.normed, bf16[8,64,2048]{2,1,0:T(8,128)(2,1)S(1)} %all_to_all.15.weights.mine, ...), custom_call_target="tpu_custom_call" | custom-call | flops 3000000000 | bytes 4194304 | tf_op jit(solution)/shard_map/pallas_call | solution.py:170
  47.4 17.9 %all-to-all-start.1 = ((bf16[32,16,1024]{2,1,0:T(8,128)(2,1)}), bf16[32,16,1024]{2,1,0:T(8,128)(2,1)}, u32[]{:S(2)}, u32[]{:S(2)}) async-start(bf16[32,16,1024]{2,1,0:T(8,128)(2,1)} %bitcast.5), calls=%async_computation.1 | async-start | bytes 2097152 | tf_op jit(solution)/shard_map/all_to_all | solution.py:226
  65.3 14.0 %all-gather = bf16[256,1536]{1,0:T(8,128)(2,1)S(1)} all-gather(bf16[64,1536]{1,0:T(8,128)(2,1)S(1)} %copy-done.4), channel_id=2, replica_groups={{0,128,256,384},{32,160,288,416},{64,192,320,448},{96,224,352,480},{1,1..., dimensions={0}, use_global_device_ids=true | all-gather | bytes 983040 | tf_op jit(solution)/shard_map/all_gather | solution.py:208
  79.4 2.8 %collective-permute-start.2 = (bf16[2,64,1536]{2,1,0:T(8,128)(2,1)S(1)}, bf16[2,64,1536]{2,1,0:T(8,128)(2,1)S(1)}, u32[]{:S(2)}, u32[]{:S(2)}) collective-permute-start(bf16[2,64,1536]{2,1,0:T(8,128)(2,1)S(1)} %bitcast.40), channel_id=1, source_target_pairs={{0,64},{1,65},{2,66},{3,67},{4,68},{5,69},{6,70},{7,71},{8,72},{9,... | collective-permute-start | bytes 1179656 | tf_op jit(solution)/shard_map/ppermute | solution.py:202
  82.2 4.5 %collective-permute-start.3 = (bf16[2,64,1536]{2,1,0:T(8,128)(2,1)S(1)}, bf16[2,64,1536]{2,1,0:T(8,128)(2,1)S(1)}, u32[]{:S(2)}, u32[]{:S(2)}) collective-permute-start(bf16[2,64,1536]{2,1,0:T(8,128)(2,1)S(1)} %bitcast.39), channel_id=1, source_target_pairs={{0,80},{1,81},{2,82},{3,83},{4,84},{5,85},{6,86},{7,87},{8,88},{9,... | collective-permute-start | bytes 1179656 | tf_op jit(solution)/shard_map/ppermute | solution.py:202
  86.7 1.9 %collective-permute-start.1 = (bf16[4,64,1536]{2,1,0:T(8,128)(2,1)S(1)}, bf16[4,64,1536]{2,1,0:T(8,128)(2,1)S(1)}, u32[]{:S(2)}, u32[]{:S(2)}) collective-permute-start(bf16[4,64,1536]{2,1,0:T(8,128)(2,1)S(1)} %bitcast.26), channel_id=1, source_target_pairs={{0,32},{32,0},{64,96},{96,64},{128,160},{160,128},{192,224},{224,1... | collective-permute-start | bytes 2359304 | tf_op jit(solution)/shard_map/ppermute | solution.py:186
  88.7 3.0 %collective-permute-done.2 = bf16[2,64,1536]{2,1,0:T(8,128)(2,1)S(1)} collective-permute-done((bf16[2,64,1536]{2,1,0:T(8,128)(2,1)S(1)}, bf16[2,64,1536]{2,1,0:T(8,128)(2,1)S(1)}, u32[]{:S(2)}, u32[]{:S(2)}) %collective-permute-start.2) | collective-permute-done | bytes 393248 | tf_op jit(solution)/shard_map/ppermute | solution.py:202
  91.7 3.7 %collective-permute-done.3 = bf16[2,64,1536]{2,1,0:T(8,128)(2,1)S(1)} collective-permute-done((bf16[2,64,1536]{2,1,0:T(8,128)(2,1)S(1)}, bf16[2,64,1536]{2,1,0:T(8,128)(2,1)S(1)}, u32[]{:S(2)}, u32[]{:S(2)}) %collective-permute-start.3) | collective-permute-done | bytes 393248 | tf_op jit(solution)/shard_map/ppermute | solution.py:202
  95.4 1.9 %collective-permute-start.4 = (bf16[4,64,1536]{2,1,0:T(8,128)(2,1)S(1)}, bf16[4,64,1536]{2,1,0:T(8,128)(2,1)S(1)}, u32[]{:S(2)}, u32[]{:S(2)}) collective-permute-start(bf16[4,64,1536]{2,1,0:T(8,128)(2,1)S(1)} %constant_dynamic-update-slice_fusion.refs_2_), channel_id=1, source_target_pairs={{0,32},{32,0},{64,96},{96,64},{128,160},{160,128},{192,224},{224,1... | collective-permute-start | bytes 2359304 | tf_op jit(solution)/shard_map/ppermute | solution.py:186
  97.4 2.2 %collective-permute-done.4.refs_3_ = bf16[4,64,1536]{2,1,0:T(8,128)(2,1)S(1)} collective-permute-done((bf16[4,64,1536]{2,1,0:T(8,128)(2,1)S(1)}, bf16[4,64,1536]{2,1,0:T(8,128)(2,1)S(1)}, u32[]{:S(2)}, u32[]{:S(2)}) %collective-permute-start.4) | collective-permute-done | bytes 786464 | tf_op jit(solution)/shard_map/ppermute | solution.py:186
  100.5 21.1 %all-to-all-done.1 = bf16[32,16,1024]{2,1,0:T(8,128)(2,1)} async-done(((bf16[32,16,1024]{2,1,0:T(8,128)(2,1)}), bf16[32,16,1024]{2,1,0:T(8,128)(2,1)}, u32[]{:S(2)}, u32[]{:S(2)}) %all-to-all-start.1) | async-done | bytes 1048608 | tf_op jit(solution)/shard_map/all_to_all | solution.py:226
  121.6 5.7 %shard_map.78 = bf16[512,512]{1,0:T(8,128)(2,1)S(1)} custom-call(bf16[512,1024]{1,0:T(8,128)(2,1)} %bitcast.6.middle, f32[1,1024]{1,0:T(1,128)S(1)} %bitcast.37, bf16[4,2,2,64,1536]{4,3,2,1,0:T(8,128)(2,1)S(1)} %shard_map.77.placed), custom_call_target="tpu_custom_call" | custom-call | flops 4000000000 | bytes 4194304 | tf_op jit(solution)/shard_map/pallas_call | solution.py:170
  128.1 4.4 %all-to-all-start.2 = ((bf16[32,16,512]{2,1,0:T(8,128)(2,1)}), bf16[32,16,512]{2,1,0:T(8,128)(2,1)S(1)}, u32[]{:S(2)}, u32[]{:S(2)}) async-start(bf16[32,16,512]{2,1,0:T(8,128)(2,1)} %bitcast.33), calls=%async_computation.2 | async-start | bytes 1048576 | tf_op jit(solution)/shard_map/all_to_all | solution.py:226
  132.5 12.4 %all-gather.1 = bf16[128,1024]{1,0:T(8,128)(2,1)S(1)} all-gather(bf16[32,1024]{1,0:T(8,128)(2,1)S(1)} %copy-done.5), channel_id=3, replica_groups={{0,128,256,384},{32,160,288,416},{64,192,320,448},{96,224,352,480},{1,1..., dimensions={0}, use_global_device_ids=true | all-gather | bytes 327680 | tf_op jit(solution)/shard_map/all_gather | solution.py:208
  144.9 2.9 %collective-permute-start.5 = (bf16[4,32,1024]{2,1,0:T(8,128)(2,1)S(1)}, bf16[4,32,1024]{2,1,0:T(8,128)(2,1)S(1)}, u32[]{:S(2)}, u32[]{:S(2)}) collective-permute-start(bf16[4,32,1024]{2,1,0:T(8,128)(2,1)S(1)} %bitcast.28), channel_id=1, source_target_pairs={{0,64},{32,96},{64,0},{96,32},{128,192},{160,224},{192,128},{224,1... | collective-permute-start | bytes 786440 | tf_op jit(solution)/shard_map/ppermute | solution.py:186
  147.9 6.6 %collective-permute-done.5.refs_2_ = bf16[4,32,1024]{2,1,0:T(8,128)(2,1)S(1)} collective-permute-done((bf16[4,32,1024]{2,1,0:T(8,128)(2,1)S(1)}, bf16[4,32,1024]{2,1,0:T(8,128)(2,1)S(1)}, u32[]{:S(2)}, u32[]{:S(2)}) %collective-permute-start.5) | collective-permute-done | bytes 262176 | tf_op jit(solution)/shard_map/ppermute | solution.py:186
  154.5 1.9 %collective-permute-start.6 = (bf16[2,4,32,1024]{3,2,1,0:T(8,128)(2,1)S(1)}, bf16[2,4,32,1024]{3,2,1,0:T(8,128)(2,1)S(1)}, u32[]{:S(2)}, u32[]{:S(2)}) collective-permute-start(bf16[2,4,32,1024]{3,2,1,0:T(8,128)(2,1)S(1)} %pad_maximum_fusion), channel_id=1, source_target_pairs={{0,32},{32,0},{64,96},{96,64},{128,160},{160,128},{192,224},{224,1... | collective-permute-start | bytes 1572872 | tf_op jit(solution)/shard_map/ppermute | solution.py:186
  156.4 1.3 shard_map.79
  159.1 7.1 %all-to-all-done.2 = bf16[32,16,512]{2,1,0:T(8,128)(2,1)S(1)} async-done(((bf16[32,16,512]{2,1,0:T(8,128)(2,1)}), bf16[32,16,512]{2,1,0:T(8,128)(2,1)S(1)}, u32[]{:S(2)}, u32[]{:S(2)}) %all-to-all-start.2) | async-done | bytes 524320 | tf_op jit(solution)/shard_map/all_to_all | solution.py:226
  166.2 1.7 %add_convert_fusion = bf16[512,1024]{1,0:T(8,128)(2,1)} fusion(bf16[512,1024]{1,0:T(8,128)(2,1)S(1)} %shard_map.79, bf16[512,512]{1,0:T(8,128)(2,1)S(1)} %bitcast.38, bf16[512,1024]{1,0:T(8,128)(2,1)S(1)} %bitcast.31), kind=kOutput, calls=%fused_computation | convolution fusion | flops 538443776 | bytes 3670016 | tf_op jit(solution)/shard_map/dot_general | solution.py:282
  (24 shorter events, 4.9 us)
Async XLA Ops:
  2.4 34.1 %copy-start.1 = (bf16[2,1,256,1024]{3,2,1,0:T(8,128)(2,1)S(1)}, bf16[2,1,256,1024]{3,2,1,0:T(8,128)(2,1)}, u32[]{:S(2)}) copy-start(bf16[2,1,256,1024]{3,2,1,0:T(8,128)(2,1)} %param.7) | copy-start | bytes 3145732
  2.4 34.1 %copy-start.2 = (f32[1024]{0:T(1024)S(1)}, f32[1024]{0:T(1024)}, u32[]{:S(2)}) copy-start(f32[1024]{0:T(1024)} %param.8) | copy-start | bytes 12292
  34.5 6.2 %collective-permute-start = (bf16[8,64,2048]{2,1,0:T(8,128)(2,1)S(1)}, bf16[8,64,2048]{2,1,0:T(8,128)(2,1)}, u32[]{:S(2)}, u32[]{:S(2)}) collective-permute-start(bf16[8,64,2048]{2,1,0:T(8,128)(2,1)S(1)} %all_to_all.15.weights.mine), channel_id=1, source_target_pairs={{0,32},{32,0},{64,96},{96,64},{128,160},{160,128},{192,224},{224,1... | collective-permute-start | bytes 6291464 | tf_op jit(solution)/shard_map/ppermute | solution.py:186
  47.4 17.9 %copy-start.4 = (bf16[64,1536]{1,0:T(8,128)(2,1)S(1)}, bf16[64,1536]{1,0:T(8,128)(2,1)}, u32[]{:S(2)}) copy-start(bf16[64,1536]{1,0:T(8,128)(2,1)} %param.12) | copy-start | bytes 589828
  47.4 74.2 %all-to-all-start.1 = ((bf16[32,16,1024]{2,1,0:T(8,128)(2,1)}), bf16[32,16,1024]{2,1,0:T(8,128)(2,1)}, u32[]{:S(2)}, u32[]{:S(2)}) async-start(bf16[32,16,1024]{2,1,0:T(8,128)(2,1)} %bitcast.5), calls=%async_computation.1 | async-start | bytes 2097152 | tf_op jit(solution)/shard_map/all_to_all | solution.py:226
  79.4 12.3 %collective-permute-start.2 = (bf16[2,64,1536]{2,1,0:T(8,128)(2,1)S(1)}, bf16[2,64,1536]{2,1,0:T(8,128)(2,1)S(1)}, u32[]{:S(2)}, u32[]{:S(2)}) collective-permute-start(bf16[2,64,1536]{2,1,0:T(8,128)(2,1)S(1)} %bitcast.40), channel_id=1, source_target_pairs={{0,64},{1,65},{2,66},{3,67},{4,68},{5,69},{6,70},{7,71},{8,72},{9,... | collective-permute-start | bytes 1179656 | tf_op jit(solution)/shard_map/ppermute | solution.py:202
  82.2 13.2 %collective-permute-start.3 = (bf16[2,64,1536]{2,1,0:T(8,128)(2,1)S(1)}, bf16[2,64,1536]{2,1,0:T(8,128)(2,1)S(1)}, u32[]{:S(2)}, u32[]{:S(2)}) collective-permute-start(bf16[2,64,1536]{2,1,0:T(8,128)(2,1)S(1)} %bitcast.39), channel_id=1, source_target_pairs={{0,80},{1,81},{2,82},{3,83},{4,84},{5,85},{6,86},{7,87},{8,88},{9,... | collective-permute-start | bytes 1179656 | tf_op jit(solution)/shard_map/ppermute | solution.py:202
  86.7 10.7 %collective-permute-start.1 = (bf16[4,64,1536]{2,1,0:T(8,128)(2,1)S(1)}, bf16[4,64,1536]{2,1,0:T(8,128)(2,1)S(1)}, u32[]{:S(2)}, u32[]{:S(2)}) collective-permute-start(bf16[4,64,1536]{2,1,0:T(8,128)(2,1)S(1)} %bitcast.26), channel_id=1, source_target_pairs={{0,32},{32,0},{64,96},{96,64},{128,160},{160,128},{192,224},{224,1... | collective-permute-start | bytes 2359304 | tf_op jit(solution)/shard_map/ppermute | solution.py:186
  95.4 26.1 %copy-start.3 = (f32[1024]{0:T(1024)S(1)}, f32[1024]{0:T(1024)}, u32[]{:S(2)}) copy-start(f32[1024]{0:T(1024)} %param.11) | copy-start | bytes 12292
  95.4 4.2 %collective-permute-start.4 = (bf16[4,64,1536]{2,1,0:T(8,128)(2,1)S(1)}, bf16[4,64,1536]{2,1,0:T(8,128)(2,1)S(1)}, u32[]{:S(2)}, u32[]{:S(2)}) collective-permute-start(bf16[4,64,1536]{2,1,0:T(8,128)(2,1)S(1)} %constant_dynamic-update-slice_fusion.refs_2_), channel_id=1, source_target_pairs={{0,32},{32,0},{64,96},{96,64},{128,160},{160,128},{192,224},{224,1... | collective-permute-start | bytes 2359304 | tf_op jit(solution)/shard_map/ppermute | solution.py:186
  121.6 10.9 %copy-start.5 = (bf16[32,1024]{1,0:T(8,128)(2,1)S(1)}, bf16[32,1024]{1,0:T(8,128)(2,1)}, u32[]{:S(2)}) copy-start(bf16[32,1024]{1,0:T(8,128)(2,1)} %param.13) | copy-start | bytes 196612
  127.3 0.8 copy-start
  128.1 38.1 %all-to-all-start.2 = ((bf16[32,16,512]{2,1,0:T(8,128)(2,1)}), bf16[32,16,512]{2,1,0:T(8,128)(2,1)S(1)}, u32[]{:S(2)}, u32[]{:S(2)}) async-start(bf16[32,16,512]{2,1,0:T(8,128)(2,1)} %bitcast.33), calls=%async_computation.2 | async-start | bytes 1048576 | tf_op jit(solution)/shard_map/all_to_all | solution.py:226
  144.9 9.5 %collective-permute-start.5 = (bf16[4,32,1024]{2,1,0:T(8,128)(2,1)S(1)}, bf16[4,32,1024]{2,1,0:T(8,128)(2,1)S(1)}, u32[]{:S(2)}, u32[]{:S(2)}) collective-permute-start(bf16[4,32,1024]{2,1,0:T(8,128)(2,1)S(1)} %bitcast.28), channel_id=1, source_target_pairs={{0,64},{32,96},{64,0},{96,32},{128,192},{160,224},{192,128},{224,1... | collective-permute-start | bytes 786440 | tf_op jit(solution)/shard_map/ppermute | solution.py:186
  154.5 3.8 %collective-permute-start.6 = (bf16[2,4,32,1024]{3,2,1,0:T(8,128)(2,1)S(1)}, bf16[2,4,32,1024]{3,2,1,0:T(8,128)(2,1)S(1)}, u32[]{:S(2)}, u32[]{:S(2)}) collective-permute-start(bf16[2,4,32,1024]{3,2,1,0:T(8,128)(2,1)S(1)} %pad_maximum_fusion), channel_id=1, source_target_pairs={{0,32},{32,0},{64,96},{96,64},{128,160},{160,128},{192,224},{224,1... | collective-permute-start | bytes 1572872 | tf_op jit(solution)/shard_map/ppermute | solution.py:186

commit v10 on v9

--- a/solution.py
+++ b/solution.py
@@ -208,6 +208,10 @@
     return lax.all_gather(shard, "fsdp", axis_index_groups=lines)
 
 
+def after(array, other):
+    return lax.optimization_barrier((array, other))[0]
+
+
 def shards(tokens, spatial_gain, spatial_qkv, spatial_out, temporal_gain, temporal_qkv, temporal_out):
     clips, _, places, depth = tokens.shape
     frames = lax.axis_size("tm")
@@ -244,8 +248,9 @@
         [shape((rows, depth // 2), BF16)] * 2,
         (here, flat, spatial_gain.reshape(1, depth)),
         gflops=2,
-    )
-    partial = kernel_call(half_kernel, "vv", shape((rows, 3 * INNER), F32), (normed, mine), gflops=1)
+        room=24,
+    )
+    partial = kernel_call(half_kernel, "vv", shape((rows, 3 * INNER), F32), (normed, mine), gflops=1, room=24)
     middle = kernel_call(
         spatial_kernel,
         "svvvvv",
@@ -258,12 +263,15 @@
             pltpu.SemaphoreType.DMA((2,)),
         ],
         gflops=3,
+        room=24,
     )
     shard, middle = lax.optimization_barrier((temporal_qkv, middle))
     arrived = exchanged(middle)
     own = along_x(shard)
+    own_o = along_x(after(temporal_out, own))
     beside = other_yl(own)
     placed = in_order(own, other_core(own), beside, other_core(beside))
+    arrived, own_o = lax.optimization_barrier((arrived, own_o))
     context = kernel_call(
         functools.partial(temporal_kernel, frames),
         "vvv",
@@ -272,9 +280,8 @@
         [pltpu.VMEM((rows, 3 * INNER), BF16)],
         gflops=4,
     )
-    shard, middle, context = lax.optimization_barrier((temporal_out, middle, context))
+    own, middle, context = lax.optimization_barrier((own_o, middle, context))
     returned = exchanged(context)
-    own = along_x(shard)
     beside = moved(own, lambda x, yl, core: (x, 1 - yl, core))
     swapped = other_core(jnp.stack([own, beside]))
     weight = in_order(own, swapped[0], beside, swapped[1]).reshape(INNER, depth)

time: 169 us -> 169 us (level)
  transfers between devices with their start and end apart: 9 -> 9, of which waited for: 8 -> 7; matrix products, arithmetic and copies ran while one was open for 0% -> 0% of each run, Pallas kernels for 4% -> 4%
where the time goes in v10:
time: 169 us; the launch traced here: 168 us
  blocking collectives  58.5 us (35%)
  waiting for transfers between devices  45.3 us (27%)
  starting transfers between devices  40.1 us (24%)
  Pallas kernels  20.9 us (12%)
  matrix products  1.69 us (1%)
    all_to_all x1, blocking collectives, shards(): lax.all_to_all(packed, 'fsdp', 0, 0, axis_index_groups=cores, tiled=True)  32.1 us
    all_to_all x2, waiting for transfers between devices, exchanged(): lax.all_to_all(sent, 'tm', split_axis=0, concat_axis=0, tiled=True)  29.1 us
    all_gather x2, blocking collectives, along_x(): return lax.all_gather(shard, 'fsdp', axis_index_groups=lines)  26.4 us
    all_to_all x2, starting transfers between devices, exchanged(): lax.all_to_all(sent, 'tm', split_axis=0, concat_axis=0, tiled=True)  22.3 us
    pallas_call x8, Pallas kernels, kernel_call(): pl.pallas_call(body, out_shape=out, in_specs=[specs[kind] for kind in kin...  20.9 us
    ppermute x5, starting transfers between devices, moved(): return lax.ppermute(array, 'fsdp', pairs)  10.4 us
    ppermute x5, waiting for transfers between devices, moved(): return lax.ppermute(array, 'fsdp', pairs)  9.35 us
    ppermute x2, starting transfers between devices, other_yl(): pieces.append(lax.ppermute(piece, ('fsdp', 'tm'), pairs))  7.36 us
  transfers between devices with their start and end apart: 9, of which 7 were waited for; matrix products, arithmetic and copies ran while one was open for 0% of the time, Pallas kernels for 4%

profile of v10, /device:TPU:32, one launch (start us, length us, event | category | flops | bytes accessed | tf_op | source)
XLA Modules:
  0.0 167.8 jit_solution(5100691570740084364)
XLA Ops:
  0.0 2.4 %shard_map.74 = bf16[8,64,2048]{2,1,0:T(8,128)(2,1)} custom-call(bf16[64,1536]{1,0:T(8,128)(2,1)} %qkv.1, bf16[32,1024]{1,0:T(8,128)(2,1)} %out.1), custom_call_target="tpu_custom_call" | custom-call | bytes 4194304 | tf_op jit(solution)/shard_map/pallas_call | solution.py:170
  2.4 32.1 %all_to_all.15.weights.mine = bf16[8,64,2048]{2,1,0:T(8,128)(2,1)S(1)} all-to-all(bf16[8,64,2048]{2,1,0:T(8,128)(2,1)} %shard_map.74), channel_id=1, replica_groups={{0,64,128,192,256,320,384,448},{32,96,160,224,288,352,416,480},{1,65,12..., dimensions={0} | all-to-all | bytes 4194304 | tf_op jit(solution)/shard_map/all_to_all | solution.py:244
  34.5 1.9 %collective-permute-start = (bf16[8,64,2048]{2,1,0:T(8,128)(2,1)S(1)}, bf16[8,64,2048]{2,1,0:T(8,128)(2,1)}, u32[]{:S(2)}, u32[]{:S(2)}) collective-permute-start(bf16[8,64,2048]{2,1,0:T(8,128)(2,1)S(1)} %all_to_all.15.weights.mine), channel_id=1, source_target_pairs={{0,32},{32,0},{64,96},{96,64},{128,160},{160,128},{192,224},{224,1... | collective-permute-start | bytes 6291464 | tf_op jit(solution)/shard_map/ppermute | solution.py:186
  36.5 2.4 %shard_map.73 = (bf16[512,512]{1,0:T(8,128)(2,1)S(1)}, bf16[512,512]{1,0:T(8,128)(2,1)S(1)}) custom-call(s32[3]{0:T(128)S(1)} %pad_add_fusion.here, bf16[512,1024]{1,0:T(8,128)(2,1)S(1)} %bitcast.34, f32[1,1024]{1,0:T(1,128)S(1)} %bitcast.36), custom_call_target="tpu_custom_call" | custom-call | flops 2000000000 | bytes 4194304 | tf_op jit(solution)/shard_map/pallas_call | solution.py:170
  38.9 1.0 shard_map.75.partial
  40.7 6.7 %shard_map.76.source = bf16[512,1024]{1,0:T(8,128)(2,1)} custom-call(s32[3]{0:T(128)S(1)} %pad_add_fusion.here, bf16[512,1024]{1,0:T(8,128)(2,1)S(1)} %bitcast.35, f32[512,1536]{1,0:T(8,128)S(1)} %shard_map.75.partial, bf16[512,512]{1,0:T(8,128)(2,1)S(1)} %get-tuple-element.16.normed, bf16[8,64,2048]{2,1,0:T(8,128)(2,1)S(1)} %all_to_all.15.weights.mine, ...), custom_call_target="tpu_custom_call" | custom-call | flops 3000000000 | bytes 4194304 | tf_op jit(solution)/shard_map/pallas_call | solution.py:170
  47.4 17.9 %all-to-all-start.1 = ((bf16[32,16,1024]{2,1,0:T(8,128)(2,1)}), bf16[32,16,1024]{2,1,0:T(8,128)(2,1)}, u32[]{:S(2)}, u32[]{:S(2)}) async-start(bf16[32,16,1024]{2,1,0:T(8,128)(2,1)} %bitcast.5), calls=%async_computation.1 | async-start | bytes 2097152 | tf_op jit(solution)/shard_map/all_to_all | solution.py:230
  65.3 14.1 %all-gather = bf16[256,1536]{1,0:T(8,128)(2,1)S(1)} all-gather(bf16[64,1536]{1,0:T(8,128)(2,1)S(1)} %copy-done.4), channel_id=2, replica_groups={{0,128,256,384},{32,160,288,416},{64,192,320,448},{96,224,352,480},{1,1..., dimensions={0}, use_global_device_ids=true | all-gather | bytes 983040 | tf_op jit(solution)/shard_map/all_gather | solution.py:208
  79.5 2.8 %collective-permute-start.2 = (bf16[2,64,1536]{2,1,0:T(8,128)(2,1)S(1)}, bf16[2,64,1536]{2,1,0:T(8,128)(2,1)S(1)}, u32[]{:S(2)}, u32[]{:S(2)}) collective-permute-start(bf16[2,64,1536]{2,1,0:T(8,128)(2,1)S(1)} %bitcast.40), channel_id=1, source_target_pairs={{0,64},{1,65},{2,66},{3,67},{4,68},{5,69},{6,70},{7,71},{8,72},{9,... | collective-permute-start | bytes 1179656 | tf_op jit(solution)/shard_map/ppermute | solution.py:202
  82.3 4.5 %collective-permute-start.3 = (bf16[2,64,1536]{2,1,0:T(8,128)(2,1)S(1)}, bf16[2,64,1536]{2,1,0:T(8,128)(2,1)S(1)}, u32[]{:S(2)}, u32[]{:S(2)}) collective-permute-start(bf16[2,64,1536]{2,1,0:T(8,128)(2,1)S(1)} %bitcast.39), channel_id=1, source_target_pairs={{0,80},{1,81},{2,82},{3,83},{4,84},{5,85},{6,86},{7,87},{8,88},{9,... | collective-permute-start | bytes 1179656 | tf_op jit(solution)/shard_map/ppermute | solution.py:202
  86.9 1.9 %collective-permute-start.1 = (bf16[4,64,1536]{2,1,0:T(8,128)(2,1)S(1)}, bf16[4,64,1536]{2,1,0:T(8,128)(2,1)S(1)}, u32[]{:S(2)}, u32[]{:S(2)}) collective-permute-start(bf16[4,64,1536]{2,1,0:T(8,128)(2,1)S(1)} %bitcast.26), channel_id=1, source_target_pairs={{0,32},{32,0},{64,96},{96,64},{128,160},{160,128},{192,224},{224,1... | collective-permute-start | bytes 2359304 | tf_op jit(solution)/shard_map/ppermute | solution.py:186
  88.8 3.0 %collective-permute-done.2 = bf16[2,64,1536]{2,1,0:T(8,128)(2,1)S(1)} collective-permute-done((bf16[2,64,1536]{2,1,0:T(8,128)(2,1)S(1)}, bf16[2,64,1536]{2,1,0:T(8,128)(2,1)S(1)}, u32[]{:S(2)}, u32[]{:S(2)}) %collective-permute-start.2) | collective-permute-done | bytes 393248 | tf_op jit(solution)/shard_map/ppermute | solution.py:202
  91.8 3.9 %collective-permute-done.3 = bf16[2,64,1536]{2,1,0:T(8,128)(2,1)S(1)} collective-permute-done((bf16[2,64,1536]{2,1,0:T(8,128)(2,1)S(1)}, bf16[2,64,1536]{2,1,0:T(8,128)(2,1)S(1)}, u32[]{:S(2)}, u32[]{:S(2)}) %collective-permute-start.3) | collective-permute-done | bytes 393248 | tf_op jit(solution)/shard_map/ppermute | solution.py:202
  95.7 1.9 %collective-permute-start.4 = (bf16[4,64,1536]{2,1,0:T(8,128)(2,1)S(1)}, bf16[4,64,1536]{2,1,0:T(8,128)(2,1)S(1)}, u32[]{:S(2)}, u32[]{:S(2)}) collective-permute-start(bf16[4,64,1536]{2,1,0:T(8,128)(2,1)S(1)} %constant_dynamic-update-slice_fusion.refs_2_), channel_id=1, source_target_pairs={{0,32},{32,0},{64,96},{96,64},{128,160},{160,128},{192,224},{224,1... | collective-permute-start | bytes 2359304 | tf_op jit(solution)/shard_map/ppermute | solution.py:186
  97.7 12.3 %all-gather.1 = bf16[128,1024]{1,0:T(8,128)(2,1)S(1)} all-gather(bf16[32,1024]{1,0:T(8,128)(2,1)S(1)} %copy-done.5), channel_id=3, replica_groups={{0,128,256,384},{32,160,288,416},{64,192,320,448},{96,224,352,480},{1,1..., dimensions={0}, use_global_device_ids=true | all-gather | bytes 327680 | tf_op jit(solution)/shard_map/all_gather | solution.py:208
  110.8 10.8 %all-to-all-done.1 = bf16[32,16,1024]{2,1,0:T(8,128)(2,1)} async-done(((bf16[32,16,1024]{2,1,0:T(8,128)(2,1)}), bf16[32,16,1024]{2,1,0:T(8,128)(2,1)}, u32[]{:S(2)}, u32[]{:S(2)}) %all-to-all-start.1) | async-done | bytes 1048608 | tf_op jit(solution)/shard_map/all_to_all | solution.py:230
  121.6 5.7 %shard_map.78 = bf16[512,512]{1,0:T(8,128)(2,1)S(1)} custom-call(bf16[512,1024]{1,0:T(8,128)(2,1)} %bitcast.6.middle, f32[1,1024]{1,0:T(1,128)S(1)} %bitcast.37, bf16[4,2,2,64,1536]{4,3,2,1,0:T(8,128)(2,1)S(1)} %shard_map.77.placed), custom_call_target="tpu_custom_call" | custom-call | flops 4000000000 | bytes 4194304 | tf_op jit(solution)/shard_map/pallas_call | solution.py:170
  128.0 4.4 %all-to-all-start.2 = ((bf16[32,16,512]{2,1,0:T(8,128)(2,1)}), bf16[32,16,512]{2,1,0:T(8,128)(2,1)S(1)}, u32[]{:S(2)}, u32[]{:S(2)}) async-start(bf16[32,16,512]{2,1,0:T(8,128)(2,1)} %bitcast.33), calls=%async_computation.2 | async-start | bytes 1048576 | tf_op jit(solution)/shard_map/all_to_all | solution.py:230
  132.5 2.8 %collective-permute-start.5 = (bf16[4,32,1024]{2,1,0:T(8,128)(2,1)S(1)}, bf16[4,32,1024]{2,1,0:T(8,128)(2,1)S(1)}, u32[]{:S(2)}, u32[]{:S(2)}) collective-permute-start(bf16[4,32,1024]{2,1,0:T(8,128)(2,1)S(1)} %bitcast.28), channel_id=1, source_target_pairs={{0,64},{32,96},{64,0},{96,32},{128,192},{160,224},{192,128},{224,1... | collective-permute-start | bytes 786440 | tf_op jit(solution)/shard_map/ppermute | solution.py:186
  135.3 8.0 %collective-permute-done.5.refs_2_ = bf16[4,32,1024]{2,1,0:T(8,128)(2,1)S(1)} collective-permute-done((bf16[4,32,1024]{2,1,0:T(8,128)(2,1)S(1)}, bf16[4,32,1024]{2,1,0:T(8,128)(2,1)S(1)}, u32[]{:S(2)}, u32[]{:S(2)}) %collective-permute-start.5) | collective-permute-done | bytes 262176 | tf_op jit(solution)/shard_map/ppermute | solution.py:186
  143.3 1.9 %collective-permute-start.6 = (bf16[2,4,32,1024]{3,2,1,0:T(8,128)(2,1)S(1)}, bf16[2,4,32,1024]{3,2,1,0:T(8,128)(2,1)S(1)}, u32[]{:S(2)}, u32[]{:S(2)}) collective-permute-start(bf16[2,4,32,1024]{3,2,1,0:T(8,128)(2,1)S(1)} %pad_maximum_fusion), channel_id=1, source_target_pairs={{0,32},{32,0},{64,96},{96,64},{128,160},{160,128},{192,224},{224,1... | collective-permute-start | bytes 1572872 | tf_op jit(solution)/shard_map/ppermute | solution.py:186
  145.2 1.3 shard_map.79
  147.8 18.3 %all-to-all-done.2 = bf16[32,16,512]{2,1,0:T(8,128)(2,1)S(1)} async-done(((bf16[32,16,512]{2,1,0:T(8,128)(2,1)}), bf16[32,16,512]{2,1,0:T(8,128)(2,1)S(1)}, u32[]{:S(2)}, u32[]{:S(2)}) %all-to-all-start.2) | async-done | bytes 524320 | tf_op jit(solution)/shard_map/all_to_all | solution.py:230
  166.1 1.7 %add_convert_fusion = bf16[512,1024]{1,0:T(8,128)(2,1)} fusion(bf16[512,1024]{1,0:T(8,128)(2,1)S(1)} %shard_map.79, bf16[512,512]{1,0:T(8,128)(2,1)S(1)} %bitcast.38, bf16[512,1024]{1,0:T(8,128)(2,1)S(1)} %bitcast.31), kind=kOutput, calls=%fused_computation | convolution fusion | flops 538443776 | bytes 3670016 | tf_op jit(solution)/shard_map/dot_general | solution.py:289
  (24 shorter events, 4.0 us)
Async XLA Ops:
  2.4 34.1 %copy-start.1 = (bf16[2,1,256,1024]{3,2,1,0:T(8,128)(2,1)S(1)}, bf16[2,1,256,1024]{3,2,1,0:T(8,128)(2,1)}, u32[]{:S(2)}) copy-start(bf16[2,1,256,1024]{3,2,1,0:T(8,128)(2,1)} %param.7) | copy-start | bytes 3145732
  2.4 34.1 %copy-start.2 = (f32[1024]{0:T(1024)S(1)}, f32[1024]{0:T(1024)}, u32[]{:S(2)}) copy-start(f32[1024]{0:T(1024)} %param.8) | copy-start | bytes 12292
  34.5 6.2 %collective-permute-start = (bf16[8,64,2048]{2,1,0:T(8,128)(2,1)S(1)}, bf16[8,64,2048]{2,1,0:T(8,128)(2,1)}, u32[]{:S(2)}, u32[]{:S(2)}) collective-permute-start(bf16[8,64,2048]{2,1,0:T(8,128)(2,1)S(1)} %all_to_all.15.weights.mine), channel_id=1, source_target_pairs={{0,32},{32,0},{64,96},{96,64},{128,160},{160,128},{192,224},{224,1... | collective-permute-start | bytes 6291464 | tf_op jit(solution)/shard_map/ppermute | solution.py:186
  47.4 17.9 %copy-start.4 = (bf16[64,1536]{1,0:T(8,128)(2,1)S(1)}, bf16[64,1536]{1,0:T(8,128)(2,1)}, u32[]{:S(2)}) copy-start(bf16[64,1536]{1,0:T(8,128)(2,1)} %param.12) | copy-start | bytes 589828
  47.4 74.2 %all-to-all-start.1 = ((bf16[32,16,1024]{2,1,0:T(8,128)(2,1)}), bf16[32,16,1024]{2,1,0:T(8,128)(2,1)}, u32[]{:S(2)}, u32[]{:S(2)}) async-start(bf16[32,16,1024]{2,1,0:T(8,128)(2,1)} %bitcast.5), calls=%async_computation.1 | async-start | bytes 2097152 | tf_op jit(solution)/shard_map/all_to_all | solution.py:230
  65.3 32.4 %copy-start.5 = (bf16[32,1024]{1,0:T(8,128)(2,1)S(1)}, bf16[32,1024]{1,0:T(8,128)(2,1)}, u32[]{:S(2)}) copy-start(bf16[32,1024]{1,0:T(8,128)(2,1)} %param.13) | copy-start | bytes 196612
  79.5 12.3 %collective-permute-start.2 = (bf16[2,64,1536]{2,1,0:T(8,128)(2,1)S(1)}, bf16[2,64,1536]{2,1,0:T(8,128)(2,1)S(1)}, u32[]{:S(2)}, u32[]{:S(2)}) collective-permute-start(bf16[2,64,1536]{2,1,0:T(8,128)(2,1)S(1)} %bitcast.40), channel_id=1, source_target_pairs={{0,64},{1,65},{2,66},{3,67},{4,68},{5,69},{6,70},{7,71},{8,72},{9,... | collective-permute-start | bytes 1179656 | tf_op jit(solution)/shard_map/ppermute | solution.py:202
  82.3 13.3 %collective-permute-start.3 = (bf16[2,64,1536]{2,1,0:T(8,128)(2,1)S(1)}, bf16[2,64,1536]{2,1,0:T(8,128)(2,1)S(1)}, u32[]{:S(2)}, u32[]{:S(2)}) collective-permute-start(bf16[2,64,1536]{2,1,0:T(8,128)(2,1)S(1)} %bitcast.39), channel_id=1, source_target_pairs={{0,80},{1,81},{2,82},{3,83},{4,84},{5,85},{6,86},{7,87},{8,88},{9,... | collective-permute-start | bytes 1179656 | tf_op jit(solution)/shard_map/ppermute | solution.py:202
  86.9 23.1 %collective-permute-start.1 = (bf16[4,64,1536]{2,1,0:T(8,128)(2,1)S(1)}, bf16[4,64,1536]{2,1,0:T(8,128)(2,1)S(1)}, u32[]{:S(2)}, u32[]{:S(2)}) collective-permute-start(bf16[4,64,1536]{2,1,0:T(8,128)(2,1)S(1)} %bitcast.26), channel_id=1, source_target_pairs={{0,32},{32,0},{64,96},{96,64},{128,160},{160,128},{192,224},{224,1... | collective-permute-start | bytes 2359304 | tf_op jit(solution)/shard_map/ppermute | solution.py:186
  95.7 14.2 %collective-permute-start.4 = (bf16[4,64,1536]{2,1,0:T(8,128)(2,1)S(1)}, bf16[4,64,1536]{2,1,0:T(8,128)(2,1)S(1)}, u32[]{:S(2)}, u32[]{:S(2)}) collective-permute-start(bf16[4,64,1536]{2,1,0:T(8,128)(2,1)S(1)} %constant_dynamic-update-slice_fusion.refs_2_), channel_id=1, source_target_pairs={{0,32},{32,0},{64,96},{96,64},{128,160},{160,128},{192,224},{224,1... | collective-permute-start | bytes 2359304 | tf_op jit(solution)/shard_map/ppermute | solution.py:186
  109.9 11.7 %copy-start.3 = (f32[1024]{0:T(1024)S(1)}, f32[1024]{0:T(1024)}, u32[]{:S(2)}) copy-start(f32[1024]{0:T(1024)} %param.11) | copy-start | bytes 12292
  127.2 0.8 copy-start
  128.0 38.1 %all-to-all-start.2 = ((bf16[32,16,512]{2,1,0:T(8,128)(2,1)}), bf16[32,16,512]{2,1,0:T(8,128)(2,1)S(1)}, u32[]{:S(2)}, u32[]{:S(2)}) async-start(bf16[32,16,512]{2,1,0:T(8,128)(2,1)} %bitcast.33), calls=%async_computation.2 | async-start | bytes 1048576 | tf_op jit(solution)/shard_map/all_to_all | solution.py:230
  132.5 10.7 %collective-permute-start.5 = (bf16[4,32,1024]{2,1,0:T(8,128)(2,1)S(1)}, bf16[4,32,1024]{2,1,0:T(8,128)(2,1)S(1)}, u32[]{:S(2)}, u32[]{:S(2)}) collective-permute-start(bf16[4,32,1024]{2,1,0:T(8,128)(2,1)S(1)} %bitcast.28), channel_id=1, source_target_pairs={{0,64},{32,96},{64,0},{96,32},{128,192},{160,224},{192,128},{224,1... | collective-permute-start | bytes 786440 | tf_op jit(solution)/shard_map/ppermute | solution.py:186
  143.3 3.8 %collective-permute-start.6 = (bf16[2,4,32,1024]{3,2,1,0:T(8,128)(2,1)S(1)}, bf16[2,4,32,1024]{3,2,1,0:T(8,128)(2,1)S(1)}, u32[]{:S(2)}, u32[]{:S(2)}) collective-permute-start(bf16[2,4,32,1024]{3,2,1,0:T(8,128)(2,1)S(1)} %pad_maximum_fusion), channel_id=1, source_target_pairs={{0,32},{32,0},{64,96},{96,64},{128,160},{160,128},{192,224},{224,1... | collective-permute-start | bytes 1572872 | tf_op jit(solution)/shard_map/ppermute | solution.py:186

commit v11 on v10

--- a/solution.py
+++ b/solution.py
@@ -190,7 +190,7 @@
     return moved(array, lambda x, yl, core: (x, yl, 1 - core))
 
 
-def other_yl(array):
+def other_yl(array, beside):
     members, frames = lax.axis_size("fsdp"), lax.axis_size("tm")
     half = array.shape[0] // 2
     pieces = []
@@ -200,7 +200,8 @@
             member, frame = source // frames, source % frames
             pairs.append((source, (member ^ 2) * frames + (frame + turn * frames // 2) % frames))
         pieces.append(lax.ppermute(piece, ("fsdp", "tm"), pairs))
-    return jnp.concatenate(pieces, axis=0)
+    *pieces, beside = lax.optimization_barrier((*pieces, beside))
+    return jnp.concatenate(pieces, axis=0), beside
 
 
 def along_x(shard):
@@ -269,7 +270,7 @@
     arrived = exchanged(middle)
     own = along_x(shard)
     own_o = along_x(after(temporal_out, own))
-    beside = other_yl(own)
+    beside, own_o = other_yl(own, own_o)
     placed = in_order(own, other_core(own), beside, other_core(beside))
     arrived, own_o = lax.optimization_barrier((arrived, own_o))
     context = kernel_call(

time: 169 us -> 169 us (level)
    ppermute x2, waiting for transfers between devices: 6.86 us -> 0.01 us  [other_yl(): pieces.append(lax.ppermute(piece, ('fsdp', 'tm'), pairs))]
    all_to_all x2, waiting for transfers between devices: 29.1 us -> 33.8 us  [exchanged(): lax.all_to_all(sent, 'tm', split_axis=0, concat_axis=0, tiled=True)]
    ppermute x5, waiting for transfers between devices: 9.35 us -> 11.6 us  [moved(): return lax.ppermute(array, 'fsdp', pairs)]
  transfers between devices with their start and end apart: 9 -> 9, of which waited for: 7 -> 6; matrix products, arithmetic and copies ran while one was open for 0% -> 0% of each run, Pallas kernels for 4% -> 4%
where the time goes in v11:
time: 169 us; the launch traced here: 168 us
  blocking collectives  58.3 us (34%)
  waiting for transfers between devices  45.5 us (27%)
  starting transfers between devices  40.1 us (24%)
  Pallas kernels  20.9 us (12%)
  matrix products  1.69 us (1%)
    all_to_all x2, waiting for transfers between devices, exchanged(): lax.all_to_all(sent, 'tm', split_axis=0, concat_axis=0, tiled=True)  33.8 us
    all_to_all x1, blocking collectives, shards(): lax.all_to_all(packed, 'fsdp', 0, 0, axis_index_groups=cores, tiled=True)  32.1 us
    all_gather x2, blocking collectives, along_x(): return lax.all_gather(shard, 'fsdp', axis_index_groups=lines)  26.3 us
    all_to_all x2, starting transfers between devices, exchanged(): lax.all_to_all(sent, 'tm', split_axis=0, concat_axis=0, tiled=True)  22.3 us
    pallas_call x8, Pallas kernels, kernel_call(): pl.pallas_call(body, out_shape=out, in_specs=[specs[kind] for kind in kin...  20.9 us
    ppermute x5, waiting for transfers between devices, moved(): return lax.ppermute(array, 'fsdp', pairs)  11.6 us
    ppermute x5, starting transfers between devices, moved(): return lax.ppermute(array, 'fsdp', pairs)  10.4 us
    ppermute x2, starting transfers between devices, other_yl(): pieces.append(lax.ppermute(piece, ('fsdp', 'tm'), pairs))  7.36 us
  transfers between devices with their start and end apart: 9, of which 6 were waited for; matrix products, arithmetic and copies ran while one was open for 0% of the time, Pallas kernels for 4%

profile of v11, /device:TPU:32, one launch (start us, length us, event | category | flops | bytes accessed | tf_op | source)
XLA Modules:
  0.0 167.8 jit_solution(15679381256812524529)
XLA Ops:
  0.0 2.4 %shard_map.74 = bf16[8,64,2048]{2,1,0:T(8,128)(2,1)} custom-call(bf16[64,1536]{1,0:T(8,128)(2,1)} %qkv.1, bf16[32,1024]{1,0:T(8,128)(2,1)} %out.1), custom_call_target="tpu_custom_call" | custom-call | bytes 4194304 | tf_op jit(solution)/shard_map/pallas_call | solution.py:170
  2.4 32.1 %all_to_all.15.weights.mine = bf16[8,64,2048]{2,1,0:T(8,128)(2,1)S(1)} all-to-all(bf16[8,64,2048]{2,1,0:T(8,128)(2,1)} %shard_map.74), channel_id=1, replica_groups={{0,64,128,192,256,320,384,448},{32,96,160,224,288,352,416,480},{1,65,12..., dimensions={0} | all-to-all | bytes 4194304 | tf_op jit(solution)/shard_map/all_to_all | solution.py:245
  34.5 1.9 %collective-permute-start = (bf16[8,64,2048]{2,1,0:T(8,128)(2,1)S(1)}, bf16[8,64,2048]{2,1,0:T(8,128)(2,1)}, u32[]{:S(2)}, u32[]{:S(2)}) collective-permute-start(bf16[8,64,2048]{2,1,0:T(8,128)(2,1)S(1)} %all_to_all.15.weights.mine), channel_id=1, source_target_pairs={{0,32},{32,0},{64,96},{96,64},{128,160},{160,128},{192,224},{224,1... | collective-permute-start | bytes 6291464 | tf_op jit(solution)/shard_map/ppermute | solution.py:186
  36.5 2.4 %shard_map.73 = (bf16[512,512]{1,0:T(8,128)(2,1)S(1)}, bf16[512,512]{1,0:T(8,128)(2,1)S(1)}) custom-call(s32[3]{0:T(128)S(1)} %pad_add_fusion.here, bf16[512,1024]{1,0:T(8,128)(2,1)S(1)} %bitcast.34, f32[1,1024]{1,0:T(1,128)S(1)} %bitcast.36), custom_call_target="tpu_custom_call" | custom-call | flops 2000000000 | bytes 4194304 | tf_op jit(solution)/shard_map/pallas_call | solution.py:170
  38.9 1.0 shard_map.75.partial
  40.7 6.7 %shard_map.76.source = bf16[512,1024]{1,0:T(8,128)(2,1)} custom-call(s32[3]{0:T(128)S(1)} %pad_add_fusion.here, bf16[512,1024]{1,0:T(8,128)(2,1)S(1)} %bitcast.35, f32[512,1536]{1,0:T(8,128)S(1)} %shard_map.75.partial, bf16[512,512]{1,0:T(8,128)(2,1)S(1)} %get-tuple-element.19.normed, bf16[8,64,2048]{2,1,0:T(8,128)(2,1)S(1)} %all_to_all.15.weights.mine, ...), custom_call_target="tpu_custom_call" | custom-call | flops 3000000000 | bytes 4194304 | tf_op jit(solution)/shard_map/pallas_call | solution.py:170
  47.4 17.9 %all-to-all-start.1 = ((bf16[32,16,1024]{2,1,0:T(8,128)(2,1)}), bf16[32,16,1024]{2,1,0:T(8,128)(2,1)}, u32[]{:S(2)}, u32[]{:S(2)}) async-start(bf16[32,16,1024]{2,1,0:T(8,128)(2,1)} %bitcast.5), calls=%async_computation.1 | async-start | bytes 2097152 | tf_op jit(solution)/shard_map/all_to_all | solution.py:231
  65.3 14.0 %all-gather = bf16[256,1536]{1,0:T(8,128)(2,1)S(1)} all-gather(bf16[64,1536]{1,0:T(8,128)(2,1)S(1)} %copy-done.4), channel_id=2, replica_groups={{0,128,256,384},{32,160,288,416},{64,192,320,448},{96,224,352,480},{1,1..., dimensions={0}, use_global_device_ids=true | all-gather | bytes 983040 | tf_op jit(solution)/shard_map/all_gather | solution.py:209
  79.4 2.8 %collective-permute-start.1 = (bf16[2,64,1536]{2,1,0:T(8,128)(2,1)S(1)}, bf16[2,64,1536]{2,1,0:T(8,128)(2,1)S(1)}, u32[]{:S(2)}, u32[]{:S(2)}) collective-permute-start(bf16[2,64,1536]{2,1,0:T(8,128)(2,1)S(1)} %bitcast.40), channel_id=1, source_target_pairs={{0,64},{1,65},{2,66},{3,67},{4,68},{5,69},{6,70},{7,71},{8,72},{9,... | collective-permute-start | bytes 1179656 | tf_op jit(solution)/shard_map/ppermute | solution.py:202
  82.2 4.5 %collective-permute-start.2 = (bf16[2,64,1536]{2,1,0:T(8,128)(2,1)S(1)}, bf16[2,64,1536]{2,1,0:T(8,128)(2,1)S(1)}, u32[]{:S(2)}, u32[]{:S(2)}) collective-permute-start(bf16[2,64,1536]{2,1,0:T(8,128)(2,1)S(1)} %bitcast.39), channel_id=1, source_target_pairs={{0,80},{1,81},{2,82},{3,83},{4,84},{5,85},{6,86},{7,87},{8,88},{9,... | collective-permute-start | bytes 1179656 | tf_op jit(solution)/shard_map/ppermute | solution.py:202
  86.7 1.9 %collective-permute-start.3 = (bf16[4,64,1536]{2,1,0:T(8,128)(2,1)S(1)}, bf16[4,64,1536]{2,1,0:T(8,128)(2,1)S(1)}, u32[]{:S(2)}, u32[]{:S(2)}) collective-permute-start(bf16[4,64,1536]{2,1,0:T(8,128)(2,1)S(1)} %bitcast.26), channel_id=1, source_target_pairs={{0,32},{32,0},{64,96},{96,64},{128,160},{160,128},{192,224},{224,1... | collective-permute-start | bytes 2359304 | tf_op jit(solution)/shard_map/ppermute | solution.py:186
  88.7 12.3 %all-gather.1 = bf16[128,1024]{1,0:T(8,128)(2,1)S(1)} all-gather(bf16[32,1024]{1,0:T(8,128)(2,1)S(1)} %copy-done.5), channel_id=3, replica_groups={{0,128,256,384},{32,160,288,416},{64,192,320,448},{96,224,352,480},{1,1..., dimensions={0}, use_global_device_ids=true | all-gather | bytes 327680 | tf_op jit(solution)/shard_map/all_gather | solution.py:209
  101.0 1.9 %collective-permute-start.4 = (bf16[4,64,1536]{2,1,0:T(8,128)(2,1)S(1)}, bf16[4,64,1536]{2,1,0:T(8,128)(2,1)S(1)}, u32[]{:S(2)}, u32[]{:S(2)}) collective-permute-start(bf16[4,64,1536]{2,1,0:T(8,128)(2,1)S(1)} %constant_dynamic-update-slice_fusion.refs_2_), channel_id=1, source_target_pairs={{0,32},{32,0},{64,96},{96,64},{128,160},{160,128},{192,224},{224,1... | collective-permute-start | bytes 2359304 | tf_op jit(solution)/shard_map/ppermute | solution.py:186
  103.0 2.2 %collective-permute-done.4.refs_3_ = bf16[4,64,1536]{2,1,0:T(8,128)(2,1)S(1)} collective-permute-done((bf16[4,64,1536]{2,1,0:T(8,128)(2,1)S(1)}, bf16[4,64,1536]{2,1,0:T(8,128)(2,1)S(1)}, u32[]{:S(2)}, u32[]{:S(2)}) %collective-permute-start.4) | collective-permute-done | bytes 786464 | tf_op jit(solution)/shard_map/ppermute | solution.py:186
  105.2 0.8 shard_map.77.placed
  106.0 15.6 %all-to-all-done.1 = bf16[32,16,1024]{2,1,0:T(8,128)(2,1)} async-done(((bf16[32,16,1024]{2,1,0:T(8,128)(2,1)}), bf16[32,16,1024]{2,1,0:T(8,128)(2,1)}, u32[]{:S(2)}, u32[]{:S(2)}) %all-to-all-start.1) | async-done | bytes 1048608 | tf_op jit(solution)/shard_map/all_to_all | solution.py:231
  121.6 5.7 %shard_map.78 = bf16[512,512]{1,0:T(8,128)(2,1)S(1)} custom-call(bf16[512,1024]{1,0:T(8,128)(2,1)} %bitcast.6.middle, f32[1,1024]{1,0:T(1,128)S(1)} %bitcast.37, bf16[4,2,2,64,1536]{4,3,2,1,0:T(8,128)(2,1)S(1)} %shard_map.77.placed), custom_call_target="tpu_custom_call" | custom-call | flops 4000000000 | bytes 4194304 | tf_op jit(solution)/shard_map/pallas_call | solution.py:170
  128.1 4.4 %all-to-all-start.2 = ((bf16[32,16,512]{2,1,0:T(8,128)(2,1)}), bf16[32,16,512]{2,1,0:T(8,128)(2,1)S(1)}, u32[]{:S(2)}, u32[]{:S(2)}) async-start(bf16[32,16,512]{2,1,0:T(8,128)(2,1)} %bitcast.33), calls=%async_computation.2 | async-start | bytes 1048576 | tf_op jit(solution)/shard_map/all_to_all | solution.py:231
  132.5 2.8 %collective-permute-start.5 = (bf16[4,32,1024]{2,1,0:T(8,128)(2,1)S(1)}, bf16[4,32,1024]{2,1,0:T(8,128)(2,1)S(1)}, u32[]{:S(2)}, u32[]{:S(2)}) collective-permute-start(bf16[4,32,1024]{2,1,0:T(8,128)(2,1)S(1)} %bitcast.28), channel_id=1, source_target_pairs={{0,64},{32,96},{64,0},{96,32},{128,192},{160,224},{192,128},{224,1... | collective-permute-start | bytes 786440 | tf_op jit(solution)/shard_map/ppermute | solution.py:186
  135.3 8.0 %collective-permute-done.5.refs_2_ = bf16[4,32,1024]{2,1,0:T(8,128)(2,1)S(1)} collective-permute-done((bf16[4,32,1024]{2,1,0:T(8,128)(2,1)S(1)}, bf16[4,32,1024]{2,1,0:T(8,128)(2,1)S(1)}, u32[]{:S(2)}, u32[]{:S(2)}) %collective-permute-start.5) | collective-permute-done | bytes 262176 | tf_op jit(solution)/shard_map/ppermute | solution.py:186
  143.3 1.9 %collective-permute-start.6 = (bf16[2,4,32,1024]{3,2,1,0:T(8,128)(2,1)S(1)}, bf16[2,4,32,1024]{3,2,1,0:T(8,128)(2,1)S(1)}, u32[]{:S(2)}, u32[]{:S(2)}) collective-permute-start(bf16[2,4,32,1024]{3,2,1,0:T(8,128)(2,1)S(1)} %pad_maximum_fusion), channel_id=1, source_target_pairs={{0,32},{32,0},{64,96},{96,64},{128,160},{160,128},{192,224},{224,1... | collective-permute-start | bytes 1572872 | tf_op jit(solution)/shard_map/ppermute | solution.py:186
  145.3 1.3 shard_map.79
  147.9 18.3 %all-to-all-done.2 = bf16[32,16,512]{2,1,0:T(8,128)(2,1)S(1)} async-done(((bf16[32,16,512]{2,1,0:T(8,128)(2,1)}), bf16[32,16,512]{2,1,0:T(8,128)(2,1)S(1)}, u32[]{:S(2)}, u32[]{:S(2)}) %all-to-all-start.2) | async-done | bytes 524320 | tf_op jit(solution)/shard_map/all_to_all | solution.py:231
  166.1 1.7 %add_convert_fusion = bf16[512,1024]{1,0:T(8,128)(2,1)} fusion(bf16[512,1024]{1,0:T(8,128)(2,1)S(1)} %shard_map.79, bf16[512,512]{1,0:T(8,128)(2,1)S(1)} %bitcast.38, bf16[512,1024]{1,0:T(8,128)(2,1)S(1)} %bitcast.31), kind=kOutput, calls=%fused_computation | convolution fusion | flops 538443776 | bytes 3670016 | tf_op jit(solution)/shard_map/dot_general | solution.py:290
  (24 shorter events, 3.1 us)
Async XLA Ops:
  2.4 34.1 %copy-start.1 = (bf16[2,1,256,1024]{3,2,1,0:T(8,128)(2,1)S(1)}, bf16[2,1,256,1024]{3,2,1,0:T(8,128)(2,1)}, u32[]{:S(2)}) copy-start(bf16[2,1,256,1024]{3,2,1,0:T(8,128)(2,1)} %param.7) | copy-start | bytes 3145732
  2.4 34.1 %copy-start.2 = (f32[1024]{0:T(1024)S(1)}, f32[1024]{0:T(1024)}, u32[]{:S(2)}) copy-start(f32[1024]{0:T(1024)} %param.8) | copy-start | bytes 12292
  34.5 6.2 %collective-permute-start = (bf16[8,64,2048]{2,1,0:T(8,128)(2,1)S(1)}, bf16[8,64,2048]{2,1,0:T(8,128)(2,1)}, u32[]{:S(2)}, u32[]{:S(2)}) collective-permute-start(bf16[8,64,2048]{2,1,0:T(8,128)(2,1)S(1)} %all_to_all.15.weights.mine), channel_id=1, source_target_pairs={{0,32},{32,0},{64,96},{96,64},{128,160},{160,128},{192,224},{224,1... | collective-permute-start | bytes 6291464 | tf_op jit(solution)/shard_map/ppermute | solution.py:186
  47.4 17.9 %copy-start.4 = (bf16[64,1536]{1,0:T(8,128)(2,1)S(1)}, bf16[64,1536]{1,0:T(8,128)(2,1)}, u32[]{:S(2)}) copy-start(bf16[64,1536]{1,0:T(8,128)(2,1)} %param.12) | copy-start | bytes 589828
  47.4 41.3 %copy-start.5 = (bf16[32,1024]{1,0:T(8,128)(2,1)S(1)}, bf16[32,1024]{1,0:T(8,128)(2,1)}, u32[]{:S(2)}) copy-start(bf16[32,1024]{1,0:T(8,128)(2,1)} %param.13) | copy-start | bytes 196612
  47.4 74.2 %all-to-all-start.1 = ((bf16[32,16,1024]{2,1,0:T(8,128)(2,1)}), bf16[32,16,1024]{2,1,0:T(8,128)(2,1)}, u32[]{:S(2)}, u32[]{:S(2)}) async-start(bf16[32,16,1024]{2,1,0:T(8,128)(2,1)} %bitcast.5), calls=%async_computation.1 | async-start | bytes 2097152 | tf_op jit(solution)/shard_map/all_to_all | solution.py:231
  79.4 21.6 %collective-permute-start.1 = (bf16[2,64,1536]{2,1,0:T(8,128)(2,1)S(1)}, bf16[2,64,1536]{2,1,0:T(8,128)(2,1)S(1)}, u32[]{:S(2)}, u32[]{:S(2)}) collective-permute-start(bf16[2,64,1536]{2,1,0:T(8,128)(2,1)S(1)} %bitcast.40), channel_id=1, source_target_pairs={{0,64},{1,65},{2,66},{3,67},{4,68},{5,69},{6,70},{7,71},{8,72},{9,... | collective-permute-start | bytes 1179656 | tf_op jit(solution)/shard_map/ppermute | solution.py:202
  82.2 18.7 %collective-permute-start.2 = (bf16[2,64,1536]{2,1,0:T(8,128)(2,1)S(1)}, bf16[2,64,1536]{2,1,0:T(8,128)(2,1)S(1)}, u32[]{:S(2)}, u32[]{:S(2)}) collective-permute-start(bf16[2,64,1536]{2,1,0:T(8,128)(2,1)S(1)} %bitcast.39), channel_id=1, source_target_pairs={{0,80},{1,81},{2,82},{3,83},{4,84},{5,85},{6,86},{7,87},{8,88},{9,... | collective-permute-start | bytes 1179656 | tf_op jit(solution)/shard_map/ppermute | solution.py:202
  86.7 16.2 %collective-permute-start.3 = (bf16[4,64,1536]{2,1,0:T(8,128)(2,1)S(1)}, bf16[4,64,1536]{2,1,0:T(8,128)(2,1)S(1)}, u32[]{:S(2)}, u32[]{:S(2)}) collective-permute-start(bf16[4,64,1536]{2,1,0:T(8,128)(2,1)S(1)} %bitcast.26), channel_id=1, source_target_pairs={{0,32},{32,0},{64,96},{96,64},{128,160},{160,128},{192,224},{224,1... | collective-permute-start | bytes 2359304 | tf_op jit(solution)/shard_map/ppermute | solution.py:186
  101.0 20.6 %copy-start.3 = (f32[1024]{0:T(1024)S(1)}, f32[1024]{0:T(1024)}, u32[]{:S(2)}) copy-start(f32[1024]{0:T(1024)} %param.11) | copy-start | bytes 12292
  101.0 4.2 %collective-permute-start.4 = (bf16[4,64,1536]{2,1,0:T(8,128)(2,1)S(1)}, bf16[4,64,1536]{2,1,0:T(8,128)(2,1)S(1)}, u32[]{:S(2)}, u32[]{:S(2)}) collective-permute-start(bf16[4,64,1536]{2,1,0:T(8,128)(2,1)S(1)} %constant_dynamic-update-slice_fusion.refs_2_), channel_id=1, source_target_pairs={{0,32},{32,0},{64,96},{96,64},{128,160},{160,128},{192,224},{224,1... | collective-permute-start | bytes 2359304 | tf_op jit(solution)/shard_map/ppermute | solution.py:186
  127.3 0.8 copy-start
  128.1 38.1 %all-to-all-start.2 = ((bf16[32,16,512]{2,1,0:T(8,128)(2,1)}), bf16[32,16,512]{2,1,0:T(8,128)(2,1)S(1)}, u32[]{:S(2)}, u32[]{:S(2)}) async-start(bf16[32,16,512]{2,1,0:T(8,128)(2,1)} %bitcast.33), calls=%async_computation.2 | async-start | bytes 1048576 | tf_op jit(solution)/shard_map/all_to_all | solution.py:231
  132.5 10.8 %collective-permute-start.5 = (bf16[4,32,1024]{2,1,0:T(8,128)(2,1)S(1)}, bf16[4,32,1024]{2,1,0:T(8,128)(2,1)S(1)}, u32[]{:S(2)}, u32[]{:S(2)}) collective-permute-start(bf16[4,32,1024]{2,1,0:T(8,128)(2,1)S(1)} %bitcast.28), channel_id=1, source_target_pairs={{0,64},{32,96},{64,0},{96,32},{128,192},{160,224},{192,128},{224,1... | collective-permute-start | bytes 786440 | tf_op jit(solution)/shard_map/ppermute | solution.py:186
  143.3 3.8 %collective-permute-start.6 = (bf16[2,4,32,1024]{3,2,1,0:T(8,128)(2,1)S(1)}, bf16[2,4,32,1024]{3,2,1,0:T(8,128)(2,1)S(1)}, u32[]{:S(2)}, u32[]{:S(2)}) collective-permute-start(bf16[2,4,32,1024]{3,2,1,0:T(8,128)(2,1)S(1)} %pad_maximum_fusion), channel_id=1, source_target_pairs={{0,32},{32,0},{64,96},{96,64},{128,160},{160,128},{192,224},{224,1... | collective-permute-start | bytes 1572872 | tf_op jit(solution)/shard_map/ppermute | solution.py:186

commit v12 on v11

--- a/solution.py
+++ b/solution.py
@@ -31,6 +31,7 @@
         queries = qkv[rows, pl.ds(pair * PAIR, PAIR)]
         keys = qkv[rows, pl.ds(INNER + pair * PAIR, PAIR)]
         values = qkv[rows, pl.ds(2 * INNER + pair * PAIR, PAIR)]
+        values = jnp.concatenate([values, jnp.ones_like(values)], axis=1)
         halves = []
         for mine in (low, ~low):
             own = jnp.where(mine, queries, jnp.zeros_like(queries))
@@ -38,8 +39,8 @@
             if same is not None:
                 scores = jnp.where(same, scores, -1e30)
             exponent = jnp.exp(scores - jnp.max(scores, axis=-1, keepdims=True))
-            weights = exponent * (1.0 / jnp.sum(exponent, axis=-1, keepdims=True))
-            halves.append(jnp.dot(weights.astype(BF16), values, preferred_element_type=F32))
+            summed = jnp.dot(exponent.astype(BF16), values, preferred_element_type=F32)
+            halves.append(summed[:, :PAIR] / summed[:, PAIR:])
         outs.append(jnp.where(low, halves[0], halves[1]))
     return jnp.concatenate(outs, axis=1)
 

time: 169 us -> 167 us (0.988)
  Pallas kernels: 20.9 us -> 19.2 us
    pallas_call x8, Pallas kernels: 20.9 us -> 19.2 us  [kernel_call(): pl.pallas_call(body, out_shape=out, in_specs=[specs[kind] for kind in kin...]
where the time goes in v12:
time: 167 us; the launch traced here: 166 us
  blocking collectives  58.3 us (35%)
  waiting for transfers between devices  45.4 us (27%)
  starting transfers between devices  40.1 us (24%)
  Pallas kernels  19.2 us (11%)
  matrix products  1.68 us (1%)
    all_to_all x2, waiting for transfers between devices, exchanged(): lax.all_to_all(sent, 'tm', split_axis=0, concat_axis=0, tiled=True)  33.8 us
    all_to_all x1, blocking collectives, shards(): lax.all_to_all(packed, 'fsdp', 0, 0, axis_index_groups=cores, tiled=True)  32.1 us
    all_gather x2, blocking collectives, along_x(): return lax.all_gather(shard, 'fsdp', axis_index_groups=lines)  26.3 us
    all_to_all x2, starting transfers between devices, exchanged(): lax.all_to_all(sent, 'tm', split_axis=0, concat_axis=0, tiled=True)  22.3 us
    pallas_call x8, Pallas kernels, kernel_call(): pl.pallas_call(body, out_shape=out, in_specs=[specs[kind] for kind in kin...  19.2 us
    ppermute x5, waiting for transfers between devices, moved(): return lax.ppermute(array, 'fsdp', pairs)  11.6 us
    ppermute x5, starting transfers between devices, moved(): return lax.ppermute(array, 'fsdp', pairs)  10.4 us
    ppermute x2, starting transfers between devices, other_yl(): pieces.append(lax.ppermute(piece, ('fsdp', 'tm'), pairs))  7.36 us
  transfers between devices with their start and end apart: 9, of which 6 were waited for; matrix products, arithmetic and copies ran while one was open for 0% of the time, Pallas kernels for 4%

profile of v12, /device:TPU:32, one launch (start us, length us, event | category | flops | bytes accessed | tf_op | source)
XLA Modules:
  0.0 166.1 jit_solution(10737601343660884377)
XLA Ops:
  0.0 2.4 %shard_map.74 = bf16[8,64,2048]{2,1,0:T(8,128)(2,1)} custom-call(bf16[64,1536]{1,0:T(8,128)(2,1)} %qkv.1, bf16[32,1024]{1,0:T(8,128)(2,1)} %out.1), custom_call_target="tpu_custom_call" | custom-call | bytes 4194304 | tf_op jit(solution)/shard_map/pallas_call | solution.py:171
  2.4 32.1 %all_to_all.15.weights.mine = bf16[8,64,2048]{2,1,0:T(8,128)(2,1)S(1)} all-to-all(bf16[8,64,2048]{2,1,0:T(8,128)(2,1)} %shard_map.74), channel_id=1, replica_groups={{0,64,128,192,256,320,384,448},{32,96,160,224,288,352,416,480},{1,65,12..., dimensions={0} | all-to-all | bytes 4194304 | tf_op jit(solution)/shard_map/all_to_all | solution.py:246
  34.5 1.9 %collective-permute-start = (bf16[8,64,2048]{2,1,0:T(8,128)(2,1)S(1)}, bf16[8,64,2048]{2,1,0:T(8,128)(2,1)}, u32[]{:S(2)}, u32[]{:S(2)}) collective-permute-start(bf16[8,64,2048]{2,1,0:T(8,128)(2,1)S(1)} %all_to_all.15.weights.mine), channel_id=1, source_target_pairs={{0,32},{32,0},{64,96},{96,64},{128,160},{160,128},{192,224},{224,1... | collective-permute-start | bytes 6291464 | tf_op jit(solution)/shard_map/ppermute | solution.py:187
  36.5 2.4 %shard_map.73 = (bf16[512,512]{1,0:T(8,128)(2,1)S(1)}, bf16[512,512]{1,0:T(8,128)(2,1)S(1)}) custom-call(s32[3]{0:T(128)S(1)} %pad_add_fusion.here, bf16[512,1024]{1,0:T(8,128)(2,1)S(1)} %bitcast.34, f32[1,1024]{1,0:T(1,128)S(1)} %bitcast.36), custom_call_target="tpu_custom_call" | custom-call | flops 2000000000 | bytes 4194304 | tf_op jit(solution)/shard_map/pallas_call | solution.py:171
  38.9 1.0 shard_map.75.partial
  40.7 5.8 %shard_map.76.source = bf16[512,1024]{1,0:T(8,128)(2,1)} custom-call(s32[3]{0:T(128)S(1)} %pad_add_fusion.here, bf16[512,1024]{1,0:T(8,128)(2,1)S(1)} %bitcast.35, f32[512,1536]{1,0:T(8,128)S(1)} %shard_map.75.partial, bf16[512,512]{1,0:T(8,128)(2,1)S(1)} %get-tuple-element.19.normed, bf16[8,64,2048]{2,1,0:T(8,128)(2,1)S(1)} %all_to_all.15.weights.mine, ...), custom_call_target="tpu_custom_call" | custom-call | flops 3000000000 | bytes 4194304 | tf_op jit(solution)/shard_map/pallas_call | solution.py:171
  46.5 17.9 %all-to-all-start.1 = ((bf16[32,16,1024]{2,1,0:T(8,128)(2,1)}), bf16[32,16,1024]{2,1,0:T(8,128)(2,1)}, u32[]{:S(2)}, u32[]{:S(2)}) async-start(bf16[32,16,1024]{2,1,0:T(8,128)(2,1)} %bitcast.5), calls=%async_computation.1 | async-start | bytes 2097152 | tf_op jit(solution)/shard_map/all_to_all | solution.py:232
  64.4 14.0 %all-gather = bf16[256,1536]{1,0:T(8,128)(2,1)S(1)} all-gather(bf16[64,1536]{1,0:T(8,128)(2,1)S(1)} %copy-done.4), channel_id=2, replica_groups={{0,128,256,384},{32,160,288,416},{64,192,320,448},{96,224,352,480},{1,1..., dimensions={0}, use_global_device_ids=true | all-gather | bytes 983040 | tf_op jit(solution)/shard_map/all_gather | solution.py:210
  78.5 2.8 %collective-permute-start.1 = (bf16[2,64,1536]{2,1,0:T(8,128)(2,1)S(1)}, bf16[2,64,1536]{2,1,0:T(8,128)(2,1)S(1)}, u32[]{:S(2)}, u32[]{:S(2)}) collective-permute-start(bf16[2,64,1536]{2,1,0:T(8,128)(2,1)S(1)} %bitcast.40), channel_id=1, source_target_pairs={{0,64},{1,65},{2,66},{3,67},{4,68},{5,69},{6,70},{7,71},{8,72},{9,... | collective-permute-start | bytes 1179656 | tf_op jit(solution)/shard_map/ppermute | solution.py:203
  81.3 4.5 %collective-permute-start.2 = (bf16[2,64,1536]{2,1,0:T(8,128)(2,1)S(1)}, bf16[2,64,1536]{2,1,0:T(8,128)(2,1)S(1)}, u32[]{:S(2)}, u32[]{:S(2)}) collective-permute-start(bf16[2,64,1536]{2,1,0:T(8,128)(2,1)S(1)} %bitcast.39), channel_id=1, source_target_pairs={{0,80},{1,81},{2,82},{3,83},{4,84},{5,85},{6,86},{7,87},{8,88},{9,... | collective-permute-start | bytes 1179656 | tf_op jit(solution)/shard_map/ppermute | solution.py:203
  85.9 1.9 %collective-permute-start.3 = (bf16[4,64,1536]{2,1,0:T(8,128)(2,1)S(1)}, bf16[4,64,1536]{2,1,0:T(8,128)(2,1)S(1)}, u32[]{:S(2)}, u32[]{:S(2)}) collective-permute-start(bf16[4,64,1536]{2,1,0:T(8,128)(2,1)S(1)} %bitcast.26), channel_id=1, source_target_pairs={{0,32},{32,0},{64,96},{96,64},{128,160},{160,128},{192,224},{224,1... | collective-permute-start | bytes 2359304 | tf_op jit(solution)/shard_map/ppermute | solution.py:187
  87.8 12.3 %all-gather.1 = bf16[128,1024]{1,0:T(8,128)(2,1)S(1)} all-gather(bf16[32,1024]{1,0:T(8,128)(2,1)S(1)} %copy-done.5), channel_id=3, replica_groups={{0,128,256,384},{32,160,288,416},{64,192,320,448},{96,224,352,480},{1,1..., dimensions={0}, use_global_device_ids=true | all-gather | bytes 327680 | tf_op jit(solution)/shard_map/all_gather | solution.py:210
  100.1 1.9 %collective-permute-start.4 = (bf16[4,64,1536]{2,1,0:T(8,128)(2,1)S(1)}, bf16[4,64,1536]{2,1,0:T(8,128)(2,1)S(1)}, u32[]{:S(2)}, u32[]{:S(2)}) collective-permute-start(bf16[4,64,1536]{2,1,0:T(8,128)(2,1)S(1)} %constant_dynamic-update-slice_fusion.refs_2_), channel_id=1, source_target_pairs={{0,32},{32,0},{64,96},{96,64},{128,160},{160,128},{192,224},{224,1... | collective-permute-start | bytes 2359304 | tf_op jit(solution)/shard_map/ppermute | solution.py:187
  102.1 2.2 %collective-permute-done.4.refs_3_ = bf16[4,64,1536]{2,1,0:T(8,128)(2,1)S(1)} collective-permute-done((bf16[4,64,1536]{2,1,0:T(8,128)(2,1)S(1)}, bf16[4,64,1536]{2,1,0:T(8,128)(2,1)S(1)}, u32[]{:S(2)}, u32[]{:S(2)}) %collective-permute-start.4) | collective-permute-done | bytes 786464 | tf_op jit(solution)/shard_map/ppermute | solution.py:187
  104.3 0.8 shard_map.77.placed
  105.1 15.5 %all-to-all-done.1 = bf16[32,16,1024]{2,1,0:T(8,128)(2,1)} async-done(((bf16[32,16,1024]{2,1,0:T(8,128)(2,1)}), bf16[32,16,1024]{2,1,0:T(8,128)(2,1)}, u32[]{:S(2)}, u32[]{:S(2)}) %all-to-all-start.1) | async-done | bytes 1048608 | tf_op jit(solution)/shard_map/all_to_all | solution.py:232
  120.7 4.8 %shard_map.78 = bf16[512,512]{1,0:T(8,128)(2,1)S(1)} custom-call(bf16[512,1024]{1,0:T(8,128)(2,1)} %bitcast.6.middle, f32[1,1024]{1,0:T(1,128)S(1)} %bitcast.37, bf16[4,2,2,64,1536]{4,3,2,1,0:T(8,128)(2,1)S(1)} %shard_map.77.placed), custom_call_target="tpu_custom_call" | custom-call | flops 4000000000 | bytes 4194304 | tf_op jit(solution)/shard_map/pallas_call | solution.py:171
  126.3 4.4 %all-to-all-start.2 = ((bf16[32,16,512]{2,1,0:T(8,128)(2,1)}), bf16[32,16,512]{2,1,0:T(8,128)(2,1)S(1)}, u32[]{:S(2)}, u32[]{:S(2)}) async-start(bf16[32,16,512]{2,1,0:T(8,128)(2,1)} %bitcast.33), calls=%async_computation.2 | async-start | bytes 1048576 | tf_op jit(solution)/shard_map/all_to_all | solution.py:232
  130.8 2.8 %collective-permute-start.5 = (bf16[4,32,1024]{2,1,0:T(8,128)(2,1)S(1)}, bf16[4,32,1024]{2,1,0:T(8,128)(2,1)S(1)}, u32[]{:S(2)}, u32[]{:S(2)}) collective-permute-start(bf16[4,32,1024]{2,1,0:T(8,128)(2,1)S(1)} %bitcast.28), channel_id=1, source_target_pairs={{0,64},{32,96},{64,0},{96,32},{128,192},{160,224},{192,128},{224,1... | collective-permute-start | bytes 786440 | tf_op jit(solution)/shard_map/ppermute | solution.py:187
  133.6 8.0 %collective-permute-done.5.refs_2_ = bf16[4,32,1024]{2,1,0:T(8,128)(2,1)S(1)} collective-permute-done((bf16[4,32,1024]{2,1,0:T(8,128)(2,1)S(1)}, bf16[4,32,1024]{2,1,0:T(8,128)(2,1)S(1)}, u32[]{:S(2)}, u32[]{:S(2)}) %collective-permute-start.5) | collective-permute-done | bytes 262176 | tf_op jit(solution)/shard_map/ppermute | solution.py:187
  141.6 1.9 %collective-permute-start.6 = (bf16[2,4,32,1024]{3,2,1,0:T(8,128)(2,1)S(1)}, bf16[2,4,32,1024]{3,2,1,0:T(8,128)(2,1)S(1)}, u32[]{:S(2)}, u32[]{:S(2)}) collective-permute-start(bf16[2,4,32,1024]{3,2,1,0:T(8,128)(2,1)S(1)} %pad_maximum_fusion), channel_id=1, source_target_pairs={{0,32},{32,0},{64,96},{96,64},{128,160},{160,128},{192,224},{224,1... | collective-permute-start | bytes 1572872 | tf_op jit(solution)/shard_map/ppermute | solution.py:187
  143.5 1.3 shard_map.79
  146.2 18.3 %all-to-all-done.2 = bf16[32,16,512]{2,1,0:T(8,128)(2,1)S(1)} async-done(((bf16[32,16,512]{2,1,0:T(8,128)(2,1)}), bf16[32,16,512]{2,1,0:T(8,128)(2,1)S(1)}, u32[]{:S(2)}, u32[]{:S(2)}) %all-to-all-start.2) | async-done | bytes 524320 | tf_op jit(solution)/shard_map/all_to_all | solution.py:232
  164.4 1.7 %add_convert_fusion = bf16[512,1024]{1,0:T(8,128)(2,1)} fusion(bf16[512,1024]{1,0:T(8,128)(2,1)S(1)} %shard_map.79, bf16[512,512]{1,0:T(8,128)(2,1)S(1)} %bitcast.38, bf16[512,1024]{1,0:T(8,128)(2,1)S(1)} %bitcast.31), kind=kOutput, calls=%fused_computation | convolution fusion | flops 538443776 | bytes 3670016 | tf_op jit(solution)/shard_map/dot_general | solution.py:291
  (24 shorter events, 3.1 us)
Async XLA Ops:
  2.4 34.1 %copy-start.1 = (bf16[2,1,256,1024]{3,2,1,0:T(8,128)(2,1)S(1)}, bf16[2,1,256,1024]{3,2,1,0:T(8,128)(2,1)}, u32[]{:S(2)}) copy-start(bf16[2,1,256,1024]{3,2,1,0:T(8,128)(2,1)} %param.7) | copy-start | bytes 3145732
  2.4 34.1 %copy-start.2 = (f32[1024]{0:T(1024)S(1)}, f32[1024]{0:T(1024)}, u32[]{:S(2)}) copy-start(f32[1024]{0:T(1024)} %param.8) | copy-start | bytes 12292
  34.5 6.2 %collective-permute-start = (bf16[8,64,2048]{2,1,0:T(8,128)(2,1)S(1)}, bf16[8,64,2048]{2,1,0:T(8,128)(2,1)}, u32[]{:S(2)}, u32[]{:S(2)}) collective-permute-start(bf16[8,64,2048]{2,1,0:T(8,128)(2,1)S(1)} %all_to_all.15.weights.mine), channel_id=1, source_target_pairs={{0,32},{32,0},{64,96},{96,64},{128,160},{160,128},{192,224},{224,1... | collective-permute-start | bytes 6291464 | tf_op jit(solution)/shard_map/ppermute | solution.py:187
  46.5 17.9 %copy-start.4 = (bf16[64,1536]{1,0:T(8,128)(2,1)S(1)}, bf16[64,1536]{1,0:T(8,128)(2,1)}, u32[]{:S(2)}) copy-start(bf16[64,1536]{1,0:T(8,128)(2,1)} %param.12) | copy-start | bytes 589828
  46.5 41.3 %copy-start.5 = (bf16[32,1024]{1,0:T(8,128)(2,1)S(1)}, bf16[32,1024]{1,0:T(8,128)(2,1)}, u32[]{:S(2)}) copy-start(bf16[32,1024]{1,0:T(8,128)(2,1)} %param.13) | copy-start | bytes 196612
  46.5 74.2 %all-to-all-start.1 = ((bf16[32,16,1024]{2,1,0:T(8,128)(2,1)}), bf16[32,16,1024]{2,1,0:T(8,128)(2,1)}, u32[]{:S(2)}, u32[]{:S(2)}) async-start(bf16[32,16,1024]{2,1,0:T(8,128)(2,1)} %bitcast.5), calls=%async_computation.1 | async-start | bytes 2097152 | tf_op jit(solution)/shard_map/all_to_all | solution.py:232
  78.5 21.6 %collective-permute-start.1 = (bf16[2,64,1536]{2,1,0:T(8,128)(2,1)S(1)}, bf16[2,64,1536]{2,1,0:T(8,128)(2,1)S(1)}, u32[]{:S(2)}, u32[]{:S(2)}) collective-permute-start(bf16[2,64,1536]{2,1,0:T(8,128)(2,1)S(1)} %bitcast.40), channel_id=1, source_target_pairs={{0,64},{1,65},{2,66},{3,67},{4,68},{5,69},{6,70},{7,71},{8,72},{9,... | collective-permute-start | bytes 1179656 | tf_op jit(solution)/shard_map/ppermute | solution.py:203
  81.3 18.7 %collective-permute-start.2 = (bf16[2,64,1536]{2,1,0:T(8,128)(2,1)S(1)}, bf16[2,64,1536]{2,1,0:T(8,128)(2,1)S(1)}, u32[]{:S(2)}, u32[]{:S(2)}) collective-permute-start(bf16[2,64,1536]{2,1,0:T(8,128)(2,1)S(1)} %bitcast.39), channel_id=1, source_target_pairs={{0,80},{1,81},{2,82},{3,83},{4,84},{5,85},{6,86},{7,87},{8,88},{9,... | collective-permute-start | bytes 1179656 | tf_op jit(solution)/shard_map/ppermute | solution.py:203
  85.9 16.2 %collective-permute-start.3 = (bf16[4,64,1536]{2,1,0:T(8,128)(2,1)S(1)}, bf16[4,64,1536]{2,1,0:T(8,128)(2,1)S(1)}, u32[]{:S(2)}, u32[]{:S(2)}) collective-permute-start(bf16[4,64,1536]{2,1,0:T(8,128)(2,1)S(1)} %bitcast.26), channel_id=1, source_target_pairs={{0,32},{32,0},{64,96},{96,64},{128,160},{160,128},{192,224},{224,1... | collective-permute-start | bytes 2359304 | tf_op jit(solution)/shard_map/ppermute | solution.py:187
  100.1 20.6 %copy-start.3 = (f32[1024]{0:T(1024)S(1)}, f32[1024]{0:T(1024)}, u32[]{:S(2)}) copy-start(f32[1024]{0:T(1024)} %param.11) | copy-start | bytes 12292
  100.1 4.2 %collective-permute-start.4 = (bf16[4,64,1536]{2,1,0:T(8,128)(2,1)S(1)}, bf16[4,64,1536]{2,1,0:T(8,128)(2,1)S(1)}, u32[]{:S(2)}, u32[]{:S(2)}) collective-permute-start(bf16[4,64,1536]{2,1,0:T(8,128)(2,1)S(1)} %constant_dynamic-update-slice_fusion.refs_2_), channel_id=1, source_target_pairs={{0,32},{32,0},{64,96},{96,64},{128,160},{160,128},{192,224},{224,1... | collective-permute-start | bytes 2359304 | tf_op jit(solution)/shard_map/ppermute | solution.py:187
  125.5 0.8 copy-start
  126.3 38.1 %all-to-all-start.2 = ((bf16[32,16,512]{2,1,0:T(8,128)(2,1)}), bf16[32,16,512]{2,1,0:T(8,128)(2,1)S(1)}, u32[]{:S(2)}, u32[]{:S(2)}) async-start(bf16[32,16,512]{2,1,0:T(8,128)(2,1)} %bitcast.33), calls=%async_computation.2 | async-start | bytes 1048576 | tf_op jit(solution)/shard_map/all_to_all | solution.py:232
  130.8 10.8 %collective-permute-start.5 = (bf16[4,32,1024]{2,1,0:T(8,128)(2,1)S(1)}, bf16[4,32,1024]{2,1,0:T(8,128)(2,1)S(1)}, u32[]{:S(2)}, u32[]{:S(2)}) collective-permute-start(bf16[4,32,1024]{2,1,0:T(8,128)(2,1)S(1)} %bitcast.28), channel_id=1, source_target_pairs={{0,64},{32,96},{64,0},{96,32},{128,192},{160,224},{192,128},{224,1... | collective-permute-start | bytes 786440 | tf_op jit(solution)/shard_map/ppermute | solution.py:187
  141.6 3.8 %collective-permute-start.6 = (bf16[2,4,32,1024]{3,2,1,0:T(8,128)(2,1)S(1)}, bf16[2,4,32,1024]{3,2,1,0:T(8,128)(2,1)S(1)}, u32[]{:S(2)}, u32[]{:S(2)}) collective-permute-start(bf16[2,4,32,1024]{3,2,1,0:T(8,128)(2,1)S(1)} %pad_maximum_fusion), channel_id=1, source_target_pairs={{0,32},{32,0},{64,96},{96,64},{128,160},{160,128},{192,224},{224,1... | collective-permute-start | bytes 1572872 | tf_op jit(solution)/shard_map/ppermute | solution.py:187

commit v13 on v12

--- a/solution.py
+++ b/solution.py
@@ -11,6 +11,7 @@
 HEADS = 8
 INNER = 512
 EPSILON = 1e-06
+LOG2_E = 1.4426950408889634
 BF16, F32 = jnp.bfloat16, jnp.float32
 GROUP = 8
 PAIR = 2 * HEAD
@@ -38,7 +39,7 @@
             scores = lax.dot_general(own, keys, (((1,), (1,)), ((), ())), preferred_element_type=F32)
             if same is not None:
                 scores = jnp.where(same, scores, -1e30)
-            exponent = jnp.exp(scores - jnp.max(scores, axis=-1, keepdims=True))
+            exponent = jnp.exp2(scores - jnp.max(scores, axis=-1, keepdims=True))
             summed = jnp.dot(exponent.astype(BF16), values, preferred_element_type=F32)
             halves.append(summed[:, :PAIR] / summed[:, PAIR:])
         outs.append(jnp.where(low, halves[0], halves[1]))
@@ -50,17 +51,17 @@
         columns = pl.ds(piece * 256, 256)
         value = product(columns)
         if piece < INNER // 256:
-            value = value * HEAD**-0.5
+            value = value * (HEAD**-0.5 * LOG2_E)
         store(columns, value)
 
 
-def pack_kernel(qkv, out, packed):
+def pack_kernel(qkv, out, packed, joined, sems):
     depth, width = qkv.shape
     half = out.shape[1] // 2
-    for index in range(packed.shape[0]):
-        packed[index, :, pl.ds(0, width)] = qkv[...]
-        packed[index, pl.ds(0, depth // 2), pl.ds(width, half)] = out[:, pl.ds(0, half)]
-        packed[index, pl.ds(depth // 2, depth // 2), pl.ds(width, half)] = out[:, pl.ds(half, half)]
+    joined[:, pl.ds(0, width)] = qkv[...]
+    joined[pl.ds(0, depth // 2), pl.ds(width, half)] = out[:, pl.ds(0, half)]
+    joined[pl.ds(depth // 2, depth // 2), pl.ds(width, half)] = out[:, pl.ds(half, half)]
+    wait(run([pltpu.make_async_copy(joined, packed.at[index], sems.at[index]) for index in range(packed.shape[0])]))
 
 
 def run(copies):
@@ -165,14 +166,14 @@
     context[...] = jnp.concatenate(outs, axis=1).reshape(rows, INNER).astype(BF16)
 
 
-def kernel_call(body, kinds, out, operands, scratch=(), gflops=0, mib=4, room=24):
+def kernel_call(body, kinds, out, operands, scratch=(), gflops=0, mib=4, room=24, away=pltpu.VMEM):
     near = pl.BlockSpec(memory_space=pltpu.VMEM)
     specs = {"s": pl.BlockSpec(memory_space=pltpu.SMEM), "v": near, "h": pl.BlockSpec(memory_space=pl.ANY)}
     return pl.pallas_call(
         body,
         out_shape=out,
         in_specs=[specs[kind] for kind in kinds],
-        out_specs=jax.tree.map(lambda _: near, out),
+        out_specs=jax.tree.map(lambda _: pl.BlockSpec(memory_space=away), out),
         scratch_shapes=scratch,
         compiler_params=pltpu.CompilerParams(vmem_limit_bytes=room * MIB),
         cost_estimate=pl.CostEstimate(flops=int(gflops * 1e9), bytes_accessed=mib * MIB, transcendentals=0),
@@ -241,7 +242,13 @@
         )
 
     packed = kernel_call(
-        pack_kernel, "vv", shape((parts, part, 4 * INNER), BF16), (spatial_qkv, spatial_out), room=60
+        pack_kernel,
+        "vv",
+        shape((parts, part, 4 * INNER), BF16),
+        (spatial_qkv, spatial_out),
+        [pltpu.VMEM((part, 4 * INNER), BF16), pltpu.SemaphoreType.DMA((parts,))],
+        room=60,
+        away=pl.ANY,
     )
     mine = lax.all_to_all(packed, "fsdp", 0, 0, axis_index_groups=cores, tiled=True)
     normed, normed_other = kernel_call(

time: 167 us -> 167 us (level)
  no operation moved by 1% of the time
where the time goes in v13:
time: 167 us; the launch traced here: 166 us
  blocking collectives  58.4 us (35%)
  waiting for transfers between devices  45.4 us (27%)
  starting transfers between devices  40.1 us (24%)
  Pallas kernels  19.1 us (11%)
  matrix products  1.69 us (1%)
    all_to_all x2, waiting for transfers between devices, exchanged(): lax.all_to_all(sent, 'tm', split_axis=0, concat_axis=0, tiled=True)  33.8 us
    all_to_all x1, blocking collectives, shards(): lax.all_to_all(packed, 'fsdp', 0, 0, axis_index_groups=cores, tiled=True)  32.1 us
    all_gather x2, blocking collectives, along_x(): return lax.all_gather(shard, 'fsdp', axis_index_groups=lines)  26.3 us
    all_to_all x2, starting transfers between devices, exchanged(): lax.all_to_all(sent, 'tm', split_axis=0, concat_axis=0, tiled=True)  22.3 us
    pallas_call x8, Pallas kernels, kernel_call(): pl.pallas_call(body, out_shape=out, in_specs=[specs[kind] for kind in kin...  19.1 us
    ppermute x5, waiting for transfers between devices, moved(): return lax.ppermute(array, 'fsdp', pairs)  11.6 us
    ppermute x5, starting transfers between devices, moved(): return lax.ppermute(array, 'fsdp', pairs)  10.4 us
    ppermute x2, starting transfers between devices, other_yl(): pieces.append(lax.ppermute(piece, ('fsdp', 'tm'), pairs))  7.36 us
  transfers between devices with their start and end apart: 9, of which 6 were waited for; matrix products, arithmetic and copies ran while one was open for 0% of the time, Pallas kernels for 4%

profile of v13, /device:TPU:32, one launch (start us, length us, event | category | flops | bytes accessed | tf_op | source)
XLA Modules:
  0.0 166.0 jit_solution(15941953761353840186)
XLA Ops:
  0.0 2.4 %shard_map.74 = bf16[8,64,2048]{2,1,0:T(8,128)(2,1)} custom-call(bf16[64,1536]{1,0:T(8,128)(2,1)} %qkv.1, bf16[32,1024]{1,0:T(8,128)(2,1)} %out.1), custom_call_target="tpu_custom_call" | custom-call | bytes 4194304 | tf_op jit(solution)/shard_map/pallas_call | solution.py:172
  2.4 32.1 %all_to_all.15.weights.mine = bf16[8,64,2048]{2,1,0:T(8,128)(2,1)S(1)} all-to-all(bf16[8,64,2048]{2,1,0:T(8,128)(2,1)} %shard_map.74), channel_id=1, replica_groups={{0,64,128,192,256,320,384,448},{32,96,160,224,288,352,416,480},{1,65,12..., dimensions={0} | all-to-all | bytes 4194304 | tf_op jit(solution)/shard_map/all_to_all | solution.py:253
  34.5 1.9 %collective-permute-start = (bf16[8,64,2048]{2,1,0:T(8,128)(2,1)S(1)}, bf16[8,64,2048]{2,1,0:T(8,128)(2,1)}, u32[]{:S(2)}, u32[]{:S(2)}) collective-permute-start(bf16[8,64,2048]{2,1,0:T(8,128)(2,1)S(1)} %all_to_all.15.weights.mine), channel_id=1, source_target_pairs={{0,32},{32,0},{64,96},{96,64},{128,160},{160,128},{192,224},{224,1... | collective-permute-start | bytes 6291464 | tf_op jit(solution)/shard_map/ppermute | solution.py:188
  36.5 2.3 %shard_map.73 = (bf16[512,512]{1,0:T(8,128)(2,1)S(1)}, bf16[512,512]{1,0:T(8,128)(2,1)S(1)}) custom-call(s32[3]{0:T(128)S(1)} %pad_add_fusion.here, bf16[512,1024]{1,0:T(8,128)(2,1)S(1)} %bitcast.34, f32[1,1024]{1,0:T(1,128)S(1)} %bitcast.36), custom_call_target="tpu_custom_call" | custom-call | flops 2000000000 | bytes 4194304 | tf_op jit(solution)/shard_map/pallas_call | solution.py:172
  38.9 1.0 shard_map.75.partial
  40.7 5.8 %shard_map.76.source = bf16[512,1024]{1,0:T(8,128)(2,1)} custom-call(s32[3]{0:T(128)S(1)} %pad_add_fusion.here, bf16[512,1024]{1,0:T(8,128)(2,1)S(1)} %bitcast.35, f32[512,1536]{1,0:T(8,128)S(1)} %shard_map.75.partial, bf16[512,512]{1,0:T(8,128)(2,1)S(1)} %get-tuple-element.19.normed, bf16[8,64,2048]{2,1,0:T(8,128)(2,1)S(1)} %all_to_all.15.weights.mine, ...), custom_call_target="tpu_custom_call" | custom-call | flops 3000000000 | bytes 4194304 | tf_op jit(solution)/shard_map/pallas_call | solution.py:172
  46.5 17.9 %all-to-all-start.1 = ((bf16[32,16,1024]{2,1,0:T(8,128)(2,1)}), bf16[32,16,1024]{2,1,0:T(8,128)(2,1)}, u32[]{:S(2)}, u32[]{:S(2)}) async-start(bf16[32,16,1024]{2,1,0:T(8,128)(2,1)} %bitcast.5), calls=%async_computation.1 | async-start | bytes 2097152 | tf_op jit(solution)/shard_map/all_to_all | solution.py:233
  64.4 14.0 %all-gather = bf16[256,1536]{1,0:T(8,128)(2,1)S(1)} all-gather(bf16[64,1536]{1,0:T(8,128)(2,1)S(1)} %copy-done.4), channel_id=2, replica_groups={{0,128,256,384},{32,160,288,416},{64,192,320,448},{96,224,352,480},{1,1..., dimensions={0}, use_global_device_ids=true | all-gather | bytes 983040 | tf_op jit(solution)/shard_map/all_gather | solution.py:211
  78.5 2.8 %collective-permute-start.1 = (bf16[2,64,1536]{2,1,0:T(8,128)(2,1)S(1)}, bf16[2,64,1536]{2,1,0:T(8,128)(2,1)S(1)}, u32[]{:S(2)}, u32[]{:S(2)}) collective-permute-start(bf16[2,64,1536]{2,1,0:T(8,128)(2,1)S(1)} %bitcast.40), channel_id=1, source_target_pairs={{0,64},{1,65},{2,66},{3,67},{4,68},{5,69},{6,70},{7,71},{8,72},{9,... | collective-permute-start | bytes 1179656 | tf_op jit(solution)/shard_map/ppermute | solution.py:204
  81.3 4.5 %collective-permute-start.2 = (bf16[2,64,1536]{2,1,0:T(8,128)(2,1)S(1)}, bf16[2,64,1536]{2,1,0:T(8,128)(2,1)S(1)}, u32[]{:S(2)}, u32[]{:S(2)}) collective-permute-start(bf16[2,64,1536]{2,1,0:T(8,128)(2,1)S(1)} %bitcast.39), channel_id=1, source_target_pairs={{0,80},{1,81},{2,82},{3,83},{4,84},{5,85},{6,86},{7,87},{8,88},{9,... | collective-permute-start | bytes 1179656 | tf_op jit(solution)/shard_map/ppermute | solution.py:204
  85.8 1.9 %collective-permute-start.3 = (bf16[4,64,1536]{2,1,0:T(8,128)(2,1)S(1)}, bf16[4,64,1536]{2,1,0:T(8,128)(2,1)S(1)}, u32[]{:S(2)}, u32[]{:S(2)}) collective-permute-start(bf16[4,64,1536]{2,1,0:T(8,128)(2,1)S(1)} %bitcast.26), channel_id=1, source_target_pairs={{0,32},{32,0},{64,96},{96,64},{128,160},{160,128},{192,224},{224,1... | collective-permute-start | bytes 2359304 | tf_op jit(solution)/shard_map/ppermute | solution.py:188
  87.8 12.3 %all-gather.1 = bf16[128,1024]{1,0:T(8,128)(2,1)S(1)} all-gather(bf16[32,1024]{1,0:T(8,128)(2,1)S(1)} %copy-done.5), channel_id=3, replica_groups={{0,128,256,384},{32,160,288,416},{64,192,320,448},{96,224,352,480},{1,1..., dimensions={0}, use_global_device_ids=true | all-gather | bytes 327680 | tf_op jit(solution)/shard_map/all_gather | solution.py:211
  100.1 1.9 %collective-permute-start.4 = (bf16[4,64,1536]{2,1,0:T(8,128)(2,1)S(1)}, bf16[4,64,1536]{2,1,0:T(8,128)(2,1)S(1)}, u32[]{:S(2)}, u32[]{:S(2)}) collective-permute-start(bf16[4,64,1536]{2,1,0:T(8,128)(2,1)S(1)} %constant_dynamic-update-slice_fusion.refs_2_), channel_id=1, source_target_pairs={{0,32},{32,0},{64,96},{96,64},{128,160},{160,128},{192,224},{224,1... | collective-permute-start | bytes 2359304 | tf_op jit(solution)/shard_map/ppermute | solution.py:188
  102.0 2.2 %collective-permute-done.4.refs_3_ = bf16[4,64,1536]{2,1,0:T(8,128)(2,1)S(1)} collective-permute-done((bf16[4,64,1536]{2,1,0:T(8,128)(2,1)S(1)}, bf16[4,64,1536]{2,1,0:T(8,128)(2,1)S(1)}, u32[]{:S(2)}, u32[]{:S(2)}) %collective-permute-start.4) | collective-permute-done | bytes 786464 | tf_op jit(solution)/shard_map/ppermute | solution.py:188
  104.3 0.8 shard_map.77.placed
  105.1 15.6 %all-to-all-done.1 = bf16[32,16,1024]{2,1,0:T(8,128)(2,1)} async-done(((bf16[32,16,1024]{2,1,0:T(8,128)(2,1)}), bf16[32,16,1024]{2,1,0:T(8,128)(2,1)}, u32[]{:S(2)}, u32[]{:S(2)}) %all-to-all-start.1) | async-done | bytes 1048608 | tf_op jit(solution)/shard_map/all_to_all | solution.py:233
  120.7 4.8 %shard_map.78 = bf16[512,512]{1,0:T(8,128)(2,1)S(1)} custom-call(bf16[512,1024]{1,0:T(8,128)(2,1)} %bitcast.6.middle, f32[1,1024]{1,0:T(1,128)S(1)} %bitcast.37, bf16[4,2,2,64,1536]{4,3,2,1,0:T(8,128)(2,1)S(1)} %shard_map.77.placed), custom_call_target="tpu_custom_call" | custom-call | flops 4000000000 | bytes 4194304 | tf_op jit(solution)/shard_map/pallas_call | solution.py:172
  126.3 4.4 %all-to-all-start.2 = ((bf16[32,16,512]{2,1,0:T(8,128)(2,1)}), bf16[32,16,512]{2,1,0:T(8,128)(2,1)S(1)}, u32[]{:S(2)}, u32[]{:S(2)}) async-start(bf16[32,16,512]{2,1,0:T(8,128)(2,1)} %bitcast.33), calls=%async_computation.2 | async-start | bytes 1048576 | tf_op jit(solution)/shard_map/all_to_all | solution.py:233
  130.7 2.8 %collective-permute-start.5 = (bf16[4,32,1024]{2,1,0:T(8,128)(2,1)S(1)}, bf16[4,32,1024]{2,1,0:T(8,128)(2,1)S(1)}, u32[]{:S(2)}, u32[]{:S(2)}) collective-permute-start(bf16[4,32,1024]{2,1,0:T(8,128)(2,1)S(1)} %bitcast.28), channel_id=1, source_target_pairs={{0,64},{32,96},{64,0},{96,32},{128,192},{160,224},{192,128},{224,1... | collective-permute-start | bytes 786440 | tf_op jit(solution)/shard_map/ppermute | solution.py:188
  133.5 8.0 %collective-permute-done.5.refs_2_ = bf16[4,32,1024]{2,1,0:T(8,128)(2,1)S(1)} collective-permute-done((bf16[4,32,1024]{2,1,0:T(8,128)(2,1)S(1)}, bf16[4,32,1024]{2,1,0:T(8,128)(2,1)S(1)}, u32[]{:S(2)}, u32[]{:S(2)}) %collective-permute-start.5) | collective-permute-done | bytes 262176 | tf_op jit(solution)/shard_map/ppermute | solution.py:188
  141.6 1.9 %collective-permute-start.6 = (bf16[2,4,32,1024]{3,2,1,0:T(8,128)(2,1)S(1)}, bf16[2,4,32,1024]{3,2,1,0:T(8,128)(2,1)S(1)}, u32[]{:S(2)}, u32[]{:S(2)}) collective-permute-start(bf16[2,4,32,1024]{3,2,1,0:T(8,128)(2,1)S(1)} %pad_maximum_fusion), channel_id=1, source_target_pairs={{0,32},{32,0},{64,96},{96,64},{128,160},{160,128},{192,224},{224,1... | collective-permute-start | bytes 1572872 | tf_op jit(solution)/shard_map/ppermute | solution.py:188
  143.5 1.3 shard_map.79
  146.1 18.3 %all-to-all-done.2 = bf16[32,16,512]{2,1,0:T(8,128)(2,1)S(1)} async-done(((bf16[32,16,512]{2,1,0:T(8,128)(2,1)}), bf16[32,16,512]{2,1,0:T(8,128)(2,1)S(1)}, u32[]{:S(2)}, u32[]{:S(2)}) %all-to-all-start.2) | async-done | bytes 524320 | tf_op jit(solution)/shard_map/all_to_all | solution.py:233
  164.4 1.7 %add_convert_fusion = bf16[512,1024]{1,0:T(8,128)(2,1)} fusion(bf16[512,1024]{1,0:T(8,128)(2,1)S(1)} %shard_map.79, bf16[512,512]{1,0:T(8,128)(2,1)S(1)} %bitcast.38, bf16[512,1024]{1,0:T(8,128)(2,1)S(1)} %bitcast.31), kind=kOutput, calls=%fused_computation | convolution fusion | flops 538443776 | bytes 3670016 | tf_op jit(solution)/shard_map/dot_general | solution.py:298
  (24 shorter events, 3.2 us)
Async XLA Ops:
  2.4 34.2 %copy-start.1 = (bf16[2,1,256,1024]{3,2,1,0:T(8,128)(2,1)S(1)}, bf16[2,1,256,1024]{3,2,1,0:T(8,128)(2,1)}, u32[]{:S(2)}) copy-start(bf16[2,1,256,1024]{3,2,1,0:T(8,128)(2,1)} %param.7) | copy-start | bytes 3145732
  2.4 34.1 %copy-start.2 = (f32[1024]{0:T(1024)S(1)}, f32[1024]{0:T(1024)}, u32[]{:S(2)}) copy-start(f32[1024]{0:T(1024)} %param.8) | copy-start | bytes 12292
  34.5 6.2 %collective-permute-start = (bf16[8,64,2048]{2,1,0:T(8,128)(2,1)S(1)}, bf16[8,64,2048]{2,1,0:T(8,128)(2,1)}, u32[]{:S(2)}, u32[]{:S(2)}) collective-permute-start(bf16[8,64,2048]{2,1,0:T(8,128)(2,1)S(1)} %all_to_all.15.weights.mine), channel_id=1, source_target_pairs={{0,32},{32,0},{64,96},{96,64},{128,160},{160,128},{192,224},{224,1... | collective-permute-start | bytes 6291464 | tf_op jit(solution)/shard_map/ppermute | solution.py:188
  46.5 17.9 %copy-start.4 = (bf16[64,1536]{1,0:T(8,128)(2,1)S(1)}, bf16[64,1536]{1,0:T(8,128)(2,1)}, u32[]{:S(2)}) copy-start(bf16[64,1536]{1,0:T(8,128)(2,1)} %param.12) | copy-start | bytes 589828
  46.5 41.3 %copy-start.5 = (bf16[32,1024]{1,0:T(8,128)(2,1)S(1)}, bf16[32,1024]{1,0:T(8,128)(2,1)}, u32[]{:S(2)}) copy-start(bf16[32,1024]{1,0:T(8,128)(2,1)} %param.13) | copy-start | bytes 196612
  46.5 74.2 %all-to-all-start.1 = ((bf16[32,16,1024]{2,1,0:T(8,128)(2,1)}), bf16[32,16,1024]{2,1,0:T(8,128)(2,1)}, u32[]{:S(2)}, u32[]{:S(2)}) async-start(bf16[32,16,1024]{2,1,0:T(8,128)(2,1)} %bitcast.5), calls=%async_computation.1 | async-start | bytes 2097152 | tf_op jit(solution)/shard_map/all_to_all | solution.py:233
  78.5 21.6 %collective-permute-start.1 = (bf16[2,64,1536]{2,1,0:T(8,128)(2,1)S(1)}, bf16[2,64,1536]{2,1,0:T(8,128)(2,1)S(1)}, u32[]{:S(2)}, u32[]{:S(2)}) collective-permute-start(bf16[2,64,1536]{2,1,0:T(8,128)(2,1)S(1)} %bitcast.40), channel_id=1, source_target_pairs={{0,64},{1,65},{2,66},{3,67},{4,68},{5,69},{6,70},{7,71},{8,72},{9,... | collective-permute-start | bytes 1179656 | tf_op jit(solution)/shard_map/ppermute | solution.py:204
  81.3 18.7 %collective-permute-start.2 = (bf16[2,64,1536]{2,1,0:T(8,128)(2,1)S(1)}, bf16[2,64,1536]{2,1,0:T(8,128)(2,1)S(1)}, u32[]{:S(2)}, u32[]{:S(2)}) collective-permute-start(bf16[2,64,1536]{2,1,0:T(8,128)(2,1)S(1)} %bitcast.39), channel_id=1, source_target_pairs={{0,80},{1,81},{2,82},{3,83},{4,84},{5,85},{6,86},{7,87},{8,88},{9,... | collective-permute-start | bytes 1179656 | tf_op jit(solution)/shard_map/ppermute | solution.py:204
  85.8 16.2 %collective-permute-start.3 = (bf16[4,64,1536]{2,1,0:T(8,128)(2,1)S(1)}, bf16[4,64,1536]{2,1,0:T(8,128)(2,1)S(1)}, u32[]{:S(2)}, u32[]{:S(2)}) collective-permute-start(bf16[4,64,1536]{2,1,0:T(8,128)(2,1)S(1)} %bitcast.26), channel_id=1, source_target_pairs={{0,32},{32,0},{64,96},{96,64},{128,160},{160,128},{192,224},{224,1... | collective-permute-start | bytes 2359304 | tf_op jit(solution)/shard_map/ppermute | solution.py:188
  100.1 20.6 %copy-start.3 = (f32[1024]{0:T(1024)S(1)}, f32[1024]{0:T(1024)}, u32[]{:S(2)}) copy-start(f32[1024]{0:T(1024)} %param.11) | copy-start | bytes 12292
  100.1 4.2 %collective-permute-start.4 = (bf16[4,64,1536]{2,1,0:T(8,128)(2,1)S(1)}, bf16[4,64,1536]{2,1,0:T(8,128)(2,1)S(1)}, u32[]{:S(2)}, u32[]{:S(2)}) collective-permute-start(bf16[4,64,1536]{2,1,0:T(8,128)(2,1)S(1)} %constant_dynamic-update-slice_fusion.refs_2_), channel_id=1, source_target_pairs={{0,32},{32,0},{64,96},{96,64},{128,160},{160,128},{192,224},{224,1... | collective-permute-start | bytes 2359304 | tf_op jit(solution)/shard_map/ppermute | solution.py:188
  125.5 0.8 copy-start
  126.3 38.1 %all-to-all-start.2 = ((bf16[32,16,512]{2,1,0:T(8,128)(2,1)}), bf16[32,16,512]{2,1,0:T(8,128)(2,1)S(1)}, u32[]{:S(2)}, u32[]{:S(2)}) async-start(bf16[32,16,512]{2,1,0:T(8,128)(2,1)} %bitcast.33), calls=%async_computation.2 | async-start | bytes 1048576 | tf_op jit(solution)/shard_map/all_to_all | solution.py:233
  130.7 10.8 %collective-permute-start.5 = (bf16[4,32,1024]{2,1,0:T(8,128)(2,1)S(1)}, bf16[4,32,1024]{2,1,0:T(8,128)(2,1)S(1)}, u32[]{:S(2)}, u32[]{:S(2)}) collective-permute-start(bf16[4,32,1024]{2,1,0:T(8,128)(2,1)S(1)} %bitcast.28), channel_id=1, source_target_pairs={{0,64},{32,96},{64,0},{96,32},{128,192},{160,224},{192,128},{224,1... | collective-permute-start | bytes 786440 | tf_op jit(solution)/shard_map/ppermute | solution.py:188
  141.6 3.8 %collective-permute-start.6 = (bf16[2,4,32,1024]{3,2,1,0:T(8,128)(2,1)S(1)}, bf16[2,4,32,1024]{3,2,1,0:T(8,128)(2,1)S(1)}, u32[]{:S(2)}, u32[]{:S(2)}) collective-permute-start(bf16[2,4,32,1024]{3,2,1,0:T(8,128)(2,1)S(1)} %pad_maximum_fusion), channel_id=1, source_target_pairs={{0,32},{32,0},{64,96},{96,64},{128,160},{160,128},{192,224},{224,1... | collective-permute-start | bytes 1572872 | tf_op jit(solution)/shard_map/ppermute | solution.py:188

commit v14 on v12

--- a/solution.py
+++ b/solution.py
@@ -74,25 +74,24 @@
         copy.wait()
 
 
-def norm_kernel(here, tokens, gain, mine, other):
+def half_kernel(here, tokens, gain, weights, partial, other):
     normed = norm_rows(tokens[...].astype(F32), gain[...]).astype(BF16)
-    depth, width = normed.shape[1], mine.shape[1]
+    depth, width = normed.shape[1], other.shape[1]
     source = lax.broadcasted_iota(jnp.int32, (depth, width), 0)
     target = lax.broadcasted_iota(jnp.int32, (depth, width), 1)
     block = depth // 16
     first = target // block * (2 * block) + target % block
-    for out, core in ((mine, here[2]), (other, 1 - here[2])):
+
+    def columns_of(core):
         chosen = (source == first + core * block).astype(F32).astype(BF16)
-        out[...] = jnp.dot(normed, chosen, preferred_element_type=F32).astype(BF16)
-
-
-def half_kernel(normed, weights, partial):
-    depth = normed.shape[1]
+        return jnp.dot(normed, chosen, preferred_element_type=F32).astype(BF16)
+
+    other[...] = columns_of(1 - here[2])
+    mine = columns_of(here[2])
     for piece in range(partial.shape[1] // 256):
         columns = pl.ds(piece * 256, 256)
-        partial[:, columns] = jnp.dot(
-            normed[...], weights[:, :, columns].reshape(depth, 256), preferred_element_type=F32
-        )
+        weight = weights[:, :, columns].reshape(width, 256)
+        partial[:, columns] = jnp.dot(mine, weight, preferred_element_type=F32)
 
 
 def spatial_kernel(here, tokens, partial, normed, mine, other, middle, out_ref, qkv, context, sems):
@@ -244,15 +243,13 @@
         pack_kernel, "vv", shape((parts, part, 4 * INNER), BF16), (spatial_qkv, spatial_out), room=60
     )
     mine = lax.all_to_all(packed, "fsdp", 0, 0, axis_index_groups=cores, tiled=True)
-    normed, normed_other = kernel_call(
-        norm_kernel,
-        "svv",
-        [shape((rows, depth // 2), BF16)] * 2,
-        (here, flat, spatial_gain.reshape(1, depth)),
-        gflops=2,
-        room=24,
-    )
-    partial = kernel_call(half_kernel, "vv", shape((rows, 3 * INNER), F32), (normed, mine), gflops=1, room=24)
+    partial, normed_other = kernel_call(
+        half_kernel,
+        "svvv",
+        [shape((rows, 3 * INNER), F32), shape((rows, depth // 2), BF16)],
+        (here, flat, spatial_gain.reshape(1, depth), mine),
+        gflops=3,
+    )
     middle = kernel_call(
         spatial_kernel,
         "svvvvv",

time: 167 us -> 167 us (level)
    pallas_call x8 -> x7, Pallas kernels: 19.2 us -> 19 us  [kernel_call(): pl.pallas_call(body, out_shape=out, in_specs=[specs[kind] for kind in kin...]
where the time goes in v14:
time: 167 us; the launch traced here: 166 us
  blocking collectives  58.3 us (35%)
  waiting for transfers between devices  45.6 us (27%)
  starting transfers between devices  40.1 us (24%)
  Pallas kernels  19 us (11%)
  matrix products  1.68 us (1%)
    all_to_all x2, waiting for transfers between devices, exchanged(): lax.all_to_all(sent, 'tm', split_axis=0, concat_axis=0, tiled=True)  33.8 us
    all_to_all x1, blocking collectives, shards(): lax.all_to_all(packed, 'fsdp', 0, 0, axis_index_groups=cores, tiled=True)  32.1 us
    all_gather x2, blocking collectives, along_x(): return lax.all_gather(shard, 'fsdp', axis_index_groups=lines)  26.3 us
    all_to_all x2, starting transfers between devices, exchanged(): lax.all_to_all(sent, 'tm', split_axis=0, concat_axis=0, tiled=True)  22.3 us
    pallas_call x7, Pallas kernels, kernel_call(): pl.pallas_call(body, out_shape=out, in_specs=[specs[kind] for kind in kin...  19 us
    ppermute x5, waiting for transfers between devices, moved(): return lax.ppermute(array, 'fsdp', pairs)  11.8 us
    ppermute x5, starting transfers between devices, moved(): return lax.ppermute(array, 'fsdp', pairs)  10.4 us
    ppermute x2, starting transfers between devices, other_yl(): pieces.append(lax.ppermute(piece, ('fsdp', 'tm'), pairs))  7.36 us
  transfers between devices with their start and end apart: 9, of which 6 were waited for; matrix products, arithmetic and copies ran while one was open for 0% of the time, Pallas kernels for 4%

profile of v14, /device:TPU:32, one launch (start us, length us, event | category | flops | bytes accessed | tf_op | source)
XLA Modules:
  0.0 166.1 jit_solution(13116359743846338952)
XLA Ops:
  0.0 2.4 %shard_map.73 = bf16[8,64,2048]{2,1,0:T(8,128)(2,1)} custom-call(bf16[64,1536]{1,0:T(8,128)(2,1)} %qkv.1, bf16[32,1024]{1,0:T(8,128)(2,1)} %out.1), custom_call_target="tpu_custom_call" | custom-call | bytes 4194304 | tf_op jit(solution)/shard_map/pallas_call | solution.py:170
  2.4 32.1 %all_to_all.15.weights.mine = bf16[8,64,2048]{2,1,0:T(8,128)(2,1)S(1)} all-to-all(bf16[8,64,2048]{2,1,0:T(8,128)(2,1)} %shard_map.73), channel_id=1, replica_groups={{0,64,128,192,256,320,384,448},{32,96,160,224,288,352,416,480},{1,65,12..., dimensions={0} | all-to-all | bytes 4194304 | tf_op jit(solution)/shard_map/all_to_all | solution.py:245
  34.5 1.9 %collective-permute-start = (bf16[8,64,2048]{2,1,0:T(8,128)(2,1)S(1)}, bf16[8,64,2048]{2,1,0:T(8,128)(2,1)}, u32[]{:S(2)}, u32[]{:S(2)}) collective-permute-start(bf16[8,64,2048]{2,1,0:T(8,128)(2,1)S(1)} %all_to_all.15.weights.mine), channel_id=1, source_target_pairs={{0,32},{32,0},{64,96},{96,64},{128,160},{160,128},{192,224},{224,1... | collective-permute-start | bytes 6291464 | tf_op jit(solution)/shard_map/ppermute | solution.py:186
  36.5 3.2 %shard_map.74 = (f32[512,1536]{1,0:T(8,128)S(1)}, bf16[512,512]{1,0:T(8,128)(2,1)S(1)}) custom-call(s32[3]{0:T(128)S(1)} %pad_add_fusion.here, bf16[512,1024]{1,0:T(8,128)(2,1)S(1)} %bitcast.34, f32[1,1024]{1,0:T(1,128)S(1)} %bitcast.36, bf16[8,64,2048]{2,1,0:T(8,128)(2,1)S(1)} %all_to_all.15.weights.mine), custom_call_target="tpu_custom_call" | custom-call | flops 3000000000 | bytes 4194304 | tf_op jit(solution)/shard_map/pallas_call | solution.py:170
  39.7 1.0 collective-permute-done.other
  40.7 5.8 %shard_map.75.source = bf16[512,1024]{1,0:T(8,128)(2,1)} custom-call(s32[3]{0:T(128)S(1)} %pad_add_fusion.here, bf16[512,1024]{1,0:T(8,128)(2,1)S(1)} %bitcast.35, f32[512,1536]{1,0:T(8,128)S(1)} %get-tuple-element.18.partial, bf16[512,512]{1,0:T(8,128)(2,1)S(1)} %get-tuple-element.19.normed, bf16[8,64,2048]{2,1,0:T(8,128)(2,1)S(1)} %all_to_all.15.weights.mine, ...), custom_call_target="tpu_custom_call" | custom-call | flops 3000000000 | bytes 4194304 | tf_op jit(solution)/shard_map/pallas_call | solution.py:170
  46.5 17.9 %all-to-all-start.1 = ((bf16[32,16,1024]{2,1,0:T(8,128)(2,1)}), bf16[32,16,1024]{2,1,0:T(8,128)(2,1)}, u32[]{:S(2)}, u32[]{:S(2)}) async-start(bf16[32,16,1024]{2,1,0:T(8,128)(2,1)} %bitcast.5), calls=%async_computation.1 | async-start | bytes 2097152 | tf_op jit(solution)/shard_map/all_to_all | solution.py:231
  64.4 14.0 %all-gather = bf16[256,1536]{1,0:T(8,128)(2,1)S(1)} all-gather(bf16[64,1536]{1,0:T(8,128)(2,1)S(1)} %copy-done.4), channel_id=2, replica_groups={{0,128,256,384},{32,160,288,416},{64,192,320,448},{96,224,352,480},{1,1..., dimensions={0}, use_global_device_ids=true | all-gather | bytes 983040 | tf_op jit(solution)/shard_map/all_gather | solution.py:209
  78.5 2.8 %collective-permute-start.1 = (bf16[2,64,1536]{2,1,0:T(8,128)(2,1)S(1)}, bf16[2,64,1536]{2,1,0:T(8,128)(2,1)S(1)}, u32[]{:S(2)}, u32[]{:S(2)}) collective-permute-start(bf16[2,64,1536]{2,1,0:T(8,128)(2,1)S(1)} %bitcast.40), channel_id=1, source_target_pairs={{0,64},{1,65},{2,66},{3,67},{4,68},{5,69},{6,70},{7,71},{8,72},{9,... | collective-permute-start | bytes 1179656 | tf_op jit(solution)/shard_map/ppermute | solution.py:202
  81.3 4.5 %collective-permute-start.2 = (bf16[2,64,1536]{2,1,0:T(8,128)(2,1)S(1)}, bf16[2,64,1536]{2,1,0:T(8,128)(2,1)S(1)}, u32[]{:S(2)}, u32[]{:S(2)}) collective-permute-start(bf16[2,64,1536]{2,1,0:T(8,128)(2,1)S(1)} %bitcast.39), channel_id=1, source_target_pairs={{0,80},{1,81},{2,82},{3,83},{4,84},{5,85},{6,86},{7,87},{8,88},{9,... | collective-permute-start | bytes 1179656 | tf_op jit(solution)/shard_map/ppermute | solution.py:202
  85.9 1.9 %collective-permute-start.3 = (bf16[4,64,1536]{2,1,0:T(8,128)(2,1)S(1)}, bf16[4,64,1536]{2,1,0:T(8,128)(2,1)S(1)}, u32[]{:S(2)}, u32[]{:S(2)}) collective-permute-start(bf16[4,64,1536]{2,1,0:T(8,128)(2,1)S(1)} %bitcast.26), channel_id=1, source_target_pairs={{0,32},{32,0},{64,96},{96,64},{128,160},{160,128},{192,224},{224,1... | collective-permute-start | bytes 2359304 | tf_op jit(solution)/shard_map/ppermute | solution.py:186
  87.8 12.3 %all-gather.1 = bf16[128,1024]{1,0:T(8,128)(2,1)S(1)} all-gather(bf16[32,1024]{1,0:T(8,128)(2,1)S(1)} %copy-done.5), channel_id=3, replica_groups={{0,128,256,384},{32,160,288,416},{64,192,320,448},{96,224,352,480},{1,1..., dimensions={0}, use_global_device_ids=true | all-gather | bytes 327680 | tf_op jit(solution)/shard_map/all_gather | solution.py:209
  100.1 1.9 %collective-permute-start.4 = (bf16[4,64,1536]{2,1,0:T(8,128)(2,1)S(1)}, bf16[4,64,1536]{2,1,0:T(8,128)(2,1)S(1)}, u32[]{:S(2)}, u32[]{:S(2)}) collective-permute-start(bf16[4,64,1536]{2,1,0:T(8,128)(2,1)S(1)} %constant_dynamic-update-slice_fusion.refs_2_), channel_id=1, source_target_pairs={{0,32},{32,0},{64,96},{96,64},{128,160},{160,128},{192,224},{224,1... | collective-permute-start | bytes 2359304 | tf_op jit(solution)/shard_map/ppermute | solution.py:186
  102.1 2.2 %collective-permute-done.4.refs_3_ = bf16[4,64,1536]{2,1,0:T(8,128)(2,1)S(1)} collective-permute-done((bf16[4,64,1536]{2,1,0:T(8,128)(2,1)S(1)}, bf16[4,64,1536]{2,1,0:T(8,128)(2,1)S(1)}, u32[]{:S(2)}, u32[]{:S(2)}) %collective-permute-start.4) | collective-permute-done | bytes 786464 | tf_op jit(solution)/shard_map/ppermute | solution.py:186
  104.3 0.8 shard_map.76.placed
  105.1 15.5 %all-to-all-done.1 = bf16[32,16,1024]{2,1,0:T(8,128)(2,1)} async-done(((bf16[32,16,1024]{2,1,0:T(8,128)(2,1)}), bf16[32,16,1024]{2,1,0:T(8,128)(2,1)}, u32[]{:S(2)}, u32[]{:S(2)}) %all-to-all-start.1) | async-done | bytes 1048608 | tf_op jit(solution)/shard_map/all_to_all | solution.py:231
  120.7 4.8 %shard_map.77 = bf16[512,512]{1,0:T(8,128)(2,1)S(1)} custom-call(bf16[512,1024]{1,0:T(8,128)(2,1)} %bitcast.6.middle, f32[1,1024]{1,0:T(1,128)S(1)} %bitcast.37, bf16[4,2,2,64,1536]{4,3,2,1,0:T(8,128)(2,1)S(1)} %shard_map.76.placed), custom_call_target="tpu_custom_call" | custom-call | flops 4000000000 | bytes 4194304 | tf_op jit(solution)/shard_map/pallas_call | solution.py:170
  126.3 4.4 %all-to-all-start.2 = ((bf16[32,16,512]{2,1,0:T(8,128)(2,1)}), bf16[32,16,512]{2,1,0:T(8,128)(2,1)S(1)}, u32[]{:S(2)}, u32[]{:S(2)}) async-start(bf16[32,16,512]{2,1,0:T(8,128)(2,1)} %bitcast.33), calls=%async_computation.2 | async-start | bytes 1048576 | tf_op jit(solution)/shard_map/all_to_all | solution.py:231
  130.8 2.8 %collective-permute-start.5 = (bf16[4,32,1024]{2,1,0:T(8,128)(2,1)S(1)}, bf16[4,32,1024]{2,1,0:T(8,128)(2,1)S(1)}, u32[]{:S(2)}, u32[]{:S(2)}) collective-permute-start(bf16[4,32,1024]{2,1,0:T(8,128)(2,1)S(1)} %bitcast.28), channel_id=1, source_target_pairs={{0,64},{32,96},{64,0},{96,32},{128,192},{160,224},{192,128},{224,1... | collective-permute-start | bytes 786440 | tf_op jit(solution)/shard_map/ppermute | solution.py:186
  133.6 8.0 %collective-permute-done.5.refs_2_ = bf16[4,32,1024]{2,1,0:T(8,128)(2,1)S(1)} collective-permute-done((bf16[4,32,1024]{2,1,0:T(8,128)(2,1)S(1)}, bf16[4,32,1024]{2,1,0:T(8,128)(2,1)S(1)}, u32[]{:S(2)}, u32[]{:S(2)}) %collective-permute-start.5) | collective-permute-done | bytes 262176 | tf_op jit(solution)/shard_map/ppermute | solution.py:186
  141.6 1.9 %collective-permute-start.6 = (bf16[2,4,32,1024]{3,2,1,0:T(8,128)(2,1)S(1)}, bf16[2,4,32,1024]{3,2,1,0:T(8,128)(2,1)S(1)}, u32[]{:S(2)}, u32[]{:S(2)}) collective-permute-start(bf16[2,4,32,1024]{3,2,1,0:T(8,128)(2,1)S(1)} %pad_maximum_fusion), channel_id=1, source_target_pairs={{0,32},{32,0},{64,96},{96,64},{128,160},{160,128},{192,224},{224,1... | collective-permute-start | bytes 1572872 | tf_op jit(solution)/shard_map/ppermute | solution.py:186
  143.5 1.3 shard_map.78
  146.2 18.3 %all-to-all-done.2 = bf16[32,16,512]{2,1,0:T(8,128)(2,1)S(1)} async-done(((bf16[32,16,512]{2,1,0:T(8,128)(2,1)}), bf16[32,16,512]{2,1,0:T(8,128)(2,1)S(1)}, u32[]{:S(2)}, u32[]{:S(2)}) %all-to-all-start.2) | async-done | bytes 524320 | tf_op jit(solution)/shard_map/all_to_all | solution.py:231
  164.4 1.7 %add_convert_fusion = bf16[512,1024]{1,0:T(8,128)(2,1)} fusion(bf16[512,1024]{1,0:T(8,128)(2,1)S(1)} %shard_map.78, bf16[512,512]{1,0:T(8,128)(2,1)S(1)} %bitcast.38, bf16[512,1024]{1,0:T(8,128)(2,1)S(1)} %bitcast.31), kind=kOutput, calls=%fused_computation | convolution fusion | flops 538443776 | bytes 3670016 | tf_op jit(solution)/shard_map/dot_general | solution.py:288
  (23 shorter events, 2.4 us)
Async XLA Ops:
  2.4 34.1 %copy-start.1 = (bf16[2,1,256,1024]{3,2,1,0:T(8,128)(2,1)S(1)}, bf16[2,1,256,1024]{3,2,1,0:T(8,128)(2,1)}, u32[]{:S(2)}) copy-start(bf16[2,1,256,1024]{3,2,1,0:T(8,128)(2,1)} %param.7) | copy-start | bytes 3145732
  2.4 34.1 %copy-start.2 = (f32[1024]{0:T(1024)S(1)}, f32[1024]{0:T(1024)}, u32[]{:S(2)}) copy-start(f32[1024]{0:T(1024)} %param.8) | copy-start | bytes 12292
  34.5 6.2 %collective-permute-start = (bf16[8,64,2048]{2,1,0:T(8,128)(2,1)S(1)}, bf16[8,64,2048]{2,1,0:T(8,128)(2,1)}, u32[]{:S(2)}, u32[]{:S(2)}) collective-permute-start(bf16[8,64,2048]{2,1,0:T(8,128)(2,1)S(1)} %all_to_all.15.weights.mine), channel_id=1, source_target_pairs={{0,32},{32,0},{64,96},{96,64},{128,160},{160,128},{192,224},{224,1... | collective-permute-start | bytes 6291464 | tf_op jit(solution)/shard_map/ppermute | solution.py:186
  46.5 17.9 %copy-start.4 = (bf16[64,1536]{1,0:T(8,128)(2,1)S(1)}, bf16[64,1536]{1,0:T(8,128)(2,1)}, u32[]{:S(2)}) copy-start(bf16[64,1536]{1,0:T(8,128)(2,1)} %param.12) | copy-start | bytes 589828
  46.5 41.3 %copy-start.5 = (bf16[32,1024]{1,0:T(8,128)(2,1)S(1)}, bf16[32,1024]{1,0:T(8,128)(2,1)}, u32[]{:S(2)}) copy-start(bf16[32,1024]{1,0:T(8,128)(2,1)} %param.13) | copy-start | bytes 196612
  46.5 74.2 %all-to-all-start.1 = ((bf16[32,16,1024]{2,1,0:T(8,128)(2,1)}), bf16[32,16,1024]{2,1,0:T(8,128)(2,1)}, u32[]{:S(2)}, u32[]{:S(2)}) async-start(bf16[32,16,1024]{2,1,0:T(8,128)(2,1)} %bitcast.5), calls=%async_computation.1 | async-start | bytes 2097152 | tf_op jit(solution)/shard_map/all_to_all | solution.py:231
  78.5 21.6 %collective-permute-start.1 = (bf16[2,64,1536]{2,1,0:T(8,128)(2,1)S(1)}, bf16[2,64,1536]{2,1,0:T(8,128)(2,1)S(1)}, u32[]{:S(2)}, u32[]{:S(2)}) collective-permute-start(bf16[2,64,1536]{2,1,0:T(8,128)(2,1)S(1)} %bitcast.40), channel_id=1, source_target_pairs={{0,64},{1,65},{2,66},{3,67},{4,68},{5,69},{6,70},{7,71},{8,72},{9,... | collective-permute-start | bytes 1179656 | tf_op jit(solution)/shard_map/ppermute | solution.py:202
  81.3 18.7 %collective-permute-start.2 = (bf16[2,64,1536]{2,1,0:T(8,128)(2,1)S(1)}, bf16[2,64,1536]{2,1,0:T(8,128)(2,1)S(1)}, u32[]{:S(2)}, u32[]{:S(2)}) collective-permute-start(bf16[2,64,1536]{2,1,0:T(8,128)(2,1)S(1)} %bitcast.39), channel_id=1, source_target_pairs={{0,80},{1,81},{2,82},{3,83},{4,84},{5,85},{6,86},{7,87},{8,88},{9,... | collective-permute-start | bytes 1179656 | tf_op jit(solution)/shard_map/ppermute | solution.py:202
  85.9 16.2 %collective-permute-start.3 = (bf16[4,64,1536]{2,1,0:T(8,128)(2,1)S(1)}, bf16[4,64,1536]{2,1,0:T(8,128)(2,1)S(1)}, u32[]{:S(2)}, u32[]{:S(2)}) collective-permute-start(bf16[4,64,1536]{2,1,0:T(8,128)(2,1)S(1)} %bitcast.26), channel_id=1, source_target_pairs={{0,32},{32,0},{64,96},{96,64},{128,160},{160,128},{192,224},{224,1... | collective-permute-start | bytes 2359304 | tf_op jit(solution)/shard_map/ppermute | solution.py:186
  100.1 20.6 %copy-start.3 = (f32[1024]{0:T(1024)S(1)}, f32[1024]{0:T(1024)}, u32[]{:S(2)}) copy-start(f32[1024]{0:T(1024)} %param.11) | copy-start | bytes 12292
  100.1 4.2 %collective-permute-start.4 = (bf16[4,64,1536]{2,1,0:T(8,128)(2,1)S(1)}, bf16[4,64,1536]{2,1,0:T(8,128)(2,1)S(1)}, u32[]{:S(2)}, u32[]{:S(2)}) collective-permute-start(bf16[4,64,1536]{2,1,0:T(8,128)(2,1)S(1)} %constant_dynamic-update-slice_fusion.refs_2_), channel_id=1, source_target_pairs={{0,32},{32,0},{64,96},{96,64},{128,160},{160,128},{192,224},{224,1... | collective-permute-start | bytes 2359304 | tf_op jit(solution)/shard_map/ppermute | solution.py:186
  125.5 0.8 copy-start
  126.3 38.1 %all-to-all-start.2 = ((bf16[32,16,512]{2,1,0:T(8,128)(2,1)}), bf16[32,16,512]{2,1,0:T(8,128)(2,1)S(1)}, u32[]{:S(2)}, u32[]{:S(2)}) async-start(bf16[32,16,512]{2,1,0:T(8,128)(2,1)} %bitcast.33), calls=%async_computation.2 | async-start | bytes 1048576 | tf_op jit(solution)/shard_map/all_to_all | solution.py:231
  130.8 10.8 %collective-permute-start.5 = (bf16[4,32,1024]{2,1,0:T(8,128)(2,1)S(1)}, bf16[4,32,1024]{2,1,0:T(8,128)(2,1)S(1)}, u32[]{:S(2)}, u32[]{:S(2)}) collective-permute-start(bf16[4,32,1024]{2,1,0:T(8,128)(2,1)S(1)} %bitcast.28), channel_id=1, source_target_pairs={{0,64},{32,96},{64,0},{96,32},{128,192},{160,224},{192,128},{224,1... | collective-permute-start | bytes 786440 | tf_op jit(solution)/shard_map/ppermute | solution.py:186
  141.6 3.8 %collective-permute-start.6 = (bf16[2,4,32,1024]{3,2,1,0:T(8,128)(2,1)S(1)}, bf16[2,4,32,1024]{3,2,1,0:T(8,128)(2,1)S(1)}, u32[]{:S(2)}, u32[]{:S(2)}) collective-permute-start(bf16[2,4,32,1024]{3,2,1,0:T(8,128)(2,1)S(1)} %pad_maximum_fusion), channel_id=1, source_target_pairs={{0,32},{32,0},{64,96},{96,64},{128,160},{160,128},{192,224},{224,1... | collective-permute-start | bytes 1572872 | tf_op jit(solution)/shard_map/ppermute | solution.py:186
